TPU v7x, 32 devices: a whole 2x2x4 slice. The times are simulated.
32 devices in a mesh: dp: 4 (over z), seq: 4 (over x, core), tensor: 2 (over y).
Axes of the slice: x: 2, y: 2, z: 4, core: 2. Of those that a mesh axis runs over, the one named last changes fastest.
Arguments:
- tokens: bfloat16 [8, 2048, 1024], P('dp', ('seq', 'tensor')), may hold values from -6 to 6
- cotangent: bfloat16 [8, 2048, 1024], P('dp', ('seq', 'tensor')), may hold values from -6 to 6
- species: int32 [8], P('dp'), may hold values from 0 to 849
- counts: int32 [8], P('dp'), may hold values from 0 to 2048, as said below
- species_scale: float32 [850], replicated, may hold values from 0.5 to 2
- norm1_gain: float32 [1024], P(('dp', 'seq', 'tensor')), may hold values from 0.5 to 1.5
- norm1_bias: float32 [1024], P(('dp', 'seq', 'tensor')), may hold values from -2.5 to 2.5
- w_query: bfloat16 [1024, 1024], P(('dp', 'seq'), 'tensor'), may hold values from -0.1875 to 0.1875
- w_key: bfloat16 [1024, 1024], P(('dp', 'seq'), 'tensor'), may hold values from -0.1875 to 0.1875
- w_value: bfloat16 [1024, 1024], P(('dp', 'seq'), 'tensor'), may hold values from -0.1875 to 0.1875
- w_out: bfloat16 [1024, 1024], P('tensor', ('dp', 'seq')), may hold values from -6 to 6
- norm2_gain: float32 [1024], P(('dp', 'seq', 'tensor')), may hold values from 0.5 to 1.5
- norm2_bias: float32 [1024], P(('dp', 'seq', 'tensor')), may hold values from -2.5 to 2.5
- w_gate: bfloat16 [1024, 4096], P(('dp', 'seq'), 'tensor'), may hold values from -0.1875 to 0.1875
- w_up: bfloat16 [1024, 4096], P(('dp', 'seq'), 'tensor'), may hold values from -0.1875 to 0.1875
- w_down: bfloat16 [4096, 1024], P('tensor', ('dp', 'seq')), may hold values from -0.09375 to 0.09375
Outputs:
- output: bfloat16 [8, 2048, 1024], P('dp', ('seq', 'tensor'))
- input_grad: float32 [8, 2048, 1024], P('dp', ('seq', 'tensor'))
- grad_norm1_gain: float32 [1024], P(('dp', 'seq', 'tensor'))
- grad_norm1_bias: float32 [1024], P(('dp', 'seq', 'tensor'))
- grad_query: float32 [1024, 1024], P(('dp', 'seq'), 'tensor')
- grad_key: float32 [1024, 1024], P(('dp', 'seq'), 'tensor')
- grad_value: float32 [1024, 1024], P(('dp', 'seq'), 'tensor')
- grad_out: float32 [1024, 1024], P('tensor', ('dp', 'seq'))
- grad_norm2_gain: float32 [1024], P(('dp', 'seq', 'tensor'))
- grad_norm2_bias: float32 [1024], P(('dp', 'seq', 'tensor'))
- grad_gate: float32 [1024, 4096], P(('dp', 'seq'), 'tensor')
- grad_up: float32 [1024, 4096], P(('dp', 'seq'), 'tensor')
- grad_down: float32 [4096, 1024], P('tensor', ('dp', 'seq'))
Inputs may be any that keep to these rules, and one draw needn't show every extreme that they name: `counts`: A slot of count 0 is padding. Within the 2 slots of one index of dp the live slots come first, and there is at least one.
All inputs are finite; a program needn't handle non-finite values.
Results may differ from a plain program's by a relative error of at most 0.019.
Values may be sent and summed in bfloat16 or wider, within the bound.
A program may use at most 320 MiB of HBM per device.

v0:
```python
import math

import jax
import jax.numpy as jnp
from jax import lax
from jax.sharding import PartitionSpec as P

HEAD_DIM = 64


EPSILON = 1e-05
ROPE_BASE = 10000.0


def rotate(matrix, cosine_table, sine_table):
    row_count, head_cols = matrix.shape
    half_dim = cosine_table.shape[1]
    halves = matrix.reshape(row_count, head_cols // (2 * half_dim), 2, half_dim)
    first_half = halves[:, :, 0, :]
    second_half = halves[:, :, 1, :]
    cos_wide = cosine_table[:, None, :]
    sin_wide = sine_table[:, None, :]
    turned = jnp.stack(
        [
            first_half * cos_wide - second_half * sin_wide,
            second_half * cos_wide + first_half * sin_wide,
        ],
        axis=2,
    )
    return turned.reshape(row_count, head_cols)


def angles(positions, head_dim):
    half_dim = head_dim // 2
    inverse = jnp.exp(
        -(math.log(ROPE_BASE) * 2.0 / head_dim) * jnp.arange(half_dim, dtype=jnp.float32)
    )
    phase_angle = positions[:, None] * inverse[None, :]
    return (jnp.cos(phase_angle), jnp.sin(phase_angle))


def layer_norm(stream, norm_gain, norm_bias):
    row_mean = jnp.mean(stream, axis=-1, keepdims=True)
    centred = stream - row_mean
    variance = jnp.mean(centred * centred, axis=-1, keepdims=True)
    inv_std = lax.rsqrt(variance + EPSILON)
    normed = centred * inv_std
    return (normed, inv_std, normed * norm_gain + norm_bias)


def norm_back(grad_normed, normed, inv_std, norm_gain):
    scaled_grad = grad_normed * norm_gain
    return inv_std * (
        scaled_grad
        - jnp.mean(scaled_grad, axis=-1, keepdims=True)
        - normed * jnp.mean(scaled_grad * normed, axis=-1, keepdims=True)
    )


def contract_rows(left_matrix, right_matrix):
    return lax.dot_general(
        left_matrix, right_matrix, (((0,), (0,)), ((), ())), preferred_element_type=jnp.float32
    )


def times_transposed(left_matrix, right_matrix):
    return lax.dot_general(
        left_matrix, right_matrix, (((1,), (1,)), ((), ())), preferred_element_type=jnp.float32
    )


def local(
    tokens,
    cotangent,
    species,
    counts,
    species_scale,
    norm1_gain,
    norm1_bias,
    w_query,
    w_key,
    w_value,
    w_out,
    norm2_gain,
    norm2_bias,
    w_gate,
    w_up,
    w_down,
):
    windows_here, own_rows, model_width = tokens.shape
    block_rows = own_rows * lax.axis_size("tensor")
    window_rows = block_rows * lax.axis_size("seq")
    head_cols = w_query.shape[1]
    hidden_cols = w_gate.shape[1]
    head_dim = HEAD_DIM
    heads_here = head_cols // head_dim
    score_scale = 1.0 / math.sqrt(head_dim)
    wq_full, wk_full, wv_full, wg_full, wu_full = (
        lax.all_gather(w_query, ("dp", "seq"), axis=0, tiled=True),
        lax.all_gather(w_key, ("dp", "seq"), axis=0, tiled=True),
        lax.all_gather(w_value, ("dp", "seq"), axis=0, tiled=True),
        lax.all_gather(w_gate, ("dp", "seq"), axis=0, tiled=True),
        lax.all_gather(w_up, ("dp", "seq"), axis=0, tiled=True),
    )
    wo_full, wd_full = (
        lax.all_gather(w_out, ("dp", "seq"), axis=1, tiled=True),
        lax.all_gather(w_down, ("dp", "seq"), axis=1, tiled=True),
    )
    gain_one, bias_one, gain_two, bias_two = (
        lax.all_gather(norm1_gain, ("dp", "seq", "tensor"), axis=0, tiled=True),
        lax.all_gather(norm1_bias, ("dp", "seq", "tensor"), axis=0, tiled=True),
        lax.all_gather(norm2_gain, ("dp", "seq", "tensor"), axis=0, tiled=True),
        lax.all_gather(norm2_bias, ("dp", "seq", "tensor"), axis=0, tiled=True),
    )
    w_qkv = jnp.concatenate([wq_full, wk_full, wv_full], axis=1)
    w_pair = jnp.concatenate([wg_full, wu_full], axis=1)
    positions = (lax.axis_index("seq") * block_rows + lax.iota(jnp.int32, block_rows)).astype(
        jnp.float32
    )
    cosine_table, sine_table = angles(positions, head_dim)
    labels = lax.broadcasted_iota(jnp.int32, (windows_here, species_scale.shape[0]), 1)
    chosen = jnp.sum(jnp.where(species[:, None] == labels, species_scale[None, :], 0.0), axis=1)
    weighted = counts.astype(jnp.float32) * chosen
    weight_total = lax.psum(jnp.sum(weighted), "dp")
    factor = weighted * float(windows_here * lax.axis_size("dp")) / weight_total

    def full_rows(matrix):
        return lax.all_gather(matrix, "tensor", axis=0, tiled=True)

    def rows_times(left_matrix, right_matrix, transpose_right):

        def row_term():
            if transpose_right:
                return times_transposed(left_matrix, right_matrix)
            return jnp.dot(left_matrix, right_matrix, preferred_element_type=jnp.float32)

        return lax.psum_scatter(row_term(), "tensor", scatter_dimension=0, tiled=True)

    def share_keys(normed_rows):
        qkv_rows = jnp.dot(normed_rows, w_qkv, preferred_element_type=jnp.float32)
        queries = rotate(qkv_rows[:, :head_cols], cosine_table, sine_table).astype(jnp.bfloat16)
        key_rows = rotate(qkv_rows[:, head_cols : 2 * head_cols], cosine_table, sine_table).astype(
            jnp.bfloat16
        )
        value_rows = qkv_rows[:, 2 * head_cols :].astype(jnp.bfloat16)
        all_keys, all_values = (
            lax.all_gather(key_rows, "seq", axis=0, tiled=True),
            lax.all_gather(value_rows, "seq", axis=0, tiled=True),
        )
        return (queries, all_keys, all_values)

    def split_heads(matrix):
        return matrix.reshape(matrix.shape[0], heads_here, head_dim)

    def scores_of(queries, all_keys):
        return (
            jnp.einsum(
                "qhd,khd->hqk",
                split_heads(queries),
                split_heads(all_keys),
                preferred_element_type=jnp.float32,
            )
            * score_scale
        )

    def mix_rows(weights, all_values):
        mixed = jnp.einsum(
            "hqk,khd->qhd", weights, split_heads(all_values), preferred_element_type=jnp.float32
        )
        return mixed.reshape(weights.shape[1], head_cols)

    def forward_window(state_carry, x_rows):
        stream = x_rows.astype(jnp.float32)
        normed_in = layer_norm(stream, gain_one, bias_one)[2]
        gathered_in = full_rows(normed_in.astype(jnp.bfloat16))
        queries, all_keys, all_values = share_keys(gathered_in)
        scores = scores_of(queries, all_keys)
        row_top = jnp.max(scores, axis=-1, keepdims=True)
        log_totals = row_top + jnp.log(jnp.sum(jnp.exp(scores - row_top), axis=-1, keepdims=True))
        probabilities = jnp.exp(scores - log_totals).astype(jnp.bfloat16)
        attended = mix_rows(probabilities, all_values).astype(jnp.bfloat16)
        middle = stream + rows_times(attended, wo_full, False)
        normed_mid = layer_norm(middle, gain_two, bias_two)[2]
        gathered_mid = full_rows(normed_mid.astype(jnp.bfloat16))
        gate_up = jnp.dot(gathered_mid, w_pair, preferred_element_type=jnp.float32)
        hidden = (jax.nn.silu(gate_up[:, :hidden_cols]) * gate_up[:, hidden_cols:]).astype(
            jnp.bfloat16
        )
        result = middle + rows_times(hidden, wd_full, False)
        kept_rows = ()
        return (state_carry, (result.astype(jnp.bfloat16), middle, log_totals, kept_rows))

    _, (output, middles, log_sums, kept_all) = lax.scan(forward_window, 0, tokens)

    def backward_window(grad_sums, inputs):
        x_rows, cot_rows, window_factor, middle, log_totals, kept_rows = inputs
        g_qkv, g_out, g_pair, g_down, g_gain_one, g_bias_one, g_gain_two, g_bias_two = grad_sums
        stream = x_rows.astype(jnp.float32)
        normed1, inv_std1, normed_in = layer_norm(stream, gain_one, bias_one)
        normed2, inv_std2, normed_mid = layer_norm(middle, gain_two, bias_two)
        gathered_in = full_rows(normed_in.astype(jnp.bfloat16))
        gathered_mid = full_rows(normed_mid.astype(jnp.bfloat16))
        queries, all_keys, all_values = share_keys(gathered_in)
        grad_y = cot_rows.astype(jnp.float32) * window_factor
        grad_y_rows = full_rows(grad_y.astype(jnp.bfloat16))
        gate_up = jnp.dot(gathered_mid, w_pair, preferred_element_type=jnp.float32)
        gate_values = gate_up[:, :hidden_cols]
        up_values = gate_up[:, hidden_cols:]
        sigmoid_gate = jax.nn.sigmoid(gate_values)
        swish = gate_values * sigmoid_gate
        hidden = (swish * up_values).astype(jnp.bfloat16)
        grad_hidden = times_transposed(grad_y_rows, wd_full)
        grad_pair = jnp.concatenate(
            [
                grad_hidden * up_values * sigmoid_gate * (1.0 + gate_values * (1.0 - sigmoid_gate)),
                grad_hidden * swish,
            ],
            axis=1,
        ).astype(jnp.bfloat16)
        grad_normed2 = rows_times(grad_pair, w_pair, True)
        grad_middle = grad_y + norm_back(grad_normed2, normed2, inv_std2, gain_two)
        grad_mid_rows = full_rows(grad_middle.astype(jnp.bfloat16))
        grad_attended = times_transposed(grad_mid_rows, wo_full).astype(jnp.bfloat16)
        scores = scores_of(queries, all_keys)
        probabilities = jnp.exp(scores - log_totals)
        probs_low = probabilities.astype(jnp.bfloat16)
        attended = mix_rows(probs_low, all_values).astype(jnp.bfloat16)
        grad_probs = jnp.einsum(
            "qhd,khd->hqk",
            split_heads(grad_attended),
            split_heads(all_values),
            preferred_element_type=jnp.float32,
        )
        grad_scores = (
            probabilities
            * (grad_probs - jnp.sum(probabilities * grad_probs, axis=-1, keepdims=True))
        ).astype(jnp.bfloat16)
        grad_queries = mix_rows(grad_scores, all_keys) * score_scale
        grad_keys = (
            jnp.einsum(
                "hqk,qhd->khd",
                grad_scores,
                split_heads(queries),
                preferred_element_type=jnp.float32,
            ).reshape(window_rows, head_cols)
            * score_scale
        )
        grad_values = jnp.einsum(
            "hqk,qhd->khd",
            probs_low,
            split_heads(grad_attended),
            preferred_element_type=jnp.float32,
        ).reshape(window_rows, head_cols)
        own_keys, own_values = (
            lax.psum_scatter(
                grad_keys.astype(jnp.bfloat16), "seq", scatter_dimension=0, tiled=True
            ).astype(jnp.float32),
            lax.psum_scatter(
                grad_values.astype(jnp.bfloat16), "seq", scatter_dimension=0, tiled=True
            ).astype(jnp.float32),
        )
        grad_qkv = jnp.concatenate(
            [
                rotate(grad_queries, cosine_table, -sine_table),
                rotate(own_keys, cosine_table, -sine_table),
                own_values,
            ],
            axis=1,
        ).astype(jnp.bfloat16)
        grad_normed1 = rows_times(grad_qkv, w_qkv, True)
        grad_x = grad_middle + norm_back(grad_normed1, normed1, inv_std1, gain_one)
        new_sums = (
            g_qkv + contract_rows(gathered_in, grad_qkv),
            g_out + contract_rows(attended, grad_mid_rows),
            g_pair + contract_rows(gathered_mid, grad_pair),
            g_down + contract_rows(hidden, grad_y_rows),
            g_gain_one + jnp.sum(grad_normed1 * normed1, axis=0),
            g_bias_one + jnp.sum(grad_normed1, axis=0),
            g_gain_two + jnp.sum(grad_normed2 * normed2, axis=0),
            g_bias_two + jnp.sum(grad_normed2, axis=0),
        )
        return (new_sums, grad_x)

    zero_grads = (
        jnp.zeros((model_width, 3 * head_cols), jnp.float32),
        jnp.zeros((head_cols, model_width), jnp.float32),
        jnp.zeros((model_width, 2 * hidden_cols), jnp.float32),
        jnp.zeros((hidden_cols, model_width), jnp.float32),
        jnp.zeros((model_width,), jnp.float32),
        jnp.zeros((model_width,), jnp.float32),
        jnp.zeros((model_width,), jnp.float32),
        jnp.zeros((model_width,), jnp.float32),
    )
    final_sums, input_grad = lax.scan(
        backward_window, zero_grads, (tokens, cotangent, factor, middles, log_sums, kept_all)
    )
    g_qkv, g_out, g_pair, g_down, g_gain_one, g_bias_one, g_gain_two, g_bias_two = final_sums
    grad_query, grad_key, grad_value, grad_gate, grad_up = (
        lax.psum_scatter(
            g_qkv[:, :head_cols].astype(jnp.bfloat16),
            ("dp", "seq"),
            scatter_dimension=0,
            tiled=True,
        ).astype(jnp.float32),
        lax.psum_scatter(
            g_qkv[:, head_cols : 2 * head_cols].astype(jnp.bfloat16),
            ("dp", "seq"),
            scatter_dimension=0,
            tiled=True,
        ).astype(jnp.float32),
        lax.psum_scatter(
            g_qkv[:, 2 * head_cols :].astype(jnp.bfloat16),
            ("dp", "seq"),
            scatter_dimension=0,
            tiled=True,
        ).astype(jnp.float32),
        lax.psum_scatter(
            g_pair[:, :hidden_cols].astype(jnp.bfloat16),
            ("dp", "seq"),
            scatter_dimension=0,
            tiled=True,
        ).astype(jnp.float32),
        lax.psum_scatter(
            g_pair[:, hidden_cols:].astype(jnp.bfloat16),
            ("dp", "seq"),
            scatter_dimension=0,
            tiled=True,
        ).astype(jnp.float32),
    )
    grad_out, grad_down = (
        lax.psum_scatter(
            g_out.astype(jnp.bfloat16), ("dp", "seq"), scatter_dimension=1, tiled=True
        ).astype(jnp.float32),
        lax.psum_scatter(
            g_down.astype(jnp.bfloat16), ("dp", "seq"), scatter_dimension=1, tiled=True
        ).astype(jnp.float32),
    )
    grad_gain_one, grad_bias_one, grad_gain_two, grad_bias_two = (
        lax.psum_scatter(g_gain_one, ("dp", "seq", "tensor"), scatter_dimension=0, tiled=True),
        lax.psum_scatter(g_bias_one, ("dp", "seq", "tensor"), scatter_dimension=0, tiled=True),
        lax.psum_scatter(g_gain_two, ("dp", "seq", "tensor"), scatter_dimension=0, tiled=True),
        lax.psum_scatter(g_bias_two, ("dp", "seq", "tensor"), scatter_dimension=0, tiled=True),
    )
    return (
        output,
        input_grad,
        grad_gain_one,
        grad_bias_one,
        grad_query,
        grad_key,
        grad_value,
        grad_out,
        grad_gain_two,
        grad_bias_two,
        grad_gate,
        grad_up,
        grad_down,
    )


def solution(mesh):
    placed = (
        P("dp", ("seq", "tensor"), None),
        P("dp", ("seq", "tensor"), None),
        P("dp"),
        P("dp"),
        P(),
        P(("dp", "seq", "tensor")),
        P(("dp", "seq", "tensor")),
        P(("dp", "seq"), "tensor"),
        P(("dp", "seq"), "tensor"),
        P(("dp", "seq"), "tensor"),
        P("tensor", ("dp", "seq")),
        P(("dp", "seq", "tensor")),
        P(("dp", "seq", "tensor")),
        P(("dp", "seq"), "tensor"),
        P(("dp", "seq"), "tensor"),
        P("tensor", ("dp", "seq")),
    )
    return jax.shard_map(
        local,
        mesh=mesh,
        in_specs=placed,
        out_specs=(
            P("dp", ("seq", "tensor"), None),
            P("dp", ("seq", "tensor"), None),
            P(("dp", "seq", "tensor")),
            P(("dp", "seq", "tensor")),
            P(("dp", "seq"), "tensor"),
            P(("dp", "seq"), "tensor"),
            P(("dp", "seq"), "tensor"),
            P("tensor", ("dp", "seq")),
            P(("dp", "seq", "tensor")),
            P(("dp", "seq", "tensor")),
            P(("dp", "seq"), "tensor"),
            P(("dp", "seq"), "tensor"),
            P("tensor", ("dp", "seq")),
        ),
        check_vma=False,
    )
```

profile of v0, /device:TPU:0, one launch (start us, length us, event | category | flops | bytes accessed | tf_op | source)
XLA Modules:
  0.0 1932.3 jit_solution(4605155990200066206)
XLA Ops:
  14.1 14.2 psum.7
  31.6 38.1 %all-reduce.9 = (f32[1024]{0:T(1024)S(1)}, f32[1024]{0:T(1024)S(1)}, f32[1024]{0:T(1024)S(1)}, f32[1024]{0:T(1024)}) all-reduce(f32[1024]{0:T(1024)S(1)} %dynamic-update-slice, f32[1024]{0:T(1024)S(1)} %dynamic-update-slice.1, f32[1024]{0:T(1024)S(1)} %dynamic-update-slice.2, ...), channel_id=1, replica_groups=mesh['dp'=4,'seq'=4,'tensor'=2] {'dp','seq','tensor'}, use_global_device_ids=true, to_apply=%add | all-reduce | flops 4096 | bytes 32768
  74.4 15.6 all-gather.18.cloned.1.call-done
  91.3 37.8 %all-gather.20.cloned.1.call-done = bf16[1024,512]{1,0:T(8,128)(2,1)} async-done(((bf16[64,512]{1,0:T(8,128)(2,1)}), bf16[1024,512]{1,0:T(8,128)(2,1)}) %all-gather.20.cloned.1.call-update) | async-done | bytes 1048592 | tf_op jit(solution)/shard_map/all_gather | solution.py:100
  130.4 37.6 %all-gather.22.cloned.1.call-done = bf16[1024,512]{1,0:T(8,128)(2,1)} async-done(((bf16[64,512]{1,0:T(8,128)(2,1)}), bf16[1024,512]{1,0:T(8,128)(2,1)}) %all-gather.22.cloned.1.call-update) | async-done | bytes 1048592 | tf_op jit(solution)/shard_map/all_gather | solution.py:101
  169.3 50.2 %all-gather.30.cloned.1.call-done = bf16[2048,1024]{0,1:T(8,128)(2,1)} async-done(((bf16[2048,64]{0,1:T(8,128)(2,1)}), bf16[2048,1024]{0,1:T(8,128)(2,1)}) %all-gather.30.cloned.1.call-update) | async-done | bytes 4194320 | tf_op jit(solution)/shard_map/all_gather | solution.py:107
  225.9 44.7 %all-gather.26.cloned.1.call-done = bf16[1024,2048]{1,0:T(8,128)(2,1)} async-done(((bf16[64,2048]{1,0:T(8,128)(2,1)}), bf16[1024,2048]{1,0:T(8,128)(2,1)}) %all-gather.26.cloned.1.call-update) | async-done | bytes 4194320 | tf_op jit(solution)/shard_map/all_gather | solution.py:102
  275.3 46.5 %all-gather.28.cloned.1.call-done = bf16[1024,2048]{1,0:T(8,128)(2,1)} async-done(((bf16[64,2048]{1,0:T(8,128)(2,1)}), bf16[1024,2048]{1,0:T(8,128)(2,1)}) %all-gather.28.cloned.1.call-update) | async-done | bytes 4194320 | tf_op jit(solution)/shard_map/all_gather | solution.py:103
  328.2 417.6 %while.46 = (s32[]{:T(128)}, bf16[2,256,1024]{2,1,0:T(8,128)(2,1)}, f32[2,256,1024]{2,1,0:T(8,128)}, f32[2,8,512,1]{2,1,3,0:T(8,128)}, bf16[2,256,1024]{2,1,0:T(...) while((s32[]{:T(128)}, bf16[2,256,1024]{2,1,0:T(8,128)(2,1)}, ...), condition=%wide.region_9.10_spmd.clone.clone, body=%wide.region_0.9_spmd.clone.clone.sunk | while | flops 10820268032 | bytes 267047664 | solution.py:193
  331.0 20.2 %all-gather.32.cloned.1.call-done = bf16[512,1024]{1,0:T(8,128)(2,1)} async-done(((bf16[256,1024]{1,0:T(8,128)(2,1)}), bf16[512,1024]{1,0:T(8,128)(2,1)}) %all-gather.32.cloned.1.call-update) | async-done | bytes 1048592 | tf_op jit(solution)/shard_map/while/body/eval_jaxpr/all_gather | solution.py:128
  364.2 19.5 %all-gather.36.cloned.1.call-done = bf16[2048,512]{0,1:T(8,128)(2,1)} async-done(((bf16[512,512]{0,1:T(8,128)(2,1)}), bf16[2048,512]{0,1:T(8,128)(2,1)}) %all-gather.36.cloned.1.call-update) | async-done | bytes 2097168 | tf_op jit(solution)/shard_map/while/body/eval_jaxpr/all_gather | solution.py:147
  383.7 15.4 multiply_reduce_fusion.13
  399.1 14.1 exponential_reduce_fusion.2
  417.2 14.3 fusion.186
  433.7 31.9 %reduce-scatter.28.cloned.1.call-done = f32[256,1024]{1,0:T(8,128)} async-done(((f32[512,1024]{1,0:T(8,128)}), f32[256,1024]{1,0:T(8,128)}) %reduce-scatter.28.cloned.1.call-update) | async-done | bytes 1048592 | tf_op jit(solution)/shard_map/while/body/eval_jaxpr/reduce_scatter | solution.py:137
  469.6 21.4 %all-gather.38.cloned.1.call-done = bf16[512,1024]{1,0:T(8,128)(2,1)} async-done(((bf16[256,1024]{1,0:T(8,128)(2,1)}), bf16[512,1024]{1,0:T(8,128)(2,1)}) %all-gather.38.cloned.1.call-update) | async-done | bytes 1048592 | tf_op jit(solution)/shard_map/while/body/eval_jaxpr/all_gather | solution.py:128
  502.2 32.0 %reduce-scatter.30.cloned.1.call-done = f32[256,1024]{1,0:T(8,128)} async-done(((f32[512,1024]{1,0:T(8,128)}), f32[256,1024]{1,0:T(8,128)}) %reduce-scatter.30.cloned.1.call-update) | async-done | bytes 1048592 | tf_op jit(solution)/shard_map/while/body/eval_jaxpr/reduce_scatter | solution.py:137
  539.1 21.5 %all-gather.32.cloned.1.call-done = bf16[512,1024]{1,0:T(8,128)(2,1)} async-done(((bf16[256,1024]{1,0:T(8,128)(2,1)}), bf16[512,1024]{1,0:T(8,128)(2,1)}) %all-gather.32.cloned.1.call-update) | async-done | bytes 1048592 | tf_op jit(solution)/shard_map/while/body/eval_jaxpr/all_gather | solution.py:128
  573.5 19.5 %all-gather.36.cloned.1.call-done = bf16[2048,512]{0,1:T(8,128)(2,1)} async-done(((bf16[512,512]{0,1:T(8,128)(2,1)}), bf16[2048,512]{0,1:T(8,128)(2,1)}) %all-gather.36.cloned.1.call-update) | async-done | bytes 2097168 | tf_op jit(solution)/shard_map/while/body/eval_jaxpr/all_gather | solution.py:147
  593.0 15.4 multiply_reduce_fusion.13
  608.4 14.1 exponential_reduce_fusion.2
  626.5 14.3 fusion.186
  643.0 31.9 %reduce-scatter.28.cloned.1.call-done = f32[256,1024]{1,0:T(8,128)} async-done(((f32[512,1024]{1,0:T(8,128)}), f32[256,1024]{1,0:T(8,128)}) %reduce-scatter.28.cloned.1.call-update) | async-done | bytes 1048592 | tf_op jit(solution)/shard_map/while/body/eval_jaxpr/reduce_scatter | solution.py:137
  679.0 21.4 %all-gather.38.cloned.1.call-done = bf16[512,1024]{1,0:T(8,128)(2,1)} async-done(((bf16[256,1024]{1,0:T(8,128)(2,1)}), bf16[512,1024]{1,0:T(8,128)(2,1)}) %all-gather.38.cloned.1.call-update) | async-done | bytes 1048592 | tf_op jit(solution)/shard_map/while/body/eval_jaxpr/all_gather | solution.py:128
  711.5 32.0 %reduce-scatter.30.cloned.1.call-done = f32[256,1024]{1,0:T(8,128)} async-done(((f32[512,1024]{1,0:T(8,128)}), f32[256,1024]{1,0:T(8,128)}) %reduce-scatter.30.cloned.1.call-update) | async-done | bytes 1048592 | tf_op jit(solution)/shard_map/while/body/eval_jaxpr/reduce_scatter | solution.py:137
  747.4 707.1 %while.47 = (s32[]{:T(128)}, f32[1024,1536]{1,0:T(8,128)}, f32[512,1024]{1,0:T(8,128)}, f32[1024,4096]{1,0:T(8,128)}, f32[2048,1024]{1,0:T(8,128)}, /*index=5*/f...) while((s32[]{:T(128)}, f32[1024,1536]{1,0:T(8,128)}, ...), condition=%wide.region_31.32_spmd.clone.clone.clone, body=%wide.region_13.31_spmd.clone.clone.clone.sunk | while | flops 29742645248 | bytes 625523968 | solution.py:294
  756.8 14.9 all-gather.40.cloned.1.call-done
  778.7 16.6 all-gather.42.cloned.1.call-done
  795.3 11.5 fusion.220
  806.7 12.1 all-gather.44.cloned.1.call-done
  846.6 31.1 %reduce-scatter.32.cloned.1.call-done = f32[256,1024]{1,0:T(8,128)} async-done(((f32[512,1024]{1,0:T(8,128)}), f32[256,1024]{1,0:T(8,128)}) %reduce-scatter.32.cloned.1.call-update) | async-done | bytes 1048592 | tf_op jit(solution)/shard_map/while/body/eval_jaxpr/reduce_scatter | solution.py:137
  883.7 18.7 all-gather.48.cloned.1.call-done
  902.4 15.2 fusion.225
  928.1 22.5 %multiply_reduce_fusion.17 = (f32[8,512]{1,0:T(8,128)S(1)}, f32[8,512,2048]{2,1,0:T(8,128)}) fusion(f32[8,512,2048]{2,1,0:T(8,128)} %fusion.225, f32[8,512]{1,0:T(8,128)S(1)} %dynamic-slice_bitcast_fusion.2, bf16[512,8,64]{0,2,1:T(8,128)(2,1)S(1)} %bitcast.319, bf16[2048,8,64]{0,2,1:T(8,128)(2,1)S(1)} %bitcast.304), kind=kOutput, calls=%fused_computation.47.clone.1 | convolution fusion | flops 1107292160 | bytes 69763072 | tf_op jit(solution)/shard_map/while/body/eval_jaxpr/qhd,khd->hqk/dot_general | solution.py:228
  950.5 27.9 %multiply_convert_fusion.12 = bf16[8,512,2048]{2,1,0:T(8,128)(2,1)} fusion(f32[8,512,2048]{2,1,0:T(8,128)} %get-tuple-element.1177, f32[8,512,2048]{2,1,0:T(8,128)} %fusion.225, f32[8,512]{1,0:T(8,128)S(1)} %get-tuple-element.1178, f32[8,512]{1,0:T(8,128)S(1)} %dynamic-slice_bitcast_fusion.2), kind=kLoop, calls=%fused_computation.46.clone.1 | loop fusion | flops 41943040 | bytes 83918848 | tf_op jit(solution)/shard_map/while/body/eval_jaxpr/convert_element_type | solution.py:237
  978.4 10.1 multiply_convert_fusion.13
  988.6 16.4 convolution_convert_fusion.5
  1006.2 13.0 select_add_fusion.16
  1019.2 11.6 convolution_multiply_fusion.2
  1032.6 21.7 %reduce-scatter.34.cloned.1.call-done = bf16[512,512]{0,1:T(8,128)(2,1)} async-done(((bf16[2048,512]{0,1:T(8,128)(2,1)}), bf16[512,512]{0,1:T(8,128)(2,1)}) %reduce-scatter.34.cloned.1.call-update) | async-done | bytes 524304 | tf_op jit(solution)/shard_map/while/body/eval_jaxpr/reduce_scatter | solution.py:258
  1069.7 13.7 fusion.226
  1105.8 14.9 all-gather.40.cloned.1.call-done
  1127.5 16.8 all-gather.42.cloned.1.call-done
  1144.3 11.5 fusion.220
  1155.7 12.1 all-gather.44.cloned.1.call-done
  1195.7 31.0 %reduce-scatter.32.cloned.1.call-done = f32[256,1024]{1,0:T(8,128)} async-done(((f32[512,1024]{1,0:T(8,128)}), f32[256,1024]{1,0:T(8,128)}) %reduce-scatter.32.cloned.1.call-update) | async-done | bytes 1048592 | tf_op jit(solution)/shard_map/while/body/eval_jaxpr/reduce_scatter | solution.py:137
  1232.7 18.7 all-gather.48.cloned.1.call-done
  1251.4 15.2 fusion.225
  1277.0 22.5 %multiply_reduce_fusion.17 = (f32[8,512]{1,0:T(8,128)S(1)}, f32[8,512,2048]{2,1,0:T(8,128)}) fusion(f32[8,512,2048]{2,1,0:T(8,128)} %fusion.225, f32[8,512]{1,0:T(8,128)S(1)} %dynamic-slice_bitcast_fusion.2, bf16[512,8,64]{0,2,1:T(8,128)(2,1)S(1)} %bitcast.319, bf16[2048,8,64]{0,2,1:T(8,128)(2,1)S(1)} %bitcast.304), kind=kOutput, calls=%fused_computation.47.clone.1 | convolution fusion | flops 1107292160 | bytes 69763072 | tf_op jit(solution)/shard_map/while/body/eval_jaxpr/qhd,khd->hqk/dot_general | solution.py:228
  1299.5 27.9 %multiply_convert_fusion.12 = bf16[8,512,2048]{2,1,0:T(8,128)(2,1)} fusion(f32[8,512,2048]{2,1,0:T(8,128)} %get-tuple-element.1177, f32[8,512,2048]{2,1,0:T(8,128)} %fusion.225, f32[8,512]{1,0:T(8,128)S(1)} %get-tuple-element.1178, f32[8,512]{1,0:T(8,128)S(1)} %dynamic-slice_bitcast_fusion.2), kind=kLoop, calls=%fused_computation.46.clone.1 | loop fusion | flops 41943040 | bytes 83918848 | tf_op jit(solution)/shard_map/while/body/eval_jaxpr/convert_element_type | solution.py:237
  1327.4 10.1 multiply_convert_fusion.13
  1337.6 16.3 convolution_convert_fusion.5
  1355.1 17.8 select_add_fusion.16
  1373.0 12.2 convolution_multiply_fusion.2
  1386.9 16.4 reduce-scatter.34.cloned.1.call-done
  1408.6 12.6 select_add_fusion.17
  1421.1 13.8 fusion.226
  1482.3 39.5 %all-reduce.8 = (f32[1024]{0:T(1024)S(1)}, f32[1024]{0:T(1024)S(1)}, f32[1024]{0:T(1024)S(1)}, f32[1024]{0:T(1024)S(1)}) all-reduce(f32[1024]{0:T(1024)S(1)} %copy-done.40, f32[1024]{0:T(1024)S(1)} %copy-done.37, f32[1024]{0:T(1024)S(1)} %copy-done.34, ...), channel_id=8, replica_groups=mesh['dp'=4,'seq'=4,'tensor'=2] {'dp','seq','tensor'}, use_global_device_ids=true, to_apply=%region_32.33.clone | all-reduce | flops 4096 | bytes 32768
  1525.6 51.5 %reduce-scatter.14.cloned.1.call-done = bf16[64,512]{1,0:T(8,128)(2,1)} async-done(((bf16[1024,512]{1,0:T(8,128)(2,1)}), bf16[64,512]{1,0:T(8,128)(2,1)}) %reduce-scatter.14.cloned.1.call-update) | async-done | bytes 65552 | tf_op jit(solution)/shard_map/reduce_scatter | solution.py:299
  1578.7 58.6 %reduce-scatter.16.cloned.1.call-done = bf16[64,512]{1,0:T(8,128)(2,1)} async-done(((bf16[1024,512]{1,0:T(8,128)(2,1)}), bf16[64,512]{1,0:T(8,128)(2,1)}) %reduce-scatter.16.cloned.1.call-update) | async-done | bytes 65552 | tf_op jit(solution)/shard_map/reduce_scatter | solution.py:305
  1638.7 58.8 %reduce-scatter.18.cloned.1.call-done = bf16[64,512]{1,0:T(8,128)(2,1)} async-done(((bf16[1024,512]{1,0:T(8,128)(2,1)}), bf16[64,512]{1,0:T(8,128)(2,1)}) %reduce-scatter.18.cloned.1.call-update) | async-done | bytes 65552 | tf_op jit(solution)/shard_map/reduce_scatter | solution.py:311
  1699.1 73.9 %reduce-scatter.26.cloned.1.call-done = bf16[2048,64]{0,1:T(8,128)(2,1)} async-done(((bf16[2048,1024]{0,1:T(8,128)(2,1)}), bf16[2048,64]{0,1:T(8,128)(2,1)}) %reduce-scatter.26.cloned.1.call-update) | async-done | bytes 262160 | tf_op jit(solution)/shard_map/reduce_scatter | solution.py:334
  1774.7 73.8 %reduce-scatter.22.cloned.1.call-done = bf16[64,2048]{1,0:T(8,128)(2,1)} async-done(((bf16[1024,2048]{1,0:T(8,128)(2,1)}), bf16[64,2048]{1,0:T(8,128)(2,1)}) %reduce-scatter.22.cloned.1.call-update) | async-done | bytes 262160 | tf_op jit(solution)/shard_map/reduce_scatter | solution.py:317
  1850.3 73.4 %reduce-scatter.24.cloned.1.call-done = bf16[64,2048]{1,0:T(8,128)(2,1)} async-done(((bf16[1024,2048]{1,0:T(8,128)(2,1)}), bf16[64,2048]{1,0:T(8,128)(2,1)}) %reduce-scatter.24.cloned.1.call-update) | async-done | bytes 262160 | tf_op jit(solution)/shard_map/reduce_scatter | solution.py:323
  (456 shorter events, 331.9 us)
Async XLA Ops:
  7.2 65.0 %all-gather.24.cloned.1.call-start = ((), (), s32[]{:S(2)}) async-start(), calls=%async_computation.16 | async-start | bytes 1114112 | tf_op jit(solution)/shard_map/all_gather | solution.py:106
  7.9 82.1 %all-gather.18.cloned.1.call-start = ((), (), s32[]{:S(2)}) async-start(), calls=%async_computation.13 | async-start | bytes 1114112 | tf_op jit(solution)/shard_map/all_gather | solution.py:99
  8.7 120.4 %all-gather.20.cloned.1.call-start = ((), (), s32[]{:S(2)}) async-start(), calls=%async_computation.14 | async-start | bytes 1114112 | tf_op jit(solution)/shard_map/all_gather | solution.py:100
  9.4 158.6 %all-gather.22.cloned.1.call-start = ((), (), s32[]{:S(2)}) async-start(), calls=%async_computation.15 | async-start | bytes 1114112 | tf_op jit(solution)/shard_map/all_gather | solution.py:101
  10.0 209.5 %all-gather.30.cloned.1.call-start = ((), (), s32[]{:S(2)}) async-start(), calls=%async_computation.19 | async-start | bytes 4456448 | tf_op jit(solution)/shard_map/all_gather | solution.py:107
  10.6 260.0 %all-gather.26.cloned.1.call-start = ((), (), s32[]{:S(2)}) async-start(), calls=%async_computation.17 | async-start | bytes 4456448 | tf_op jit(solution)/shard_map/all_gather | solution.py:102
  11.1 310.7 %all-gather.28.cloned.1.call-start = ((), (), s32[]{:S(2)}) async-start(), calls=%async_computation.18 | async-start | bytes 4456448 | tf_op jit(solution)/shard_map/all_gather | solution.py:103
  169.3 56.6 %copy-start.25 = (bf16[1024,1536]{1,0:T(8,128)(2,1)}, bf16[1024,1536]{1,0:T(8,128)(2,1)S(1)}, u32[]{:S(2)}) copy-start(bf16[1024,1536]{1,0:T(8,128)(2,1)S(1)} %constant_dynamic-update-slice_fusion) | copy-start | bytes 9437188
  275.3 52.9 %copy-start = (bf16[2,256,1024]{2,1,0:T(8,128)(2,1)S(1)}, bf16[2,256,1024]{2,1,0:T(8,128)(2,1)}, u32[]{:S(2)}) copy-start(bf16[2,256,1024]{2,1,0:T(8,128)(2,1)} %param.20) | copy-start | bytes 3145732
  328.3 22.9 %all-gather.32.cloned.1.call-start = ((), (), s32[]{:S(2)}) async-start(), calls=%async_computation.27 | async-start | bytes 1572864 | tf_op jit(solution)/shard_map/while/body/eval_jaxpr/all_gather | solution.py:128
  330.0 53.8 %all-gather.36.cloned.1.call-start = ((), (), s32[]{:S(2)}) async-start(), calls=%async_computation.29 | async-start | bytes 2621440 | tf_op jit(solution)/shard_map/while/body/eval_jaxpr/all_gather | solution.py:147
  361.0 52.3 %all-gather.34.cloned.1.call-start = ((), (), s32[]{:S(2)}) async-start(), calls=%async_computation.28 | async-start | bytes 2621440 | tf_op jit(solution)/shard_map/while/body/eval_jaxpr/all_gather | solution.py:148
  363.2 102.5 %reduce-scatter.28.cloned.1.call-start = ((), (), s32[]{:S(2)}) async-start(), calls=%async_computation.30 | async-start | bytes 3145728 | tf_op jit(solution)/shard_map/while/body/eval_jaxpr/reduce_scatter | solution.py:137
  399.1 14.1 copy-start.26
  413.2 18.3 copy-start.27
  417.2 14.4 copy-start.11
  433.6 34.9 %copy-start.21 = (f32[1024]{0:T(1024)S(1)}, f32[1024]{0:T(1024)}, u32[]{:S(2)}) copy-start(f32[1024]{0:T(1024)} %get-tuple-element.1240) | copy-start | bytes 12292 | tf_op jit(solution)/shard_map/while
  433.6 57.4 %all-gather.38.cloned.1.call-start = ((), (), s32[]{:S(2)}) async-start(), calls=%async_computation.31 | async-start | bytes 1572864 | tf_op jit(solution)/shard_map/while/body/eval_jaxpr/all_gather | solution.py:128
  469.6 64.6 %reduce-scatter.30.cloned.1.call-start = ((), (), s32[]{:S(2)}) async-start(), calls=%async_computation.32 | async-start | bytes 3145728 | tf_op jit(solution)/shard_map/while/body/eval_jaxpr/reduce_scatter | solution.py:137
  498.4 35.7 %copy-start.42 = (bf16[2,256,1024]{2,1,0:T(8,128)(2,1)S(1)}, bf16[2,256,1024]{2,1,0:T(8,128)(2,1)}, u32[]{:S(2)}) copy-start(bf16[2,256,1024]{2,1,0:T(8,128)(2,1)} %get-tuple-element.1214) | copy-start | bytes 3145732 | tf_op jit(solution)/shard_map/while
  536.5 24.0 %all-gather.32.cloned.1.call-start = ((), (), s32[]{:S(2)}) async-start(), calls=%async_computation.27 | async-start | bytes 1572864 | tf_op jit(solution)/shard_map/while/body/eval_jaxpr/all_gather | solution.py:128
  538.0 55.0 %all-gather.36.cloned.1.call-start = ((), (), s32[]{:S(2)}) async-start(), calls=%async_computation.29 | async-start | bytes 2621440 | tf_op jit(solution)/shard_map/while/body/eval_jaxpr/all_gather | solution.py:147
  570.3 52.3 %all-gather.34.cloned.1.call-start = ((), (), s32[]{:S(2)}) async-start(), calls=%async_computation.28 | async-start | bytes 2621440 | tf_op jit(solution)/shard_map/while/body/eval_jaxpr/all_gather | solution.py:148
  572.5 102.5 %reduce-scatter.28.cloned.1.call-start = ((), (), s32[]{:S(2)}) async-start(), calls=%async_computation.30 | async-start | bytes 3145728 | tf_op jit(solution)/shard_map/while/body/eval_jaxpr/reduce_scatter | solution.py:137
  608.4 14.1 copy-start.26
  622.6 18.3 copy-start.27
  626.5 14.4 copy-start.11
  642.9 34.9 %copy-start.21 = (f32[1024]{0:T(1024)S(1)}, f32[1024]{0:T(1024)}, u32[]{:S(2)}) copy-start(f32[1024]{0:T(1024)} %get-tuple-element.1240) | copy-start | bytes 12292 | tf_op jit(solution)/shard_map/while
  642.9 57.4 %all-gather.38.cloned.1.call-start = ((), (), s32[]{:S(2)}) async-start(), calls=%async_computation.31 | async-start | bytes 1572864 | tf_op jit(solution)/shard_map/while/body/eval_jaxpr/all_gather | solution.py:128
  678.9 64.6 %reduce-scatter.30.cloned.1.call-start = ((), (), s32[]{:S(2)}) async-start(), calls=%async_computation.32 | async-start | bytes 3145728 | tf_op jit(solution)/shard_map/while/body/eval_jaxpr/reduce_scatter | solution.py:137
  707.7 35.7 %copy-start.42 = (bf16[2,256,1024]{2,1,0:T(8,128)(2,1)S(1)}, bf16[2,256,1024]{2,1,0:T(8,128)(2,1)}, u32[]{:S(2)}) copy-start(bf16[2,256,1024]{2,1,0:T(8,128)(2,1)} %get-tuple-element.1214) | copy-start | bytes 3145732 | tf_op jit(solution)/shard_map/while
  747.7 24.1 %all-gather.40.cloned.1.call-start = ((), (), s32[]{:S(2)}) async-start(), calls=%async_computation.33 | async-start | bytes 1572864 | tf_op jit(solution)/shard_map/while/body/eval_jaxpr/all_gather | solution.py:128
  747.9 27.9 %copy-start.17 = (f32[256]{0:T(256)}, f32[256]{0:T(256)S(1)}, u32[]{:S(2)}) copy-start(f32[256]{0:T(256)S(1)} %broadcast_multiply_fusion.17) | copy-start | bytes 3076 | tf_op jit(solution)/shard_map/while
  749.3 46.0 %all-gather.42.cloned.1.call-start = ((), (), s32[]{:S(2)}) async-start(), calls=%async_computation.34 | async-start | bytes 1572864 | tf_op jit(solution)/shard_map/while/body/eval_jaxpr/all_gather | solution.py:128
  754.5 64.3 %all-gather.44.cloned.1.call-start = ((), (), s32[]{:S(2)}) async-start(), calls=%async_computation.35 | async-start | bytes 1572864 | tf_op jit(solution)/shard_map/while/body/eval_jaxpr/all_gather | solution.py:128
  756.8 86.9 %all-gather.50.cloned.1.call-start = ((), (), s32[]{:S(2)}) async-start(), calls=%async_computation.40 | async-start | bytes 2621440 | tf_op jit(solution)/shard_map/while/body/eval_jaxpr/all_gather | solution.py:148
  778.3 99.4 %reduce-scatter.32.cloned.1.call-start = ((), (), s32[]{:S(2)}) async-start(), calls=%async_computation.36 | async-start | bytes 3145728 | tf_op jit(solution)/shard_map/while/body/eval_jaxpr/reduce_scatter | solution.py:137
  838.5 63.9 %all-gather.48.cloned.1.call-start = ((), (), s32[]{:S(2)}) async-start(), calls=%async_computation.38 | async-start | bytes 2621440 | tf_op jit(solution)/shard_map/while/body/eval_jaxpr/all_gather | solution.py:147
  843.2 82.6 %all-gather.46.cloned.1.call-start = ((), (), s32[]{:S(2)}) async-start(), calls=%async_computation.37 | async-start | bytes 1572864 | tf_op jit(solution)/shard_map/while/body/eval_jaxpr/all_gather | solution.py:128
  883.7 147.2 %reduce-scatter.36.cloned.1.call-start = ((), (), s32[]{:S(2)}) async-start(), calls=%async_computation.41 | async-start | bytes 2621440 | tf_op jit(solution)/shard_map/while/body/eval_jaxpr/reduce_scatter | solution.py:255
  988.6 65.7 %reduce-scatter.34.cloned.1.call-start = ((), (), s32[]{:S(2)}) async-start(), calls=%async_computation.39 | async-start | bytes 2621440 | tf_op jit(solution)/shard_map/while/body/eval_jaxpr/reduce_scatter | solution.py:258
  1005.0 86.6 %reduce-scatter.38.cloned.1.call-start = ((), (), s32[]{:S(2)}) async-start(), calls=%async_computation.42 | async-start | bytes 3145728 | tf_op jit(solution)/shard_map/while/body/eval_jaxpr/reduce_scatter | solution.py:137
  1032.5 27.0 %copy-start.8 = (bf16[512,8,2,32]{0,3,2,1:T(8,128)(2,1)}, bf16[512,8,2,32]{0,3,2,1:T(8,128)(2,1)S(1)}, u32[]{:S(2)}) copy-start(bf16[512,8,2,32]{0,3,2,1:T(8,128)(2,1)S(1)} %pad_maximum_fusion.31) | copy-start | bytes 1572868 | tf_op jit(solution)/shard_map/while
  1096.6 24.1 %all-gather.40.cloned.1.call-start = ((), (), s32[]{:S(2)}) async-start(), calls=%async_computation.33 | async-start | bytes 1572864 | tf_op jit(solution)/shard_map/while/body/eval_jaxpr/all_gather | solution.py:128
  1096.8 27.9 %copy-start.17 = (f32[256]{0:T(256)}, f32[256]{0:T(256)S(1)}, u32[]{:S(2)}) copy-start(f32[256]{0:T(256)S(1)} %broadcast_multiply_fusion.17) | copy-start | bytes 3076 | tf_op jit(solution)/shard_map/while
  1098.2 46.0 %all-gather.42.cloned.1.call-start = ((), (), s32[]{:S(2)}) async-start(), calls=%async_computation.34 | async-start | bytes 1572864 | tf_op jit(solution)/shard_map/while/body/eval_jaxpr/all_gather | solution.py:128
  1103.5 64.3 %all-gather.44.cloned.1.call-start = ((), (), s32[]{:S(2)}) async-start(), calls=%async_computation.35 | async-start | bytes 1572864 | tf_op jit(solution)/shard_map/while/body/eval_jaxpr/all_gather | solution.py:128
  1105.7 87.0 %all-gather.50.cloned.1.call-start = ((), (), s32[]{:S(2)}) async-start(), calls=%async_computation.40 | async-start | bytes 2621440 | tf_op jit(solution)/shard_map/while/body/eval_jaxpr/all_gather | solution.py:148
  1127.2 99.5 %reduce-scatter.32.cloned.1.call-start = ((), (), s32[]{:S(2)}) async-start(), calls=%async_computation.36 | async-start | bytes 3145728 | tf_op jit(solution)/shard_map/while/body/eval_jaxpr/reduce_scatter | solution.py:137
  1187.5 63.9 %all-gather.48.cloned.1.call-start = ((), (), s32[]{:S(2)}) async-start(), calls=%async_computation.38 | async-start | bytes 2621440 | tf_op jit(solution)/shard_map/while/body/eval_jaxpr/all_gather | solution.py:147
  1192.2 82.6 %all-gather.46.cloned.1.call-start = ((), (), s32[]{:S(2)}) async-start(), calls=%async_computation.37 | async-start | bytes 1572864 | tf_op jit(solution)/shard_map/while/body/eval_jaxpr/all_gather | solution.py:128
  1232.7 152.6 %reduce-scatter.36.cloned.1.call-start = ((), (), s32[]{:S(2)}) async-start(), calls=%async_computation.41 | async-start | bytes 2621440 | tf_op jit(solution)/shard_map/while/body/eval_jaxpr/reduce_scatter | solution.py:255
  1337.5 65.7 %reduce-scatter.34.cloned.1.call-start = ((), (), s32[]{:S(2)}) async-start(), calls=%async_computation.39 | async-start | bytes 2621440 | tf_op jit(solution)/shard_map/while/body/eval_jaxpr/reduce_scatter | solution.py:258
  1354.0 92.8 %reduce-scatter.38.cloned.1.call-start = ((), (), s32[]{:S(2)}) async-start(), calls=%async_computation.42 | async-start | bytes 3145728 | tf_op jit(solution)/shard_map/while/body/eval_jaxpr/reduce_scatter | solution.py:137
  1386.9 21.7 %copy-start.8 = (bf16[512,8,2,32]{0,3,2,1:T(8,128)(2,1)}, bf16[512,8,2,32]{0,3,2,1:T(8,128)(2,1)S(1)}, u32[]{:S(2)}) copy-start(bf16[512,8,2,32]{0,3,2,1:T(8,128)(2,1)S(1)} %pad_maximum_fusion.31) | copy-start | bytes 1572868 | tf_op jit(solution)/shard_map/while
  1421.1 13.8 copy-start.29
  1421.1 13.8 copy-start.32
  1454.6 69.6 %reduce-scatter.20.cloned.1.call-start = ((), (), s32[]{:S(2)}) async-start(), calls=%async_computation.23 | async-start | bytes 1114112 | tf_op jit(solution)/shard_map/reduce_scatter | solution.py:331
  1457.2 120.0 %reduce-scatter.14.cloned.1.call-start = ((), (), s32[]{:S(2)}) async-start(), calls=%async_computation.20 | async-start | bytes 1114112 | tf_op jit(solution)/shard_map/reduce_scatter | solution.py:299
  1462.1 175.1 %reduce-scatter.16.cloned.1.call-start = ((), (), s32[]{:S(2)}) async-start(), calls=%async_computation.21 | async-start | bytes 1114112 | tf_op jit(solution)/shard_map/reduce_scatter | solution.py:305
  1462.9 234.7 %reduce-scatter.18.cloned.1.call-start = ((), (), s32[]{:S(2)}) async-start(), calls=%async_computation.22 | async-start | bytes 1114112 | tf_op jit(solution)/shard_map/reduce_scatter | solution.py:311
  1463.5 309.5 %reduce-scatter.26.cloned.1.call-start = ((), (), s32[]{:S(2)}) async-start(), calls=%async_computation.26 | async-start | bytes 4456448 | tf_op jit(solution)/shard_map/reduce_scatter | solution.py:334
  1470.9 377.6 %reduce-scatter.22.cloned.1.call-start = ((), (), s32[]{:S(2)}) async-start(), calls=%async_computation.24 | async-start | bytes 4456448 | tf_op jit(solution)/shard_map/reduce_scatter | solution.py:317
  1481.6 442.1 %reduce-scatter.24.cloned.1.call-start = ((), (), s32[]{:S(2)}) async-start(), calls=%async_computation.25 | async-start | bytes 4456448 | tf_op jit(solution)/shard_map/reduce_scatter | solution.py:323
  (64 other events, 343.1 us)
Sparse Core Ops, SparseCore 0:
  10.2 40.6 all-gather.23
  53.1 36.8 all-gather.17
  92.2 36.8 all-gather.19
  131.1 36.8 all-gather.21
  170.0 49.4 all-gather.29
  221.5 49.0 all-gather.25
  272.7 49.0 all-gather.27
  331.4 19.7 all-gather.31
  361.1 22.5 all-gather.35
  385.8 22.5 all-gather.33
  433.8 31.8 reduce-scatter.27
  469.7 21.2 all-gather.37
  502.3 31.8 reduce-scatter.29
  539.2 21.2 all-gather.31
  570.4 22.5 all-gather.35
  595.1 22.5 all-gather.33
  643.1 31.8 reduce-scatter.27
  679.0 21.2 all-gather.37
  711.6 31.8 reduce-scatter.29
  750.4 21.2 all-gather.39
  773.9 21.2 all-gather.41
  797.5 21.2 all-gather.43
  821.0 22.5 all-gather.49
  845.8 31.8 reduce-scatter.31
  879.8 22.5 all-gather.47
  904.4 21.3 all-gather.45
  988.7 31.4 reduce-scatter.35
  1022.8 31.4 reduce-scatter.33
  1059.7 31.8 reduce-scatter.37
  1099.3 21.3 all-gather.39
  1122.9 21.2 all-gather.41
  1146.5 21.2 all-gather.43
  1169.9 22.5 all-gather.49
  1194.8 31.8 reduce-scatter.31
  1228.8 22.5 all-gather.47
  1253.4 21.3 all-gather.45
  1337.7 31.4 reduce-scatter.35
  1371.8 31.3 reduce-scatter.33
  1408.7 31.8 reduce-scatter.37
  1459.0 57.6 reduce-scatter.19
  1520.7 56.3 reduce-scatter.13
  1580.8 56.3 reduce-scatter.15
  1641.1 56.3 reduce-scatter.17
  1701.4 71.4 reduce-scatter.25
  1777.2 71.3 reduce-scatter.21
  1852.2 71.3 reduce-scatter.23
where the time goes:
time: 1940 us; the launch traced here: 1930 us
  waiting for transfers between devices  1120 us (58%)
  matrix products  428 us (22%)
  other arithmetic  178 us (9%)
  blocking collectives  91.9 us (5%)
  local copies, waits for them, and re-layouts  89.3 us (5%)
    reduce_scatter x8, waiting for transfers between devices, rows_times(): lax.psum_scatter(row_term(), 'tensor', scatter_dimension=0, tiled=True)  190 us
    all_gather x12, waiting for transfers between devices, full_rows(): return lax.all_gather(matrix, 'tensor', axis=0, tiled=True)  188 us
    dot_general x6, matrix products, mix_rows(): jnp.einsum('hqk,khd->qhd', weights, split_heads(all_values), preferred_el...  80 us
    unnamed x2, blocking collectives  77.7 us
    all_gather x4, waiting for transfers between devices, share_keys(): lax.all_gather(key_rows, 'seq', axis=0, tiled=True)  76.5 us
    reduce_scatter x1, waiting for transfers between devices, local(): lax.psum_scatter(g_down.astype(jnp.bfloat16), ('dp', 'seq'), scatter_dime...  73.9 us
    reduce_scatter x1, waiting for transfers between devices, local(): lax.psum_scatter(g_pair[:, :hidden_cols].astype(jnp.bfloat16), ('dp', 'se...  73.8 us
    reduce_scatter x1, waiting for transfers between devices, local(): lax.psum_scatter(g_pair[:, hidden_cols:].astype(jnp.bfloat16), ('dp', 'se...  73.4 us
  transfers between devices with their start and end apart: 46, of which 38 were waited for; matrix products, arithmetic and copies ran while one was open for 22% of the time, Pallas kernels for 0%

commit v1 on v0

v1 whole, which is shorter than its diff:
```python
import functools
import math

import jax
import jax.numpy as jnp
from jax import lax
from jax.experimental import pallas as pl
from jax.experimental.pallas import tpu as pltpu
from jax.sharding import PartitionSpec as P

HEAD_DIM = 64
EPSILON = 1e-05
ROPE_BASE = 10000.0
PAIR = 2 * HEAD_DIM
LOG2E = math.log2(math.e)
BF16 = jnp.bfloat16
F32 = jnp.float32
VMEM_BYTES = 56 * 1024 * 1024


def angles(positions, head_dim):
    half_dim = head_dim // 2
    inverse = jnp.exp(
        -(math.log(ROPE_BASE) * 2.0 / head_dim) * jnp.arange(half_dim, dtype=F32)
    )
    phase_angle = positions[:, None] * inverse[None, :]
    return (jnp.cos(phase_angle), jnp.sin(phase_angle))


def layer_norm(stream, norm_gain, norm_bias):
    row_mean = jnp.mean(stream, axis=-1, keepdims=True)
    centred = stream - row_mean
    variance = jnp.mean(centred * centred, axis=-1, keepdims=True)
    inv_std = lax.rsqrt(variance + EPSILON)
    normed = centred * inv_std
    return (normed, inv_std, normed * norm_gain + norm_bias)


def norm_back(grad_normed, normed, inv_std, norm_gain):
    scaled_grad = grad_normed * norm_gain
    return inv_std * (
        scaled_grad
        - jnp.mean(scaled_grad, axis=-1, keepdims=True)
        - normed * jnp.mean(scaled_grad * normed, axis=-1, keepdims=True)
    )


def dot_nn(left, right):
    return lax.dot_general(left, right, (((1,), (0,)), ((), ())), preferred_element_type=F32)


def dot_nt(left, right):
    return lax.dot_general(left, right, (((1,), (1,)), ((), ())), preferred_element_type=F32)


def dot_tn(left, right):
    return lax.dot_general(left, right, (((0,), (0,)), ((), ())), preferred_element_type=F32)


def swap(array, axis, bit):
    size = lax.axis_size(axis)
    return lax.ppermute(array, axis, [(i, i ^ bit) for i in range(size)])


def spread(array, axis):
    blocks = [array]
    bit = 1
    while bit < lax.axis_size(axis):
        blocks = blocks + [swap(block, axis, bit) for block in blocks]
        bit *= 2
    return blocks


def gather_rows(array, axis):
    return jnp.concatenate(spread(array, axis), axis=0)


def scatter_rows(partial, axis):
    bit = lax.axis_size(axis) // 2
    while bit >= 1:
        rows = partial.shape[0] // 2
        arrived = swap(partial[rows:].astype(BF16), axis, bit)
        partial = partial[:rows] + arrived.astype(F32)
        bit //= 2
    return partial


def gather_ordered(array, axes):
    for axis in reversed(axes):
        bit = 1
        while bit < lax.axis_size(axis):
            arrived = swap(array, axis, bit)
            upper = (lax.axis_index(axis) // bit) % 2 == 1
            array = jnp.where(
                upper,
                jnp.concatenate([arrived, array], axis=0),
                jnp.concatenate([array, arrived], axis=0),
            )
            bit *= 2
    return array


def scatter_ordered(array, axes):
    for axis in axes:
        bit = lax.axis_size(axis) // 2
        while bit >= 1:
            rows = array.shape[0] // 2
            upper = (lax.axis_index(axis) // bit) % 2 == 1
            kept = jnp.where(upper, array[rows:], array[:rows])
            sent = jnp.where(upper, array[:rows], array[rows:])
            array = kept + swap(sent, axis, bit)
            bit //= 2
    return array


def first_head(shape):
    return lax.broadcasted_iota(jnp.int32, shape, 1) % PAIR < HEAD_DIM


def swap_halves(values):
    half = HEAD_DIM // 2
    lane = lax.broadcasted_iota(jnp.int32, values.shape, 1)
    ahead = pltpu.roll(values, PAIR - half, 1)
    behind = pltpu.roll(values, half, 1)
    return jnp.where(lane % HEAD_DIM < half, ahead, behind)


def qkv_kernel(x_ref, w_ref, cos_ref, sin_ref, q_ref, kv_ref):
    cols = q_ref.shape[1]
    rows = dot_nn(x_ref[...], w_ref[...])
    cosine = cos_ref[...]
    sine = sin_ref[...]
    for at in range(0, cols, PAIR):
        query = rows[:, at : at + PAIR]
        q_ref[:, at : at + PAIR] = (query * cosine + swap_halves(query) * sine).astype(BF16)
        key = rows[:, cols + at : cols + at + PAIR]
        kv_ref[0, :, at : at + PAIR] = (key * cosine + swap_halves(key) * sine).astype(BF16)
    kv_ref[1] = rows[:, 2 * cols :].astype(BF16)


def project_qkv(x_rows, w_qkv, cosine, sine):
    rows, width = x_rows.shape
    cols = w_qkv.shape[1] // 3
    step = min(256, rows)
    return pl.pallas_call(
        qkv_kernel,
        grid=(rows // step,),
        in_specs=[
            pl.BlockSpec((step, width), lambda i: (i, 0)),
            pl.BlockSpec((width, 3 * cols), lambda i: (0, 0)),
            pl.BlockSpec((step, PAIR), lambda i: (i, 0)),
            pl.BlockSpec((step, PAIR), lambda i: (i, 0)),
        ],
        out_specs=[
            pl.BlockSpec((step, cols), lambda i: (i, 0)),
            pl.BlockSpec((2, step, cols), lambda i: (0, i, 0)),
        ],
        out_shape=[
            jax.ShapeDtypeStruct((rows, cols), BF16),
            jax.ShapeDtypeStruct((2, rows, cols), BF16),
        ],
        compiler_params=pltpu.CompilerParams(vmem_limit_bytes=VMEM_BYTES),
        cost_estimate=pl.CostEstimate(
            flops=2 * rows * width * 3 * cols,
            bytes_accessed=2 * (rows * width + width * 3 * cols + rows * 3 * cols),
            transcendentals=0,
        ),
        name="project_qkv",
    )(x_rows, w_qkv, cosine, sine)


def attend_kernel(slots, last, first, exp_scale, *refs):
    refs = list(refs)
    q_ref = refs.pop(0)
    kv_refs = [refs.pop(0) for _ in range(slots)]
    if not first:
        acc_in, top_in, total_in = refs.pop(0), refs.pop(0), refs.pop(0)
    query = q_ref[...]
    is_first = first_head(query.shape)
    outs, tops = [], []
    for head in range(2):
        mine = is_first if head == 0 else jnp.logical_not(is_first)
        own_query = jnp.where(mine, query, jnp.zeros_like(query))
        scores = [dot_nt(own_query, kv[0]) for kv in kv_refs]
        top = scores[0].max(axis=1, keepdims=True)
        for one in scores[1:]:
            top = jnp.maximum(top, one.max(axis=1, keepdims=True))
        if not first:
            at = head * HEAD_DIM
            top = jnp.maximum(top, top_in[:, at : at + 1])
        shift = top * exp_scale
        mixed = None
        for one, kv in zip(scores, kv_refs):
            weight = jnp.exp2(one * exp_scale - shift).astype(BF16)
            value = kv[1]
            lane_first = first_head(value.shape)
            lane_mine = lane_first if head == 0 else jnp.logical_not(lane_first)
            term = dot_nn(weight, jnp.where(lane_mine, value, jnp.ones_like(value)))
            mixed = term if mixed is None else mixed + term
        outs.append(mixed)
        tops.append(jnp.broadcast_to(top, mixed.shape))
    acc = jnp.where(is_first, outs[0], outs[1])
    total = pltpu.roll(jnp.where(is_first, outs[1], outs[0]), HEAD_DIM, 1)
    top_wide = jnp.where(is_first, tops[0], tops[1])
    if not first:
        fade = jnp.exp2((top_in[...] - top_wide) * exp_scale)
        acc = acc + acc_in[...] * fade
        total = total + total_in[...] * fade
    if last:
        low_ref, wide_ref, log_ref = refs
        attended = acc / total
        low_ref[...] = attended.astype(BF16)
        wide_ref[...] = attended
        log_ref[...] = (top_wide * exp_scale + jnp.log2(total)).T
    else:
        acc_ref, top_ref, total_ref = refs
        acc_ref[...] = acc
        top_ref[...] = top_wide
        total_ref[...] = total


def attend(queries, blocks, carried, last):
    rows, cols = queries.shape
    keys = blocks[0].shape[1]
    slots = len(blocks)
    first = carried is None
    exp_scale = LOG2E / math.sqrt(HEAD_DIM)
    wide = pl.BlockSpec((rows, PAIR), lambda i: (0, i))
    block = pl.BlockSpec((2, keys, PAIR), lambda i: (0, 0, i))
    shape = jax.ShapeDtypeStruct((rows, cols), F32)
    if last:
        out_shape = [jax.ShapeDtypeStruct((rows, cols), BF16), shape, jax.ShapeDtypeStruct((cols, rows), F32)]
        out_specs = [wide, wide, pl.BlockSpec((PAIR, rows), lambda i: (i, 0))]
    else:
        out_shape = [shape] * 3
        out_specs = [wide] * 3
    scored = rows * keys * slots * (cols // HEAD_DIM)
    return pl.pallas_call(
        functools.partial(attend_kernel, slots, last, first, exp_scale),
        grid=(cols // PAIR,),
        in_specs=[wide] + [block] * slots + ([] if first else [wide] * 3),
        out_specs=out_specs,
        out_shape=out_shape,
        compiler_params=pltpu.CompilerParams(vmem_limit_bytes=VMEM_BYTES),
        cost_estimate=pl.CostEstimate(
            flops=scored * HEAD_DIM * 4 * 4,
            bytes_accessed=rows * cols * 20 + slots * keys * cols * 4,
            transcendentals=scored,
        ),
        name="attend",
    )(queries, *blocks, *([] if first else carried))


def attend_back_kernel(slots, last, first, exp_scale, score_scale, *refs):
    refs = list(refs)
    q_ref, do_ref, wide_ref, log_ref = [refs.pop(0) for _ in range(4)]
    kv_refs = [refs.pop(0) for _ in range(slots)]
    if not first:
        dq_in = refs.pop(0)
    if last:
        cos_ref, sin_ref = refs.pop(0), refs.pop(0)
    dq_ref = refs.pop(0)
    dkv_refs = refs
    query = q_ref[...]
    grad_out = do_ref[...]
    is_first = first_head(query.shape)
    overlap = (grad_out.astype(F32) * wide_ref[...]).T
    logs = log_ref[...]
    zero = jnp.zeros_like(query)
    own_q, own_do, row_log, row_sum = [], [], [], []
    for head in range(2):
        mine = is_first if head == 0 else jnp.logical_not(is_first)
        own_q.append(jnp.where(mine, query, zero))
        own_do.append(jnp.where(mine, grad_out, zero))
        at = head * HEAD_DIM
        row_log.append(logs[at : at + 1, :])
        row_sum.append(jnp.sum(overlap[at : at + HEAD_DIM, :], axis=0, keepdims=True))
    dq_parts = [None, None]
    for kv, dkv_ref in zip(kv_refs, dkv_refs):
        key, value = kv[0], kv[1]
        key_turned = key.T
        grad_key, grad_value = None, None
        for head in range(2):
            scores = dot_nt(key, own_q[head])
            probs = jnp.exp2(scores * exp_scale - row_log[head])
            grad_probs = dot_nt(value, own_do[head])
            grad_scores = (probs * (grad_probs - row_sum[head])).astype(BF16)
            term_v = dot_nn(probs.astype(BF16), own_do[head])
            term_k = dot_nn(grad_scores, own_q[head])
            at = head * HEAD_DIM
            term_q = dot_nn(key_turned[at : at + HEAD_DIM, :], grad_scores)
            grad_value = term_v if grad_value is None else grad_value + term_v
            grad_key = term_k if grad_key is None else grad_key + term_k
            dq_parts[head] = term_q if dq_parts[head] is None else dq_parts[head] + term_q
        dkv_ref[0] = (grad_key * score_scale).astype(BF16)
        dkv_ref[1] = grad_value.astype(BF16)
    grad_query = jnp.concatenate(dq_parts, axis=0).T * score_scale
    if not first:
        grad_query = grad_query + dq_in[...]
    if last:
        grad_query = grad_query * cos_ref[...] - swap_halves(grad_query) * sin_ref[...]
    dq_ref[...] = grad_query.astype(dq_ref.dtype)


def attend_back(queries, grad_out, wide, logs, blocks, carried, tables):
    rows, cols = queries.shape
    keys = blocks[0].shape[1]
    slots = len(blocks)
    first = carried is None
    last = tables is not None
    score_scale = 1.0 / math.sqrt(HEAD_DIM)
    row_spec = pl.BlockSpec((rows, PAIR), lambda i: (0, i))
    block = pl.BlockSpec((2, keys, PAIR), lambda i: (0, 0, i))
    table = pl.BlockSpec((rows, PAIR), lambda i: (0, 0))
    scored = rows * keys * slots * (cols // HEAD_DIM)
    return pl.pallas_call(
        functools.partial(
            attend_back_kernel, slots, last, first, score_scale * LOG2E, score_scale
        ),
        grid=(cols // PAIR,),
        in_specs=[row_spec] * 3
        + [pl.BlockSpec((PAIR, rows), lambda i: (i, 0))]
        + [block] * slots
        + ([] if first else [row_spec])
        + ([table] * 2 if last else []),
        out_specs=[row_spec] + [block] * slots,
        out_shape=[jax.ShapeDtypeStruct((rows, cols), BF16 if last else F32)]
        + [jax.ShapeDtypeStruct((2, keys, cols), BF16)] * slots,
        compiler_params=pltpu.CompilerParams(vmem_limit_bytes=VMEM_BYTES),
        cost_estimate=pl.CostEstimate(
            flops=scored * HEAD_DIM * 10 * 4,
            bytes_accessed=rows * cols * 20 + slots * keys * cols * 8,
            transcendentals=scored,
        ),
        name="attend_back",
    )(
        queries,
        grad_out,
        wide,
        logs,
        *blocks,
        *([] if first else [carried]),
        *(tables if last else []),
    )


def turn_back_kernel(dq_ref, own_ref, near_ref, far_ref, cos_ref, sin_ref, out_ref):
    cols = dq_ref.shape[1]
    out_ref[:, :cols] = dq_ref[...]
    cosine, sine = cos_ref[...], sin_ref[...]
    for at in range(0, cols, PAIR):
        part = slice(at, at + PAIR)
        key = (
            own_ref[0, :, part].astype(F32)
            + near_ref[0, :, part].astype(F32)
            + far_ref[0, :, part].astype(F32)
        )
        out_ref[:, cols + at : cols + at + PAIR] = (
            key * cosine - swap_halves(key) * sine
        ).astype(BF16)
    out_ref[:, 2 * cols :] = (
        own_ref[1].astype(F32) + near_ref[1].astype(F32) + far_ref[1].astype(F32)
    ).astype(BF16)


def turn_back(grad_query, own, near, far, cosine, sine):
    rows, cols = grad_query.shape
    step = min(256, rows)
    row_spec = pl.BlockSpec((step, cols), lambda i: (i, 0))
    block = pl.BlockSpec((2, step, cols), lambda i: (0, i, 0))
    table = pl.BlockSpec((step, PAIR), lambda i: (i, 0))
    return pl.pallas_call(
        turn_back_kernel,
        grid=(rows // step,),
        in_specs=[row_spec, block, block, block, table, table],
        out_specs=pl.BlockSpec((step, 3 * cols), lambda i: (i, 0)),
        out_shape=jax.ShapeDtypeStruct((rows, 3 * cols), BF16),
        compiler_params=pltpu.CompilerParams(vmem_limit_bytes=VMEM_BYTES),
        cost_estimate=pl.CostEstimate(
            flops=rows * cols * 10, bytes_accessed=rows * cols * 20, transcendentals=0
        ),
        name="turn_back",
    )(grad_query, own, near, far, cosine, sine)


def local(
    tokens,
    cotangent,
    species,
    counts,
    species_scale,
    norm1_gain,
    norm1_bias,
    w_query,
    w_key,
    w_value,
    w_out,
    norm2_gain,
    norm2_bias,
    w_gate,
    w_up,
    w_down,
):
    windows_here, own_rows, model_width = tokens.shape
    tensor_size = lax.axis_size("tensor")
    seq_size = lax.axis_size("seq")
    block_rows = own_rows * tensor_size
    head_cols = w_query.shape[1]
    hidden_cols = w_gate.shape[1]
    every = ("dp", "seq", "tensor")
    shards = ("dp", "seq")

    w_qkv = lax.all_gather(
        jnp.concatenate([w_query, w_key, w_value], axis=1), shards, axis=0, tiled=True
    )
    w_rest = lax.all_gather(
        jnp.concatenate([w_out.T, w_gate, w_up, w_down.T], axis=1), shards, axis=0, tiled=True
    )
    w_out_t = w_rest[:, :head_cols]
    w_pair = w_rest[:, head_cols : head_cols + 2 * hidden_cols]
    w_down_t = w_rest[:, head_cols + 2 * hidden_cols :]

    norms = gather_ordered(
        jnp.stack([norm1_gain, norm1_bias, norm2_gain, norm2_bias])[None], every
    )
    norms = norms.transpose(1, 0, 2).reshape(4, model_width)
    gain_one, bias_one, gain_two, bias_two = norms[0], norms[1], norms[2], norms[3]

    own_at = lax.axis_index("tensor")
    starts = jnp.concatenate(
        [
            lax.iota(jnp.int32, own_rows) + (own_at ^ other) * own_rows
            for other in range(tensor_size)
        ]
    )
    positions = (lax.axis_index("seq") * block_rows + starts).astype(F32)
    cos_half, sin_half = angles(positions, HEAD_DIM)
    cosine = jnp.concatenate([cos_half] * 4, axis=1)
    sine = jnp.concatenate([-sin_half, sin_half] * 2, axis=1)

    labels = lax.broadcasted_iota(jnp.int32, (windows_here, species_scale.shape[0]), 1)
    chosen = jnp.sum(jnp.where(species[:, None] == labels, species_scale[None, :], 0.0), axis=1)
    weighted = counts.astype(F32) * chosen
    weight_total = jnp.broadcast_to(jnp.sum(weighted), (8, 128))
    bit = 1
    while bit < lax.axis_size("dp"):
        weight_total = weight_total + swap(weight_total, "dp", bit)
        bit *= 2
    factor = weighted * float(windows_here * lax.axis_size("dp")) / weight_total[0, 0]

    windows = range(windows_here)
    streams = [tokens[w].astype(F32) for w in windows]
    grad_ys = [cotangent[w].astype(F32) * factor[w] for w in windows]

    token_rows = [gather_rows(tokens[w], "tensor") for w in windows]
    normed_rows, queries, near_blocks, far_blocks, states = [], [], [], [], []
    top_bit = seq_size // 2
    for w in windows:
        normed_in = layer_norm(token_rows[w].astype(F32), gain_one, bias_one)[2].astype(BF16)
        normed_rows.append(normed_in)
        query, own_kv = project_qkv(normed_in, w_qkv, cosine, sine)
        queries.append(query)
        far_own = swap(own_kv, "seq", top_bit)
        near, far = [own_kv], [far_own]
        bit = 1
        while bit < top_bit:
            near = near + [swap(block, "seq", bit) for block in near]
            far = far + [swap(block, "seq", bit) for block in far]
            bit *= 2
        near_blocks.append(near)
        far_blocks.append(far)
    for w in windows:
        states.append(attend(queries[w], near_blocks[w], None, False))
    grad_y_rows = [gather_rows(grad_ys[w].astype(BF16), "tensor") for w in windows]
    attended, wide_attended, logs, middles = [], [], [], []
    for w in windows:
        low, wide, log_row = attend(queries[w], far_blocks[w], states[w], True)
        attended.append(low)
        wide_attended.append(wide)
        logs.append(log_row)
        middles.append(streams[w] + scatter_rows(dot_nt(low, w_out_t), "tensor"))

    outputs, mid_rows, hiddens, grad_pairs, grad_middles, grad_mid_rows = [], [], [], [], [], []
    gain_two_sum = jnp.zeros((model_width,), F32)
    bias_two_sum = jnp.zeros((model_width,), F32)
    for w in windows:
        normed2, inv_std2, normed_mid = layer_norm(middles[w], gain_two, bias_two)
        gathered_mid = gather_rows(normed_mid.astype(BF16), "tensor")
        gate_up = dot_nn(gathered_mid, w_pair)
        gate_values = gate_up[:, :hidden_cols]
        up_values = gate_up[:, hidden_cols:]
        sigmoid_gate = jax.nn.sigmoid(gate_values)
        swish = gate_values * sigmoid_gate
        hidden = (swish * up_values).astype(BF16)
        grad_hidden = dot_nn(grad_y_rows[w], w_down_t)
        grad_pair = jnp.concatenate(
            [
                grad_hidden * up_values * sigmoid_gate * (1.0 + gate_values * (1.0 - sigmoid_gate)),
                grad_hidden * swish,
            ],
            axis=1,
        ).astype(BF16)
        grad_normed2 = scatter_rows(dot_nt(grad_pair, w_pair), "tensor")
        grad_middle = grad_ys[w] + norm_back(grad_normed2, normed2, inv_std2, gain_two)
        gain_two_sum = gain_two_sum + jnp.sum(grad_normed2 * normed2, axis=0)
        bias_two_sum = bias_two_sum + jnp.sum(grad_normed2, axis=0)
        grad_mid_rows.append(gather_rows(grad_middle.astype(BF16), "tensor"))
        result = middles[w] + scatter_rows(dot_nt(hidden, w_down_t), "tensor")
        outputs.append(result.astype(BF16))
        mid_rows.append(gathered_mid)
        hiddens.append(hidden)
        grad_pairs.append(grad_pair)
        grad_middles.append(grad_middle)

    mid_all = jnp.concatenate(mid_rows, axis=0)
    g_pair = dot_tn(mid_all, jnp.concatenate(grad_pairs, axis=0)).astype(BF16)
    grad_y_all = jnp.concatenate(grad_y_rows, axis=0)
    g_down = dot_tn(grad_y_all, jnp.concatenate(hiddens, axis=0)).astype(BF16)
    g_ffn = lax.psum_scatter(
        jnp.concatenate([g_pair, g_down], axis=1), shards, scatter_dimension=0, tiled=True
    ).astype(F32)

    grad_atts = [
        dot_nn(grad_mid_rows[w], w_out_t).astype(BF16) for w in windows
    ]
    grad_mid_all = jnp.concatenate(grad_mid_rows, axis=0)
    g_out = dot_tn(grad_mid_all, jnp.concatenate(attended, axis=0)).astype(BF16)

    def send_home(blocks):
        while len(blocks) > 1:
            half = len(blocks) // 2
            arrived = [swap(block, "seq", half) for block in blocks[half:]]
            blocks = [
                (kept.astype(F32) + new.astype(F32)).astype(BF16)
                for kept, new in zip(blocks[:half], arrived)
            ]
        return blocks[0]

    far_sums, dq_states = [], []
    for w in windows:
        results = attend_back(
            queries[w], grad_atts[w], wide_attended[w], logs[w], far_blocks[w], None, None
        )
        dq_states.append(results[0])
        far_sums.append(swap(send_home(list(results[1:])), "seq", top_bit))
    grad_qkvs = []
    for w in windows:
        results = attend_back(
            queries[w],
            grad_atts[w],
            wide_attended[w],
            logs[w],
            near_blocks[w],
            dq_states[w],
            (cosine, sine),
        )
        blocks = list(results[1:])
        while len(blocks) > 2:
            half = len(blocks) // 2
            arrived = [swap(block, "seq", half) for block in blocks[half:]]
            blocks = [
                (kept.astype(F32) + new.astype(F32)).astype(BF16)
                for kept, new in zip(blocks[:half], arrived)
            ]
        near_sum = swap(blocks[1], "seq", 1)
        grad_qkvs.append(turn_back(results[0], blocks[0], near_sum, far_sums[w], cosine, sine))

    gain_one_sum = jnp.zeros((model_width,), F32)
    bias_one_sum = jnp.zeros((model_width,), F32)
    input_grads = []
    for w in windows:
        grad_normed1 = scatter_rows(dot_nt(grad_qkvs[w], w_qkv), "tensor")
        normed1, inv_std1, _ = layer_norm(streams[w], gain_one, bias_one)
        input_grads.append(grad_middles[w] + norm_back(grad_normed1, normed1, inv_std1, gain_one))
        gain_one_sum = gain_one_sum + jnp.sum(grad_normed1 * normed1, axis=0)
        bias_one_sum = bias_one_sum + jnp.sum(grad_normed1, axis=0)
    g_qkv = dot_tn(
        jnp.concatenate(normed_rows, axis=0), jnp.concatenate(grad_qkvs, axis=0)
    ).astype(BF16)
    g_att = lax.psum_scatter(
        jnp.concatenate([g_qkv, g_out], axis=1), shards, scatter_dimension=0, tiled=True
    ).astype(F32)

    norm_sums = jnp.stack([gain_one_sum, bias_one_sum, gain_two_sum, bias_two_sum])
    devices = model_width // norm1_gain.shape[0]
    norm_sums = norm_sums.reshape(4, devices, -1).transpose(1, 0, 2)
    norm_sums = scatter_ordered(norm_sums, every)[0]

    return (
        jnp.stack(outputs),
        jnp.stack(input_grads),
        norm_sums[0],
        norm_sums[1],
        g_att[:, :head_cols],
        g_att[:, head_cols : 2 * head_cols],
        g_att[:, 2 * head_cols : 3 * head_cols],
        g_att[:, 3 * head_cols :].T,
        norm_sums[2],
        norm_sums[3],
        g_ffn[:, :hidden_cols],
        g_ffn[:, hidden_cols : 2 * hidden_cols],
        g_ffn[:, 2 * hidden_cols :].T,
    )


def solution(mesh):
    rows = P("dp", ("seq", "tensor"), None)
    vector = P(("dp", "seq", "tensor"))
    tall = P(("dp", "seq"), "tensor")
    flat = P("tensor", ("dp", "seq"))
    return jax.shard_map(
        local,
        mesh=mesh,
        in_specs=(
            rows, rows, P("dp"), P("dp"), P(), vector, vector,
            tall, tall, tall, flat, vector, vector, tall, tall, flat,
        ),
        out_specs=(
            rows, rows, vector, vector, tall, tall, tall, flat,
            vector, vector, tall, tall, flat,
        ),
        check_vma=False,
    )
```

time: 1940 us -> 686 us (0.35)
  waiting for transfers between devices: 1120 us -> 315 us
  matrix products: 428 us -> 114 us
  other arithmetic: 178 us -> 52.9 us
  Pallas kernels: 0 us -> 120 us
  blocking collectives: 91.9 us -> 0 us
  local copies, waits for them, and re-layouts: 89.3 us -> 20.5 us
  starting transfers between devices: 3.46 us -> 39.3 us
    reduce_scatter x19 -> x2, waiting for transfers between devices: 618 us -> 116 us  [the longest x1 116 us: local(): lax.psum_scatter(jnp.concatenate([g_pair, g_down], axis=1), shards, scatt...]
    all_gather x27 -> x2, waiting for transfers between devices: 497 us -> 18.3 us  [the longest x1 16.8 us: local(): lax.all_gather(jnp.concatenate([w_query, w_key, w_value], axis=1), shards...]
    dot_general x44 -> x18, matrix products: 428 us -> 114 us  [the longest x6 45 us: dot_nn(): lax.dot_general(left, right, (((1,), (0,)), ((), ())), preferred_element_...]
    ppermute x0 -> x40, waiting for transfers between devices: none -> 180 us  [swap(): return lax.ppermute(array, axis, [(i, i ^ bit) for i in range(size)])]
    pallas_call x0 -> x12, Pallas kernels: none -> 120 us  [the longest x4 58.2 us: attend_back(): pl.pallas_call(functools.partial(attend_back_kernel, slots, last, first,...]
    convert_element_type x22 -> x9, other arithmetic: 88.9 us -> 9.79 us  [the longest x1 2.52 us: local(): layer_norm(token_rows[w].astype(F32), gain_one, bias_one)[2].astype(BF16)]
    unnamed x2 -> x0, blocking collectives: 77.7 us -> none
    ppermute x0 -> x40, starting transfers between devices: none -> 39 us  [swap(): return lax.ppermute(array, axis, [(i, i ^ bit) for i in range(size)])]
  transfers between devices with their start and end apart: 46 -> 44, of which waited for: 38 -> 25; matrix products, arithmetic and copies ran while one was open for 22% -> 23% of each run, Pallas kernels for 0% -> 17%
where the time goes in v1:
time: 686 us; the launch traced here: 677 us
  waiting for transfers between devices  315 us (46%)
  Pallas kernels  120 us (17%)
  matrix products  114 us (17%)
  other arithmetic  52.9 us (8%)
  starting transfers between devices  39.3 us (6%)
  local copies, waits for them, and re-layouts  20.5 us (3%)
  between operations  15.2 us (2%)
    ppermute x40, waiting for transfers between devices, swap(): return lax.ppermute(array, axis, [(i, i ^ bit) for i in range(size)])  180 us
    reduce_scatter x1, waiting for transfers between devices, local(): lax.psum_scatter(jnp.concatenate([g_pair, g_down], axis=1), shards, scatt...  116 us
    pallas_call x4, Pallas kernels, attend_back(): pl.pallas_call(functools.partial(attend_back_kernel, slots, last, first,...  58.2 us
    dot_general x6, matrix products, dot_nn(): lax.dot_general(left, right, (((1,), (0,)), ((), ())), preferred_element_...  45 us
    pallas_call x4, Pallas kernels, attend(): pl.pallas_call(functools.partial(attend_kernel, slots, last, first, exp_s...  44.9 us
    ppermute x40, starting transfers between devices, swap(): return lax.ppermute(array, axis, [(i, i ^ bit) for i in range(size)])  39 us
    dot_general x8, matrix products, dot_nt(): lax.dot_general(left, right, (((1,), (1,)), ((), ())), preferred_element_...  35.6 us
    dot_general x4, matrix products, dot_tn(): lax.dot_general(left, right, (((0,), (0,)), ((), ())), preferred_element_...  33.8 us
  transfers between devices with their start and end apart: 44, of which 25 were waited for; matrix products, arithmetic and copies ran while one was open for 23% of the time, Pallas kernels for 17%

profile of v1, /device:TPU:0, one launch (start us, length us, event | category | flops | bytes accessed | tf_op | source)
XLA Modules:
  0.0 677.3 jit_solution(1948550737645138631)
XLA Ops:
  9.0 2.1 pad_maximum_fusion.6
  11.2 3.0 collective-permute-start.1
  14.4 2.0 collective-permute-start.12
  23.0 2.4 pad_maximum_fusion.7.cos_ref.refs_7_
  25.4 2.7 collective-permute-start.5
  28.1 2.0 pad_maximum_fusion.8.sin_ref.refs_8_
  30.1 1.9 collective-permute-done.5
  32.6 6.5 collective-permute-done.12
  40.1 2.5 fusion.56
  42.6 16.8 %all-gather.3.cloned.1.call-done.w_ref = bf16[1024,1536]{1,0:T(8,128)(2,1)} async-done(((bf16[64,1536]{1,0:T(8,128)(2,1)}), bf16[1024,1536]{1,0:T(8,128)(2,1)}) %all-gather.3.cloned.1.call-update) | async-done | bytes 3145744 | tf_op jit(solution)/shard_map/all_gather | solution.py:413
  59.5 5.0 project_qkv.2
  65.1 5.1 project_qkv.3
  72.4 27.5 %collective-permute-done.6.refs_1_.refs_4_ = bf16[2,512,512]{2,1,0:T(8,128)(2,1)S(1)} collective-permute-done((bf16[2,512,512]{2,1,0:T(8,128)(2,1)}, bf16[2,512,512]{2,1,0:T(8,128)(2,1)S(1)}, u32[]{:S(2)}, u32[]{:S(2)}) %collective-permute-start.6) | collective-permute-done | bytes 1048608 | tf_op jit(solution)/shard_map/ppermute | solution.py:62
  101.2 2.0 collective-permute-start.19
  103.3 29.4 %collective-permute-done.13.refs_1_.refs_4_ = bf16[2,512,512]{2,1,0:T(8,128)(2,1)S(1)} collective-permute-done((bf16[2,512,512]{2,1,0:T(8,128)(2,1)}, bf16[2,512,512]{2,1,0:T(8,128)(2,1)S(1)}, u32[]{:S(2)}, u32[]{:S(2)}) %collective-permute-start.13) | collective-permute-done | bytes 1048608 | tf_op jit(solution)/shard_map/ppermute | solution.py:62
  133.8 10.1 %attend.4 = (f32[512,512]{1,0:T(8,128)}, f32[512,512]{1,0:T(8,128)}, f32[512,512]{1,0:T(8,128)}) custom-call(bf16[512,512]{1,0:T(8,128)(2,1)} %get-tuple-element.41.refs_0_, bf16[2,512,512]{2,1,0:T(8,128)(2,1)} %get-tuple-element.42.refs_1_.refs_4_, bf16[2,512,512]{2,1,0:T(8,128)(2,1)} %copy-done.49), custom_call_target="tpu_custom_call" | custom-call | flops 4294967296 | bytes 7340032 | tf_op jit(solution)/shard_map/attend/pallas_call | solution.py:238
  145.0 10.1 %attend.6 = (f32[512,512]{1,0:T(8,128)}, f32[512,512]{1,0:T(8,128)}, f32[512,512]{1,0:T(8,128)}) custom-call(bf16[512,512]{1,0:T(8,128)(2,1)} %get-tuple-element.47.refs_0_, bf16[2,512,512]{2,1,0:T(8,128)(2,1)} %get-tuple-element.48.refs_1_.refs_4_, bf16[2,512,512]{2,1,0:T(8,128)(2,1)} %copy-done.52), custom_call_target="tpu_custom_call" | custom-call | flops 4294967296 | bytes 7340032 | tf_op jit(solution)/shard_map/attend/pallas_call | solution.py:238
  156.1 12.4 %attend.5 = (bf16[512,512]{1,0:T(8,128)(2,1)}, f32[512,512]{1,0:T(8,128)}, f32[512,512]{1,0:T(8,128)}) custom-call(bf16[512,512]{1,0:T(8,128)(2,1)} %get-tuple-element.41.refs_0_, bf16[2,512,512]{2,1,0:T(8,128)(2,1)} %copy-done.48, bf16[2,512,512]{2,1,0:T(8,128)(2,1)} %copy-done.50, f32[512,512]{1,0:T(8,128)} %get-tuple-element.43.refs_3_, ...), custom_call_target="tpu_custom_call" | custom-call | flops 4294967296 | bytes 7340032 | tf_op jit(solution)/shard_map/attend/pallas_call | solution.py:238
  168.5 12.3 %attend.7 = (bf16[512,512]{1,0:T(8,128)(2,1)}, f32[512,512]{1,0:T(8,128)}, f32[512,512]{1,0:T(8,128)}) custom-call(bf16[512,512]{1,0:T(8,128)(2,1)} %get-tuple-element.47.refs_0_, bf16[2,512,512]{2,1,0:T(8,128)(2,1)} %copy-done.51, bf16[2,512,512]{2,1,0:T(8,128)(2,1)} %collective-permute-done.14.refs_2_.refs_5_, f32[512,512]{1,0:T(8,128)} %get-tuple-element.49.refs_3_, ...), custom_call_target="tpu_custom_call" | custom-call | flops 4294967296 | bytes 7340032 | tf_op jit(solution)/shard_map/attend/pallas_call | solution.py:238
  182.2 2.2 fusion.138
  186.8 2.0 fusion.136
  192.8 3.9 collective-permute-done.20
  198.0 2.3 collective-permute-done.9
  200.3 10.6 %collective-permute-done.16 = bf16[256,1024]{1,0:T(8,128)(2,1)} collective-permute-done((bf16[256,1024]{1,0:T(8,128)(2,1)}, bf16[256,1024]{1,0:T(8,128)(2,1)}, u32[]{:S(2)}, u32[]{:S(2)}) %collective-permute-start.16) | collective-permute-done | bytes 524320 | tf_op jit(solution)/shard_map/ppermute | solution.py:62
  210.9 2.8 convert_reduce_fusion.3
  221.7 8.0 %collective-permute-done.10 = bf16[256,1024]{1,0:T(8,128)(2,1)S(1)} collective-permute-done((bf16[256,1024]{1,0:T(8,128)(2,1)S(1)}, bf16[256,1024]{1,0:T(8,128)(2,1)S(1)}, u32[]{:S(2)}, u32[]{:S(2)}) %collective-permute-start.10) | collective-permute-done | bytes 524320 | tf_op jit(solution)/shard_map/ppermute | solution.py:62
  229.7 10.7 %fusion.17 = f32[512,4096]{1,0:T(8,128)} fusion(bf16[1024,6656]{1,0:T(8,128)(2,1)} %all-gather.5.cloned.1.call-done, bf16[256,1024]{1,0:T(8,128)(2,1)S(1)} %collective-permute-done.10, bf16[256,1024]{1,0:T(8,128)(2,1)S(1)} %get-tuple-element.125), kind=kOutput, calls=%fused_computation.16 | convolution fusion | flops 4297064448 | bytes 17825792 | tf_op jit(solution)/shard_map/dot_general | solution.py:49
  240.9 8.0 %multiply_convert_fusion.3 = (bf16[512,2048]{1,0:T(8,128)(2,1)S(1)}, bf16[512,2048]{1,0:T(8,128)(2,1)S(1)}, bf16[512,2048]{1,0:T(8,128)(2,1)S(1)}) fusion(f32[512,4096]{1,0:T(8,128)} %fusion.17, bf16[1024,6656]{1,0:T(8,128)(2,1)} %all-gather.5.cloned.1.call-done, bf16[256,1024]{1,0:T(8,128)(2,1)S(1)} %collective-permute-done.21, ...), kind=kOutput, calls=%fused_computation.32 | convolution fusion | flops 2165309440 | bytes 19922944 | tf_op jit(solution)/shard_map/dot_general | solution.py:49
  250.3 7.8 %fusion.13 = f32[512,1024]{1,0:T(8,128)S(1)} fusion(bf16[1024,6656]{1,0:T(8,128)(2,1)} %all-gather.5.cloned.1.call-done, bf16[512,2048]{1,0:T(8,128)(2,1)S(1)} %get-tuple-element.101, bf16[512,2048]{1,0:T(8,128)(2,1)S(1)} %get-tuple-element.100), kind=kOutput, calls=%fused_computation.12 | convolution fusion | flops 4303355904 | bytes 14680064 | tf_op jit(solution)/shard_map/dot_general | solution.py:53
  259.8 4.6 fusion.43
  265.0 10.7 %fusion.15 = f32[512,4096]{1,0:T(8,128)} fusion(bf16[1024,6656]{1,0:T(8,128)(2,1)} %all-gather.5.cloned.1.call-done, bf16[256,1024]{1,0:T(8,128)(2,1)S(1)} %collective-permute-done.17, bf16[256,1024]{1,0:T(8,128)(2,1)S(1)} %get-tuple-element.126), kind=kOutput, calls=%fused_computation.14 | convolution fusion | flops 4297064448 | bytes 17825792 | tf_op jit(solution)/shard_map/dot_general | solution.py:49
  275.7 9.7 %multiply_convert_fusion.1 = (bf16[512,2048]{1,0:T(8,128)(2,1)}, bf16[512,2048]{1,0:T(8,128)(2,1)}, bf16[512,2048]{1,0:T(8,128)(2,1)S(1)}) fusion(f32[512,4096]{1,0:T(8,128)} %fusion.15, bf16[1024,6656]{1,0:T(8,128)(2,1)} %all-gather.5.cloned.1.call-done, bf16[256,1024]{1,0:T(8,128)(2,1)S(1)} %collective-permute-done.28, ...), kind=kOutput, calls=%fused_computation.30 | convolution fusion | flops 2165309440 | bytes 19922944 | tf_op jit(solution)/shard_map/dot_general | solution.py:49
  285.4 5.3 fusion.41
  292.5 7.7 %fusion.11 = f32[512,1024]{1,0:T(8,128)S(1)} fusion(bf16[1024,6656]{1,0:T(8,128)(2,1)} %all-gather.5.cloned.1.call-done, bf16[512,2048]{1,0:T(8,128)(2,1)} %get-tuple-element.103, bf16[512,2048]{1,0:T(8,128)(2,1)S(1)} %copy-done.66), kind=kOutput, calls=%fused_computation.10 | convolution fusion | flops 4303355904 | bytes 14680064 | tf_op jit(solution)/shard_map/dot_general | solution.py:53
  300.8 2.6 collective-permute-done.18
  303.4 9.0 %collective-permute-done.29 = bf16[256,1024]{1,0:T(8,128)(2,1)S(1)} collective-permute-done((bf16[256,1024]{1,0:T(8,128)(2,1)S(1)}, bf16[256,1024]{1,0:T(8,128)(2,1)S(1)}, u32[]{:S(2)}, u32[]{:S(2)}) %collective-permute-start.29) | collective-permute-done | bytes 524320 | tf_op jit(solution)/shard_map/ppermute | solution.py:62
  312.4 2.2 multiply_reduce_fusion.1
  314.6 2.4 fusion.163
  319.2 12.8 %collective-permute-done.30 = bf16[256,1024]{1,0:T(8,128)(2,1)S(1)} collective-permute-done((bf16[256,1024]{1,0:T(8,128)(2,1)S(1)}, bf16[256,1024]{1,0:T(8,128)(2,1)S(1)}, u32[]{:S(2)}, u32[]{:S(2)}) %collective-permute-start.30) | collective-permute-done | bytes 524320 | tf_op jit(solution)/shard_map/ppermute | solution.py:62
  332.0 2.9 convolution_convert_fusion.1.refs_1_
  335.0 13.9 %attend_back.6 = (f32[512,512]{1,0:T(8,128)}, bf16[2,512,512]{2,1,0:T(8,128)(2,1)}, bf16[2,512,512]{2,1,0:T(8,128)(2,1)}) custom-call(bf16[512,512]{1,0:T(8,128)(2,1)} %get-tuple-element.47.refs_0_, bf16[512,512]{1,0:T(8,128)(2,1)} %convolution_convert_fusion.1.refs_1_, f32[512,512]{1,0:T(8,128)} %get-tuple-element.61.refs_2_, ...), custom_call_target="tpu_custom_call" | custom-call | flops 10737418240 | bytes 9437184 | tf_op jit(solution)/shard_map/attend_back/pallas_call | solution.py:316
  348.9 15.3 %attend_back.7 = (bf16[512,512]{1,0:T(8,128)(2,1)}, bf16[2,512,512]{2,1,0:T(8,128)(2,1)}, bf16[2,512,512]{2,1,0:T(8,128)(2,1)}) custom-call(bf16[512,512]{1,0:T(8,128)(2,1)} %get-tuple-element.47.refs_0_, bf16[512,512]{1,0:T(8,128)(2,1)} %convolution_convert_fusion.1.refs_1_, f32[512,512]{1,0:T(8,128)} %get-tuple-element.61.refs_2_, ...), custom_call_target="tpu_custom_call" | custom-call | flops 10737418240 | bytes 9437184 | tf_op jit(solution)/shard_map/attend_back/pallas_call | solution.py:316
  364.7 2.9 convolution_convert_fusion.2.refs_1_
  367.7 13.9 %attend_back.4 = (f32[512,512]{1,0:T(8,128)}, bf16[2,512,512]{2,1,0:T(8,128)(2,1)}, bf16[2,512,512]{2,1,0:T(8,128)(2,1)}) custom-call(bf16[512,512]{1,0:T(8,128)(2,1)} %get-tuple-element.41.refs_0_, bf16[512,512]{1,0:T(8,128)(2,1)} %convolution_convert_fusion.2.refs_1_, f32[512,512]{1,0:T(8,128)} %get-tuple-element.53.refs_2_, ...), custom_call_target="tpu_custom_call" | custom-call | flops 10737418240 | bytes 9437184 | tf_op jit(solution)/shard_map/attend_back/pallas_call | solution.py:316
  381.7 15.1 %attend_back.5 = (bf16[512,512]{1,0:T(8,128)(2,1)}, bf16[2,512,512]{2,1,0:T(8,128)(2,1)}, bf16[2,512,512]{2,1,0:T(8,128)(2,1)}) custom-call(bf16[512,512]{1,0:T(8,128)(2,1)} %get-tuple-element.41.refs_0_, bf16[512,512]{1,0:T(8,128)(2,1)} %convolution_convert_fusion.2.refs_1_, f32[512,512]{1,0:T(8,128)} %get-tuple-element.53.refs_2_, ...), custom_call_target="tpu_custom_call" | custom-call | flops 10737418240 | bytes 9437184 | tf_op jit(solution)/shard_map/attend_back/pallas_call | solution.py:316
  400.2 2.4 fusion.82
  402.6 21.2 %collective-permute-done.33.far_ref = bf16[2,512,512]{2,1,0:T(8,128)(2,1)S(1)} collective-permute-done((bf16[2,512,512]{2,1,0:T(8,128)(2,1)S(1)}, bf16[2,512,512]{2,1,0:T(8,128)(2,1)S(1)}, u32[]{:S(2)}, u32[]{:S(2)}) %collective-permute-start.33) | collective-permute-done | bytes 1048608 | tf_op jit(solution)/shard_map/ppermute | solution.py:62
  424.7 3.5 turn_back.3
  428.3 17.1 %collective-permute-done.26.far_ref = bf16[2,512,512]{2,1,0:T(8,128)(2,1)S(1)} collective-permute-done((bf16[2,512,512]{2,1,0:T(8,128)(2,1)S(1)}, bf16[2,512,512]{2,1,0:T(8,128)(2,1)S(1)}, u32[]{:S(2)}, u32[]{:S(2)}) %collective-permute-start.26) | collective-permute-done | bytes 1048608 | tf_op jit(solution)/shard_map/ppermute | solution.py:62
  446.4 3.6 turn_back.2
  450.1 5.2 convolution_convert_fusion
  455.3 2.7 pad_maximum_fusion.1
  458.3 9.5 %fusion.31 = bf16[1024,2048]{1,0:T(8,128)(2,1)} fusion(bf16[512,2048]{1,0:T(8,128)(2,1)} %copy-done.63, bf16[512,2048]{1,0:T(8,128)(2,1)} %copy-done.62, bf16[256,1024]{1,0:T(8,128)(2,1)} %copy-done.57, bf16[256,1024]{1,0:T(8,128)(2,1)} %copy-done.28, bf16[256,1024]{1,0:T(8,128)(2,1)} %copy-done.55, bf16[256,1024]{1,0:T(8,128)(2,1)} %copy-done.27), kind=kOutput, calls=%fused_computation.39 | convolution fusion | flops 4313841664 | bytes 10485760 | tf_op jit(solution)/shard_map/dot_general | solution.py:57
  467.8 16.7 %fusion.8 = bf16[1024,4096]{1,0:T(8,128)(2,1)} fusion(bf16[512,2048]{1,0:T(8,128)(2,1)} %get-tuple-element.103, bf16[512,2048]{1,0:T(8,128)(2,1)} %get-tuple-element.102, bf16[512,2048]{1,0:T(8,128)(2,1)} %copy-done.65, bf16[512,2048]{1,0:T(8,128)(2,1)} %copy-done.64, bf16[256,1024]{1,0:T(8,128)(2,1)} %copy-done.56, bf16[256,1024]{1,0:T(8,128)(2,1)S(1)} %copy-done.26, ...), kind=kOutput, calls=%fused_computation.9 | convolution fusion | flops 8636071936 | bytes 18874368 | tf_op jit(solution)/shard_map/dot_general | solution.py:57
  484.5 10.9 %pad_maximum_fusion = bf16[1024,6144]{1,0:T(8,128)(2,1)} fusion(bf16[1024,2048]{1,0:T(8,128)(2,1)} %fusion.31, bf16[1024,4096]{1,0:T(8,128)(2,1)} %fusion.8), kind=kLoop, calls=%fused_computation | loop fusion | flops 25165824 | bytes 25165824 | tf_op jit(solution)/shard_map/concatenate | solution.py:520
  496.1 4.3 fusion.171
  508.0 8.6 %collective-permute-done.34 = bf16[256,1024]{1,0:T(8,128)(2,1)} collective-permute-done((bf16[256,1024]{1,0:T(8,128)(2,1)}, bf16[256,1024]{1,0:T(8,128)(2,1)}, u32[]{:S(2)}, u32[]{:S(2)}) %collective-permute-start.34) | collective-permute-done | bytes 524320 | tf_op jit(solution)/shard_map/ppermute | solution.py:62
  516.6 2.1 fusion.100
  518.7 7.4 %collective-permute-done.27 = bf16[256,1024]{1,0:T(8,128)(2,1)} collective-permute-done((bf16[256,1024]{1,0:T(8,128)(2,1)}, bf16[256,1024]{1,0:T(8,128)(2,1)}, u32[]{:S(2)}, u32[]{:S(2)}) %collective-permute-start.27) | collective-permute-done | bytes 524320 | tf_op jit(solution)/shard_map/ppermute | solution.py:62
  528.8 4.2 collective-permute-done.35
  534.6 2.2 collective-permute-done.36
  537.5 3.0 collective-permute-done.37
  540.6 3.1 fusion.106
  551.4 115.8 %reduce-scatter.5.cloned.1.call-done = bf16[64,6144]{1,0:T(8,128)(2,1)} async-done(((bf16[1024,6144]{1,0:T(8,128)(2,1)}), bf16[64,6144]{1,0:T(8,128)(2,1)}) %reduce-scatter.5.cloned.1.call-update) | async-done | bytes 786448 | tf_op jit(solution)/shard_map/reduce_scatter | solution.py:519
  (296 shorter events, 73.6 us)
Async XLA Ops:
  7.2 52.3 %all-gather.3.cloned.1.call-start = ((), (), s32[]{:S(2)}) async-start(), calls=%async_computation.2 | async-start | bytes 3342336 | tf_op jit(solution)/shard_map/all_gather | solution.py:413
  9.0 173.2 %all-gather.5.cloned.1.call-start = ((), (), s32[]{:S(2)}) async-start(), calls=%async_computation.3 | async-start | bytes 14483456 | tf_op jit(solution)/shard_map/all_gather | solution.py:416
  11.1 536.8 %reduce-scatter.3.cloned.1.call-start = ((), (), s32[]{:S(2)}) async-start(), calls=%async_computation.4 | async-start | bytes 4456448 | tf_op jit(solution)/shard_map/reduce_scatter | solution.py:580
  11.2 5.2 collective-permute-start.1
  14.4 18.0 %collective-permute-start = (bf16[256,1024]{1,0:T(8,128)(2,1)S(1)}, bf16[256,1024]{1,0:T(8,128)(2,1)S(1)}, u32[]{:S(2)}, u32[]{:S(2)}) collective-permute-start(bf16[256,1024]{1,0:T(8,128)(2,1)S(1)} %get-tuple-element.118), channel_id=1, source_target_pairs={{0,1},{1,0},{2,3},{3,2},{4,5},{5,4},{6,7},{7,6},{8,9},{9,8},{10,11... | collective-permute-start | bytes 1572872 | tf_op jit(solution)/shard_map/ppermute | solution.py:62
  14.4 24.6 %collective-permute-start.12 = (bf16[256,1024]{1,0:T(8,128)(2,1)S(1)}, bf16[256,1024]{1,0:T(8,128)(2,1)S(1)}, u32[]{:S(2)}, u32[]{:S(2)}) collective-permute-start(bf16[256,1024]{1,0:T(8,128)(2,1)S(1)} %get-tuple-element.119), channel_id=1, source_target_pairs={{0,1},{1,0},{2,3},{3,2},{4,5},{5,4},{6,7},{7,6},{8,9},{9,8},{10,11... | collective-permute-start | bytes 1572872 | tf_op jit(solution)/shard_map/ppermute | solution.py:62
  16.5 1.2 collective-permute-start.2
  17.7 3.7 collective-permute-start.3
  21.4 4.0 collective-permute-start.4
  25.4 6.6 collective-permute-start.5
  64.5 35.3 %collective-permute-start.6 = (bf16[2,512,512]{2,1,0:T(8,128)(2,1)}, bf16[2,512,512]{2,1,0:T(8,128)(2,1)S(1)}, u32[]{:S(2)}, u32[]{:S(2)}) collective-permute-start(bf16[2,512,512]{2,1,0:T(8,128)(2,1)} %get-tuple-element.42.refs_1_.refs_4_), channel_id=1, source_target_pairs={{0,4},{2,6},{4,0},{6,2},{1,5},{3,7},{5,1},{7,3},{8,12},{10,14},{12... | collective-permute-start | bytes 3145736 | tf_op jit(solution)/shard_map/ppermute | solution.py:62
  65.1 34.8 %copy-start.41 = (s32[2]{0:T(128)S(1)}, s32[2]{0:T(128)}, u32[]{:S(2)}) copy-start(s32[2]{0:T(128)} %param.19) | copy-start | bytes 28
  70.2 62.5 %collective-permute-start.13 = (bf16[2,512,512]{2,1,0:T(8,128)(2,1)}, bf16[2,512,512]{2,1,0:T(8,128)(2,1)S(1)}, u32[]{:S(2)}, u32[]{:S(2)}) collective-permute-start(bf16[2,512,512]{2,1,0:T(8,128)(2,1)} %get-tuple-element.48.refs_1_.refs_4_), channel_id=1, source_target_pairs={{0,4},{2,6},{4,0},{6,2},{1,5},{3,7},{5,1},{7,3},{8,12},{10,14},{12... | collective-permute-start | bytes 3145736 | tf_op jit(solution)/shard_map/ppermute | solution.py:62
  71.7 61.1 %collective-permute-start.8 = (bf16[2,512,512]{2,1,0:T(8,128)(2,1)S(1)}, bf16[2,512,512]{2,1,0:T(8,128)(2,1)S(1)}, u32[]{:S(2)}, u32[]{:S(2)}) collective-permute-start(bf16[2,512,512]{2,1,0:T(8,128)(2,1)S(1)} %copy-done.47), channel_id=1, source_target_pairs={{0,2},{2,0},{4,6},{6,4},{1,3},{3,1},{5,7},{7,5},{8,10},{10,8},{12,... | collective-permute-start | bytes 3145736 | tf_op jit(solution)/shard_map/ppermute | solution.py:62
  71.7 72.3 %collective-permute-start.15 = (bf16[2,512,512]{2,1,0:T(8,128)(2,1)}, bf16[2,512,512]{2,1,0:T(8,128)(2,1)S(1)}, u32[]{:S(2)}, u32[]{:S(2)}) collective-permute-start(bf16[2,512,512]{2,1,0:T(8,128)(2,1)} %get-tuple-element.48.refs_1_.refs_4_), channel_id=1, source_target_pairs={{0,2},{2,0},{4,6},{6,4},{1,3},{3,1},{5,7},{7,5},{8,10},{10,8},{12,... | collective-permute-start | bytes 3145736 | tf_op jit(solution)/shard_map/ppermute | solution.py:62
  99.8 44.1 %copy-start.48 = (bf16[2,512,512]{2,1,0:T(8,128)(2,1)}, bf16[2,512,512]{2,1,0:T(8,128)(2,1)S(1)}, u32[]{:S(2)}) copy-start(bf16[2,512,512]{2,1,0:T(8,128)(2,1)S(1)} %collective-permute-done.6.refs_1_.refs_4_) | copy-start | bytes 3145732
  99.8 55.2 %collective-permute-start.7 = (bf16[2,512,512]{2,1,0:T(8,128)(2,1)S(1)}, bf16[2,512,512]{2,1,0:T(8,128)(2,1)S(1)}, u32[]{:S(2)}, u32[]{:S(2)}) collective-permute-start(bf16[2,512,512]{2,1,0:T(8,128)(2,1)S(1)} %collective-permute-done.6.refs_1_.refs_4_), channel_id=1, source_target_pairs={{0,2},{2,0},{4,6},{6,4},{1,3},{3,1},{5,7},{7,5},{8,10},{10,8},{12,... | collective-permute-start | bytes 3145736 | tf_op jit(solution)/shard_map/ppermute | solution.py:62
  101.2 90.3 %collective-permute-start.19 = (f32[8,128]{1,0:T(8,128)S(1)}, f32[8,128]{1,0:T(8,128)S(1)}, u32[]{:S(2)}, u32[]{:S(2)}) collective-permute-start(f32[8,128]{1,0:T(8,128)S(1)} %broadcast_in_dim.19), channel_id=1, source_target_pairs={{0,8},{8,0},{16,24},{24,16},{1,9},{9,1},{17,25},{25,17},{2,10},{10... | collective-permute-start | bytes 12296 | tf_op jit(solution)/shard_map/ppermute | solution.py:62
  132.7 11.3 %copy-start.51 = (bf16[2,512,512]{2,1,0:T(8,128)(2,1)}, bf16[2,512,512]{2,1,0:T(8,128)(2,1)S(1)}, u32[]{:S(2)}) copy-start(bf16[2,512,512]{2,1,0:T(8,128)(2,1)S(1)} %collective-permute-done.13.refs_1_.refs_4_) | copy-start | bytes 3145732
  132.7 35.8 %collective-permute-start.14 = (bf16[2,512,512]{2,1,0:T(8,128)(2,1)S(1)}, bf16[2,512,512]{2,1,0:T(8,128)(2,1)}, u32[]{:S(2)}, u32[]{:S(2)}) collective-permute-start(bf16[2,512,512]{2,1,0:T(8,128)(2,1)S(1)} %collective-permute-done.13.refs_1_.refs_4_), channel_id=1, source_target_pairs={{0,2},{2,0},{4,6},{6,4},{1,3},{3,1},{5,7},{7,5},{8,10},{10,8},{12,... | collective-permute-start | bytes 3145736 | tf_op jit(solution)/shard_map/ppermute | solution.py:62
  185.3 15.1 %collective-permute-start.9 = (bf16[256,1024]{1,0:T(8,128)(2,1)}, bf16[256,1024]{1,0:T(8,128)(2,1)}, u32[]{:S(2)}, u32[]{:S(2)}) collective-permute-start(bf16[256,1024]{1,0:T(8,128)(2,1)} %slice.471), channel_id=1, source_target_pairs={{0,1},{1,0},{2,3},{3,2},{4,5},{5,4},{6,7},{7,6},{8,9},{9,8},{10,11... | collective-permute-start | bytes 1572872 | tf_op jit(solution)/shard_map/ppermute | solution.py:62
  191.0 19.9 %collective-permute-start.16 = (bf16[256,1024]{1,0:T(8,128)(2,1)}, bf16[256,1024]{1,0:T(8,128)(2,1)}, u32[]{:S(2)}, u32[]{:S(2)}) collective-permute-start(bf16[256,1024]{1,0:T(8,128)(2,1)} %slice.469), channel_id=1, source_target_pairs={{0,1},{1,0},{2,3},{3,2},{4,5},{5,4},{6,7},{7,6},{8,9},{9,8},{10,11... | collective-permute-start | bytes 1572872 | tf_op jit(solution)/shard_map/ppermute | solution.py:62
  192.1 4.6 collective-permute-start.20
  192.8 20.9 %copy-start.35 = (f32[256]{0:T(256)}, f32[256]{0:T(256)S(1)}, u32[]{:S(2)}) copy-start(f32[256]{0:T(256)S(1)} %broadcast_multiply_fusion.4) | copy-start | bytes 3076
  214.7 25.6 %copy-start.23 = (bf16[256,1024]{1,0:T(8,128)(2,1)}, bf16[256,1024]{1,0:T(8,128)(2,1)S(1)}, u32[]{:S(2)}) copy-start(bf16[256,1024]{1,0:T(8,128)(2,1)S(1)} %get-tuple-element.125) | copy-start | bytes 1572868
  214.7 50.2 %copy-start.25 = (bf16[256,1024]{1,0:T(8,128)(2,1)}, bf16[256,1024]{1,0:T(8,128)(2,1)S(1)}, u32[]{:S(2)}) copy-start(bf16[256,1024]{1,0:T(8,128)(2,1)S(1)} %get-tuple-element.126) | copy-start | bytes 1572868
  214.7 14.9 %collective-permute-start.10 = (bf16[256,1024]{1,0:T(8,128)(2,1)S(1)}, bf16[256,1024]{1,0:T(8,128)(2,1)S(1)}, u32[]{:S(2)}, u32[]{:S(2)}) collective-permute-start(bf16[256,1024]{1,0:T(8,128)(2,1)S(1)} %get-tuple-element.125), channel_id=1, source_target_pairs={{0,1},{1,0},{2,3},{3,2},{4,5},{5,4},{6,7},{7,6},{8,9},{9,8},{10,11... | collective-permute-start | bytes 1572872 | tf_op jit(solution)/shard_map/ppermute | solution.py:62
  219.1 21.8 %copy-start.27 = (bf16[256,1024]{1,0:T(8,128)(2,1)}, bf16[256,1024]{1,0:T(8,128)(2,1)S(1)}, u32[]{:S(2)}) copy-start(bf16[256,1024]{1,0:T(8,128)(2,1)S(1)} %get-tuple-element.111) | copy-start | bytes 1572868
  219.1 56.6 %copy-start.28 = (bf16[256,1024]{1,0:T(8,128)(2,1)}, bf16[256,1024]{1,0:T(8,128)(2,1)S(1)}, u32[]{:S(2)}) copy-start(bf16[256,1024]{1,0:T(8,128)(2,1)S(1)} %get-tuple-element.112) | copy-start | bytes 1572868
  219.1 21.8 %collective-permute-start.21 = (bf16[256,1024]{1,0:T(8,128)(2,1)S(1)}, bf16[256,1024]{1,0:T(8,128)(2,1)S(1)}, u32[]{:S(2)}, u32[]{:S(2)}) collective-permute-start(bf16[256,1024]{1,0:T(8,128)(2,1)S(1)} %get-tuple-element.111), channel_id=1, source_target_pairs={{0,1},{1,0},{2,3},{3,2},{4,5},{5,4},{6,7},{7,6},{8,9},{9,8},{10,11... | collective-permute-start | bytes 1572872 | tf_op jit(solution)/shard_map/ppermute | solution.py:62
  219.7 56.0 %collective-permute-start.28 = (bf16[256,1024]{1,0:T(8,128)(2,1)S(1)}, bf16[256,1024]{1,0:T(8,128)(2,1)S(1)}, u32[]{:S(2)}, u32[]{:S(2)}) collective-permute-start(bf16[256,1024]{1,0:T(8,128)(2,1)S(1)} %get-tuple-element.112), channel_id=1, source_target_pairs={{0,1},{1,0},{2,3},{3,2},{4,5},{5,4},{6,7},{7,6},{8,9},{9,8},{10,11... | collective-permute-start | bytes 1572872 | tf_op jit(solution)/shard_map/ppermute | solution.py:62
  221.2 43.7 %collective-permute-start.17 = (bf16[256,1024]{1,0:T(8,128)(2,1)S(1)}, bf16[256,1024]{1,0:T(8,128)(2,1)S(1)}, u32[]{:S(2)}, u32[]{:S(2)}) collective-permute-start(bf16[256,1024]{1,0:T(8,128)(2,1)S(1)} %get-tuple-element.126), channel_id=1, source_target_pairs={{0,1},{1,0},{2,3},{3,2},{4,5},{5,4},{6,7},{7,6},{8,9},{9,8},{10,11... | collective-permute-start | bytes 1572872 | tf_op jit(solution)/shard_map/ppermute | solution.py:62
  229.7 10.7 %copy-start.54 = (bf16[256,1024]{1,0:T(8,128)(2,1)}, bf16[256,1024]{1,0:T(8,128)(2,1)S(1)}, u32[]{:S(2)}) copy-start(bf16[256,1024]{1,0:T(8,128)(2,1)S(1)} %collective-permute-done.10) | copy-start | bytes 1572868
  249.0 10.8 %copy-start.62 = (bf16[512,2048]{1,0:T(8,128)(2,1)}, bf16[512,2048]{1,0:T(8,128)(2,1)S(1)}, u32[]{:S(2)}) copy-start(bf16[512,2048]{1,0:T(8,128)(2,1)S(1)} %get-tuple-element.104) | copy-start | bytes 6291460
  258.2 42.6 %collective-permute-start.22 = (bf16[256,1024]{1,0:T(8,128)(2,1)S(1)}, bf16[256,1024]{1,0:T(8,128)(2,1)S(1)}, u32[]{:S(2)}, u32[]{:S(2)}) collective-permute-start(bf16[256,1024]{1,0:T(8,128)(2,1)S(1)} %slice.467), channel_id=1, source_target_pairs={{0,1},{1,0},{2,3},{3,2},{4,5},{5,4},{6,7},{7,6},{8,9},{9,8},{10,11... | collective-permute-start | bytes 1572872 | tf_op jit(solution)/shard_map/ppermute | solution.py:62
  264.4 36.4 %collective-permute-start.11 = (bf16[256,1024]{1,0:T(8,128)(2,1)S(1)}, bf16[256,1024]{1,0:T(8,128)(2,1)S(1)}, u32[]{:S(2)}, u32[]{:S(2)}) collective-permute-start(bf16[256,1024]{1,0:T(8,128)(2,1)S(1)} %slice.470), channel_id=1, source_target_pairs={{0,1},{1,0},{2,3},{3,2},{4,5},{5,4},{6,7},{7,6},{8,9},{9,8},{10,11... | collective-permute-start | bytes 1572872 | tf_op jit(solution)/shard_map/ppermute | solution.py:62
  265.0 10.7 %copy-start.56 = (bf16[256,1024]{1,0:T(8,128)(2,1)}, bf16[256,1024]{1,0:T(8,128)(2,1)S(1)}, u32[]{:S(2)}) copy-start(bf16[256,1024]{1,0:T(8,128)(2,1)S(1)} %collective-permute-done.17) | copy-start | bytes 1572868
  290.9 12.5 %collective-permute-start.18 = (bf16[256,1024]{1,0:T(8,128)(2,1)S(1)}, bf16[256,1024]{1,0:T(8,128)(2,1)S(1)}, u32[]{:S(2)}, u32[]{:S(2)}) collective-permute-start(bf16[256,1024]{1,0:T(8,128)(2,1)S(1)} %slice.468), channel_id=1, source_target_pairs={{0,1},{1,0},{2,3},{3,2},{4,5},{5,4},{6,7},{7,6},{8,9},{9,8},{10,11... | collective-permute-start | bytes 1572872 | tf_op jit(solution)/shard_map/ppermute | solution.py:62
  300.2 12.2 %collective-permute-start.29 = (bf16[256,1024]{1,0:T(8,128)(2,1)S(1)}, bf16[256,1024]{1,0:T(8,128)(2,1)S(1)}, u32[]{:S(2)}, u32[]{:S(2)}) collective-permute-start(bf16[256,1024]{1,0:T(8,128)(2,1)S(1)} %slice.465), channel_id=1, source_target_pairs={{0,1},{1,0},{2,3},{3,2},{4,5},{5,4},{6,7},{7,6},{8,9},{9,8},{10,11... | collective-permute-start | bytes 1572872 | tf_op jit(solution)/shard_map/ppermute | solution.py:62
  317.1 17.9 %copy-start.31 = (bf16[256,1024]{1,0:T(8,128)(2,1)}, bf16[256,1024]{1,0:T(8,128)(2,1)S(1)}, u32[]{:S(2)}) copy-start(bf16[256,1024]{1,0:T(8,128)(2,1)S(1)} %get-tuple-element.108) | copy-start | bytes 1572868
  317.1 47.7 %copy-start.29 = (bf16[256,1024]{1,0:T(8,128)(2,1)}, bf16[256,1024]{1,0:T(8,128)(2,1)S(1)}, u32[]{:S(2)}) copy-start(bf16[256,1024]{1,0:T(8,128)(2,1)S(1)} %get-tuple-element.92) | copy-start | bytes 1572868
  317.1 14.9 %collective-permute-start.30 = (bf16[256,1024]{1,0:T(8,128)(2,1)S(1)}, bf16[256,1024]{1,0:T(8,128)(2,1)S(1)}, u32[]{:S(2)}, u32[]{:S(2)}) collective-permute-start(bf16[256,1024]{1,0:T(8,128)(2,1)S(1)} %get-tuple-element.108), channel_id=1, source_target_pairs={{0,1},{1,0},{2,3},{3,2},{4,5},{5,4},{6,7},{7,6},{8,9},{9,8},{10,11... | collective-permute-start | bytes 1572872 | tf_op jit(solution)/shard_map/ppermute | solution.py:62
  318.7 46.0 %collective-permute-start.23 = (bf16[256,1024]{1,0:T(8,128)(2,1)S(1)}, bf16[256,1024]{1,0:T(8,128)(2,1)S(1)}, u32[]{:S(2)}, u32[]{:S(2)}) collective-permute-start(bf16[256,1024]{1,0:T(8,128)(2,1)S(1)} %get-tuple-element.92), channel_id=1, source_target_pairs={{0,1},{1,0},{2,3},{3,2},{4,5},{5,4},{6,7},{7,6},{8,9},{9,8},{10,11... | collective-permute-start | bytes 1572872 | tf_op jit(solution)/shard_map/ppermute | solution.py:62
  348.9 15.4 %copy-start.53 = (bf16[2,512,512]{2,1,0:T(8,128)(2,1)S(1)}, bf16[2,512,512]{2,1,0:T(8,128)(2,1)}, u32[]{:S(2)}) copy-start(bf16[2,512,512]{2,1,0:T(8,128)(2,1)} %get-tuple-element.68) | copy-start | bytes 3145732
  364.2 38.4 %collective-permute-start.31 = (bf16[2,512,512]{2,1,0:T(8,128)(2,1)}, bf16[2,512,512]{2,1,0:T(8,128)(2,1)S(1)}, u32[]{:S(2)}, u32[]{:S(2)}) collective-permute-start(bf16[2,512,512]{2,1,0:T(8,128)(2,1)} %get-tuple-element.66), channel_id=1, source_target_pairs={{0,2},{2,0},{4,6},{6,4},{1,3},{3,1},{5,7},{7,5},{8,10},{10,8},{12,... | collective-permute-start | bytes 3145736 | tf_op jit(solution)/shard_map/ppermute | solution.py:62
  364.2 33.1 %collective-permute-start.32 = (bf16[2,512,512]{2,1,0:T(8,128)(2,1)S(1)}, bf16[2,512,512]{2,1,0:T(8,128)(2,1)S(1)}, u32[]{:S(2)}, u32[]{:S(2)}) collective-permute-start(bf16[2,512,512]{2,1,0:T(8,128)(2,1)S(1)} %copy-done.53), channel_id=1, source_target_pairs={{0,2},{2,0},{4,6},{6,4},{1,3},{3,1},{5,7},{7,5},{8,10},{10,8},{12,... | collective-permute-start | bytes 3145736 | tf_op jit(solution)/shard_map/ppermute | solution.py:62
  381.6 16.8 %collective-permute-start.25 = (bf16[2,512,512]{2,1,0:T(8,128)(2,1)}, bf16[2,512,512]{2,1,0:T(8,128)(2,1)S(1)}, u32[]{:S(2)}, u32[]{:S(2)}) collective-permute-start(bf16[2,512,512]{2,1,0:T(8,128)(2,1)} %get-tuple-element.60), channel_id=1, source_target_pairs={{0,2},{2,0},{4,6},{6,4},{1,3},{3,1},{5,7},{7,5},{8,10},{10,8},{12,... | collective-permute-start | bytes 3145736 | tf_op jit(solution)/shard_map/ppermute | solution.py:62
  381.7 15.6 %copy-start.12 = (bf16[2,512,512]{2,1,0:T(8,128)(2,1)S(1)}, bf16[2,512,512]{2,1,0:T(8,128)(2,1)}, u32[]{:S(2)}) copy-start(bf16[2,512,512]{2,1,0:T(8,128)(2,1)} %get-tuple-element.67) | copy-start | bytes 3145732
  396.8 31.4 %collective-permute-start.24 = (bf16[2,512,512]{2,1,0:T(8,128)(2,1)}, bf16[2,512,512]{2,1,0:T(8,128)(2,1)}, u32[]{:S(2)}, u32[]{:S(2)}) collective-permute-start(bf16[2,512,512]{2,1,0:T(8,128)(2,1)} %get-tuple-element.58), channel_id=1, source_target_pairs={{0,2},{2,0},{4,6},{6,4},{1,3},{3,1},{5,7},{7,5},{8,10},{10,8},{12,... | collective-permute-start | bytes 3145736 | tf_op jit(solution)/shard_map/ppermute | solution.py:62
  397.7 26.1 %collective-permute-start.33 = (bf16[2,512,512]{2,1,0:T(8,128)(2,1)S(1)}, bf16[2,512,512]{2,1,0:T(8,128)(2,1)S(1)}, u32[]{:S(2)}, u32[]{:S(2)}) collective-permute-start(bf16[2,512,512]{2,1,0:T(8,128)(2,1)S(1)} %add_convert_fusion), channel_id=1, source_target_pairs={{0,4},{2,6},{4,0},{6,2},{1,5},{3,7},{5,1},{7,3},{8,12},{10,14},{12... | collective-permute-start | bytes 3145736 | tf_op jit(solution)/shard_map/ppermute | solution.py:62
  398.7 46.7 %collective-permute-start.26 = (bf16[2,512,512]{2,1,0:T(8,128)(2,1)S(1)}, bf16[2,512,512]{2,1,0:T(8,128)(2,1)S(1)}, u32[]{:S(2)}, u32[]{:S(2)}) collective-permute-start(bf16[2,512,512]{2,1,0:T(8,128)(2,1)S(1)} %add_convert_fusion.1), channel_id=1, source_target_pairs={{0,4},{2,6},{4,0},{6,2},{1,5},{3,7},{5,1},{7,3},{8,12},{10,14},{12... | collective-permute-start | bytes 3145736 | tf_op jit(solution)/shard_map/ppermute | solution.py:62
  402.6 22.2 %copy-start.16 = (bf16[2,512,512]{2,1,0:T(8,128)(2,1)}, bf16[2,512,512]{2,1,0:T(8,128)(2,1)S(1)}, u32[]{:S(2)}) copy-start(bf16[2,512,512]{2,1,0:T(8,128)(2,1)S(1)} %collective-permute-done.31.near_ref) | copy-start | bytes 3145732
  458.0 209.1 %reduce-scatter.5.cloned.1.call-start = ((), (), s32[]{:S(2)}) async-start(), calls=%async_computation.5 | async-start | bytes 13369344 | tf_op jit(solution)/shard_map/reduce_scatter | solution.py:519
  501.4 15.2 %collective-permute-start.34 = (bf16[256,1024]{1,0:T(8,128)(2,1)}, bf16[256,1024]{1,0:T(8,128)(2,1)}, u32[]{:S(2)}, u32[]{:S(2)}) collective-permute-start(bf16[256,1024]{1,0:T(8,128)(2,1)} %slice.464), channel_id=1, source_target_pairs={{0,1},{1,0},{2,3},{3,2},{4,5},{5,4},{6,7},{7,6},{8,9},{9,8},{10,11... | collective-permute-start | bytes 1572872 | tf_op jit(solution)/shard_map/ppermute | solution.py:62
  504.9 11.8 %copy-start.1 = (bf16[2,256,1024]{2,1,0:T(8,128)(2,1)S(1)}, bf16[2,256,1024]{2,1,0:T(8,128)(2,1)}, u32[]{:S(2)}) copy-start(bf16[2,256,1024]{2,1,0:T(8,128)(2,1)} %param.16) | copy-start | bytes 3145732
  504.9 11.7 %copy-start.34 = (f32[1024]{0:T(1024)S(1)}, f32[1024]{0:T(1024)}, u32[]{:S(2)}) copy-start(f32[1024]{0:T(1024)} %copy-done.33) | copy-start | bytes 12292
  504.9 11.7 %copy-start.36 = (f32[256]{0:T(256)S(1)}, f32[256]{0:T(256)}, u32[]{:S(2)}) copy-start(f32[256]{0:T(256)} %copy-done.35) | copy-start | bytes 3076
  506.3 19.8 %collective-permute-start.27 = (bf16[256,1024]{1,0:T(8,128)(2,1)}, bf16[256,1024]{1,0:T(8,128)(2,1)}, u32[]{:S(2)}, u32[]{:S(2)}) collective-permute-start(bf16[256,1024]{1,0:T(8,128)(2,1)} %slice.466), channel_id=1, source_target_pairs={{0,1},{1,0},{2,3},{3,2},{4,5},{5,4},{6,7},{7,6},{8,9},{9,8},{10,11... | collective-permute-start | bytes 1572872 | tf_op jit(solution)/shard_map/ppermute | solution.py:62
  508.0 18.1 %copy-start.7 = (f32[512,1024]{1,0:T(8,128)S(1)}, f32[512,1024]{1,0:T(8,128)}, u32[]{:S(2)}) copy-start(f32[512,1024]{1,0:T(8,128)} %copy-done.6) | copy-start | bytes 6291460
  528.1 4.9 collective-permute-start.35
  533.0 3.8 collective-permute-start.36
  536.8 3.7 collective-permute-start.37
  540.6 3.2 collective-permute-start.38
  543.8 3.7 collective-permute-start.39
  (47 other events, 199.1 us)
Sparse Core Ops, SparseCore 0:
  10.9 48.5 all-gather.2
  61.8 120.3 all-gather.4
  458.1 70.8 reduce-scatter.2
  533.4 133.6 reduce-scatter.4

commit v2 on v1

v2 whole, which is shorter than its diff:
```python
import functools
import math

import jax
import jax.numpy as jnp
from jax import lax
from jax.experimental import pallas as pl
from jax.experimental.pallas import tpu as pltpu
from jax.sharding import PartitionSpec as P

HEAD_DIM = 64
EPSILON = 1e-05
ROPE_BASE = 10000.0
PAIR = 2 * HEAD_DIM
LOG2E = math.log2(math.e)
BF16 = jnp.bfloat16
F32 = jnp.float32
VMEM_BYTES = 56 * 1024 * 1024


def angles(positions, head_dim):
    half_dim = head_dim // 2
    inverse = jnp.exp(
        -(math.log(ROPE_BASE) * 2.0 / head_dim) * jnp.arange(half_dim, dtype=F32)
    )
    phase_angle = positions[:, None] * inverse[None, :]
    return (jnp.cos(phase_angle), jnp.sin(phase_angle))


def dot_nn(left, right):
    return lax.dot_general(left, right, (((1,), (0,)), ((), ())), preferred_element_type=F32)


def dot_nt(left, right):
    return lax.dot_general(left, right, (((1,), (1,)), ((), ())), preferred_element_type=F32)


def dot_tn(left, right):
    return lax.dot_general(left, right, (((0,), (0,)), ((), ())), preferred_element_type=F32)


def swap(array, axis, bit):
    size = lax.axis_size(axis)
    return lax.ppermute(array, axis, [(i, i ^ bit) for i in range(size)])


def spread(array, axis):
    blocks = [array]
    bit = 1
    while bit < lax.axis_size(axis):
        blocks = blocks + [swap(block, axis, bit) for block in blocks]
        bit *= 2
    return blocks


def scatter_pair(kept, sent, axis):
    bit = lax.axis_size(axis) // 2
    while bit > 1:
        partial = kept + swap(sent, axis, bit).astype(F32)
        bit //= 2
        rows = partial.shape[0] // 2
        kept, sent = partial[:rows], partial[rows:].astype(BF16)
    return kept, swap(sent, axis, 1)


def hold(values, *others):
    return lax.optimization_barrier((values, others))[0]


def gather_ordered(array, axes):
    for axis in reversed(axes):
        bit = 1
        while bit < lax.axis_size(axis):
            arrived = swap(array, axis, bit)
            upper = (lax.axis_index(axis) // bit) % 2 == 1
            array = jnp.where(
                upper,
                jnp.concatenate([arrived, array], axis=0),
                jnp.concatenate([array, arrived], axis=0),
            )
            bit *= 2
    return array


def scatter_ordered(array, axes):
    for axis in axes:
        bit = lax.axis_size(axis) // 2
        while bit >= 1:
            rows = array.shape[0] // 2
            upper = (lax.axis_index(axis) // bit) % 2 == 1
            kept = jnp.where(upper, array[rows:], array[:rows])
            sent = jnp.where(upper, array[:rows], array[rows:])
            array = kept + swap(sent, axis, bit)
            bit //= 2
    return array


def gather_ordered(array, axes):
    for axis in reversed(axes):
        bit = 1
        while bit < lax.axis_size(axis):
            arrived = swap(array, axis, bit)
            upper = (lax.axis_index(axis) // bit) % 2 == 1
            array = jnp.where(
                upper,
                jnp.concatenate([arrived, array], axis=0),
                jnp.concatenate([array, arrived], axis=0),
            )
            bit *= 2
    return array


def scatter_ordered(array, axes):
    for axis in axes:
        bit = lax.axis_size(axis) // 2
        while bit >= 1:
            rows = array.shape[0] // 2
            upper = (lax.axis_index(axis) // bit) % 2 == 1
            kept = jnp.where(upper, array[rows:], array[:rows])
            sent = jnp.where(upper, array[:rows], array[rows:])
            array = kept + swap(sent, axis, bit)
            bit //= 2
    return array


def run(kernel, name, out_shape, flops, args, **options):
    args = [array for array in args]
    moved = sum(math.prod(array.shape) * array.dtype.itemsize for array in args)
    outs = out_shape if isinstance(out_shape, list) else [out_shape]
    moved += sum(math.prod(array.shape) * array.dtype.itemsize for array in outs)
    return pl.pallas_call(
        kernel,
        out_shape=out_shape,
        compiler_params=pltpu.CompilerParams(vmem_limit_bytes=VMEM_BYTES),
        cost_estimate=pl.CostEstimate(
            flops=int(flops), bytes_accessed=int(moved), transcendentals=0
        ),
        name=name,
        **options,
    )(*args)


def shaped(shape, dtype):
    return jax.ShapeDtypeStruct(shape, dtype)


SCALAR = pl.BlockSpec(memory_space=pltpu.SMEM)


def normalise(stream):
    row_mean = jnp.mean(stream, axis=-1, keepdims=True)
    centred = stream - row_mean
    variance = jnp.mean(centred * centred, axis=-1, keepdims=True)
    inv_std = lax.rsqrt(variance + EPSILON)
    return centred * inv_std, inv_std


def norm_back(grad_normed, normed, inv_std, norm_gain):
    scaled_grad = grad_normed * norm_gain
    return inv_std * (
        scaled_grad
        - jnp.mean(scaled_grad, axis=-1, keepdims=True)
        - normed * jnp.mean(scaled_grad * normed, axis=-1, keepdims=True)
    )


def first_head(shape):
    return lax.broadcasted_iota(jnp.int32, shape, 1) % PAIR < HEAD_DIM


def swap_halves(values):
    half = HEAD_DIM // 2
    lane = lax.broadcasted_iota(jnp.int32, values.shape, 1)
    ahead = pltpu.roll(values, PAIR - half, 1)
    behind = pltpu.roll(values, half, 1)
    return jnp.where(lane % HEAD_DIM < half, ahead, behind)


def project_kernel(blocks, norms_ref, w_ref, cos_ref, sin_ref, *refs):
    x_refs = refs[:blocks]
    normed_ref, q_ref, kv_ref = refs[blocks:]
    cols = q_ref.shape[1]
    gain, bias = norms_ref[0:1, :], norms_ref[1:2, :]
    at_row = 0
    for x_ref in x_refs:
        rows = slice(at_row, at_row + x_ref.shape[0])
        at_row += x_ref.shape[0]
        normed = (normalise(x_ref[...].astype(F32))[0] * gain + bias).astype(BF16)
        normed_ref[rows, :] = normed
        cosine, sine = cos_ref[rows, :], sin_ref[rows, :]
        query = dot_nn(normed, w_ref[:, :cols])
        key = dot_nn(normed, w_ref[:, cols : 2 * cols])
        for at in range(0, cols, PAIR):
            part = slice(at, at + PAIR)
            one = query[:, part]
            q_ref[rows, part] = (one * cosine + swap_halves(one) * sine).astype(BF16)
            one = key[:, part]
            kv_ref[0, rows, part] = (one * cosine + swap_halves(one) * sine).astype(BF16)
        kv_ref[1, rows, :] = dot_nn(normed, w_ref[:, 2 * cols : 3 * cols]).astype(BF16)


def project(x_blocks, norms, w_att, cosine, sine):
    width, cols = w_att.shape[0], w_att.shape[1] // 4
    rows = sum(block.shape[0] for block in x_blocks)
    return run(
        functools.partial(project_kernel, len(x_blocks)),
        "project",
        [
            shaped((rows, width), BF16),
            shaped((rows, cols), BF16),
            shaped((2, rows, cols), BF16),
        ],
        6 * rows * width * cols,
        [norms, w_att, cosine, sine, *x_blocks],
    )


def attend_kernel(slots, last, first, exp_scale, *refs):
    refs = list(refs)
    q_ref = refs.pop(0)
    kv_refs = [refs.pop(0) for _ in range(slots)]
    if not first:
        acc_in, top_in, total_in = refs.pop(0), refs.pop(0), refs.pop(0)
    query = q_ref[...]
    is_first = first_head(query.shape)
    outs, tops = [], []
    for head in range(2):
        mine = is_first if head == 0 else jnp.logical_not(is_first)
        own_query = jnp.where(mine, query, jnp.zeros_like(query))
        scores = [dot_nt(own_query, kv[0]) for kv in kv_refs]
        top = scores[0].max(axis=1, keepdims=True)
        for one in scores[1:]:
            top = jnp.maximum(top, one.max(axis=1, keepdims=True))
        if not first:
            at = head * HEAD_DIM
            top = jnp.maximum(top, top_in[:, at : at + 1])
        shift = top * exp_scale
        mixed = None
        for one, kv in zip(scores, kv_refs):
            weight = jnp.exp2(one * exp_scale - shift).astype(BF16)
            value = kv[1]
            lane_first = first_head(value.shape)
            lane_mine = lane_first if head == 0 else jnp.logical_not(lane_first)
            term = dot_nn(weight, jnp.where(lane_mine, value, jnp.ones_like(value)))
            mixed = term if mixed is None else mixed + term
        outs.append(mixed)
        tops.append(jnp.broadcast_to(top, mixed.shape))
    acc = jnp.where(is_first, outs[0], outs[1])
    total = pltpu.roll(jnp.where(is_first, outs[1], outs[0]), HEAD_DIM, 1)
    top_wide = jnp.where(is_first, tops[0], tops[1])
    if not first:
        fade = jnp.exp2((top_in[...] - top_wide) * exp_scale)
        acc = acc + acc_in[...] * fade
        total = total + total_in[...] * fade
    if last:
        w_ref, low_ref, wide_ref, log_ref, kept_ref, sent_ref, mixed_rows = refs
        attended = acc / total
        low = attended.astype(BF16)
        low_ref[...] = low
        wide_ref[...] = attended
        log_ref[...] = (top_wide * exp_scale + jnp.log2(total)).T
        term = dot_nt(low, w_ref[...])
        step = pl.program_id(0)

        @pl.when(step == 0)
        def _():
            mixed_rows[...] = term

        @pl.when(step > 0)
        def _():
            mixed_rows[...] += term

        @pl.when(step == pl.num_programs(0) - 1)
        def _():
            half = kept_ref.shape[0]
            kept_ref[...] = mixed_rows[:half]
            sent_ref[...] = mixed_rows[half:].astype(BF16)

    else:
        acc_ref, top_ref, total_ref = refs
        acc_ref[...] = acc
        top_ref[...] = top_wide
        total_ref[...] = total


def attend(queries, blocks, carried, w_att):
    rows, cols = queries.shape
    keys = blocks[0].shape[1]
    slots = len(blocks)
    first = carried is None
    last = w_att is not None
    wide = pl.BlockSpec((rows, PAIR), lambda i: (0, i))
    block = pl.BlockSpec((2, keys, PAIR), lambda i: (0, 0, i))
    shape = shaped((rows, cols), F32)
    args = [queries, *blocks, *([] if first else carried)]
    in_specs = [wide] + [block] * slots + ([] if first else [wide] * 3)
    scratch = []
    if last:
        width = w_att.shape[0]
        out_at = 3 * cols // PAIR
        args.append(w_att)
        in_specs.append(pl.BlockSpec((width, PAIR), lambda i: (0, out_at + i)))
        out_shape = [
            shaped((rows, cols), BF16),
            shape,
            shaped((cols, rows), F32),
            shaped((rows // 2, width), F32),
            shaped((rows // 2, width), BF16),
        ]
        half = pl.BlockSpec((rows // 2, width), lambda i: (0, 0))
        out_specs = [wide, wide, pl.BlockSpec((PAIR, rows), lambda i: (i, 0)), half, half]
        scratch = [pltpu.VMEM((rows, width), F32)]
    else:
        out_shape = [shape] * 3
        out_specs = [wide] * 3
    return run(
        functools.partial(attend_kernel, slots, last, first, LOG2E / math.sqrt(HEAD_DIM)),
        "attend_far" if last else "attend_near",
        out_shape,
        16 * rows * keys * slots * cols,
        args,
        grid=(cols // PAIR,),
        in_specs=in_specs,
        out_specs=out_specs,
        scratch_shapes=scratch,
    )


def attend_back_kernel(slots, first, grad_blocks, exp_scale, score_scale, *refs):
    refs = list(refs)
    q_ref, wide_ref, log_ref = [refs.pop(0) for _ in range(3)]
    if first:
        grad_refs = [refs.pop(0) for _ in range(grad_blocks)]
        w_ref = refs.pop(0)
    else:
        do_ref = refs.pop(0)
    kv_refs = [refs.pop(0) for _ in range(slots)]
    if not first:
        dq_in = refs.pop(0)
        cos_ref, sin_ref = refs.pop(0), refs.pop(0)
    dq_ref = refs.pop(0)
    dkv_refs = [refs.pop(0) for _ in range(slots)]
    query = q_ref[...]
    if first:
        do_ref, rows_ref = refs

        @pl.when(pl.program_id(0) == 0)
        def _():
            at_row = 0
            for grad_ref in grad_refs:
                rows_ref[at_row : at_row + grad_ref.shape[0], :] = grad_ref[...]
                at_row += grad_ref.shape[0]

        grad_out = dot_nn(rows_ref[...], w_ref[...]).astype(BF16)
        do_ref[...] = grad_out
    else:
        grad_out = do_ref[...]
    is_first = first_head(query.shape)
    overlap = (grad_out.astype(F32) * wide_ref[...]).T
    logs = log_ref[...]
    zero = jnp.zeros_like(query)
    own_q, own_do, row_log, row_sum = [], [], [], []
    for head in range(2):
        mine = is_first if head == 0 else jnp.logical_not(is_first)
        own_q.append(jnp.where(mine, query, zero))
        own_do.append(jnp.where(mine, grad_out, zero))
        at = head * HEAD_DIM
        row_log.append(logs[at : at + 1, :])
        row_sum.append(jnp.sum(overlap[at : at + HEAD_DIM, :], axis=0, keepdims=True))
    dq_parts = [None, None]
    for kv, dkv_ref in zip(kv_refs, dkv_refs):
        key, value = kv[0], kv[1]
        key_turned = key.T
        grad_key, grad_value = None, None
        for head in range(2):
            scores = dot_nt(key, own_q[head])
            probs = jnp.exp2(scores * exp_scale - row_log[head])
            grad_probs = dot_nt(value, own_do[head])
            grad_scores = (probs * (grad_probs - row_sum[head])).astype(BF16)
            term_v = dot_nn(probs.astype(BF16), own_do[head])
            term_k = dot_nn(grad_scores, own_q[head])
            at = head * HEAD_DIM
            term_q = dot_nn(key_turned[at : at + HEAD_DIM, :], grad_scores)
            grad_value = term_v if grad_value is None else grad_value + term_v
            grad_key = term_k if grad_key is None else grad_key + term_k
            dq_parts[head] = term_q if dq_parts[head] is None else dq_parts[head] + term_q
        dkv_ref[0] = (grad_key * score_scale).astype(BF16)
        dkv_ref[1] = grad_value.astype(BF16)
    grad_query = jnp.concatenate(dq_parts, axis=0).T * score_scale
    if not first:
        grad_query = grad_query + dq_in[...]
        grad_query = grad_query * cos_ref[...] - swap_halves(grad_query) * sin_ref[...]
    dq_ref[...] = grad_query.astype(dq_ref.dtype)


def attend_back(queries, wide, logs, blocks, grads, w_att, tables):
    rows, cols = queries.shape
    keys = blocks[0].shape[1]
    slots = len(blocks)
    first = tables is None
    score_scale = 1.0 / math.sqrt(HEAD_DIM)
    row_spec = pl.BlockSpec((rows, PAIR), lambda i: (0, i))
    block = pl.BlockSpec((2, keys, PAIR), lambda i: (0, 0, i))
    in_specs = [row_spec] * 2 + [pl.BlockSpec((PAIR, rows), lambda i: (i, 0))]
    args = [queries, wide, logs]
    out_shape = [shaped((rows, cols), F32 if first else BF16)]
    out_shape += [shaped((2, keys, cols), BF16)] * slots
    out_specs = [row_spec] + [block] * slots
    if first:
        width = w_att.shape[0]
        out_at = 3 * cols // PAIR
        args += [*grads, w_att]
        in_specs += [pl.BlockSpec(grad.shape, lambda i: (0, 0)) for grad in grads]
        in_specs += [pl.BlockSpec((width, PAIR), lambda i: (0, out_at + i))]
        out_shape += [shaped((rows, cols), BF16), shaped((rows, width), BF16)]
        out_specs += [row_spec, pl.BlockSpec((rows, width), lambda i: (0, 0))]
    else:
        args.append(grads[1])
        in_specs.append(row_spec)
    args += blocks
    in_specs += [block] * slots
    if not first:
        args += [grads[0], *tables]
        in_specs += [row_spec] + [pl.BlockSpec((rows, PAIR), lambda i: (0, 0))] * 2
    return run(
        functools.partial(
            attend_back_kernel, slots, first, len(grads), score_scale * LOG2E, score_scale
        ),
        "attend_back_far" if first else "attend_back_near",
        out_shape,
        40 * rows * keys * slots * cols,
        args,
        grid=(cols // PAIR,),
        in_specs=in_specs,
        out_specs=out_specs,
    )


def middle_kernel(x_ref, kept_ref, arrived_ref, norms_ref, middle_ref, normed_ref):
    middle = x_ref[...].astype(F32) + (kept_ref[...] + arrived_ref[...].astype(F32))
    middle_ref[...] = middle
    normed_ref[...] = (
        normalise(middle)[0] * norms_ref[2:3, :] + norms_ref[3:4, :]
    ).astype(BF16)


def second_norm(x_rows, kept, arrived, norms):
    return run(
        middle_kernel,
        "second_norm",
        [shaped(kept.shape, F32), shaped(kept.shape, BF16)],
        20 * kept.size,
        [x_rows, kept, arrived, norms],
    )


def feed_kernel(blocks, factor_ref, gate_w_ref, up_w_ref, down_w_ref, *refs):
    x_refs, cot_refs = refs[:blocks], refs[blocks : 2 * blocks]
    x_all, gy_all, hidden_ref, grad_gate_ref, grad_up_ref = refs[2 * blocks : 2 * blocks + 5]
    kept_ref, sent_ref, grad_kept_ref, grad_sent_ref, total, grad_total = refs[2 * blocks + 5 :]
    step = pl.program_id(0)

    @pl.when(step == 0)
    def _():
        at_row = 0
        for x_ref, cot_ref in zip(x_refs, cot_refs):
            rows = slice(at_row, at_row + x_ref.shape[0])
            at_row += x_ref.shape[0]
            x_all[rows, :] = x_ref[...]
            gy_all[rows, :] = (cot_ref[...].astype(F32) * factor_ref[0, 0]).astype(BF16)

    x_rows = x_all[...]
    gate = dot_nn(x_rows, gate_w_ref[...])
    up = dot_nn(x_rows, up_w_ref[...])
    grad_hidden = dot_nn(gy_all[...], down_w_ref[...])
    sig = jax.nn.sigmoid(gate)
    swish = gate * sig
    hidden = (swish * up).astype(BF16)
    grad_gate = (grad_hidden * up * sig * (1.0 + gate * (1.0 - sig))).astype(BF16)
    grad_up = (grad_hidden * swish).astype(BF16)
    hidden_ref[...] = hidden
    grad_gate_ref[...] = grad_gate
    grad_up_ref[...] = grad_up
    grad_term = dot_nt(grad_gate, gate_w_ref[...]) + dot_nt(grad_up, up_w_ref[...])
    term = dot_nt(hidden, down_w_ref[...])

    @pl.when(step == 0)
    def _():
        total[...] = term
        grad_total[...] = grad_term

    @pl.when(step > 0)
    def _():
        total[...] += term
        grad_total[...] += grad_term

    @pl.when(step == pl.num_programs(0) - 1)
    def _():
        half = kept_ref.shape[0]
        kept_ref[...] = total[:half]
        sent_ref[...] = total[half:].astype(BF16)
        grad_kept_ref[...] = grad_total[:half]
        grad_sent_ref[...] = grad_total[half:].astype(BF16)


def feed(x_blocks, cot_blocks, factor, weights):
    width = x_blocks[0].shape[1]
    rows = sum(block.shape[0] for block in x_blocks)
    hidden_cols = weights.shape[1] // 3
    step = min(512, hidden_cols)
    steps = hidden_cols // step
    full = pl.BlockSpec((rows, width), lambda i: (0, 0))
    half = pl.BlockSpec((rows // 2, width), lambda i: (0, 0))
    block = pl.BlockSpec((rows, step), lambda i: (0, i))
    return run(
        functools.partial(feed_kernel, len(x_blocks)),
        "feed",
        [shaped((rows, width), BF16)] * 2
        + [shaped((rows, hidden_cols), BF16)] * 3
        + [shaped((rows // 2, width), F32), shaped((rows // 2, width), BF16)] * 2,
        12 * rows * width * hidden_cols,
        [factor, weights, weights, weights, *x_blocks, *cot_blocks],
        grid=(steps,),
        in_specs=[SCALAR]
        + [
            pl.BlockSpec((width, step), functools.partial(lambda at, i: (0, at + i), k * steps))
            for k in range(3)
        ]
        + [pl.BlockSpec(array.shape, lambda i: (0, 0)) for array in (*x_blocks, *cot_blocks)],
        out_specs=[full] * 2 + [block] * 3 + [half] * 4,
        scratch_shapes=[pltpu.VMEM((rows, width), F32)] * 2,
    )


def weights_kernel(windows, starts, *refs):
    out_ref = refs[-1]
    at = pl.program_id(0)
    for group, (start, stop) in enumerate(starts):
        pairs = refs[2 * windows * group : 2 * windows * (group + 1)]

        @pl.when(jnp.logical_and(at >= start, at < stop))
        def _(pairs=pairs):
            total = None
            for left, right in zip(pairs[:windows], pairs[windows:]):
                term = dot_tn(left[...], right[...])
                total = term if total is None else total + term
            out_ref[...] = total.astype(BF16)


def weight_grads(groups, step, name):
    windows = len(groups[0][0])
    rows, width = groups[0][0][0].shape
    args, in_specs, starts = [], [], []
    at = 0
    for lefts, rights in groups:
        count = rights[0].shape[1] // step
        args += [*lefts, *rights]
        in_specs += [pl.BlockSpec((rows, width), lambda i: (0, 0))] * windows
        in_specs += [
            pl.BlockSpec(
                (rows, step),
                functools.partial(lambda at, count, i: (0, jnp.clip(i - at, 0, count - 1)), at, count),
            )
        ] * windows
        starts.append((at, at + count))
        at += count
    return run(
        functools.partial(weights_kernel, windows, starts),
        name,
        shaped((width, at * step), BF16),
        2 * windows * rows * width * at * step,
        args,
        grid=(at,),
        in_specs=in_specs,
        out_specs=pl.BlockSpec((width, step), lambda i: (0, i)),
    )


def norm_grad(kept_ref, arrived_ref, stream, gain, sums_ref):
    grad_normed = kept_ref[...] + arrived_ref[...].astype(F32)
    normed, inv_std = normalise(stream)
    sums_ref[0:1, :] = jnp.sum(grad_normed * normed, axis=0, keepdims=True)
    sums_ref[1:2, :] = jnp.sum(grad_normed, axis=0, keepdims=True)
    return norm_back(grad_normed, normed, inv_std, gain)


def middle_back_kernel(
    factor_ref, kept_ref, arrived_ref, middle_ref, cot_ref, norms_ref, grad_ref, low_ref, sums_ref
):
    grad_y = cot_ref[...].astype(F32) * factor_ref[0, 0]
    grad = grad_y + norm_grad(
        kept_ref, arrived_ref, middle_ref[...], norms_ref[2:3, :], sums_ref
    )
    grad_ref[...] = grad
    low_ref[...] = grad.astype(BF16)


def second_norm_back(factor, kept, arrived, middle, cot_rows, norms):
    return run(
        middle_back_kernel,
        "second_norm_back",
        [
            shaped(kept.shape, F32),
            shaped(kept.shape, BF16),
            shaped((2, kept.shape[1]), F32),
        ],
        40 * kept.size,
        [factor, kept, arrived, middle, cot_rows, norms],
        in_specs=[SCALAR] + [pl.BlockSpec(memory_space=pltpu.VMEM)] * 5,
    )


def turn_back_kernel(
    dq_ref, own_ref, near_ref, far_ref, cos_ref, sin_ref, w_ref, out_ref, kept_ref, sent_ref
):
    cols = dq_ref.shape[1]
    cosine, sine = cos_ref[...], sin_ref[...]
    out_ref[:, :cols] = dq_ref[...]
    for at in range(0, cols, PAIR):
        part = slice(at, at + PAIR)
        key = (
            own_ref[0, :, part].astype(F32)
            + near_ref[0, :, part].astype(F32)
            + far_ref[0, :, part].astype(F32)
        )
        out_ref[:, cols + at : cols + at + PAIR] = (
            key * cosine - swap_halves(key) * sine
        ).astype(BF16)
    out_ref[:, 2 * cols :] = (
        own_ref[1].astype(F32) + near_ref[1].astype(F32) + far_ref[1].astype(F32)
    ).astype(BF16)
    half = kept_ref.shape[0]
    sent_ref[...] = dot_nt(out_ref[half:, :], w_ref[:, : 3 * cols]).astype(BF16)
    kept_ref[...] = dot_nt(out_ref[:half, :], w_ref[:, : 3 * cols])


def turn_back(grad_query, own, near, far, cosine, sine, w_att):
    rows, cols = grad_query.shape
    width = w_att.shape[0]
    return run(
        turn_back_kernel,
        "turn_back",
        [
            shaped((rows, 3 * cols), BF16),
            shaped((rows // 2, width), F32),
            shaped((rows // 2, width), BF16),
        ],
        6 * rows * cols * width,
        [grad_query, own, near, far, cosine, sine, w_att],
    )


def input_back_kernel(window, kept_ref, arrived_ref, x_ref, grad_ref, norms_ref, *refs):
    out_ref, sums_ref = refs[-2:]
    out_ref[0] = grad_ref[...] + norm_grad(
        kept_ref, arrived_ref, x_ref[...].astype(F32), norms_ref[0:1, :], sums_ref
    )


def first_norm_back(window, windows, kept, arrived, x_rows, grad_middle, norms, earlier):
    rows, width = kept.shape
    args = [kept, arrived, x_rows, grad_middle, norms] + ([] if earlier is None else [earlier])
    whole = [pl.BlockSpec(array.shape, lambda i: (0, 0)) for array in args[:5]]
    return run(
        functools.partial(input_back_kernel, window),
        "first_norm_back",
        [shaped((windows, rows, width), F32), shaped((2, width), F32)],
        40 * rows * width,
        args,
        grid=(1,),
        in_specs=whole + ([] if earlier is None else [pl.BlockSpec(memory_space=pl.ANY)]),
        out_specs=[
            pl.BlockSpec((1, rows, width), lambda i: (window, 0, 0)),
            pl.BlockSpec((2, width), lambda i: (0, 0)),
        ],
        input_output_aliases={} if earlier is None else {5: 0},
    )


def result_kernel(windows, *refs):
    out_ref = refs[-1]
    for w in range(windows):
        middle_ref, kept_ref, arrived_ref = refs[3 * w : 3 * w + 3]
        out_ref[w] = (
            middle_ref[...] + (kept_ref[...] + arrived_ref[...].astype(F32))
        ).astype(BF16)


def results(parts):
    rows, width = parts[0][0].shape
    return run(
        functools.partial(result_kernel, len(parts)),
        "results",
        shaped((len(parts), rows, width), BF16),
        2 * len(parts) * rows * width,
        [array for part in parts for array in part],
    )


def local(
    tokens,
    cotangent,
    species,
    counts,
    species_scale,
    norm1_gain,
    norm1_bias,
    w_query,
    w_key,
    w_value,
    w_out,
    norm2_gain,
    norm2_bias,
    w_gate,
    w_up,
    w_down,
):
    windows_here, own_rows, model_width = tokens.shape
    tensor_size = lax.axis_size("tensor")
    seq_size = lax.axis_size("seq")
    block_rows = own_rows * tensor_size
    head_cols = w_query.shape[1]
    hidden_cols = w_gate.shape[1]
    every = ("dp", "seq", "tensor")
    shards = ("dp", "seq")

    w_att = lax.all_gather(
        jnp.concatenate([w_query, w_key, w_value, w_out.T], axis=1), shards, axis=0, tiled=True
    )
    w_ffn = lax.all_gather(
        jnp.concatenate([w_gate, w_up, w_down.T], axis=1), shards, axis=0, tiled=True
    )

    norms = gather_ordered(
        jnp.stack([norm1_gain, norm1_bias, norm2_gain, norm2_bias])[None], every
    )
    norms = norms.transpose(1, 0, 2).reshape(4, model_width)

    own_at = lax.axis_index("tensor")
    starts = jnp.concatenate(
        [
            lax.iota(jnp.int32, own_rows) + (own_at ^ other) * own_rows
            for other in range(tensor_size)
        ]
    )
    positions = (lax.axis_index("seq") * block_rows + starts).astype(F32)
    cos_half, sin_half = angles(positions, HEAD_DIM)
    cosine = jnp.concatenate([cos_half] * 4, axis=1)
    sine = jnp.concatenate([-sin_half, sin_half] * 2, axis=1)

    labels = lax.broadcasted_iota(jnp.int32, (windows_here, species_scale.shape[0]), 1)
    chosen = jnp.sum(jnp.where(species[:, None] == labels, species_scale[None, :], 0.0), axis=1)
    weighted = counts.astype(F32) * chosen
    weight_total = jnp.broadcast_to(jnp.sum(weighted), (8, 128))
    bit = 1
    while bit < lax.axis_size("dp"):
        weight_total = weight_total + swap(weight_total, "dp", bit)
        bit *= 2
    factor = weighted * float(windows_here * lax.axis_size("dp")) / weight_total[0, 0]

    windows = range(windows_here)
    factors = [factor[w].reshape(1, 1) for w in windows]
    top_bit = seq_size // 2

    def on_chip(block):
        blocks = [block]
        bit = 1
        while bit < top_bit:
            blocks = blocks + [swap(one, "seq", bit) for one in blocks]
            bit *= 2
        return blocks

    token_blocks = [spread(tokens[w], "tensor") for w in windows]
    normed_rows, queries, near_blocks, far_first = [], [], [], []
    for w in windows:
        normed, query, own_kv = project(token_blocks[w], norms, w_att, cosine, sine)
        normed_rows.append(normed)
        queries.append(query)
        far_first.append(swap(own_kv, "seq", top_bit))
        near_blocks.append(on_chip(own_kv))
    states = []
    for w in windows:
        query = hold(queries[w], states[-1] if states else ())
        states.append(attend(query, near_blocks[w], None, None))
    far_blocks = [on_chip(hold(far_first[w], states[w])) for w in windows]
    cot_blocks = [spread(hold(cotangent[w], states[0]), "tensor") for w in windows]
    attended, wide_attended, logs, middles, mid_blocks = [], [], [], [], []
    for w in windows:
        query = hold(queries[w], states[-1], attended[-1] if attended else ())
        low, wide, log_row, kept, sent = attend(query, far_blocks[w], states[w], w_att)
        attended.append(low)
        wide_attended.append(wide)
        logs.append(log_row)
        middle, normed_mid = second_norm(tokens[w], *scatter_pair(kept, sent, "tensor"), norms)
        middles.append(middle)
        mid_blocks.append(spread(normed_mid, "tensor"))

    fed = []
    for w in windows:
        blocks = hold(mid_blocks[w], fed[-1] if fed else ())
        fed.append(feed(blocks, cot_blocks[w], factors[w], w_ffn))
    mid_rows, grad_y_rows, hiddens, grad_gates, grad_ups = [
        [one[at] for one in fed] for at in range(5)
    ]
    grad_middles, grad_mid_blocks, second_sums = [], [], []

    def through_second_norm(w, *after):
        kept, arrived = scatter_pair(fed[w][7], fed[w][8], "tensor")
        grad_middle, low, sums = second_norm_back(
            factors[w], hold(kept, *after), arrived, middles[w], cotangent[w], norms
        )
        grad_middles.append(grad_middle)
        grad_mid_blocks.append(spread(low, "tensor"))
        second_sums.append(sums)

    for w in windows[:-1]:
        through_second_norm(w)
    g_ffn_part = weight_grads(
        [
            (mid_rows, grad_gates),
            (mid_rows, grad_ups),
            (grad_y_rows, hold(hiddens, grad_middles)),
        ],
        min(512, hidden_cols),
        "feed_weights",
    )
    g_ffn = lax.psum_scatter(g_ffn_part, shards, scatter_dimension=0, tiled=True).astype(F32)
    through_second_norm(windows[-1], g_ffn_part)

    def fold(blocks, down_to):
        while len(blocks) > down_to:
            half = len(blocks) // 2
            arrived = [swap(block, "seq", half) for block in blocks[half:]]
            blocks = [
                (kept.astype(F32) + new.astype(F32)).astype(BF16)
                for kept, new in zip(blocks[:half], arrived)
            ]
        return blocks

    slots = seq_size // 2
    far_sums, dq_states, grad_mid_rows = [], [], []
    for w in windows:
        query = hold(queries[w], dq_states[-1][0] if dq_states else grad_middles[-1])
        parts = attend_back(
            query, wide_attended[w], logs[w], far_blocks[w], grad_mid_blocks[w], w_att, None
        )
        dq_states.append((parts[0], parts[1 + slots]))
        grad_mid_rows.append(parts[2 + slots])
        far_sums.append(swap(fold(list(parts[1 : 1 + slots]), 1)[0], "seq", top_bit))
    result_parts = [
        (middles[w], *scatter_pair(fed[w][5], hold(fed[w][6], dq_states[0]), "tensor"))
        for w in windows
    ]
    grad_queries, near_pairs = [], []
    for w in windows:
        query = hold(queries[w], grad_queries[-1] if grad_queries else dq_states[-1][0])
        parts = attend_back(
            query, wide_attended[w], logs[w], near_blocks[w], dq_states[w], None, (cosine, sine)
        )
        grad_queries.append(parts[0])
        blocks = fold(list(parts[1:]), 2)
        near_pairs.append((blocks[0], swap(blocks[1], "seq", 1)))
    output = results(result_parts)

    grad_qkvs, first_parts = [], []
    for w in windows:
        grad_qkv, kept, sent = turn_back(
            grad_queries[w], *near_pairs[w], far_sums[w], cosine, sine, w_att
        )
        grad_qkvs.append(grad_qkv)
        first_parts.append(scatter_pair(kept, sent, "tensor"))
    g_att_part = weight_grads(
        [(normed_rows, grad_qkvs), (grad_mid_rows, attended)], head_cols, "attend_weights"
    )
    g_att = lax.psum_scatter(
        hold(g_att_part, g_ffn), shards, scatter_dimension=0, tiled=True
    ).astype(F32)
    input_grad = None
    first_sums = []
    for w in windows:
        kept, arrived = first_parts[w]
        input_grad, sums = first_norm_back(
            w,
            windows_here,
            hold(kept, g_att_part),
            arrived,
            tokens[w],
            grad_middles[w],
            norms,
            input_grad,
        )
        first_sums.append(sums)

    norm_sums = jnp.concatenate([sum(first_sums), sum(second_sums)], axis=0)
    devices = model_width // norm1_gain.shape[0]
    norm_sums = norm_sums.reshape(4, devices, -1).transpose(1, 0, 2)
    norm_sums = scatter_ordered(norm_sums, every)[0]

    return (
        output,
        input_grad,
        norm_sums[0],
        norm_sums[1],
        g_att[:, :head_cols],
        g_att[:, head_cols : 2 * head_cols],
        g_att[:, 2 * head_cols : 3 * head_cols],
        g_att[:, 3 * head_cols :].T,
        norm_sums[2],
        norm_sums[3],
        g_ffn[:, :hidden_cols],
        g_ffn[:, hidden_cols : 2 * hidden_cols],
        g_ffn[:, 2 * hidden_cols :].T,
    )


def solution(mesh):
    rows = P("dp", ("seq", "tensor"), None)
    vector = P(("dp", "seq", "tensor"))
    tall = P(("dp", "seq"), "tensor")
    flat = P("tensor", ("dp", "seq"))
    return jax.shard_map(
        local,
        mesh=mesh,
        in_specs=(
            rows, rows, P("dp"), P("dp"), P(), vector, vector,
            tall, tall, tall, flat, vector, vector, tall, tall, flat,
        ),
        out_specs=(
            rows, rows, vector, vector, tall, tall, tall, flat,
            vector, vector, tall, tall, flat,
        ),
        check_vma=False,
    )
```

time: 686 us -> 546 us (0.80)
  Pallas kernels: 120 us -> 246 us
  matrix products: 114 us -> 0 us
  waiting for transfers between devices: 315 us -> 205 us
  other arithmetic: 52.9 us -> 13.2 us
    pallas_call x12 -> x23, Pallas kernels: 120 us -> 246 us  [run(): pl.pallas_call(kernel, out_shape=out_shape, compiler_params=pltpu.Compile...]
    reduce_scatter x2, waiting for transfers between devices: 116 us -> 0.01 us  [the longest x1 0.01 us: local(): lax.psum_scatter(g_ffn_part, shards, scatter_dimension=0, tiled=True)]
    dot_general x18 -> x0, matrix products: 114 us -> none  [the longest x6 45 us: dot_nn(): lax.dot_general(left, right, (((1,), (0,)), ((), ())), preferred_element_...]
    all_gather x2, waiting for transfers between devices: 18.3 us -> 32.8 us  [the longest x1 32.8 us: local(): lax.all_gather(jnp.concatenate([w_query, w_key, w_value, w_out.T], axis=1...]
    concatenate x4 -> x3, other arithmetic: 17.3 us -> 3.79 us  [the longest x1 2.04 us: local(): jnp.concatenate([w_gate, w_up, w_down.T], axis=1)]
    reduce_sum x11 -> x0, other arithmetic: 10.7 us -> none  [the longest x2 3.79 us: local(): gain_one_sum = gain_one_sum + jnp.sum(grad_normed1 * normed1, axis=0)]
    unnamed x134 -> x102, local copies, waits for them, and re-layouts: 9.13 us -> 17.8 us
    ppermute x40, waiting for transfers between devices: 180 us -> 172 us  [swap(): return lax.ppermute(array, axis, [(i, i ^ bit) for i in range(size)])]
  transfers between devices with their start and end apart: 44 -> 44, of which waited for: 25 -> 21; matrix products, arithmetic and copies ran while one was open for 23% -> 3% of each run, Pallas kernels for 17% -> 41%
where the time goes in v2:
time: 546 us; the launch traced here: 539 us
  Pallas kernels  246 us (45%)
  waiting for transfers between devices  205 us (38%)
  starting transfers between devices  34.9 us (6%)
  local copies, waits for them, and re-layouts  25.3 us (5%)
  between operations  14.9 us (3%)
  other arithmetic  13.2 us (2%)
    pallas_call x23, Pallas kernels, run(): pl.pallas_call(kernel, out_shape=out_shape, compiler_params=pltpu.Compile...  246 us
    ppermute x40, waiting for transfers between devices, swap(): return lax.ppermute(array, axis, [(i, i ^ bit) for i in range(size)])  172 us
    ppermute x40, starting transfers between devices, swap(): return lax.ppermute(array, axis, [(i, i ^ bit) for i in range(size)])  34.8 us
    all_gather x1, waiting for transfers between devices, local(): lax.all_gather(jnp.concatenate([w_query, w_key, w_value, w_out.T], axis=1...  32.8 us
    unnamed x102, local copies, waits for them, and re-layouts  17.8 us
  transfers between devices with their start and end apart: 44, of which 21 were waited for; matrix products, arithmetic and copies ran while one was open for 3% of the time, Pallas kernels for 41%

profile of v2, /device:TPU:0, one launch (start us, length us, event | category | flops | bytes accessed | tf_op | source)
XLA Modules:
  0.0 539.0 jit_solution(6373313692777618477)
XLA Ops:
  7.3 1.7 pad_maximum_fusion.1
  9.1 2.0 pad_maximum_fusion
  11.3 3.0 collective-permute-start
  14.5 2.0 collective-permute-start.6
  16.6 1.1 collective-permute-done.1
  17.8 1.5 collective-permute-start.2
  20.3 1.1 collective-permute-done.2
  21.4 1.6 collective-permute-start.3
  24.1 1.2 collective-permute-done.3
  25.3 2.7 collective-permute-start.4
  28.9 2.9 collective-permute-done.4
  32.5 32.8 %all-gather.3.cloned.1.call-done.w_ref.refs_6_.refs_5_ = bf16[1024,2048]{1,0:T(8,128)(2,1)} async-done(((bf16[64,2048]{1,0:T(8,128)(2,1)}), bf16[1024,2048]{1,0:T(8,128)(2,1)}) %all-gather.3.cloned.1.call-update) | async-done | bytes 4194320 | tf_op jit(solution)/shard_map/all_gather | solution.py:727
  65.3 5.8 %project.2 = (bf16[512,1024]{1,0:T(8,128)(2,1)}, bf16[512,512]{1,0:T(8,128)(2,1)}, bf16[2,512,512]{2,1,0:T(8,128)(2,1)}) custom-call(f32[4,1024]{1,0:T(4,128)} %reshape.61.norms_ref, bf16[1024,2048]{1,0:T(8,128)(2,1)} %all-gather.3.cloned.1.call-done.w_ref.refs_6_.refs_5_, f32[512,128]{1,0:T(8,128)} %pad_maximum_fusion.2.cos_ref.refs_7_, ...), custom_call_target="tpu_custom_call" | custom-call | flops 1610612736 | bytes 8404992 | tf_op jit(solution)/shard_map/project/pallas_call | solution.py:131
  72.7 6.3 %project.3 = (bf16[512,1024]{1,0:T(8,128)(2,1)}, bf16[512,512]{1,0:T(8,128)(2,1)}, bf16[2,512,512]{2,1,0:T(8,128)(2,1)}) custom-call(f32[4,1024]{1,0:T(4,128)} %reshape.61.norms_ref, bf16[1024,2048]{1,0:T(8,128)(2,1)} %all-gather.3.cloned.1.call-done.w_ref.refs_6_.refs_5_, f32[512,128]{1,0:T(8,128)} %pad_maximum_fusion.2.cos_ref.refs_7_, ...), custom_call_target="tpu_custom_call" | custom-call | flops 1610612736 | bytes 8404992 | tf_op jit(solution)/shard_map/project/pallas_call | solution.py:131
  79.0 1.5 collective-permute-start.16
  81.5 10.6 %attend_near.2 = (f32[512,512]{1,0:T(8,128)}, f32[512,512]{1,0:T(8,128)}, f32[512,512]{1,0:T(8,128)}) custom-call(bf16[512,512]{1,0:T(8,128)(2,1)} %get-tuple-element.178.refs_0_, bf16[2,512,512]{2,1,0:T(8,128)(2,1)} %get-tuple-element.114.refs_1_.refs_4_, bf16[2,512,512]{2,1,0:T(8,128)(2,1)} %copy-done.32), custom_call_target="tpu_custom_call" | custom-call | flops 4294967296 | bytes 5767168 | tf_op jit(solution)/shard_map/attend_near/pallas_call | solution.py:131
  92.1 13.9 %collective-permute-done.9.refs_1_.refs_6_ = bf16[2,512,512]{2,1,0:T(8,128)(2,1)S(1)} collective-permute-done((bf16[2,512,512]{2,1,0:T(8,128)(2,1)}, bf16[2,512,512]{2,1,0:T(8,128)(2,1)S(1)}, u32[]{:S(2)}, u32[]{:S(2)}) %collective-permute-start.9) | collective-permute-done | bytes 1048608 | tf_op jit(solution)/shard_map/ppermute | solution.py:44
  107.0 10.2 %attend_near.3 = (f32[512,512]{1,0:T(8,128)}, f32[512,512]{1,0:T(8,128)}, f32[512,512]{1,0:T(8,128)}) custom-call(bf16[512,512]{1,0:T(8,128)(2,1)} %get-tuple-element.180.refs_0_, bf16[2,512,512]{2,1,0:T(8,128)(2,1)} %get-tuple-element.119.refs_1_.refs_4_, bf16[2,512,512]{2,1,0:T(8,128)(2,1)} %copy-done.31), custom_call_target="tpu_custom_call" | custom-call | flops 4294967296 | bytes 5767168 | tf_op jit(solution)/shard_map/attend_near/pallas_call | solution.py:131
  117.2 24.6 %collective-permute-done.16.refs_1_.refs_6_ = bf16[2,512,512]{2,1,0:T(8,128)(2,1)S(1)} collective-permute-done((bf16[2,512,512]{2,1,0:T(8,128)(2,1)}, bf16[2,512,512]{2,1,0:T(8,128)(2,1)S(1)}, u32[]{:S(2)}, u32[]{:S(2)}) %collective-permute-start.16) | collective-permute-done | bytes 1048608 | tf_op jit(solution)/shard_map/ppermute | solution.py:44
  143.4 1.6 collective-permute-start.12
  146.1 14.8 %attend_far.2 = (bf16[512,512]{1,0:T(8,128)(2,1)}, f32[512,512]{1,0:T(8,128)}, f32[512,512]{1,0:T(8,128)}, f32[256,1024]{1,0:T(8,128)}, bf16[256,1024]{1,0:T(8,128)(2,1)}) custom-call(bf16[512,512]{1,0:T(8,128)(2,1)} %get-tuple-element.178.refs_0_, bf16[2,512,512]{2,1,0:T(8,128)(2,1)} %copy-done.34, bf16[2,512,512]{2,1,0:T(8,128)(2,1)} %copy-done.36, ...), custom_call_target="tpu_custom_call" | custom-call | flops 4294967296 | bytes 14155776 | tf_op jit(solution)/shard_map/attend_far/pallas_call | solution.py:131
  160.9 1.5 collective-permute-start.11
  164.8 14.8 %attend_far.3 = (bf16[512,512]{1,0:T(8,128)(2,1)}, f32[512,512]{1,0:T(8,128)}, f32[512,512]{1,0:T(8,128)}, f32[256,1024]{1,0:T(8,128)}, bf16[256,1024]{1,0:T(8,128)(2,1)}) custom-call(bf16[512,512]{1,0:T(8,128)(2,1)} %get-tuple-element.180.refs_0_, bf16[2,512,512]{2,1,0:T(8,128)(2,1)} %copy-done.33, bf16[2,512,512]{2,1,0:T(8,128)(2,1)} %copy-done.35, ...), custom_call_target="tpu_custom_call" | custom-call | flops 4294967296 | bytes 14155776 | tf_op jit(solution)/shard_map/attend_far/pallas_call | solution.py:131
  179.6 1.6 collective-permute-start.18
  181.9 3.0 second_norm.2
  187.8 1.6 collective-permute-start.20
  189.4 9.0 %collective-permute-done.18.arrived_ref = bf16[256,1024]{1,0:T(8,128)(2,1)S(1)} collective-permute-done((bf16[256,1024]{1,0:T(8,128)(2,1)}, bf16[256,1024]{1,0:T(8,128)(2,1)S(1)}, u32[]{:S(2)}, u32[]{:S(2)}) %collective-permute-start.18) | collective-permute-done | bytes 524320 | tf_op jit(solution)/shard_map/ppermute | solution.py:44
  199.2 2.8 second_norm.3
  202.0 1.5 collective-permute-start.19
  203.5 6.1 %collective-permute-done.14.refs_1_ = bf16[256,1024]{1,0:T(8,128)(2,1)S(1)} collective-permute-done((bf16[256,1024]{1,0:T(8,128)(2,1)}, bf16[256,1024]{1,0:T(8,128)(2,1)S(1)}, u32[]{:S(2)}, u32[]{:S(2)}) %collective-permute-start.14) | collective-permute-done | bytes 524320 | tf_op jit(solution)/shard_map/ppermute | solution.py:44
  210.6 23.5 %feed.2 = (bf16[512,1024]{1,0:T(8,128)(2,1)}, bf16[512,1024]{1,0:T(8,128)(2,1)}, bf16[512,2048]{1,0:T(8,128)(2,1)}, bf16[512,2048]{1,0:T(8,128)(2,1)}, bf16[512,...) custom-call(f32[1,1]{1,0:T(1,128)} %bitcast.10.factor_ref, ...), custom_call_target="tpu_custom_call" | custom-call | flops 12884901888 | bytes 51380228 | tf_op jit(solution)/shard_map/feed/pallas_call | solution.py:131
  234.1 1.5 collective-permute-start.21
  236.6 23.4 %feed.3 = (bf16[512,1024]{1,0:T(8,128)(2,1)}, bf16[512,1024]{1,0:T(8,128)(2,1)}, bf16[512,2048]{1,0:T(8,128)(2,1)}, bf16[512,2048]{1,0:T(8,128)(2,1)}, bf16[512,...) custom-call(f32[1,1]{1,0:T(1,128)} %bitcast.13.factor_ref, ...), custom_call_target="tpu_custom_call" | custom-call | flops 12884901888 | bytes 51380228 | tf_op jit(solution)/shard_map/feed/pallas_call | solution.py:131
  260.8 4.6 second_norm_back.2
  265.4 22.5 %feed_weights.1 = bf16[1024,6144]{1,0:T(8,128)(2,1)} custom-call(bf16[512,1024]{1,0:T(8,128)(2,1)} %get-tuple-element.140.refs_0_.refs_4_, bf16[512,1024]{1,0:T(8,128)(2,1)} %get-tuple-element.151.refs_1_.refs_5_, bf16[512,2048]{1,0:T(8,128)(2,1)} %get-tuple-element.143.refs_2_, bf16[512,2048]{1,0:T(8,128)(2,1)} %get-tuple-element.152.refs_3_, ...), custom_call_target="tpu_custom_call" | custom-call | flops 12884901888 | bytes 31457280 | tf_op jit(solution)/shard_map/feed_weights/pallas_call | solution.py:131
  289.5 1.5 collective-permute-start.23
  291.0 12.8 %collective-permute-done.22.arrived_ref = bf16[256,1024]{1,0:T(8,128)(2,1)S(1)} collective-permute-done((bf16[256,1024]{1,0:T(8,128)(2,1)S(1)}, bf16[256,1024]{1,0:T(8,128)(2,1)S(1)}, u32[]{:S(2)}, u32[]{:S(2)}) %collective-permute-start.22) | collective-permute-done | bytes 524320 | tf_op jit(solution)/shard_map/ppermute | solution.py:44
  304.6 4.9 second_norm_back.3
  310.1 4.9 collective-permute-done.23.refs_4_
  315.8 17.2 %attend_back_far.2 = (f32[512,512]{1,0:T(8,128)}, bf16[2,512,512]{2,1,0:T(8,128)(2,1)}, bf16[2,512,512]{2,1,0:T(8,128)(2,1)}, bf16[512,512]{1,0:T(8,128)(2,1)}, bf16[512,1024]{1,0:T(8,128)(2,1)}) custom-call(bf16[512,512]{1,0:T(8,128)(2,1)} %get-tuple-element.178.refs_0_, f32[512,512]{1,0:T(8,128)} %get-tuple-element.164.refs_1_, ...), custom_call_target="tpu_custom_call" | custom-call | flops 10737418240 | bytes 14680064 | tf_op jit(solution)/shard_map/attend_back_far/pallas_call | solution.py:131
  333.9 16.8 %attend_back_far.3 = (f32[512,512]{1,0:T(8,128)}, bf16[2,512,512]{2,1,0:T(8,128)(2,1)}, bf16[2,512,512]{2,1,0:T(8,128)(2,1)}, bf16[512,512]{1,0:T(8,128)(2,1)}, bf16[512,1024]{1,0:T(8,128)(2,1)}) custom-call(bf16[512,512]{1,0:T(8,128)(2,1)} %get-tuple-element.180.refs_0_, f32[512,512]{1,0:T(8,128)} %get-tuple-element.174.refs_1_, ...), custom_call_target="tpu_custom_call" | custom-call | flops 10737418240 | bytes 14680064 | tf_op jit(solution)/shard_map/attend_back_far/pallas_call | solution.py:131
  350.7 15.1 %attend_back_near.2 = (bf16[512,512]{1,0:T(8,128)(2,1)}, bf16[2,512,512]{2,1,0:T(8,128)(2,1)}, bf16[2,512,512]{2,1,0:T(8,128)(2,1)}) custom-call(bf16[512,512]{1,0:T(8,128)(2,1)} %get-tuple-element.178.refs_0_, f32[512,512]{1,0:T(8,128)} %get-tuple-element.164.refs_1_, f32[512,512]{1,0:T(8,128)} %get-tuple-element.165.refs_2_, ...), custom_call_target="tpu_custom_call" | custom-call | flops 10737418240 | bytes 9437184 | tf_op jit(solution)/shard_map/attend_back_near/pallas_call | solution.py:131
  366.5 15.4 %attend_back_near.3 = (bf16[512,512]{1,0:T(8,128)(2,1)}, bf16[2,512,512]{2,1,0:T(8,128)(2,1)}, bf16[2,512,512]{2,1,0:T(8,128)(2,1)}) custom-call(bf16[512,512]{1,0:T(8,128)(2,1)} %get-tuple-element.180.refs_0_, f32[512,512]{1,0:T(8,128)} %get-tuple-element.174.refs_1_, f32[512,512]{1,0:T(8,128)} %get-tuple-element.175.refs_2_, ...), custom_call_target="tpu_custom_call" | custom-call | flops 10737418240 | bytes 9437184 | tf_op jit(solution)/shard_map/attend_back_near/pallas_call | solution.py:131
  383.6 1.5 collective-permute-start.29
  385.1 32.0 %collective-permute-done.32.far_ref = bf16[2,512,512]{2,1,0:T(8,128)(2,1)S(1)} collective-permute-done((bf16[2,512,512]{2,1,0:T(8,128)(2,1)S(1)}, bf16[2,512,512]{2,1,0:T(8,128)(2,1)S(1)}, u32[]{:S(2)}, u32[]{:S(2)}) %collective-permute-start.32) | collective-permute-done | bytes 1048608 | tf_op jit(solution)/shard_map/ppermute | solution.py:44
  418.1 6.6 %turn_back.3 = (bf16[512,1536]{1,0:T(8,128)(2,1)}, f32[256,1024]{1,0:T(8,128)}, bf16[256,1024]{1,0:T(8,128)(2,1)}) custom-call(bf16[512,512]{1,0:T(8,128)(2,1)} %get-tuple-element.179.dq_ref, bf16[2,512,512]{2,1,0:T(8,128)(2,1)} %get-tuple-element.190.own_ref, bf16[2,512,512]{2,1,0:T(8,128)(2,1)} %copy-done.10, bf16[2,512,512]{2,1,0:T(8,128)(2,1)} %copy-done.12, ...), custom_call_target="tpu_custom_call" | custom-call | flops 1610612736 | bytes 11534336 | tf_op jit(solution)/shard_map/turn_back/pallas_call | solution.py:131
  424.7 14.1 %collective-permute-done.29.far_ref = bf16[2,512,512]{2,1,0:T(8,128)(2,1)S(1)} collective-permute-done((bf16[2,512,512]{2,1,0:T(8,128)(2,1)S(1)}, bf16[2,512,512]{2,1,0:T(8,128)(2,1)S(1)}, u32[]{:S(2)}, u32[]{:S(2)}) %collective-permute-start.29) | collective-permute-done | bytes 1048608 | tf_op jit(solution)/shard_map/ppermute | solution.py:44
  439.8 6.5 %turn_back.2 = (bf16[512,1536]{1,0:T(8,128)(2,1)}, f32[256,1024]{1,0:T(8,128)}, bf16[256,1024]{1,0:T(8,128)(2,1)}) custom-call(bf16[512,512]{1,0:T(8,128)(2,1)} %get-tuple-element.182.dq_ref, bf16[2,512,512]{2,1,0:T(8,128)(2,1)} %get-tuple-element.183.own_ref, bf16[2,512,512]{2,1,0:T(8,128)(2,1)} %copy-done.9, bf16[2,512,512]{2,1,0:T(8,128)(2,1)} %copy-done.11, ...), custom_call_target="tpu_custom_call" | custom-call | flops 1610612736 | bytes 11534336 | tf_op jit(solution)/shard_map/turn_back/pallas_call | solution.py:131
  446.3 9.6 %attend_weights.1 = bf16[1024,2048]{1,0:T(8,128)(2,1)} custom-call(bf16[512,1024]{1,0:T(8,128)(2,1)} %get-tuple-element.188.refs_0_, bf16[512,1024]{1,0:T(8,128)(2,1)} %get-tuple-element.189.refs_1_, bf16[512,1536]{1,0:T(8,128)(2,1)} %get-tuple-element.194.refs_2_, bf16[512,1536]{1,0:T(8,128)(2,1)} %get-tuple-element.195.refs_3_, ...), custom_call_target="tpu_custom_call" | custom-call | flops 4294967296 | bytes 12582912 | tf_op jit(solution)/shard_map/attend_weights/pallas_call | solution.py:131
  455.9 1.2 convert_element_type.42
  458.8 1.4 collective-permute-start.33
  460.2 12.8 %collective-permute-done.34.arrived_ref = bf16[256,1024]{1,0:T(8,128)(2,1)S(1)} collective-permute-done((bf16[256,1024]{1,0:T(8,128)(2,1)S(1)}, bf16[256,1024]{1,0:T(8,128)(2,1)S(1)}, u32[]{:S(2)}, u32[]{:S(2)}) %collective-permute-start.34) | collective-permute-done | bytes 524320 | tf_op jit(solution)/shard_map/ppermute | solution.py:44
  473.8 3.7 first_norm_back.2
  477.5 5.0 collective-permute-done.33.arrived_ref
  483.4 4.0 first_norm_back.3
  488.3 6.8 %collective-permute-done.35 = f32[16,4,32]{2,1,0:T(4,128)S(1)} collective-permute-done((f32[16,4,32]{2,1,0:T(4,128)S(1)}, f32[16,4,32]{2,1,0:T(4,128)S(1)}, u32[]{:S(2)}, u32[]{:S(2)}) %collective-permute-start.35) | collective-permute-done | bytes 8224 | tf_op jit(solution)/shard_map/ppermute | solution.py:44
  495.2 3.7 collective-permute-done.36
  499.7 1.7 collective-permute-start.24
  501.4 1.2 collective-permute-done.37
  502.7 1.2 collective-permute-done.38
  504.4 9.9 %collective-permute-done.25.refs_5_ = bf16[256,1024]{1,0:T(8,128)(2,1)S(1)} collective-permute-done((bf16[256,1024]{1,0:T(8,128)(2,1)S(1)}, bf16[256,1024]{1,0:T(8,128)(2,1)S(1)}, u32[]{:S(2)}, u32[]{:S(2)}) %collective-permute-start.25) | collective-permute-done | bytes 524320 | tf_op jit(solution)/shard_map/ppermute | solution.py:44
  514.3 7.4 %collective-permute-done.24.refs_2_ = bf16[256,1024]{1,0:T(8,128)(2,1)S(1)} collective-permute-done((bf16[256,1024]{1,0:T(8,128)(2,1)S(1)}, bf16[256,1024]{1,0:T(8,128)(2,1)S(1)}, u32[]{:S(2)}, u32[]{:S(2)}) %collective-permute-start.24) | collective-permute-done | bytes 524320 | tf_op jit(solution)/shard_map/ppermute | solution.py:44
  522.5 3.8 results.1
  530.4 1.7 fusion.6
  (203 shorter events, 39.3 us)
Async XLA Ops:
  7.2 4.0 copy-start.30
  7.2 7.1 %copy-start.7 = (bf16[2,256,1024]{2,1,0:T(8,128)(2,1)S(1)}, bf16[2,256,1024]{2,1,0:T(8,128)(2,1)}, u32[]{:S(2)}) copy-start(bf16[2,256,1024]{2,1,0:T(8,128)(2,1)} %param.16) | copy-start | bytes 3145732
  7.2 58.0 %all-gather.3.cloned.1.call-start = ((), (), s32[]{:S(2)}) async-start(), calls=%async_computation.2 | async-start | bytes 4456448 | tf_op jit(solution)/shard_map/all_gather | solution.py:727
  9.0 200.6 %all-gather.5.cloned.1.call-start = ((), (), s32[]{:S(2)}) async-start(), calls=%async_computation.3 | async-start | bytes 13369344 | tf_op jit(solution)/shard_map/all_gather | solution.py:730
  11.2 444.7 %reduce-scatter.3.cloned.1.call-start = ((), (), s32[]{:S(2)}) async-start(), calls=%async_computation.4 | async-start | bytes 13369344 | tf_op jit(solution)/shard_map/reduce_scatter | solution.py:827
  11.3 5.2 collective-permute-start
  14.4 50.9 %copy-start.1 = (bf16[256,1024]{1,0:T(8,128)(2,1)}, bf16[256,1024]{1,0:T(8,128)(2,1)S(1)}, u32[]{:S(2)}) copy-start(bf16[256,1024]{1,0:T(8,128)(2,1)S(1)} %get-tuple-element.214.refs_0_.x_ref) | copy-start | bytes 1572868
  14.4 56.7 %copy-start = (bf16[256,1024]{1,0:T(8,128)(2,1)}, bf16[256,1024]{1,0:T(8,128)(2,1)S(1)}, u32[]{:S(2)}) copy-start(bf16[256,1024]{1,0:T(8,128)(2,1)S(1)} %get-tuple-element.213.refs_0_.x_ref) | copy-start | bytes 1572868
  14.4 18.1 %collective-permute-start.5 = (bf16[256,1024]{1,0:T(8,128)(2,1)S(1)}, bf16[256,1024]{1,0:T(8,128)(2,1)}, u32[]{:S(2)}, u32[]{:S(2)}) collective-permute-start(bf16[256,1024]{1,0:T(8,128)(2,1)S(1)} %get-tuple-element.214.refs_0_.x_ref), channel_id=1, source_target_pairs={{0,1},{1,0},{2,3},{3,2},{4,5},{5,4},{6,7},{7,6},{8,9},{9,8},{10,11... | collective-permute-start | bytes 1572872 | tf_op jit(solution)/shard_map/ppermute | solution.py:44
  14.5 57.4 %collective-permute-start.6 = (bf16[256,1024]{1,0:T(8,128)(2,1)S(1)}, bf16[256,1024]{1,0:T(8,128)(2,1)S(1)}, u32[]{:S(2)}, u32[]{:S(2)}) collective-permute-start(bf16[256,1024]{1,0:T(8,128)(2,1)S(1)} %get-tuple-element.213.refs_0_.x_ref), channel_id=1, source_target_pairs={{0,1},{1,0},{2,3},{3,2},{4,5},{5,4},{6,7},{7,6},{8,9},{9,8},{10,11... | collective-permute-start | bytes 1572872 | tf_op jit(solution)/shard_map/ppermute | solution.py:44
  16.5 1.2 collective-permute-start.1
  17.8 3.7 collective-permute-start.2
  21.4 3.8 collective-permute-start.3
  25.3 6.5 %collective-permute-start.4 = (f32[16,4,32]{2,1,0:T(4,128)S(1)}, f32[16,4,32]{2,1,0:T(4,128)S(1)}, u32[]{:S(2)}, u32[]{:S(2)}) collective-permute-start(f32[16,4,32]{2,1,0:T(4,128)S(1)} %maximum_select_fusion.1), channel_id=1, source_target_pairs={{0,16},{8,24},{16,0},{24,8},{1,17},{9,25},{17,1},{25,9},{2,18},{10... | collective-permute-start | bytes 24584 | tf_op jit(solution)/shard_map/ppermute | solution.py:44
  71.1 9.4 %collective-permute-start.7 = (bf16[2,512,512]{2,1,0:T(8,128)(2,1)}, bf16[2,512,512]{2,1,0:T(8,128)(2,1)S(1)}, u32[]{:S(2)}, u32[]{:S(2)}) collective-permute-start(bf16[2,512,512]{2,1,0:T(8,128)(2,1)} %get-tuple-element.114.refs_1_.refs_4_), channel_id=1, source_target_pairs={{0,2},{2,0},{4,6},{6,4},{1,3},{3,1},{5,7},{7,5},{8,10},{10,8},{12,... | collective-permute-start | bytes 3145736 | tf_op jit(solution)/shard_map/ppermute | solution.py:44
  71.4 34.6 %collective-permute-start.9 = (bf16[2,512,512]{2,1,0:T(8,128)(2,1)}, bf16[2,512,512]{2,1,0:T(8,128)(2,1)S(1)}, u32[]{:S(2)}, u32[]{:S(2)}) collective-permute-start(bf16[2,512,512]{2,1,0:T(8,128)(2,1)} %get-tuple-element.114.refs_1_.refs_4_), channel_id=1, source_target_pairs={{0,4},{2,6},{4,0},{6,2},{1,5},{3,7},{5,1},{7,3},{8,12},{10,14},{12... | collective-permute-start | bytes 3145736 | tf_op jit(solution)/shard_map/ppermute | solution.py:44
  79.0 27.0 %collective-permute-start.8 = (bf16[2,512,512]{2,1,0:T(8,128)(2,1)}, bf16[2,512,512]{2,1,0:T(8,128)(2,1)S(1)}, u32[]{:S(2)}, u32[]{:S(2)}) collective-permute-start(bf16[2,512,512]{2,1,0:T(8,128)(2,1)} %get-tuple-element.119.refs_1_.refs_4_), channel_id=1, source_target_pairs={{0,2},{2,0},{4,6},{6,4},{1,3},{3,1},{5,7},{7,5},{8,10},{10,8},{12,... | collective-permute-start | bytes 3145736 | tf_op jit(solution)/shard_map/ppermute | solution.py:44
  79.0 62.8 %collective-permute-start.16 = (bf16[2,512,512]{2,1,0:T(8,128)(2,1)}, bf16[2,512,512]{2,1,0:T(8,128)(2,1)S(1)}, u32[]{:S(2)}, u32[]{:S(2)}) collective-permute-start(bf16[2,512,512]{2,1,0:T(8,128)(2,1)} %get-tuple-element.119.refs_1_.refs_4_), channel_id=1, source_target_pairs={{0,4},{2,6},{4,0},{6,2},{1,5},{3,7},{5,1},{7,3},{8,12},{10,14},{12... | collective-permute-start | bytes 3145736 | tf_op jit(solution)/shard_map/ppermute | solution.py:44
  106.0 11.2 %copy-start.34 = (bf16[2,512,512]{2,1,0:T(8,128)(2,1)}, bf16[2,512,512]{2,1,0:T(8,128)(2,1)S(1)}, u32[]{:S(2)}) copy-start(bf16[2,512,512]{2,1,0:T(8,128)(2,1)S(1)} %collective-permute-done.9.refs_1_.refs_6_) | copy-start | bytes 3145732
  106.0 39.1 %collective-permute-start.10 = (bf16[2,512,512]{2,1,0:T(8,128)(2,1)S(1)}, bf16[2,512,512]{2,1,0:T(8,128)(2,1)S(1)}, u32[]{:S(2)}, u32[]{:S(2)}) collective-permute-start(bf16[2,512,512]{2,1,0:T(8,128)(2,1)S(1)} %collective-permute-done.9.refs_1_.refs_6_), channel_id=1, source_target_pairs={{0,2},{2,0},{4,6},{6,4},{1,3},{3,1},{5,7},{7,5},{8,10},{10,8},{12,... | collective-permute-start | bytes 3145736 | tf_op jit(solution)/shard_map/ppermute | solution.py:44
  106.0 35.9 %copy-start.24 = (f32[850]{0:T(1024)S(1)}, f32[850]{0:T(1024)}, u32[]{:S(2)}) copy-start(f32[850]{0:T(1024)} %param.20) | copy-start | bytes 10204
  106.0 35.9 %copy-start.25 = (s32[2]{0:T(128)S(1)}, s32[2]{0:T(128)}, u32[]{:S(2)}) copy-start(s32[2]{0:T(128)} %param.18) | copy-start | bytes 28
  106.0 36.1 %copy-start.26 = (s32[2]{0:T(128)S(1)}, s32[2]{0:T(128)}, u32[]{:S(2)}) copy-start(s32[2]{0:T(128)} %param.19) | copy-start | bytes 28
  106.0 38.9 %copy-start.8 = (bf16[2,256,1024]{2,1,0:T(8,128)(2,1)S(1)}, bf16[2,256,1024]{2,1,0:T(8,128)(2,1)}, u32[]{:S(2)}) copy-start(bf16[2,256,1024]{2,1,0:T(8,128)(2,1)} %param.17) | copy-start | bytes 3145732
  141.9 19.0 %copy-start.33 = (bf16[2,512,512]{2,1,0:T(8,128)(2,1)}, bf16[2,512,512]{2,1,0:T(8,128)(2,1)S(1)}, u32[]{:S(2)}) copy-start(bf16[2,512,512]{2,1,0:T(8,128)(2,1)S(1)} %collective-permute-done.16.refs_1_.refs_6_) | copy-start | bytes 3145732
  141.9 21.9 %collective-permute-start.17 = (bf16[2,512,512]{2,1,0:T(8,128)(2,1)S(1)}, bf16[2,512,512]{2,1,0:T(8,128)(2,1)S(1)}, u32[]{:S(2)}, u32[]{:S(2)}) collective-permute-start(bf16[2,512,512]{2,1,0:T(8,128)(2,1)S(1)} %collective-permute-done.16.refs_1_.refs_6_), channel_id=1, source_target_pairs={{0,2},{2,0},{4,6},{6,4},{1,3},{3,1},{5,7},{7,5},{8,10},{10,8},{12,... | collective-permute-start | bytes 3145736 | tf_op jit(solution)/shard_map/ppermute | solution.py:44
  143.4 19.1 %collective-permute-start.12 = (f32[8,128]{1,0:T(8,128)S(1)}, f32[8,128]{1,0:T(8,128)S(1)}, u32[]{:S(2)}, u32[]{:S(2)}) collective-permute-start(f32[8,128]{1,0:T(8,128)S(1)} %broadcast_in_dim.25), channel_id=1, source_target_pairs={{0,8},{8,0},{16,24},{24,16},{1,9},{9,1},{17,25},{25,17},{2,10},{10... | collective-permute-start | bytes 12296 | tf_op jit(solution)/shard_map/ppermute | solution.py:44
  145.0 18.2 %copy-start.4 = (bf16[256,1024]{1,0:T(8,128)(2,1)}, bf16[256,1024]{1,0:T(8,128)(2,1)S(1)}, u32[]{:S(2)}) copy-start(bf16[256,1024]{1,0:T(8,128)(2,1)S(1)} %get-tuple-element.131.refs_2_.cot_ref) | copy-start | bytes 1572868
  145.0 42.7 %copy-start.3 = (bf16[256,1024]{1,0:T(8,128)(2,1)}, bf16[256,1024]{1,0:T(8,128)(2,1)S(1)}, u32[]{:S(2)}) copy-start(bf16[256,1024]{1,0:T(8,128)(2,1)S(1)} %get-tuple-element.149.refs_2_.cot_ref) | copy-start | bytes 1572868
  160.9 20.3 %collective-permute-start.11 = (bf16[256,1024]{1,0:T(8,128)(2,1)}, bf16[256,1024]{1,0:T(8,128)(2,1)S(1)}, u32[]{:S(2)}, u32[]{:S(2)}) collective-permute-start(bf16[256,1024]{1,0:T(8,128)(2,1)} %get-tuple-element.126), channel_id=1, source_target_pairs={{0,1},{1,0},{2,3},{3,2},{4,5},{5,4},{6,7},{7,6},{8,9},{9,8},{10,11... | collective-permute-start | bytes 1572872 | tf_op jit(solution)/shard_map/ppermute | solution.py:44
  163.1 22.3 %collective-permute-start.13 = (f32[8,128]{1,0:T(8,128)S(1)}, f32[8,128]{1,0:T(8,128)S(1)}, u32[]{:S(2)}, u32[]{:S(2)}) collective-permute-start(f32[8,128]{1,0:T(8,128)S(1)} %broadcast_add_fusion), channel_id=1, source_target_pairs={{0,16},{8,24},{16,0},{24,8},{1,17},{9,25},{17,1},{25,9},{2,18},{10... | collective-permute-start | bytes 12296 | tf_op jit(solution)/shard_map/ppermute | solution.py:44
  163.2 46.5 %collective-permute-start.15 = (bf16[256,1024]{1,0:T(8,128)(2,1)S(1)}, bf16[256,1024]{1,0:T(8,128)(2,1)S(1)}, u32[]{:S(2)}, u32[]{:S(2)}) collective-permute-start(bf16[256,1024]{1,0:T(8,128)(2,1)S(1)} %get-tuple-element.131.refs_2_.cot_ref), channel_id=1, source_target_pairs={{0,1},{1,0},{2,3},{3,2},{4,5},{5,4},{6,7},{7,6},{8,9},{9,8},{10,11... | collective-permute-start | bytes 1572872 | tf_op jit(solution)/shard_map/ppermute | solution.py:44
  179.6 18.8 %collective-permute-start.18 = (bf16[256,1024]{1,0:T(8,128)(2,1)}, bf16[256,1024]{1,0:T(8,128)(2,1)S(1)}, u32[]{:S(2)}, u32[]{:S(2)}) collective-permute-start(bf16[256,1024]{1,0:T(8,128)(2,1)} %get-tuple-element.138), channel_id=1, source_target_pairs={{0,1},{1,0},{2,3},{3,2},{4,5},{5,4},{6,7},{7,6},{8,9},{9,8},{10,11... | collective-permute-start | bytes 1572872 | tf_op jit(solution)/shard_map/ppermute | solution.py:44
  185.0 24.7 %collective-permute-start.14 = (bf16[256,1024]{1,0:T(8,128)(2,1)}, bf16[256,1024]{1,0:T(8,128)(2,1)S(1)}, u32[]{:S(2)}, u32[]{:S(2)}) collective-permute-start(bf16[256,1024]{1,0:T(8,128)(2,1)} %get-tuple-element.129.refs_0_), channel_id=1, source_target_pairs={{0,1},{1,0},{2,3},{3,2},{4,5},{5,4},{6,7},{7,6},{8,9},{9,8},{10,11... | collective-permute-start | bytes 1572872 | tf_op jit(solution)/shard_map/ppermute | solution.py:44
  187.8 47.9 %collective-permute-start.20 = (bf16[256,1024]{1,0:T(8,128)(2,1)S(1)}, bf16[256,1024]{1,0:T(8,128)(2,1)S(1)}, u32[]{:S(2)}, u32[]{:S(2)}) collective-permute-start(bf16[256,1024]{1,0:T(8,128)(2,1)S(1)} %get-tuple-element.149.refs_2_.cot_ref), channel_id=1, source_target_pairs={{0,1},{1,0},{2,3},{3,2},{4,5},{5,4},{6,7},{7,6},{8,9},{9,8},{10,11... | collective-permute-start | bytes 1572872 | tf_op jit(solution)/shard_map/ppermute | solution.py:44
  202.0 33.6 %collective-permute-start.19 = (bf16[256,1024]{1,0:T(8,128)(2,1)}, bf16[256,1024]{1,0:T(8,128)(2,1)S(1)}, u32[]{:S(2)}, u32[]{:S(2)}) collective-permute-start(bf16[256,1024]{1,0:T(8,128)(2,1)} %get-tuple-element.147.refs_0_), channel_id=1, source_target_pairs={{0,1},{1,0},{2,3},{3,2},{4,5},{5,4},{6,7},{7,6},{8,9},{9,8},{10,11... | collective-permute-start | bytes 1572872 | tf_op jit(solution)/shard_map/ppermute | solution.py:44
  234.1 25.9 %collective-permute-start.21 = (bf16[256,1024]{1,0:T(8,128)(2,1)}, bf16[256,1024]{1,0:T(8,128)(2,1)S(1)}, u32[]{:S(2)}, u32[]{:S(2)}) collective-permute-start(bf16[256,1024]{1,0:T(8,128)(2,1)} %get-tuple-element.146), channel_id=1, source_target_pairs={{0,1},{1,0},{2,3},{3,2},{4,5},{5,4},{6,7},{7,6},{8,9},{9,8},{10,11... | collective-permute-start | bytes 1572872 | tf_op jit(solution)/shard_map/ppermute | solution.py:44
  287.9 240.8 %reduce-scatter.5.cloned.1.call-start = ((), (), s32[]{:S(2)}) async-start(), calls=%async_computation.5 | async-start | bytes 4456448 | tf_op jit(solution)/shard_map/reduce_scatter | solution.py:875
  288.9 14.9 %collective-permute-start.22 = (bf16[256,1024]{1,0:T(8,128)(2,1)S(1)}, bf16[256,1024]{1,0:T(8,128)(2,1)S(1)}, u32[]{:S(2)}, u32[]{:S(2)}) collective-permute-start(bf16[256,1024]{1,0:T(8,128)(2,1)S(1)} %copy-done.47), channel_id=1, source_target_pairs={{0,1},{1,0},{2,3},{3,2},{4,5},{5,4},{6,7},{7,6},{8,9},{9,8},{10,11... | collective-permute-start | bytes 1572872 | tf_op jit(solution)/shard_map/ppermute | solution.py:44
  289.5 25.5 %collective-permute-start.23 = (bf16[256,1024]{1,0:T(8,128)(2,1)S(1)}, bf16[256,1024]{1,0:T(8,128)(2,1)S(1)}, u32[]{:S(2)}, u32[]{:S(2)}) collective-permute-start(bf16[256,1024]{1,0:T(8,128)(2,1)S(1)} %copy-done.43), channel_id=1, source_target_pairs={{0,1},{1,0},{2,3},{3,2},{4,5},{5,4},{6,7},{7,6},{8,9},{9,8},{10,11... | collective-permute-start | bytes 1572872 | tf_op jit(solution)/shard_map/ppermute | solution.py:44
  309.5 23.6 %collective-permute-start.26 = (bf16[256,1024]{1,0:T(8,128)(2,1)}, bf16[256,1024]{1,0:T(8,128)(2,1)S(1)}, u32[]{:S(2)}, u32[]{:S(2)}) collective-permute-start(bf16[256,1024]{1,0:T(8,128)(2,1)} %get-tuple-element.176.refs_3_), channel_id=1, source_target_pairs={{0,1},{1,0},{2,3},{3,2},{4,5},{5,4},{6,7},{7,6},{8,9},{9,8},{10,11... | collective-permute-start | bytes 1572872 | tf_op jit(solution)/shard_map/ppermute | solution.py:44
  333.0 49.3 %collective-permute-start.31 = (bf16[2,512,512]{2,1,0:T(8,128)(2,1)}, bf16[2,512,512]{2,1,0:T(8,128)(2,1)S(1)}, u32[]{:S(2)}, u32[]{:S(2)}) collective-permute-start(bf16[2,512,512]{2,1,0:T(8,128)(2,1)} %get-tuple-element.193), channel_id=1, source_target_pairs={{0,2},{2,0},{4,6},{6,4},{1,3},{3,1},{5,7},{7,5},{8,10},{10,8},{12,... | collective-permute-start | bytes 3145736 | tf_op jit(solution)/shard_map/ppermute | solution.py:44
  350.7 15.7 %copy-start.37 = (bf16[2,512,512]{2,1,0:T(8,128)(2,1)S(1)}, bf16[2,512,512]{2,1,0:T(8,128)(2,1)}, u32[]{:S(2)}) copy-start(bf16[2,512,512]{2,1,0:T(8,128)(2,1)} %get-tuple-element.186) | copy-start | bytes 3145732
  365.8 19.3 %collective-permute-start.30 = (bf16[2,512,512]{2,1,0:T(8,128)(2,1)}, bf16[2,512,512]{2,1,0:T(8,128)(2,1)S(1)}, u32[]{:S(2)}, u32[]{:S(2)}) collective-permute-start(bf16[2,512,512]{2,1,0:T(8,128)(2,1)} %get-tuple-element.191), channel_id=1, source_target_pairs={{0,2},{2,0},{4,6},{6,4},{1,3},{3,1},{5,7},{7,5},{8,10},{10,8},{12,... | collective-permute-start | bytes 3145736 | tf_op jit(solution)/shard_map/ppermute | solution.py:44
  366.4 16.9 %collective-permute-start.28 = (bf16[2,512,512]{2,1,0:T(8,128)(2,1)S(1)}, bf16[2,512,512]{2,1,0:T(8,128)(2,1)S(1)}, u32[]{:S(2)}, u32[]{:S(2)}) collective-permute-start(bf16[2,512,512]{2,1,0:T(8,128)(2,1)S(1)} %copy-done.37), channel_id=1, source_target_pairs={{0,2},{2,0},{4,6},{6,4},{1,3},{3,1},{5,7},{7,5},{8,10},{10,8},{12,... | collective-permute-start | bytes 3145736 | tf_op jit(solution)/shard_map/ppermute | solution.py:44
  366.5 15.9 %copy-start.5 = (bf16[2,512,512]{2,1,0:T(8,128)(2,1)S(1)}, bf16[2,512,512]{2,1,0:T(8,128)(2,1)}, u32[]{:S(2)}) copy-start(bf16[2,512,512]{2,1,0:T(8,128)(2,1)} %get-tuple-element.192) | copy-start | bytes 3145732
  381.9 42.8 %collective-permute-start.27 = (bf16[2,512,512]{2,1,0:T(8,128)(2,1)}, bf16[2,512,512]{2,1,0:T(8,128)(2,1)S(1)}, u32[]{:S(2)}, u32[]{:S(2)}) collective-permute-start(bf16[2,512,512]{2,1,0:T(8,128)(2,1)} %get-tuple-element.184), channel_id=1, source_target_pairs={{0,2},{2,0},{4,6},{6,4},{1,3},{3,1},{5,7},{7,5},{8,10},{10,8},{12,... | collective-permute-start | bytes 3145736 | tf_op jit(solution)/shard_map/ppermute | solution.py:44
  382.6 34.5 %collective-permute-start.32 = (bf16[2,512,512]{2,1,0:T(8,128)(2,1)S(1)}, bf16[2,512,512]{2,1,0:T(8,128)(2,1)S(1)}, u32[]{:S(2)}, u32[]{:S(2)}) collective-permute-start(bf16[2,512,512]{2,1,0:T(8,128)(2,1)S(1)} %add_convert_fusion), channel_id=1, source_target_pairs={{0,4},{2,6},{4,0},{6,2},{1,5},{3,7},{5,1},{7,3},{8,12},{10,14},{12... | collective-permute-start | bytes 3145736 | tf_op jit(solution)/shard_map/ppermute | solution.py:44
  383.6 55.2 %collective-permute-start.29 = (bf16[2,512,512]{2,1,0:T(8,128)(2,1)S(1)}, bf16[2,512,512]{2,1,0:T(8,128)(2,1)S(1)}, u32[]{:S(2)}, u32[]{:S(2)}) collective-permute-start(bf16[2,512,512]{2,1,0:T(8,128)(2,1)S(1)} %add_convert_fusion.1), channel_id=1, source_target_pairs={{0,4},{2,6},{4,0},{6,2},{1,5},{3,7},{5,1},{7,3},{8,12},{10,14},{12... | collective-permute-start | bytes 3145736 | tf_op jit(solution)/shard_map/ppermute | solution.py:44
  385.1 32.0 %copy-start.10 = (bf16[2,512,512]{2,1,0:T(8,128)(2,1)}, bf16[2,512,512]{2,1,0:T(8,128)(2,1)S(1)}, u32[]{:S(2)}) copy-start(bf16[2,512,512]{2,1,0:T(8,128)(2,1)S(1)} %collective-permute-done.30.near_ref) | copy-start | bytes 3145732
  424.7 14.1 %copy-start.9 = (bf16[2,512,512]{2,1,0:T(8,128)(2,1)}, bf16[2,512,512]{2,1,0:T(8,128)(2,1)S(1)}, u32[]{:S(2)}) copy-start(bf16[2,512,512]{2,1,0:T(8,128)(2,1)S(1)} %collective-permute-done.27.near_ref) | copy-start | bytes 3145732
  458.1 14.9 %collective-permute-start.34 = (bf16[256,1024]{1,0:T(8,128)(2,1)S(1)}, bf16[256,1024]{1,0:T(8,128)(2,1)S(1)}, u32[]{:S(2)}, u32[]{:S(2)}) collective-permute-start(bf16[256,1024]{1,0:T(8,128)(2,1)S(1)} %copy-done.42), channel_id=1, source_target_pairs={{0,1},{1,0},{2,3},{3,2},{4,5},{5,4},{6,7},{7,6},{8,9},{9,8},{10,11... | collective-permute-start | bytes 1572872 | tf_op jit(solution)/shard_map/ppermute | solution.py:44
  458.8 23.7 %collective-permute-start.33 = (bf16[256,1024]{1,0:T(8,128)(2,1)S(1)}, bf16[256,1024]{1,0:T(8,128)(2,1)S(1)}, u32[]{:S(2)}, u32[]{:S(2)}) collective-permute-start(bf16[256,1024]{1,0:T(8,128)(2,1)S(1)} %copy-done.44), channel_id=1, source_target_pairs={{0,1},{1,0},{2,3},{3,2},{4,5},{5,4},{6,7},{7,6},{8,9},{9,8},{10,11... | collective-permute-start | bytes 1572872 | tf_op jit(solution)/shard_map/ppermute | solution.py:44
  483.3 16.0 %copy-start.39 = (bf16[256,1024]{1,0:T(8,128)(2,1)S(1)}, bf16[256,1024]{1,0:T(8,128)(2,1)}, u32[]{:S(2)}) copy-start(bf16[256,1024]{1,0:T(8,128)(2,1)} %get-tuple-element.172) | copy-start | bytes 1572868
  483.4 16.4 %copy-start.38 = (bf16[256,1024]{1,0:T(8,128)(2,1)S(1)}, bf16[256,1024]{1,0:T(8,128)(2,1)}, u32[]{:S(2)}) copy-start(bf16[256,1024]{1,0:T(8,128)(2,1)} %get-tuple-element.169) | copy-start | bytes 1572868
  488.2 6.9 %collective-permute-start.35 = (f32[16,4,32]{2,1,0:T(4,128)S(1)}, f32[16,4,32]{2,1,0:T(4,128)S(1)}, u32[]{:S(2)}, u32[]{:S(2)}) collective-permute-start(f32[16,4,32]{2,1,0:T(4,128)S(1)} %slice_select_fusion), channel_id=1, source_target_pairs={{0,16},{8,24},{16,0},{24,8},{1,17},{9,25},{17,1},{25,9},{2,18},{10... | collective-permute-start | bytes 24584 | tf_op jit(solution)/shard_map/ppermute | solution.py:44
  495.1 3.8 collective-permute-start.36
  498.9 3.7 collective-permute-start.37
  499.4 14.9 %collective-permute-start.25 = (bf16[256,1024]{1,0:T(8,128)(2,1)S(1)}, bf16[256,1024]{1,0:T(8,128)(2,1)S(1)}, u32[]{:S(2)}, u32[]{:S(2)}) collective-permute-start(bf16[256,1024]{1,0:T(8,128)(2,1)S(1)} %copy-done.39), channel_id=1, source_target_pairs={{0,1},{1,0},{2,3},{3,2},{4,5},{5,4},{6,7},{7,6},{8,9},{9,8},{10,11... | collective-permute-start | bytes 1572872 | tf_op jit(solution)/shard_map/ppermute | solution.py:44
  499.7 22.0 %collective-permute-start.24 = (bf16[256,1024]{1,0:T(8,128)(2,1)S(1)}, bf16[256,1024]{1,0:T(8,128)(2,1)S(1)}, u32[]{:S(2)}, u32[]{:S(2)}) collective-permute-start(bf16[256,1024]{1,0:T(8,128)(2,1)S(1)} %copy-done.38), channel_id=1, source_target_pairs={{0,1},{1,0},{2,3},{3,2},{4,5},{5,4},{6,7},{7,6},{8,9},{9,8},{10,11... | collective-permute-start | bytes 1572872 | tf_op jit(solution)/shard_map/ppermute | solution.py:44
  502.7 1.2 collective-permute-start.38
  503.9 22.4 %collective-permute-start.39 = (f32[1,4,32]{2,1,0:T(4,128)S(1)}, f32[1,4,32]{2,1,0:T(4,128)S(1)}, u32[]{:S(2)}, u32[]{:S(2)}) collective-permute-start(f32[1,4,32]{2,1,0:T(4,128)S(1)} %slice_select_fusion.4), channel_id=1, source_target_pairs={{0,1},{1,0},{2,3},{3,2},{4,5},{5,4},{6,7},{7,6},{8,9},{9,8},{10,11... | collective-permute-start | bytes 1544 | tf_op jit(solution)/shard_map/ppermute | solution.py:44
  514.3 7.4 %copy-start.13 = (bf16[256,1024]{1,0:T(8,128)(2,1)}, bf16[256,1024]{1,0:T(8,128)(2,1)S(1)}, u32[]{:S(2)}) copy-start(bf16[256,1024]{1,0:T(8,128)(2,1)S(1)} %collective-permute-done.25.refs_5_) | copy-start | bytes 1572868
  522.5 5.2 copy-start.2
  (31 other events, 46.4 us)
Sparse Core Ops, SparseCore 0:
  10.8 54.4 all-gather.2
  67.6 116.3 all-gather.4
  288.1 136.4 reduce-scatter.2
  457.3 69.7 reduce-scatter.4

commit v3 on v2

--- a/solution.py
+++ b/solution.py
@@ -16,6 +16,7 @@
 BF16 = jnp.bfloat16
 F32 = jnp.float32
 VMEM_BYTES = 56 * 1024 * 1024
+MESH = pl.DeviceIdType.MESH
 
 
 def angles(positions, head_dim):
@@ -123,15 +124,15 @@
     return array
 
 
-def run(kernel, name, out_shape, flops, args, **options):
-    args = [array for array in args]
+def run(kernel, name, out_shape, flops, args, collective_id=None, **options):
+    trading = {} if collective_id is None else dict(collective_id=collective_id, has_side_effects=True)
     moved = sum(math.prod(array.shape) * array.dtype.itemsize for array in args)
     outs = out_shape if isinstance(out_shape, list) else [out_shape]
     moved += sum(math.prod(array.shape) * array.dtype.itemsize for array in outs)
     return pl.pallas_call(
         kernel,
         out_shape=out_shape,
-        compiler_params=pltpu.CompilerParams(vmem_limit_bytes=VMEM_BYTES),
+        compiler_params=pltpu.CompilerParams(vmem_limit_bytes=VMEM_BYTES, **trading),
         cost_estimate=pl.CostEstimate(
             flops=int(flops), bytes_accessed=int(moved), transcendentals=0
         ),
@@ -179,150 +180,287 @@
 def project_kernel(blocks, norms_ref, w_ref, cos_ref, sin_ref, *refs):
     x_refs = refs[:blocks]
     normed_ref, q_ref, kv_ref = refs[blocks:]
-    cols = q_ref.shape[1]
+    cols = q_ref.shape[2]
     gain, bias = norms_ref[0:1, :], norms_ref[1:2, :]
     at_row = 0
     for x_ref in x_refs:
-        rows = slice(at_row, at_row + x_ref.shape[0])
-        at_row += x_ref.shape[0]
-        normed = (normalise(x_ref[...].astype(F32))[0] * gain + bias).astype(BF16)
-        normed_ref[rows, :] = normed
+        rows = slice(at_row, at_row + x_ref.shape[1])
+        at_row += x_ref.shape[1]
+        normed = (normalise(x_ref[0].astype(F32))[0] * gain + bias).astype(BF16)
+        normed_ref[0, rows, :] = normed
         cosine, sine = cos_ref[rows, :], sin_ref[rows, :]
         query = dot_nn(normed, w_ref[:, :cols])
         key = dot_nn(normed, w_ref[:, cols : 2 * cols])
         for at in range(0, cols, PAIR):
             part = slice(at, at + PAIR)
             one = query[:, part]
-            q_ref[rows, part] = (one * cosine + swap_halves(one) * sine).astype(BF16)
+            q_ref[0, rows, part] = (one * cosine + swap_halves(one) * sine).astype(BF16)
             one = key[:, part]
-            kv_ref[0, rows, part] = (one * cosine + swap_halves(one) * sine).astype(BF16)
-        kv_ref[1, rows, :] = dot_nn(normed, w_ref[:, 2 * cols : 3 * cols]).astype(BF16)
+            kv_ref[0, 0, rows, part] = (one * cosine + swap_halves(one) * sine).astype(BF16)
+        kv_ref[0, 1, rows, :] = dot_nn(normed, w_ref[:, 2 * cols : 3 * cols]).astype(BF16)
 
 
 def project(x_blocks, norms, w_att, cosine, sine):
+    windows = x_blocks[0].shape[0]
     width, cols = w_att.shape[0], w_att.shape[1] // 4
-    rows = sum(block.shape[0] for block in x_blocks)
+    rows = sum(block.shape[1] for block in x_blocks)
+    args = [norms, w_att, cosine, sine, *x_blocks]
     return run(
         functools.partial(project_kernel, len(x_blocks)),
         "project",
         [
-            shaped((rows, width), BF16),
-            shaped((rows, cols), BF16),
-            shaped((2, rows, cols), BF16),
+            shaped((windows, rows, width), BF16),
+            shaped((windows, rows, cols), BF16),
+            shaped((windows, 2, rows, cols), BF16),
         ],
-        6 * rows * width * cols,
-        [norms, w_att, cosine, sine, *x_blocks],
-    )
-
-
-def attend_kernel(slots, last, first, exp_scale, *refs):
-    refs = list(refs)
-    q_ref = refs.pop(0)
-    kv_refs = [refs.pop(0) for _ in range(slots)]
-    if not first:
-        acc_in, top_in, total_in = refs.pop(0), refs.pop(0), refs.pop(0)
-    query = q_ref[...]
+        6 * windows * rows * width * cols,
+        args,
+        grid=(windows,),
+        in_specs=[pl.BlockSpec(array.shape, lambda i: (0, 0)) for array in args[:4]]
+        + [pl.BlockSpec((1,) + block.shape[1:], lambda i: (i, 0, 0)) for block in x_blocks],
+        out_specs=[
+            pl.BlockSpec((1, rows, width), lambda i: (i, 0, 0)),
+            pl.BlockSpec((1, rows, cols), lambda i: (i, 0, 0)),
+            pl.BlockSpec((1, 2, rows, cols), lambda i: (i, 0, 0, 0)),
+        ],
+    )
+
+
+def flipped(index, mask):
+    bit = 1
+    while bit <= mask:
+        if mask & bit:
+            index = index + bit - 2 * bit * ((index // bit) % 2)
+        bit *= 2
+    return index
+
+
+def greet(peers):
+    barrier = pltpu.get_barrier_semaphore()
+    for peer in peers:
+        pl.semaphore_signal(barrier, inc=1, device_id=peer, device_id_type=MESH)
+    pl.semaphore_wait(barrier, len(peers))
+
+
+def send(source, target, send_sem, recv_sem, peer):
+    return pltpu.make_async_remote_copy(
+        src_ref=source,
+        dst_ref=target,
+        send_sem=send_sem,
+        recv_sem=recv_sem,
+        device_id=peer,
+        device_id_type=MESH,
+    )
+
+
+def attend_kernel(windows, pairs, trades, exp_scale, *refs):
+    q_ref, w_ref, kv_ref, cot_ref = refs[:4]
+    low_ref, wide_ref, log_ref, kept_ref, sent_ref, slots_ref, cots_ref = refs[4:11]
+    slots, acc_all, top_all, total_all, mixed_rows = refs[11:16]
+    own_sem, send_sem, recv_sem, save_sem, cot_send, cot_recv = refs[16:]
+    step = pl.program_id(0)
+    near_steps = windows * pairs
+    steps = 2 * near_steps
+    seq, tensor = lax.axis_index("seq"), lax.axis_index("tensor")
+    core_peer = {"seq": flipped(seq, 1)}
+    far_peer = {"seq": flipped(seq, 2)}
+    cot_peers = [{"tensor": flipped(tensor, other + 1)} for other in range(trades)]
+
+    def piece(number):
+        columns = pl.ds(pl.multiple_of((number % pairs) * PAIR, PAIR), PAIR)
+        return kv_ref.at[number // pairs, :, :, columns]
+
+    def own_copy(number):
+        return pltpu.make_async_copy(piece(number), slots.at[number, 0], own_sem.at[number])
+
+    def trade(number, slot):
+        peer = far_peer if slot == 2 else core_peer
+        source = slots.at[number, 2] if slot == 3 else piece(number)
+        return send(
+            source,
+            slots.at[number, slot],
+            send_sem.at[number, slot - 1],
+            recv_sem.at[number, slot - 1],
+            peer,
+        )
+
+    def cot_trade(other):
+        return send(
+            cot_ref, cots_ref.at[other], cot_send.at[other], cot_recv.at[other], cot_peers[other]
+        )
+
+    def save(number, slot):
+        return pltpu.make_async_copy(
+            slots.at[number, slot], slots_ref.at[number, slot], save_sem.at[number, slot]
+        )
+
+    @pl.when(step == 0)
+    def _():
+        greet([core_peer, far_peer] + cot_peers)
+
+        @pl.loop(0, near_steps)
+        def _(number):
+            own_copy(number).start()
+            trade(number, 1).start()
+            trade(number, 2).start()
+
+        for other in range(trades):
+            cot_trade(other).start()
+
+    relayed = step - (near_steps - 1)
+
+    @pl.when(jnp.logical_and(relayed >= 0, relayed < near_steps))
+    def _():
+        trade(relayed, 2).wait_recv()
+        trade(relayed, 3).start()
+        save(relayed, 2).start()
+
+    query = q_ref[0]
     is_first = first_head(query.shape)
-    outs, tops = [], []
-    for head in range(2):
-        mine = is_first if head == 0 else jnp.logical_not(is_first)
-        own_query = jnp.where(mine, query, jnp.zeros_like(query))
-        scores = [dot_nt(own_query, kv[0]) for kv in kv_refs]
-        top = scores[0].max(axis=1, keepdims=True)
-        for one in scores[1:]:
-            top = jnp.maximum(top, one.max(axis=1, keepdims=True))
-        if not first:
-            at = head * HEAD_DIM
-            top = jnp.maximum(top, top_in[:, at : at + 1])
-        shift = top * exp_scale
-        mixed = None
-        for one, kv in zip(scores, kv_refs):
-            weight = jnp.exp2(one * exp_scale - shift).astype(BF16)
-            value = kv[1]
-            lane_first = first_head(value.shape)
-            lane_mine = lane_first if head == 0 else jnp.logical_not(lane_first)
-            term = dot_nn(weight, jnp.where(lane_mine, value, jnp.ones_like(value)))
-            mixed = term if mixed is None else mixed + term
-        outs.append(mixed)
-        tops.append(jnp.broadcast_to(top, mixed.shape))
-    acc = jnp.where(is_first, outs[0], outs[1])
-    total = pltpu.roll(jnp.where(is_first, outs[1], outs[0]), HEAD_DIM, 1)
-    top_wide = jnp.where(is_first, tops[0], tops[1])
-    if not first:
-        fade = jnp.exp2((top_in[...] - top_wide) * exp_scale)
-        acc = acc + acc_in[...] * fade
-        total = total + total_in[...] * fade
-    if last:
-        w_ref, low_ref, wide_ref, log_ref, kept_ref, sent_ref, mixed_rows = refs
+
+    def partial_of(number, used, carried_top):
+        outs, tops = [], []
+        for head in range(2):
+            mine = is_first if head == 0 else jnp.logical_not(is_first)
+            own_query = jnp.where(mine, query, jnp.zeros_like(query))
+            scores = [dot_nt(own_query, slots[number, slot, 0]) for slot in used]
+            top = scores[0].max(axis=1, keepdims=True)
+            for one in scores[1:]:
+                top = jnp.maximum(top, one.max(axis=1, keepdims=True))
+            if carried_top is not None:
+                at = head * HEAD_DIM
+                top = jnp.maximum(top, carried_top[:, at : at + 1])
+            shift = top * exp_scale
+            mixed = None
+            for one, slot in zip(scores, used):
+                weight = jnp.exp2(one * exp_scale - shift).astype(BF16)
+                value = slots[number, slot, 1]
+                lane_first = first_head(value.shape)
+                lane_mine = lane_first if head == 0 else jnp.logical_not(lane_first)
+                term = dot_nn(weight, jnp.where(lane_mine, value, jnp.ones_like(value)))
+                mixed = term if mixed is None else mixed + term
+            outs.append(mixed)
+            tops.append(jnp.broadcast_to(top, mixed.shape))
+        acc = jnp.where(is_first, outs[0], outs[1])
+        total = pltpu.roll(jnp.where(is_first, outs[1], outs[0]), HEAD_DIM, 1)
+        return acc, jnp.where(is_first, tops[0], tops[1]), total
+
+    @pl.when(step < near_steps)
+    def _():
+        own_copy(step).wait()
+        trade(step, 1).wait_recv()
+        save(step, 0).start()
+        save(step, 1).start()
+        acc, top, total = partial_of(step, (0, 1), None)
+        acc_all[step] = acc
+        top_all[step] = top
+        total_all[step] = total
+
+    @pl.when(step >= near_steps)
+    def _():
+        number = step - near_steps
+        trade(number, 3).wait_recv()
+        save(number, 3).start()
+        carried_top = top_all[number]
+        acc, top, total = partial_of(number, (2, 3), carried_top)
+        fade = jnp.exp2((carried_top - top) * exp_scale)
+        acc = acc + acc_all[number] * fade
+        total = total + total_all[number] * fade
         attended = acc / total
         low = attended.astype(BF16)
-        low_ref[...] = low
-        wide_ref[...] = attended
-        log_ref[...] = (top_wide * exp_scale + jnp.log2(total)).T
+        low_ref[0] = low
+        wide_ref[0] = attended
+        log_ref[0] = (top * exp_scale + jnp.log2(total)).T
         term = dot_nt(low, w_ref[...])
-        step = pl.program_id(0)
-
-        @pl.when(step == 0)
+        pair = number % pairs
+
+        @pl.when(pair == 0)
         def _():
             mixed_rows[...] = term
 
-        @pl.when(step > 0)
+        @pl.when(pair > 0)
         def _():
             mixed_rows[...] += term
 
-        @pl.when(step == pl.num_programs(0) - 1)
+        @pl.when(pair == pairs - 1)
         def _():
-            half = kept_ref.shape[0]
-            kept_ref[...] = mixed_rows[:half]
-            sent_ref[...] = mixed_rows[half:].astype(BF16)
-
-    else:
-        acc_ref, top_ref, total_ref = refs
-        acc_ref[...] = acc
-        top_ref[...] = top_wide
-        total_ref[...] = total
-
-
-def attend(queries, blocks, carried, w_att):
-    rows, cols = queries.shape
-    keys = blocks[0].shape[1]
-    slots = len(blocks)
-    first = carried is None
-    last = w_att is not None
-    wide = pl.BlockSpec((rows, PAIR), lambda i: (0, i))
-    block = pl.BlockSpec((2, keys, PAIR), lambda i: (0, 0, i))
-    shape = shaped((rows, cols), F32)
-    args = [queries, *blocks, *([] if first else carried)]
-    in_specs = [wide] + [block] * slots + ([] if first else [wide] * 3)
-    scratch = []
-    if last:
-        width = w_att.shape[0]
-        out_at = 3 * cols // PAIR
-        args.append(w_att)
-        in_specs.append(pl.BlockSpec((width, PAIR), lambda i: (0, out_at + i)))
-        out_shape = [
-            shaped((rows, cols), BF16),
-            shape,
-            shaped((cols, rows), F32),
-            shaped((rows // 2, width), F32),
-            shaped((rows // 2, width), BF16),
-        ]
-        half = pl.BlockSpec((rows // 2, width), lambda i: (0, 0))
-        out_specs = [wide, wide, pl.BlockSpec((PAIR, rows), lambda i: (i, 0)), half, half]
-        scratch = [pltpu.VMEM((rows, width), F32)]
-    else:
-        out_shape = [shape] * 3
-        out_specs = [wide] * 3
+            half = kept_ref.shape[1]
+            kept_ref[0] = mixed_rows[:half]
+            sent_ref[0] = mixed_rows[half:].astype(BF16)
+
+    @pl.when(step == steps - 1)
+    def _():
+        @pl.loop(0, near_steps)
+        def _(number):
+            for slot in range(1, 4):
+                trade(number, slot).wait_send()
+            for slot in range(4):
+                save(number, slot).wait()
+
+        for other in range(trades):
+            cot_trade(other).wait_send()
+            cot_trade(other).wait_recv()
+
+
+def attend(queries, own_kv, w_att, cotangent, trades):
+    windows, rows, cols = queries.shape
+    width = w_att.shape[0]
+    pairs = cols // PAIR
+    near = windows * pairs
+    out_at = 3 * pairs
+
+    def far(i):
+        return jnp.maximum(i - near, 0)
+
+    anywhere = pl.BlockSpec(memory_space=pl.ANY)
+    wide = pl.BlockSpec((1, rows, PAIR), lambda i: (far(i) // pairs, 0, far(i) % pairs))
+    half = pl.BlockSpec((1, rows // 2, width), lambda i: (far(i) // pairs, 0, 0))
+    state = pltpu.VMEM((near, rows, PAIR), F32)
+    dma = pltpu.SemaphoreType.DMA
     return run(
-        functools.partial(attend_kernel, slots, last, first, LOG2E / math.sqrt(HEAD_DIM)),
-        "attend_far" if last else "attend_near",
-        out_shape,
-        16 * rows * keys * slots * cols,
-        args,
-        grid=(cols // PAIR,),
-        in_specs=in_specs,
-        out_specs=out_specs,
-        scratch_shapes=scratch,
+        functools.partial(attend_kernel, windows, pairs, trades, LOG2E / math.sqrt(HEAD_DIM)),
+        "attend",
+        [
+            shaped((windows, rows, cols), BF16),
+            shaped((windows, rows, cols), F32),
+            shaped((windows, cols, rows), F32),
+            shaped((windows, rows // 2, width), F32),
+            shaped((windows, rows // 2, width), BF16),
+            shaped((near, 4, 2, rows, PAIR), BF16),
+            shaped((trades,) + cotangent.shape, BF16),
+        ],
+        64 * windows * rows * rows * cols,
+        [queries, w_att, own_kv, cotangent],
+        collective_id=0,
+        grid=(2 * near,),
+        in_specs=[
+            pl.BlockSpec((1, rows, PAIR), lambda i: ((i // pairs) % windows, 0, i % pairs)),
+            pl.BlockSpec((width, PAIR), lambda i: (0, out_at + far(i) % pairs)),
+            anywhere,
+            anywhere,
+        ],
+        out_specs=[
+            wide,
+            wide,
+            pl.BlockSpec((1, PAIR, rows), lambda i: (far(i) // pairs, far(i) % pairs, 0)),
+            half,
+            half,
+            anywhere,
+            anywhere,
+        ],
+        scratch_shapes=[
+            pltpu.VMEM((near, 4, 2, rows, PAIR), BF16),
+            state,
+            state,
+            state,
+            pltpu.VMEM((rows, width), F32),
+            dma((near,)),
+            dma((near, 3)),
+            dma((near, 3)),
+            dma((near, 4)),
+            dma((trades,)),
+            dma((trades,)),
+        ],
     )
 
 
@@ -334,13 +472,13 @@
         w_ref = refs.pop(0)
     else:
         do_ref = refs.pop(0)
-    kv_refs = [refs.pop(0) for _ in range(slots)]
+    slots_ref = refs.pop(0)
     if not first:
         dq_in = refs.pop(0)
         cos_ref, sin_ref = refs.pop(0), refs.pop(0)
     dq_ref = refs.pop(0)
     dkv_refs = [refs.pop(0) for _ in range(slots)]
-    query = q_ref[...]
+    query = q_ref[0]
     if first:
         do_ref, rows_ref = refs
 
@@ -356,8 +494,8 @@
     else:
         grad_out = do_ref[...]
     is_first = first_head(query.shape)
-    overlap = (grad_out.astype(F32) * wide_ref[...]).T
-    logs = log_ref[...]
+    overlap = (grad_out.astype(F32) * wide_ref[0]).T
+    logs = log_ref[0]
     zero = jnp.zeros_like(query)
     own_q, own_do, row_log, row_sum = [], [], [], []
     for head in range(2):
@@ -368,8 +506,8 @@
         row_log.append(logs[at : at + 1, :])
         row_sum.append(jnp.sum(overlap[at : at + HEAD_DIM, :], axis=0, keepdims=True))
     dq_parts = [None, None]
-    for kv, dkv_ref in zip(kv_refs, dkv_refs):
-        key, value = kv[0], kv[1]
+    for slot, dkv_ref in enumerate(dkv_refs):
+        key, value = slots_ref[0, slot, 0], slots_ref[0, slot, 1]
         key_turned = key.T
         grad_key, grad_value = None, None
         for head in range(2):
@@ -393,15 +531,17 @@
     dq_ref[...] = grad_query.astype(dq_ref.dtype)
 
 
-def attend_back(queries, wide, logs, blocks, grads, w_att, tables):
-    rows, cols = queries.shape
-    keys = blocks[0].shape[1]
-    slots = len(blocks)
+def attend_back(window, queries, wide, logs, slots_all, grads, w_att, tables):
+    rows, cols = queries.shape[1:]
+    keys = rows
+    slots = slots_all.shape[1] // 2
+    pairs = cols // PAIR
     first = tables is None
     score_scale = 1.0 / math.sqrt(HEAD_DIM)
     row_spec = pl.BlockSpec((rows, PAIR), lambda i: (0, i))
     block = pl.BlockSpec((2, keys, PAIR), lambda i: (0, 0, i))
-    in_specs = [row_spec] * 2 + [pl.BlockSpec((PAIR, rows), lambda i: (i, 0))]
+    stacked = pl.BlockSpec((1, rows, PAIR), lambda i: (window, 0, i))
+    in_specs = [stacked] * 2 + [pl.BlockSpec((1, PAIR, rows), lambda i: (window, i, 0))]
     args = [queries, wide, logs]
     out_shape = [shaped((rows, cols), F32 if first else BF16)]
     out_shape += [shaped((2, keys, cols), BF16)] * slots
@@ -417,8 +557,11 @@
     else:
         args.append(grads[1])
         in_specs.append(row_spec)
-    args += blocks
-    in_specs += [block] * slots
+    args.append(slots_all)
+    half = 1 if first else 0
+    in_specs.append(
+        pl.BlockSpec((1, slots, 2, keys, PAIR), lambda i: (window * pairs + i, half, 0, 0, 0))
+    )
     if not first:
         args += [grads[0], *tables]
         in_specs += [row_spec] + [pl.BlockSpec((rows, PAIR), lambda i: (0, 0))] * 2
@@ -762,36 +905,19 @@
     factors = [factor[w].reshape(1, 1) for w in windows]
     top_bit = seq_size // 2
 
-    def on_chip(block):
-        blocks = [block]
-        bit = 1
-        while bit < top_bit:
-            blocks = blocks + [swap(one, "seq", bit) for one in blocks]
-            bit *= 2
-        return blocks
-
-    token_blocks = [spread(tokens[w], "tensor") for w in windows]
-    normed_rows, queries, near_blocks, far_first = [], [], [], []
+    token_blocks = spread(tokens, "tensor")
+    normed_rows, queries, own_kv = project(token_blocks, norms, w_att, cosine, sine)
+    attended, wide_attended, logs, kept_all, sent_all, slots_all, cots = attend(
+        queries, own_kv, w_att, cotangent, tensor_size - 1
+    )
+    cot_blocks = [
+        [cotangent[w]] + [cots[other, w] for other in range(tensor_size - 1)] for w in windows
+    ]
+    middles, mid_blocks = [], []
     for w in windows:
-        normed, query, own_kv = project(token_blocks[w], norms, w_att, cosine, sine)
-        normed_rows.append(normed)
-        queries.append(query)
-        far_first.append(swap(own_kv, "seq", top_bit))
-        near_blocks.append(on_chip(own_kv))
-    states = []
-    for w in windows:
-        query = hold(queries[w], states[-1] if states else ())
-        states.append(attend(query, near_blocks[w], None, None))
-    far_blocks = [on_chip(hold(far_first[w], states[w])) for w in windows]
-    cot_blocks = [spread(hold(cotangent[w], states[0]), "tensor") for w in windows]
-    attended, wide_attended, logs, middles, mid_blocks = [], [], [], [], []
-    for w in windows:
-        query = hold(queries[w], states[-1], attended[-1] if attended else ())
-        low, wide, log_row, kept, sent = attend(query, far_blocks[w], states[w], w_att)
-        attended.append(low)
-        wide_attended.append(wide)
-        logs.append(log_row)
-        middle, normed_mid = second_norm(tokens[w], *scatter_pair(kept, sent, "tensor"), norms)
+        middle, normed_mid = second_norm(
+            tokens[w], *scatter_pair(kept_all[w], sent_all[w], "tensor"), norms
+        )
         middles.append(middle)
         mid_blocks.append(spread(normed_mid, "tensor"))
 
@@ -840,9 +966,9 @@
     slots = seq_size // 2
     far_sums, dq_states, grad_mid_rows = [], [], []
     for w in windows:
-        query = hold(queries[w], dq_states[-1][0] if dq_states else grad_middles[-1])
+        query = hold(queries, dq_states[-1][0] if dq_states else grad_middles[-1])
         parts = attend_back(
-            query, wide_attended[w], logs[w], far_blocks[w], grad_mid_blocks[w], w_att, None
+            w, query, wide_attended, logs, slots_all, grad_mid_blocks[w], w_att, None
         )
         dq_states.append((parts[0], parts[1 + slots]))
         grad_mid_rows.append(parts[2 + slots])
@@ -853,9 +979,9 @@
     ]
     grad_queries, near_pairs = [], []
     for w in windows:
-        query = hold(queries[w], grad_queries[-1] if grad_queries else dq_states[-1][0])
+        query = hold(queries, grad_queries[-1] if grad_queries else dq_states[-1][0])
         parts = attend_back(
-            query, wide_attended[w], logs[w], near_blocks[w], dq_states[w], None, (cosine, sine)
+            w, query, wide_attended, logs, slots_all, dq_states[w], None, (cosine, sine)
         )
         grad_queries.append(parts[0])
         blocks = fold(list(parts[1:]), 2)
@@ -870,7 +996,12 @@
         grad_qkvs.append(grad_qkv)
         first_parts.append(scatter_pair(kept, sent, "tensor"))
     g_att_part = weight_grads(
-        [(normed_rows, grad_qkvs), (grad_mid_rows, attended)], head_cols, "attend_weights"
+        [
+            ([normed_rows[w] for w in windows], grad_qkvs),
+            (grad_mid_rows, [attended[w] for w in windows]),
+        ],
+        head_cols,
+        "attend_weights",
     )
     g_att = lax.psum_scatter(
         hold(g_att_part, g_ffn), shards, scatter_dimension=0, tiled=True

time: 546 us -> 533 us (0.976)
  waiting for transfers between devices: 205 us -> 162 us
  Pallas kernels: 246 us -> 273 us
    ppermute x40 -> x31, waiting for transfers between devices: 172 us -> 134 us  [swap(): return lax.ppermute(array, axis, [(i, i ^ bit) for i in range(size)])]
    pallas_call x23 -> x19, Pallas kernels: 246 us -> 273 us  [run(): pl.pallas_call(kernel, out_shape=out_shape, compiler_params=pltpu.Compile...]
    squeeze x1 -> x6, local copies, waits for them, and re-layouts: 0.07 us -> 7.44 us  [the longest x1 1.47 us: local(): normed_rows[w]]
    all_gather x1, waiting for transfers between devices: 32.8 us -> 26.3 us  [local(): lax.all_gather(jnp.concatenate([w_query, w_key, w_value, w_out.T], axis=1...]
    unnamed x102 -> x86, local copies, waits for them, and re-layouts: 17.8 us -> 12.7 us
    ppermute x40 -> x31, starting transfers between devices: 34.8 us -> 31.5 us  [swap(): return lax.ppermute(array, axis, [(i, i ^ bit) for i in range(size)])]
  transfers between devices with their start and end apart: 44 -> 35, of which waited for: 21 -> 22; matrix products, arithmetic and copies ran while one was open for 3% -> 4% of each run, Pallas kernels for 41% -> 47%
where the time goes in v3:
time: 533 us; the launch traced here: 523 us
  Pallas kernels  273 us (51%)
  waiting for transfers between devices  162 us (30%)
  starting transfers between devices  31.6 us (6%)
  local copies, waits for them, and re-layouts  28.5 us (5%)
  between operations  14.5 us (3%)
  other arithmetic  13.2 us (2%)
    pallas_call x19, Pallas kernels, run(): pl.pallas_call(kernel, out_shape=out_shape, compiler_params=pltpu.Compile...  273 us
    ppermute x31, waiting for transfers between devices, swap(): return lax.ppermute(array, axis, [(i, i ^ bit) for i in range(size)])  134 us
    ppermute x31, starting transfers between devices, swap(): return lax.ppermute(array, axis, [(i, i ^ bit) for i in range(size)])  31.5 us
    all_gather x1, waiting for transfers between devices, local(): lax.all_gather(jnp.concatenate([w_query, w_key, w_value, w_out.T], axis=1...  26.3 us
    unnamed x86, local copies, waits for them, and re-layouts  12.7 us
  transfers between devices with their start and end apart: 35, of which 22 were waited for; matrix products, arithmetic and copies ran while one was open for 4% of the time, Pallas kernels for 47%

profile of v3, /device:TPU:0, one launch (start us, length us, event | category | flops | bytes accessed | tf_op | source)
XLA Modules:
  0.0 523.0 jit_solution(12296683770321140739)
XLA Ops:
  7.3 1.7 pad_maximum_fusion.1
  9.1 2.1 pad_maximum_fusion
  11.4 3.0 collective-permute-start
  16.0 2.1 collective-permute-start.7
  18.1 1.0 slice_bitcast_fusion.10
  19.1 1.0 slice_bitcast_fusion.8
  21.4 1.5 collective-permute-start.2
  23.9 1.2 collective-permute-done.2
  26.2 2.9 collective-permute-done.3
  29.0 2.5 collective-permute-start.4
  32.7 3.1 collective-permute-done.4
  36.5 2.5 collective-permute-done.5.refs_1_
  39.1 26.3 %all-gather.3.cloned.1.call-done.w_ref.refs_1_.refs_5_ = bf16[1024,2048]{1,0:T(8,128)(2,1)} async-done(((bf16[64,2048]{1,0:T(8,128)(2,1)}), bf16[1024,2048]{1,0:T(8,128)(2,1)}) %all-gather.3.cloned.1.call-update) | async-done | bytes 4194320 | tf_op jit(solution)/shard_map/all_gather | solution.py:870
  65.4 8.4 %project.1 = (bf16[2,512,1024]{2,1,0:T(8,128)(2,1)}, bf16[2,512,512]{2,1,0:T(8,128)(2,1)}, bf16[2,2,512,512]{3,2,1,0:T(8,128)(2,1)}) custom-call(f32[4,1024]{1,0:T(4,128)} %reshape.61.norms_ref, bf16[1024,2048]{1,0:T(8,128)(2,1)} %all-gather.3.cloned.1.call-done.w_ref.refs_1_.refs_5_, f32[512,128]{1,0:T(8,128)} %pad_maximum_fusion.2.cos_ref.refs_6_, ...), custom_call_target="tpu_custom_call" | custom-call | flops 3221225472 | bytes 12075008 | tf_op jit(solution)/shard_map/project/pallas_call | solution.py:132
  73.7 81.7 %attend.1 = (bf16[2,512,512]{2,1,0:T(8,128)(2,1)}, f32[2,512,512]{2,1,0:T(8,128)}, f32[2,512,512]{2,1,0:T(8,128)}, f32[2,256,1024]{2,1,0:T(8,128)}, bf16[2,256,1...) custom-call(bf16[2,512,512]{2,1,0:T(8,128)(2,1)} %get-tuple-element.143.refs_0_, ...), custom_call_target="tpu_custom_call" | custom-call | flops 17179869184 | bytes 26214400 | tf_op jit(solution)/shard_map/attend/pallas_call | solution.py:132
  155.4 1.4 slice_bitcast_fusion.9
  156.9 1.5 collective-permute-start.6
  160.1 1.5 slice_bitcast_fusion.2
  161.6 10.2 %collective-permute-done.6.arrived_ref = bf16[256,1024]{1,0:T(8,128)(2,1)S(1)} collective-permute-done((bf16[256,1024]{1,0:T(8,128)(2,1)S(1)}, bf16[256,1024]{1,0:T(8,128)(2,1)S(1)}, u32[]{:S(2)}, u32[]{:S(2)}) %collective-permute-start.6) | collective-permute-done | bytes 524320 | tf_op jit(solution)/shard_map/ppermute | solution.py:45
  172.6 3.0 second_norm.2
  175.5 1.5 collective-permute-start.9
  179.3 3.7 collective-permute-done.10.arrived_ref
  183.8 2.8 second_norm.3
  186.6 1.5 collective-permute-start.11
  188.1 6.1 %collective-permute-done.9.refs_1_ = bf16[256,1024]{1,0:T(8,128)(2,1)S(1)} collective-permute-done((bf16[256,1024]{1,0:T(8,128)(2,1)}, bf16[256,1024]{1,0:T(8,128)(2,1)S(1)}, u32[]{:S(2)}, u32[]{:S(2)}) %collective-permute-start.9) | collective-permute-done | bytes 524320 | tf_op jit(solution)/shard_map/ppermute | solution.py:45
  195.0 23.7 %feed.2 = (bf16[512,1024]{1,0:T(8,128)(2,1)}, bf16[512,1024]{1,0:T(8,128)(2,1)}, bf16[512,2048]{1,0:T(8,128)(2,1)}, bf16[512,2048]{1,0:T(8,128)(2,1)}, bf16[512,...) custom-call(f32[1,1]{1,0:T(1,128)} %bitcast.11.factor_ref, ...), custom_call_target="tpu_custom_call" | custom-call | flops 12884901888 | bytes 51380228 | tf_op jit(solution)/shard_map/feed/pallas_call | solution.py:132
  218.7 1.5 collective-permute-start.12
  221.0 23.5 %feed.3 = (bf16[512,1024]{1,0:T(8,128)(2,1)}, bf16[512,1024]{1,0:T(8,128)(2,1)}, bf16[512,2048]{1,0:T(8,128)(2,1)}, bf16[512,2048]{1,0:T(8,128)(2,1)}, bf16[512,...) custom-call(f32[1,1]{1,0:T(1,128)} %bitcast.15.factor_ref, ...), custom_call_target="tpu_custom_call" | custom-call | flops 12884901888 | bytes 51380228 | tf_op jit(solution)/shard_map/feed/pallas_call | solution.py:132
  245.4 4.5 second_norm_back.2
  249.9 22.4 %feed_weights.1 = bf16[1024,6144]{1,0:T(8,128)(2,1)} custom-call(bf16[512,1024]{1,0:T(8,128)(2,1)} %get-tuple-element.105.refs_0_.refs_4_, bf16[512,1024]{1,0:T(8,128)(2,1)} %get-tuple-element.115.refs_1_.refs_5_, bf16[512,2048]{1,0:T(8,128)(2,1)} %get-tuple-element.108.refs_2_, bf16[512,2048]{1,0:T(8,128)(2,1)} %get-tuple-element.116.refs_3_, ...), custom_call_target="tpu_custom_call" | custom-call | flops 12884901888 | bytes 31457280 | tf_op jit(solution)/shard_map/feed_weights/pallas_call | solution.py:132
  273.9 1.5 collective-permute-start.14
  275.4 12.8 %collective-permute-done.13.arrived_ref = bf16[256,1024]{1,0:T(8,128)(2,1)S(1)} collective-permute-done((bf16[256,1024]{1,0:T(8,128)(2,1)S(1)}, bf16[256,1024]{1,0:T(8,128)(2,1)S(1)}, u32[]{:S(2)}, u32[]{:S(2)}) %collective-permute-start.13) | collective-permute-done | bytes 524320 | tf_op jit(solution)/shard_map/ppermute | solution.py:45
  289.0 4.9 second_norm_back.3
  294.5 5.0 collective-permute-done.14.refs_4_
  300.2 17.0 %attend_back_far.2 = (f32[512,512]{1,0:T(8,128)}, bf16[2,512,512]{2,1,0:T(8,128)(2,1)}, bf16[2,512,512]{2,1,0:T(8,128)(2,1)}, bf16[512,512]{1,0:T(8,128)(2,1)}, bf16[512,1024]{1,0:T(8,128)(2,1)}) custom-call(bf16[2,512,512]{2,1,0:T(8,128)(2,1)} %get-tuple-element.143.refs_0_, f32[2,512,512]{2,1,0:T(8,128)} %get-tuple-element.128.refs_1_, ...), custom_call_target="tpu_custom_call" | custom-call | flops 10737418240 | bytes 23592960 | tf_op jit(solution)/shard_map/attend_back_far/pallas_call | solution.py:132
  318.2 16.9 %attend_back_far.3 = (f32[512,512]{1,0:T(8,128)}, bf16[2,512,512]{2,1,0:T(8,128)(2,1)}, bf16[2,512,512]{2,1,0:T(8,128)(2,1)}, bf16[512,512]{1,0:T(8,128)(2,1)}, bf16[512,1024]{1,0:T(8,128)(2,1)}) custom-call(bf16[2,512,512]{2,1,0:T(8,128)(2,1)} %get-tuple-element.143.refs_0_, f32[2,512,512]{2,1,0:T(8,128)} %get-tuple-element.128.refs_1_, ...), custom_call_target="tpu_custom_call" | custom-call | flops 10737418240 | bytes 23592960 | tf_op jit(solution)/shard_map/attend_back_far/pallas_call | solution.py:132
  335.1 15.1 %attend_back_near.2 = (bf16[512,512]{1,0:T(8,128)(2,1)}, bf16[2,512,512]{2,1,0:T(8,128)(2,1)}, bf16[2,512,512]{2,1,0:T(8,128)(2,1)}) custom-call(bf16[2,512,512]{2,1,0:T(8,128)(2,1)} %get-tuple-element.143.refs_0_, f32[2,512,512]{2,1,0:T(8,128)} %get-tuple-element.128.refs_1_, f32[2,512,512]{2,1,0:T(8,128)} %get-tuple-element.129.refs_2_, ...), custom_call_target="tpu_custom_call" | custom-call | flops 10737418240 | bytes 18350080 | tf_op jit(solution)/shard_map/attend_back_near/pallas_call | solution.py:132
  350.8 15.2 %attend_back_near.3 = (bf16[512,512]{1,0:T(8,128)(2,1)}, bf16[2,512,512]{2,1,0:T(8,128)(2,1)}, bf16[2,512,512]{2,1,0:T(8,128)(2,1)}) custom-call(bf16[2,512,512]{2,1,0:T(8,128)(2,1)} %get-tuple-element.143.refs_0_, f32[2,512,512]{2,1,0:T(8,128)} %get-tuple-element.128.refs_1_, f32[2,512,512]{2,1,0:T(8,128)} %get-tuple-element.129.refs_2_, ...), custom_call_target="tpu_custom_call" | custom-call | flops 10737418240 | bytes 18350080 | tf_op jit(solution)/shard_map/attend_back_near/pallas_call | solution.py:132
  367.8 1.6 collective-permute-start.20
  369.4 1.0 slice_bitcast_fusion.5
  370.5 1.5 slice_bitcast_fusion
  372.0 29.5 %collective-permute-done.23.far_ref = bf16[2,512,512]{2,1,0:T(8,128)(2,1)S(1)} collective-permute-done((bf16[2,512,512]{2,1,0:T(8,128)(2,1)S(1)}, bf16[2,512,512]{2,1,0:T(8,128)(2,1)S(1)}, u32[]{:S(2)}, u32[]{:S(2)}) %collective-permute-start.23) | collective-permute-done | bytes 1048608 | tf_op jit(solution)/shard_map/ppermute | solution.py:45
  402.5 6.6 %turn_back.3 = (bf16[512,1536]{1,0:T(8,128)(2,1)}, f32[256,1024]{1,0:T(8,128)}, bf16[256,1024]{1,0:T(8,128)(2,1)}) custom-call(bf16[512,512]{1,0:T(8,128)(2,1)} %get-tuple-element.142.dq_ref, bf16[2,512,512]{2,1,0:T(8,128)(2,1)} %get-tuple-element.152.own_ref, bf16[2,512,512]{2,1,0:T(8,128)(2,1)} %copy-done.10, bf16[2,512,512]{2,1,0:T(8,128)(2,1)} %copy-done.12, ...), custom_call_target="tpu_custom_call" | custom-call | flops 1610612736 | bytes 11534336 | tf_op jit(solution)/shard_map/turn_back/pallas_call | solution.py:132
  409.0 14.0 %collective-permute-done.20.far_ref = bf16[2,512,512]{2,1,0:T(8,128)(2,1)S(1)} collective-permute-done((bf16[2,512,512]{2,1,0:T(8,128)(2,1)S(1)}, bf16[2,512,512]{2,1,0:T(8,128)(2,1)S(1)}, u32[]{:S(2)}, u32[]{:S(2)}) %collective-permute-start.20) | collective-permute-done | bytes 1048608 | tf_op jit(solution)/shard_map/ppermute | solution.py:45
  424.0 6.5 %turn_back.2 = (bf16[512,1536]{1,0:T(8,128)(2,1)}, f32[256,1024]{1,0:T(8,128)}, bf16[256,1024]{1,0:T(8,128)(2,1)}) custom-call(bf16[512,512]{1,0:T(8,128)(2,1)} %get-tuple-element.145.dq_ref, bf16[2,512,512]{2,1,0:T(8,128)(2,1)} %get-tuple-element.146.own_ref, bf16[2,512,512]{2,1,0:T(8,128)(2,1)} %copy-done.9, bf16[2,512,512]{2,1,0:T(8,128)(2,1)} %copy-done.11, ...), custom_call_target="tpu_custom_call" | custom-call | flops 1610612736 | bytes 11534336 | tf_op jit(solution)/shard_map/turn_back/pallas_call | solution.py:132
  430.5 9.6 %attend_weights.1 = bf16[1024,2048]{1,0:T(8,128)(2,1)} custom-call(bf16[512,1024]{1,0:T(8,128)(2,1)} %get-tuple-element.174.refs_0_, bf16[512,1024]{1,0:T(8,128)(2,1)} %get-tuple-element.173.refs_1_, bf16[512,1536]{1,0:T(8,128)(2,1)} %get-tuple-element.156.refs_2_, bf16[512,1536]{1,0:T(8,128)(2,1)} %get-tuple-element.157.refs_3_, ...), custom_call_target="tpu_custom_call" | custom-call | flops 4294967296 | bytes 12582912 | tf_op jit(solution)/shard_map/attend_weights/pallas_call | solution.py:132
  440.1 1.2 convert_element_type.42
  442.9 1.5 collective-permute-start.24
  444.5 12.8 %collective-permute-done.25.arrived_ref = bf16[256,1024]{1,0:T(8,128)(2,1)S(1)} collective-permute-done((bf16[256,1024]{1,0:T(8,128)(2,1)S(1)}, bf16[256,1024]{1,0:T(8,128)(2,1)S(1)}, u32[]{:S(2)}, u32[]{:S(2)}) %collective-permute-start.25) | collective-permute-done | bytes 524320 | tf_op jit(solution)/shard_map/ppermute | solution.py:45
  458.1 3.8 first_norm_back.2
  461.9 4.8 collective-permute-done.24.arrived_ref
  467.5 3.7 first_norm_back.3
  472.1 2.3 collective-permute-start.26
  474.4 4.4 collective-permute-done.26
  479.3 3.7 collective-permute-done.27
  483.0 1.3 collective-permute-start.28
  484.4 1.9 collective-permute-start.15
  486.8 1.2 collective-permute-done.29
  488.8 10.3 %collective-permute-done.16.refs_5_ = bf16[256,1024]{1,0:T(8,128)(2,1)S(1)} collective-permute-done((bf16[256,1024]{1,0:T(8,128)(2,1)S(1)}, bf16[256,1024]{1,0:T(8,128)(2,1)S(1)}, u32[]{:S(2)}, u32[]{:S(2)}) %collective-permute-start.16) | collective-permute-done | bytes 524320 | tf_op jit(solution)/shard_map/ppermute | solution.py:45
  499.1 5.7 %collective-permute-done.15.refs_2_ = bf16[256,1024]{1,0:T(8,128)(2,1)S(1)} collective-permute-done((bf16[256,1024]{1,0:T(8,128)(2,1)S(1)}, bf16[256,1024]{1,0:T(8,128)(2,1)S(1)}, u32[]{:S(2)}, u32[]{:S(2)}) %collective-permute-start.15) | collective-permute-done | bytes 524320 | tf_op jit(solution)/shard_map/ppermute | solution.py:45
  505.6 3.8 results.1
  510.8 1.1 fusion.5
  511.9 1.1 reduce-scatter.5.cloned.1.call-done
  514.6 1.7 fusion.6
  (170 shorter events, 33.5 us)
Async XLA Ops:
  7.2 4.2 copy-start.30
  7.2 4.2 copy-start.29
  7.2 4.2 copy-start.28
  7.2 4.2 copy-start.27
  7.2 7.2 %copy-start.5 = (bf16[2,256,1024]{2,1,0:T(8,128)(2,1)S(1)}, bf16[2,256,1024]{2,1,0:T(8,128)(2,1)}, u32[]{:S(2)}) copy-start(bf16[2,256,1024]{2,1,0:T(8,128)(2,1)} %refs_0_.1) | copy-start | bytes 3145732
  7.2 7.3 %copy-start.25 = (s32[2]{0:T(128)S(1)}, s32[2]{0:T(128)}, u32[]{:S(2)}) copy-start(s32[2]{0:T(128)} %param.18) | copy-start | bytes 28
  7.2 7.3 %copy-start.24 = (f32[850]{0:T(1024)S(1)}, f32[850]{0:T(1024)}, u32[]{:S(2)}) copy-start(f32[850]{0:T(1024)} %param.20) | copy-start | bytes 10204
  7.3 7.5 %copy-start.26 = (s32[2]{0:T(128)S(1)}, s32[2]{0:T(128)}, u32[]{:S(2)}) copy-start(s32[2]{0:T(128)} %param.19) | copy-start | bytes 28
  7.3 58.1 %all-gather.3.cloned.1.call-start = ((), (), s32[]{:S(2)}) async-start(), calls=%async_computation.2 | async-start | bytes 4456448 | tf_op jit(solution)/shard_map/all_gather | solution.py:870
  9.1 185.2 %all-gather.5.cloned.1.call-start = ((), (), s32[]{:S(2)}) async-start(), calls=%async_computation.3 | async-start | bytes 13369344 | tf_op jit(solution)/shard_map/all_gather | solution.py:873
  9.1 10.0 %copy-start.6 = (bf16[2,256,1024]{2,1,0:T(8,128)(2,1)S(1)}, bf16[2,256,1024]{2,1,0:T(8,128)(2,1)}, u32[]{:S(2)}) copy-start(bf16[2,256,1024]{2,1,0:T(8,128)(2,1)} %refs_3_.1) | copy-start | bytes 3145732
  11.3 428.8 %reduce-scatter.3.cloned.1.call-start = ((), (), s32[]{:S(2)}) async-start(), calls=%async_computation.4 | async-start | bytes 13369344 | tf_op jit(solution)/shard_map/reduce_scatter | solution.py:953
  11.4 8.7 %collective-permute-start = (f32[1,4,32]{2,1,0:T(4,128)S(1)}, f32[1,4,32]{2,1,0:T(4,128)S(1)}, u32[]{:S(2)}, u32[]{:S(2)}) collective-permute-start(f32[1,4,32]{2,1,0:T(4,128)S(1)} %maximum_bitcast_fusion), channel_id=1, source_target_pairs={{0,1},{1,0},{2,3},{3,2},{4,5},{5,4},{6,7},{7,6},{8,9},{9,8},{10,11... | collective-permute-start | bytes 1544 | tf_op jit(solution)/shard_map/ppermute | solution.py:45
  14.4 24.6 %collective-permute-start.5 = (bf16[2,256,1024]{2,1,0:T(8,128)(2,1)S(1)}, bf16[2,256,1024]{2,1,0:T(8,128)(2,1)S(1)}, u32[]{:S(2)}, u32[]{:S(2)}) collective-permute-start(bf16[2,256,1024]{2,1,0:T(8,128)(2,1)S(1)} %copy-done.5), channel_id=1, source_target_pairs={{0,1},{1,0},{2,3},{3,2},{4,5},{5,4},{6,7},{7,6},{8,9},{9,8},{10,11... | collective-permute-start | bytes 3145736 | tf_op jit(solution)/shard_map/ppermute | solution.py:45
  16.0 15.6 %collective-permute-start.7 = (f32[8,128]{1,0:T(8,128)S(1)}, f32[8,128]{1,0:T(8,128)S(1)}, u32[]{:S(2)}, u32[]{:S(2)}) collective-permute-start(f32[8,128]{1,0:T(8,128)S(1)} %broadcast_in_dim.25), channel_id=1, source_target_pairs={{0,8},{8,0},{16,24},{24,16},{1,9},{9,1},{17,25},{25,17},{2,10},{10... | collective-permute-start | bytes 12296 | tf_op jit(solution)/shard_map/ppermute | solution.py:45
  20.2 1.2 collective-permute-start.1
  21.4 3.7 collective-permute-start.2
  25.1 3.9 collective-permute-start.3
  29.0 6.8 %collective-permute-start.4 = (f32[16,4,32]{2,1,0:T(4,128)S(1)}, f32[16,4,32]{2,1,0:T(4,128)S(1)}, u32[]{:S(2)}, u32[]{:S(2)}) collective-permute-start(f32[16,4,32]{2,1,0:T(4,128)S(1)} %maximum_select_fusion.1), channel_id=1, source_target_pairs={{0,16},{8,24},{16,0},{24,8},{1,17},{9,25},{17,1},{25,9},{2,18},{10... | collective-permute-start | bytes 24584 | tf_op jit(solution)/shard_map/ppermute | solution.py:45
  32.2 126.2 %collective-permute-start.8 = (f32[8,128]{1,0:T(8,128)S(1)}, f32[8,128]{1,0:T(8,128)S(1)}, u32[]{:S(2)}, u32[]{:S(2)}) collective-permute-start(f32[8,128]{1,0:T(8,128)S(1)} %broadcast_add_fusion), channel_id=1, source_target_pairs={{0,16},{8,24},{16,0},{24,8},{1,17},{9,25},{17,1},{25,9},{2,18},{10... | collective-permute-start | bytes 12296 | tf_op jit(solution)/shard_map/ppermute | solution.py:45
  39.1 26.3 %copy-start.31 = (bf16[2,256,1024]{2,1,0:T(8,128)(2,1)}, bf16[2,256,1024]{2,1,0:T(8,128)(2,1)S(1)}, u32[]{:S(2)}) copy-start(bf16[2,256,1024]{2,1,0:T(8,128)(2,1)S(1)} %collective-permute-done.5.refs_1_) | copy-start | bytes 3145732
  155.4 4.7 copy-start.2
  156.9 14.9 %collective-permute-start.6 = (bf16[256,1024]{1,0:T(8,128)(2,1)S(1)}, bf16[256,1024]{1,0:T(8,128)(2,1)S(1)}, u32[]{:S(2)}, u32[]{:S(2)}) collective-permute-start(bf16[256,1024]{1,0:T(8,128)(2,1)S(1)} %get-tuple-element.184), channel_id=1, source_target_pairs={{0,1},{1,0},{2,3},{3,2},{4,5},{5,4},{6,7},{7,6},{8,9},{9,8},{10,11... | collective-permute-start | bytes 1572872 | tf_op jit(solution)/shard_map/ppermute | solution.py:45
  159.6 23.5 %collective-permute-start.10 = (bf16[256,1024]{1,0:T(8,128)(2,1)S(1)}, bf16[256,1024]{1,0:T(8,128)(2,1)S(1)}, u32[]{:S(2)}, u32[]{:S(2)}) collective-permute-start(bf16[256,1024]{1,0:T(8,128)(2,1)S(1)} %get-tuple-element.183), channel_id=1, source_target_pairs={{0,1},{1,0},{2,3},{3,2},{4,5},{5,4},{6,7},{7,6},{8,9},{9,8},{10,11... | collective-permute-start | bytes 1572872 | tf_op jit(solution)/shard_map/ppermute | solution.py:45
  161.6 16.7 %copy-start.8 = (bf16[1,2,256,1024]{3,2,1,0:T(8,128)(2,1)S(1)}, bf16[1,2,256,1024]{3,2,1,0:T(8,128)(2,1)}, u32[]{:S(2)}) copy-start(bf16[1,2,256,1024]{3,2,1,0:T(8,128)(2,1)} %get-tuple-element.101) | copy-start | bytes 3145732
  175.5 18.7 %collective-permute-start.9 = (bf16[256,1024]{1,0:T(8,128)(2,1)}, bf16[256,1024]{1,0:T(8,128)(2,1)S(1)}, u32[]{:S(2)}, u32[]{:S(2)}) collective-permute-start(bf16[256,1024]{1,0:T(8,128)(2,1)} %get-tuple-element.99.refs_0_), channel_id=1, source_target_pairs={{0,1},{1,0},{2,3},{3,2},{4,5},{5,4},{6,7},{7,6},{8,9},{9,8},{10,11... | collective-permute-start | bytes 1572872 | tf_op jit(solution)/shard_map/ppermute | solution.py:45
  186.6 33.6 %collective-permute-start.11 = (bf16[256,1024]{1,0:T(8,128)(2,1)}, bf16[256,1024]{1,0:T(8,128)(2,1)S(1)}, u32[]{:S(2)}, u32[]{:S(2)}) collective-permute-start(bf16[256,1024]{1,0:T(8,128)(2,1)} %get-tuple-element.112.refs_0_), channel_id=1, source_target_pairs={{0,1},{1,0},{2,3},{3,2},{4,5},{5,4},{6,7},{7,6},{8,9},{9,8},{10,11... | collective-permute-start | bytes 1572872 | tf_op jit(solution)/shard_map/ppermute | solution.py:45
  218.7 25.9 %collective-permute-start.12 = (bf16[256,1024]{1,0:T(8,128)(2,1)}, bf16[256,1024]{1,0:T(8,128)(2,1)S(1)}, u32[]{:S(2)}, u32[]{:S(2)}) collective-permute-start(bf16[256,1024]{1,0:T(8,128)(2,1)} %get-tuple-element.111), channel_id=1, source_target_pairs={{0,1},{1,0},{2,3},{3,2},{4,5},{5,4},{6,7},{7,6},{8,9},{9,8},{10,11... | collective-permute-start | bytes 1572872 | tf_op jit(solution)/shard_map/ppermute | solution.py:45
  272.3 1.6 copy-start.36
  272.3 240.6 %reduce-scatter.5.cloned.1.call-start = ((), (), s32[]{:S(2)}) async-start(), calls=%async_computation.5 | async-start | bytes 4456448 | tf_op jit(solution)/shard_map/reduce_scatter | solution.py:1006
  273.3 14.9 %collective-permute-start.13 = (bf16[256,1024]{1,0:T(8,128)(2,1)S(1)}, bf16[256,1024]{1,0:T(8,128)(2,1)S(1)}, u32[]{:S(2)}, u32[]{:S(2)}) collective-permute-start(bf16[256,1024]{1,0:T(8,128)(2,1)S(1)} %copy-done.38), channel_id=1, source_target_pairs={{0,1},{1,0},{2,3},{3,2},{4,5},{5,4},{6,7},{7,6},{8,9},{9,8},{10,11... | collective-permute-start | bytes 1572872 | tf_op jit(solution)/shard_map/ppermute | solution.py:45
  273.9 25.5 %collective-permute-start.14 = (bf16[256,1024]{1,0:T(8,128)(2,1)S(1)}, bf16[256,1024]{1,0:T(8,128)(2,1)S(1)}, u32[]{:S(2)}, u32[]{:S(2)}) collective-permute-start(bf16[256,1024]{1,0:T(8,128)(2,1)S(1)} %copy-done.36), channel_id=1, source_target_pairs={{0,1},{1,0},{2,3},{3,2},{4,5},{5,4},{6,7},{7,6},{8,9},{9,8},{10,11... | collective-permute-start | bytes 1572872 | tf_op jit(solution)/shard_map/ppermute | solution.py:45
  293.9 23.5 %collective-permute-start.17 = (bf16[256,1024]{1,0:T(8,128)(2,1)}, bf16[256,1024]{1,0:T(8,128)(2,1)S(1)}, u32[]{:S(2)}, u32[]{:S(2)}) collective-permute-start(bf16[256,1024]{1,0:T(8,128)(2,1)} %get-tuple-element.139.refs_3_), channel_id=1, source_target_pairs={{0,1},{1,0},{2,3},{3,2},{4,5},{5,4},{6,7},{7,6},{8,9},{9,8},{10,11... | collective-permute-start | bytes 1572872 | tf_op jit(solution)/shard_map/ppermute | solution.py:45
  317.3 49.4 %collective-permute-start.22 = (bf16[2,512,512]{2,1,0:T(8,128)(2,1)}, bf16[2,512,512]{2,1,0:T(8,128)(2,1)S(1)}, u32[]{:S(2)}, u32[]{:S(2)}) collective-permute-start(bf16[2,512,512]{2,1,0:T(8,128)(2,1)} %get-tuple-element.155), channel_id=1, source_target_pairs={{0,2},{2,0},{4,6},{6,4},{1,3},{3,1},{5,7},{7,5},{8,10},{10,8},{12,... | collective-permute-start | bytes 3145736 | tf_op jit(solution)/shard_map/ppermute | solution.py:45
  335.1 15.6 %copy-start.32 = (bf16[2,512,512]{2,1,0:T(8,128)(2,1)S(1)}, bf16[2,512,512]{2,1,0:T(8,128)(2,1)}, u32[]{:S(2)}) copy-start(bf16[2,512,512]{2,1,0:T(8,128)(2,1)} %get-tuple-element.149) | copy-start | bytes 3145732
  350.2 21.7 %collective-permute-start.21 = (bf16[2,512,512]{2,1,0:T(8,128)(2,1)}, bf16[2,512,512]{2,1,0:T(8,128)(2,1)S(1)}, u32[]{:S(2)}, u32[]{:S(2)}) collective-permute-start(bf16[2,512,512]{2,1,0:T(8,128)(2,1)} %get-tuple-element.153), channel_id=1, source_target_pairs={{0,2},{2,0},{4,6},{6,4},{1,3},{3,1},{5,7},{7,5},{8,10},{10,8},{12,... | collective-permute-start | bytes 3145736 | tf_op jit(solution)/shard_map/ppermute | solution.py:45
  350.7 16.8 %collective-permute-start.19 = (bf16[2,512,512]{2,1,0:T(8,128)(2,1)S(1)}, bf16[2,512,512]{2,1,0:T(8,128)(2,1)S(1)}, u32[]{:S(2)}, u32[]{:S(2)}) collective-permute-start(bf16[2,512,512]{2,1,0:T(8,128)(2,1)S(1)} %copy-done.32), channel_id=1, source_target_pairs={{0,2},{2,0},{4,6},{6,4},{1,3},{3,1},{5,7},{7,5},{8,10},{10,8},{12,... | collective-permute-start | bytes 3145736 | tf_op jit(solution)/shard_map/ppermute | solution.py:45
  350.8 15.9 %copy-start.3 = (bf16[2,512,512]{2,1,0:T(8,128)(2,1)S(1)}, bf16[2,512,512]{2,1,0:T(8,128)(2,1)}, u32[]{:S(2)}) copy-start(bf16[2,512,512]{2,1,0:T(8,128)(2,1)} %get-tuple-element.154) | copy-start | bytes 3145732
  366.1 1.5 copy-start.4
  366.1 43.0 %collective-permute-start.18 = (bf16[2,512,512]{2,1,0:T(8,128)(2,1)}, bf16[2,512,512]{2,1,0:T(8,128)(2,1)S(1)}, u32[]{:S(2)}, u32[]{:S(2)}) collective-permute-start(bf16[2,512,512]{2,1,0:T(8,128)(2,1)} %get-tuple-element.147), channel_id=1, source_target_pairs={{0,2},{2,0},{4,6},{6,4},{1,3},{3,1},{5,7},{7,5},{8,10},{10,8},{12,... | collective-permute-start | bytes 3145736 | tf_op jit(solution)/shard_map/ppermute | solution.py:45
  367.0 2.5 copy-start.7
  367.0 34.5 %collective-permute-start.23 = (bf16[2,512,512]{2,1,0:T(8,128)(2,1)S(1)}, bf16[2,512,512]{2,1,0:T(8,128)(2,1)S(1)}, u32[]{:S(2)}, u32[]{:S(2)}) collective-permute-start(bf16[2,512,512]{2,1,0:T(8,128)(2,1)S(1)} %add_convert_fusion), channel_id=1, source_target_pairs={{0,4},{2,6},{4,0},{6,2},{1,5},{3,7},{5,1},{7,3},{8,12},{10,14},{12... | collective-permute-start | bytes 3145736 | tf_op jit(solution)/shard_map/ppermute | solution.py:45
  367.5 3.0 copy-start.1
  367.8 55.2 %collective-permute-start.20 = (bf16[2,512,512]{2,1,0:T(8,128)(2,1)S(1)}, bf16[2,512,512]{2,1,0:T(8,128)(2,1)S(1)}, u32[]{:S(2)}, u32[]{:S(2)}) collective-permute-start(bf16[2,512,512]{2,1,0:T(8,128)(2,1)S(1)} %add_convert_fusion.1), channel_id=1, source_target_pairs={{0,4},{2,6},{4,0},{6,2},{1,5},{3,7},{5,1},{7,3},{8,12},{10,14},{12... | collective-permute-start | bytes 3145736 | tf_op jit(solution)/shard_map/ppermute | solution.py:45
  372.0 29.5 %copy-start.10 = (bf16[2,512,512]{2,1,0:T(8,128)(2,1)}, bf16[2,512,512]{2,1,0:T(8,128)(2,1)S(1)}, u32[]{:S(2)}) copy-start(bf16[2,512,512]{2,1,0:T(8,128)(2,1)S(1)} %collective-permute-done.21.near_ref) | copy-start | bytes 3145732
  409.0 14.0 %copy-start.9 = (bf16[2,512,512]{2,1,0:T(8,128)(2,1)}, bf16[2,512,512]{2,1,0:T(8,128)(2,1)S(1)}, u32[]{:S(2)}) copy-start(bf16[2,512,512]{2,1,0:T(8,128)(2,1)S(1)} %collective-permute-done.18.near_ref) | copy-start | bytes 3145732
  441.4 1.0 copy-start.35
  441.4 1.6 copy-start.37
  441.4 3.1 copy-start.21
  441.4 3.0 copy-start.22
  442.4 14.9 %collective-permute-start.25 = (bf16[256,1024]{1,0:T(8,128)(2,1)S(1)}, bf16[256,1024]{1,0:T(8,128)(2,1)S(1)}, u32[]{:S(2)}, u32[]{:S(2)}) collective-permute-start(bf16[256,1024]{1,0:T(8,128)(2,1)S(1)} %copy-done.35), channel_id=1, source_target_pairs={{0,1},{1,0},{2,3},{3,2},{4,5},{5,4},{6,7},{7,6},{8,9},{9,8},{10,11... | collective-permute-start | bytes 1572872 | tf_op jit(solution)/shard_map/ppermute | solution.py:45
  442.9 23.7 %collective-permute-start.24 = (bf16[256,1024]{1,0:T(8,128)(2,1)S(1)}, bf16[256,1024]{1,0:T(8,128)(2,1)S(1)}, u32[]{:S(2)}, u32[]{:S(2)}) collective-permute-start(bf16[256,1024]{1,0:T(8,128)(2,1)S(1)} %copy-done.37), channel_id=1, source_target_pairs={{0,1},{1,0},{2,3},{3,2},{4,5},{5,4},{6,7},{7,6},{8,9},{9,8},{10,11... | collective-permute-start | bytes 1572872 | tf_op jit(solution)/shard_map/ppermute | solution.py:45
  467.4 3.7 copy-start.23
  467.4 16.8 %copy-start.34 = (bf16[256,1024]{1,0:T(8,128)(2,1)S(1)}, bf16[256,1024]{1,0:T(8,128)(2,1)}, u32[]{:S(2)}) copy-start(bf16[256,1024]{1,0:T(8,128)(2,1)} %get-tuple-element.137) | copy-start | bytes 1572868
  467.5 16.9 %copy-start.33 = (bf16[256,1024]{1,0:T(8,128)(2,1)S(1)}, bf16[256,1024]{1,0:T(8,128)(2,1)}, u32[]{:S(2)}) copy-start(bf16[256,1024]{1,0:T(8,128)(2,1)} %get-tuple-element.134) | copy-start | bytes 1572868
  472.1 6.8 %collective-permute-start.26 = (f32[16,4,32]{2,1,0:T(4,128)S(1)}, f32[16,4,32]{2,1,0:T(4,128)S(1)}, u32[]{:S(2)}, u32[]{:S(2)}) collective-permute-start(f32[16,4,32]{2,1,0:T(4,128)S(1)} %slice_select_fusion), channel_id=1, source_target_pairs={{0,16},{8,24},{16,0},{24,8},{1,17},{9,25},{17,1},{25,9},{2,18},{10... | collective-permute-start | bytes 24584 | tf_op jit(solution)/shard_map/ppermute | solution.py:45
  478.8 4.1 collective-permute-start.27
  483.0 3.7 collective-permute-start.28
  484.2 14.9 %collective-permute-start.16 = (bf16[256,1024]{1,0:T(8,128)(2,1)S(1)}, bf16[256,1024]{1,0:T(8,128)(2,1)S(1)}, u32[]{:S(2)}, u32[]{:S(2)}) collective-permute-start(bf16[256,1024]{1,0:T(8,128)(2,1)S(1)} %copy-done.34), channel_id=1, source_target_pairs={{0,1},{1,0},{2,3},{3,2},{4,5},{5,4},{6,7},{7,6},{8,9},{9,8},{10,11... | collective-permute-start | bytes 1572872 | tf_op jit(solution)/shard_map/ppermute | solution.py:45
  484.4 20.5 %collective-permute-start.15 = (bf16[256,1024]{1,0:T(8,128)(2,1)S(1)}, bf16[256,1024]{1,0:T(8,128)(2,1)S(1)}, u32[]{:S(2)}, u32[]{:S(2)}) collective-permute-start(bf16[256,1024]{1,0:T(8,128)(2,1)S(1)} %copy-done.33), channel_id=1, source_target_pairs={{0,1},{1,0},{2,3},{3,2},{4,5},{5,4},{6,7},{7,6},{8,9},{9,8},{10,11... | collective-permute-start | bytes 1572872 | tf_op jit(solution)/shard_map/ppermute | solution.py:45
  486.7 1.2 collective-permute-start.29
  488.0 21.5 %collective-permute-start.30 = (f32[1,4,32]{2,1,0:T(4,128)S(1)}, f32[1,4,32]{2,1,0:T(4,128)S(1)}, u32[]{:S(2)}, u32[]{:S(2)}) collective-permute-start(f32[1,4,32]{2,1,0:T(4,128)S(1)} %slice_select_fusion.4), channel_id=1, source_target_pairs={{0,1},{1,0},{2,3},{3,2},{4,5},{5,4},{6,7},{7,6},{8,9},{9,8},{10,11... | collective-permute-start | bytes 1544 | tf_op jit(solution)/shard_map/ppermute | solution.py:45
  499.1 5.7 %copy-start.13 = (bf16[256,1024]{1,0:T(8,128)(2,1)}, bf16[256,1024]{1,0:T(8,128)(2,1)S(1)}, u32[]{:S(2)}) copy-start(bf16[256,1024]{1,0:T(8,128)(2,1)S(1)} %collective-permute-done.16.refs_5_) | copy-start | bytes 1572868
  505.6 5.2 copy-start
  (14 other events, 11.7 us)
Sparse Core Ops, SparseCore 0:
  10.8 54.4 all-gather.2
  67.7 119.4 all-gather.4
  272.5 138.4 reduce-scatter.2
  441.6 71.3 reduce-scatter.4

commit v4 on v3

--- a/solution.py
+++ b/solution.py
@@ -66,21 +66,6 @@
 
 def hold(values, *others):
     return lax.optimization_barrier((values, others))[0]
-
-
-def gather_ordered(array, axes):
-    for axis in reversed(axes):
-        bit = 1
-        while bit < lax.axis_size(axis):
-            arrived = swap(array, axis, bit)
-            upper = (lax.axis_index(axis) // bit) % 2 == 1
-            array = jnp.where(
-                upper,
-                jnp.concatenate([arrived, array], axis=0),
-                jnp.concatenate([array, arrived], axis=0),
-            )
-            bit *= 2
-    return array
 
 
 def scatter_ordered(array, axes):
@@ -253,11 +238,205 @@
     )
 
 
+def half_chip_peers():
+    seq, depth = lax.axis_index("seq"), lax.axis_index("dp")
+    size = lax.axis_size("dp")
+    return {
+        "far": {"seq": flipped(seq, 2)},
+        "up": {"dp": (depth + 1) % size},
+        "down": {"dp": (depth + size - 1) % size},
+        "core": {"seq": flipped(seq, 1)},
+    }
+
+
+class Route:
+    PARTS = ((0, 0), (0, 1), (3, 0), (1, 0), (3, 1), (1, 1), (2, 0), (2, 1))
+
+    def __init__(self, whole, rows, send_sem, recv_sem, own=None):
+        self.whole, self.rows = whole, rows
+        self.send_sem, self.recv_sem = send_sem, recv_sem
+        self.seq, self.depth = lax.axis_index("seq"), lax.axis_index("dp")
+        self.peers = half_chip_peers()
+        self.own = self.part((0, 0)) if own is None else own
+
+    def part(self, place, half=None):
+        turn, other = place
+        seq = flipped(self.seq, 2) if other else self.seq
+        at = (((self.depth + turn) % lax.axis_size("dp")) * lax.axis_size("seq") + seq) * self.rows
+        count = self.rows if half is None else self.rows // 2
+        if half == 1:
+            at = at + count
+        return self.whole.at[pl.ds(pl.multiple_of(at, count), count), :]
+
+    def message(self, number):
+        if number >= 9:
+            place, peer, half = self.PARTS[number - 9], "core", None
+        else:
+            place, peer, half = (
+                ((0, 0), "far", None),
+                ((0, 0), "up", None),
+                ((0, 0), "down", None),
+                ((0, 1), "up", None),
+                ((0, 1), "down", None),
+                ((3, 0), "up", 0),
+                ((1, 0), "down", 1),
+                ((3, 1), "up", 0),
+                ((1, 1), "down", 1),
+            )[number]
+        target = self.part(place, half)
+        return send(
+            self.own if place == (0, 0) else target,
+            target,
+            self.send_sem.at[number],
+            self.recv_sem.at[number],
+            self.peers[peer],
+        )
+
+    def start(self, *numbers):
+        for number in numbers:
+            self.message(number).start()
+
+    def arrived(self, *numbers):
+        for number in numbers:
+            self.message(number).wait_recv()
+
+    def sent(self, *numbers):
+        for number in numbers:
+            self.message(number).wait_send()
+
+
+MESSAGES = 17
+
+
+def gather_kernel(trades, att_ref, ffn_ref, tile_ref, tokens_ref, *refs):
+    att_all, ffn_all, norms_ref, tokens_all = refs[:4]
+    tiles, pair_of_tiles = refs[4:6]
+    att_send, att_recv, ffn_send, ffn_recv, tile_send, tile_recv = refs[6:12]
+    own_sem, tokens_send, tokens_recv, pair_send, pair_recv = refs[12:]
+    tensor = lax.axis_index("tensor")
+    others = [{"tensor": flipped(tensor, other + 1)} for other in range(trades)]
+    rows = att_ref.shape[0]
+    att = Route(att_all, rows, att_send, att_recv, att_ref)
+    ffn = Route(ffn_all, rows, ffn_send, ffn_recv, ffn_ref)
+    tile_rows = tile_ref.shape[0]
+    group = pair_of_tiles.shape[0]
+    small = Route(tiles, group, tile_send, tile_recv, pair_of_tiles)
+
+    def tokens_trade(other):
+        return send(
+            tokens_ref,
+            tokens_all.at[other],
+            tokens_send.at[other],
+            tokens_recv.at[other],
+            others[other],
+        )
+
+    own_rows = pl.ds(pl.multiple_of(tensor * tile_rows, tile_rows), tile_rows)
+
+    def pair_trade(other):
+        return send(
+            tile_ref,
+            pair_of_tiles.at[own_rows, :],
+            pair_send.at[other],
+            pair_recv.at[other],
+            others[other],
+        )
+
+    own_copies = [
+        pltpu.make_async_copy(att_ref, att.part((0, 0)), own_sem.at[0]),
+        pltpu.make_async_copy(ffn_ref, ffn.part((0, 0)), own_sem.at[1]),
+        pltpu.make_async_copy(tile_ref, pair_of_tiles.at[own_rows, :], own_sem.at[2]),
+        pltpu.make_async_copy(pair_of_tiles, small.part((0, 0)), own_sem.at[3]),
+    ]
+
+    greet(list(att.peers.values()) + others)
+    for other in range(trades):
+        pair_trade(other).start()
+    att.start(0, 1, 2, 9)
+    own_copies[2].start()
+    own_copies[0].start()
+    own_copies[1].start()
+    for other in range(trades):
+        tokens_trade(other).start()
+    own_copies[2].wait()
+    for other in range(trades):
+        pair_trade(other).wait_recv()
+    own_copies[3].start()
+    small.start(0, 1, 2, 9)
+    ffn.start(0)
+    att.arrived(0)
+    att.start(3, 4, 10)
+    small.arrived(0)
+    small.start(3, 4, 10)
+    for route in (att, small):
+        route.arrived(1, 2)
+        route.start(5, 6, 11, 12)
+    for route in (att, small):
+        route.arrived(3, 4)
+        route.start(7, 8, 13, 14)
+    for route in (small, att):
+        route.arrived(5, 6)
+        route.start(15)
+        route.arrived(7, 8)
+        route.start(16)
+        route.arrived(*range(9, 17))
+    own_copies[3].wait()
+    shard = norms_ref.shape[1] // (tiles.shape[0] // tile_rows)
+    total = None
+    for device in range(tiles.shape[0] // tile_rows):
+        tile = tiles[device * tile_rows : (device + 1) * tile_rows, :]
+        norms_ref[:, device * shard : (device + 1) * shard] = tile[:, :shard]
+    for depth in range(lax.axis_size("dp")):
+        at = depth * (tiles.shape[0] // lax.axis_size("dp"))
+        one = tiles[at + 4 : at + 5, :]
+        total = one if total is None else total + one
+    norms_ref[4:5, : total.shape[1]] = total
+    for route in (att, small):
+        route.sent(*range(MESSAGES))
+    ffn.arrived(0)
+    ffn.sent(0)
+    own_copies[0].wait()
+    own_copies[1].wait()
+    for other in range(trades):
+        pair_trade(other).wait_send()
+        tokens_trade(other).wait_recv()
+        tokens_trade(other).wait_send()
+
+
+def gather(att, ffn, tile, tokens, trades):
+    count = lax.axis_size("dp") * lax.axis_size("seq")
+    rows = att.shape[0]
+    group = tile.shape[0] * (trades + 1)
+    anywhere = pl.BlockSpec(memory_space=pl.ANY)
+    vmem = pl.BlockSpec(memory_space=pltpu.VMEM)
+    dma = pltpu.SemaphoreType.DMA
+    return run(
+        functools.partial(gather_kernel, trades),
+        "gather",
+        [
+            shaped((count * rows, att.shape[1]), BF16),
+            shaped((count * rows, ffn.shape[1]), BF16),
+            shaped((tile.shape[0], count * rows), F32),
+            shaped((trades,) + tokens.shape, BF16),
+        ],
+        0,
+        [att, ffn, tile, tokens],
+        collective_id=1,
+        in_specs=[vmem, vmem, vmem, anywhere],
+        out_specs=[anywhere, anywhere, vmem, anywhere],
+        scratch_shapes=[pltpu.VMEM((count * group, 128), F32), pltpu.VMEM((group, 128), F32)]
+        + [dma((MESSAGES,))] * 6
+        + [dma((4,)), dma((trades,)), dma((trades,)), dma((trades,)), dma((trades,))],
+    )
+
+
 def attend_kernel(windows, pairs, trades, exp_scale, *refs):
     q_ref, w_ref, kv_ref, cot_ref = refs[:4]
-    low_ref, wide_ref, log_ref, kept_ref, sent_ref, slots_ref, cots_ref = refs[4:11]
-    slots, acc_all, top_all, total_all, mixed_rows = refs[11:16]
-    own_sem, send_sem, recv_sem, save_sem, cot_send, cot_recv = refs[16:]
+    low_ref, wide_ref, log_ref, kept_ref, sent_ref, slots_ref, cots_ref, ffn_ref = refs[5:13]
+    slots, acc_all, top_all, total_all, mixed_rows = refs[13:18]
+    own_sem, send_sem, recv_sem, save_sem, cot_send, cot_recv, ffn_send, ffn_recv = refs[18:]
+    shards = lax.axis_size("dp") * lax.axis_size("seq")
+    ffn = Route(ffn_ref, ffn_ref.shape[0] // shards, ffn_send, ffn_recv)
     step = pl.program_id(0)
     near_steps = windows * pairs
     steps = 2 * near_steps
@@ -296,7 +475,8 @@
 
     @pl.when(step == 0)
     def _():
-        greet([core_peer, far_peer] + cot_peers)
+        greet(list(ffn.peers.values()) + cot_peers)
+        ffn.start(1, 2, 3, 4, 9, 10)
 
         @pl.loop(0, near_steps)
         def _(number):
@@ -306,6 +486,16 @@
 
         for other in range(trades):
             cot_trade(other).start()
+
+    @pl.when(step == near_steps - 1)
+    def _():
+        ffn.arrived(1, 2)
+        ffn.start(5, 6, 11, 12)
+
+    @pl.when(step == near_steps + near_steps // 2)
+    def _():
+        ffn.arrived(3, 4)
+        ffn.start(7, 8, 13, 14)
 
     relayed = step - (near_steps - 1)
 
@@ -390,6 +580,11 @@
 
     @pl.when(step == steps - 1)
     def _():
+        ffn.arrived(5, 6)
+        ffn.start(15)
+        ffn.arrived(7, 8)
+        ffn.start(16)
+
         @pl.loop(0, near_steps)
         def _(number):
             for slot in range(1, 4):
@@ -400,9 +595,11 @@
         for other in range(trades):
             cot_trade(other).wait_send()
             cot_trade(other).wait_recv()
-
-
-def attend(queries, own_kv, w_att, cotangent, trades):
+        ffn.arrived(*range(9, MESSAGES))
+        ffn.sent(*range(1, MESSAGES))
+
+
+def attend(queries, own_kv, w_att, cotangent, w_ffn, trades):
     windows, rows, cols = queries.shape
     width = w_att.shape[0]
     pairs = cols // PAIR
@@ -428,14 +625,17 @@
             shaped((windows, rows // 2, width), BF16),
             shaped((near, 4, 2, rows, PAIR), BF16),
             shaped((trades,) + cotangent.shape, BF16),
+            shaped(w_ffn.shape, BF16),
         ],
         64 * windows * rows * rows * cols,
-        [queries, w_att, own_kv, cotangent],
+        [queries, w_att, own_kv, cotangent, w_ffn],
         collective_id=0,
+        input_output_aliases={4: 7},
         grid=(2 * near,),
         in_specs=[
             pl.BlockSpec((1, rows, PAIR), lambda i: ((i // pairs) % windows, 0, i % pairs)),
             pl.BlockSpec((width, PAIR), lambda i: (0, out_at + far(i) % pairs)),
+            anywhere,
             anywhere,
             anywhere,
         ],
@@ -445,6 +645,7 @@
             pl.BlockSpec((1, PAIR, rows), lambda i: (far(i) // pairs, far(i) % pairs, 0)),
             half,
             half,
+            anywhere,
             anywhere,
             anywhere,
         ],
@@ -460,6 +661,8 @@
             dma((near, 4)),
             dma((trades,)),
             dma((trades,)),
+            dma((MESSAGES,)),
+            dma((MESSAGES,)),
         ],
     )
 
@@ -867,18 +1070,6 @@
     every = ("dp", "seq", "tensor")
     shards = ("dp", "seq")
 
-    w_att = lax.all_gather(
-        jnp.concatenate([w_query, w_key, w_value, w_out.T], axis=1), shards, axis=0, tiled=True
-    )
-    w_ffn = lax.all_gather(
-        jnp.concatenate([w_gate, w_up, w_down.T], axis=1), shards, axis=0, tiled=True
-    )
-
-    norms = gather_ordered(
-        jnp.stack([norm1_gain, norm1_bias, norm2_gain, norm2_bias])[None], every
-    )
-    norms = norms.transpose(1, 0, 2).reshape(4, model_width)
-
     own_at = lax.axis_index("tensor")
     starts = jnp.concatenate(
         [
@@ -894,21 +1085,27 @@
     labels = lax.broadcasted_iota(jnp.int32, (windows_here, species_scale.shape[0]), 1)
     chosen = jnp.sum(jnp.where(species[:, None] == labels, species_scale[None, :], 0.0), axis=1)
     weighted = counts.astype(F32) * chosen
-    weight_total = jnp.broadcast_to(jnp.sum(weighted), (8, 128))
-    bit = 1
-    while bit < lax.axis_size("dp"):
-        weight_total = weight_total + swap(weight_total, "dp", bit)
-        bit *= 2
-    factor = weighted * float(windows_here * lax.axis_size("dp")) / weight_total[0, 0]
+
+    lanes = jnp.zeros((8, 128), F32)
+    vectors = jnp.stack([norm1_gain, norm1_bias, norm2_gain, norm2_bias])
+    tile = lanes.at[:4, : vectors.shape[1]].set(vectors).at[4, :].set(jnp.sum(weighted))
+    w_att, w_ffn, norms, arrived_tokens = gather(
+        jnp.concatenate([w_query, w_key, w_value, w_out.T], axis=1),
+        jnp.concatenate([w_gate, w_up, w_down.T], axis=1),
+        tile,
+        tokens,
+        tensor_size - 1,
+    )
+    factor = weighted * float(windows_here * lax.axis_size("dp")) / norms[4, 0]
 
     windows = range(windows_here)
     factors = [factor[w].reshape(1, 1) for w in windows]
     top_bit = seq_size // 2
 
-    token_blocks = spread(tokens, "tensor")
+    token_blocks = [tokens] + [arrived_tokens[other] for other in range(tensor_size - 1)]
     normed_rows, queries, own_kv = project(token_blocks, norms, w_att, cosine, sine)
-    attended, wide_attended, logs, kept_all, sent_all, slots_all, cots = attend(
-        queries, own_kv, w_att, cotangent, tensor_size - 1
+    attended, wide_attended, logs, kept_all, sent_all, slots_all, cots, w_ffn = attend(
+        queries, own_kv, w_att, cotangent, w_ffn, tensor_size - 1
     )
     cot_blocks = [
         [cotangent[w]] + [cots[other, w] for other in range(tensor_size - 1)] for w in windows

time: 533 us -> 559 us (1.049)
  Pallas kernels: 273 us -> 349 us
  waiting for transfers between devices: 162 us -> 124 us
  starting transfers between devices: 31.6 us -> 23.1 us
    pallas_call x19 -> x20, Pallas kernels: 273 us -> 349 us  [run(): pl.pallas_call(kernel, out_shape=out_shape, compiler_params=pltpu.Compile...]
    all_gather x2 -> x0, waiting for transfers between devices: 26.3 us -> none  [the longest x1 26.3 us: local(): lax.all_gather(jnp.concatenate([w_query, w_key, w_value, w_out.T], axis=1...]
    ppermute x31 -> x23, waiting for transfers between devices: 134 us -> 121 us  [swap(): return lax.ppermute(array, axis, [(i, i ^ bit) for i in range(size)])]
    ppermute x31 -> x23, starting transfers between devices: 31.5 us -> 23 us  [swap(): return lax.ppermute(array, axis, [(i, i ^ bit) for i in range(size)])]
    unnamed x86 -> x96, local copies, waits for them, and re-layouts: 12.7 us -> 12.7 us
  transfers between devices with their start and end apart: 35 -> 25, of which waited for: 22 -> 16; matrix products, arithmetic and copies ran while one was open for 4% -> 2% of each run, Pallas kernels for 47% -> 28%
where the time goes in v4:
time: 559 us; the launch traced here: 550 us
  Pallas kernels  349 us (62%)
  waiting for transfers between devices  124 us (22%)
  local copies, waits for them, and re-layouts  28.8 us (5%)
  starting transfers between devices  23.1 us (4%)
  between operations  14.8 us (3%)
  other arithmetic  9.71 us (2%)
    pallas_call x20, Pallas kernels, run(): pl.pallas_call(kernel, out_shape=out_shape, compiler_params=pltpu.Compile...  349 us
    ppermute x23, waiting for transfers between devices, swap(): return lax.ppermute(array, axis, [(i, i ^ bit) for i in range(size)])  121 us
    ppermute x23, starting transfers between devices, swap(): return lax.ppermute(array, axis, [(i, i ^ bit) for i in range(size)])  23 us
    unnamed x96, local copies, waits for them, and re-layouts  12.7 us
  transfers between devices with their start and end apart: 25, of which 16 were waited for; matrix products, arithmetic and copies ran while one was open for 2% of the time, Pallas kernels for 28%

profile of v4, /device:TPU:0, one launch (start us, length us, event | category | flops | bytes accessed | tf_op | source)
XLA Modules:
  0.0 549.5 jit_solution(489669026189705800)
XLA Ops:
  7.4 1.0 fusion
  8.4 1.0 pad_maximum_fusion.2.cos_ref.refs_6_
  9.4 1.0 pad_maximum_fusion.3.sin_ref.refs_7_
  13.6 47.6 %gather.1 = (bf16[1024,2048]{1,0:T(8,128)(2,1)}, bf16[1024,6144]{1,0:T(8,128)(2,1)}, f32[8,1024]{1,0:T(8,128)}, bf16[1,2,256,1024]{3,2,1,0:T(8,128)(2,1)}) custom-call(bf16[64,2048]{1,0:T(8,128)(2,1)} %pad_maximum_fusion.1.att_ref, bf16[64,6144]{1,0:T(8,128)(2,1)} %pad_maximum_fusion.ffn_ref, f32[8,128]{1,0:T(8,128)} %copy-done.28, bf16[2,256,1024]{2,1,0:T(8,128)(2,1)} %refs_0_.1), custom_call_target="tpu_custom_call" | custom-call | bytes 19959808 | tf_op jit(solution)/shard_map/gather/pallas_call | solution.py:117
  61.2 8.4 %project.1 = (bf16[2,512,1024]{2,1,0:T(8,128)(2,1)}, bf16[2,512,512]{2,1,0:T(8,128)(2,1)}, bf16[2,2,512,512]{3,2,1,0:T(8,128)(2,1)}) custom-call(f32[8,1024]{1,0:T(8,128)} %get-tuple-element.122.norms_ref, bf16[1024,2048]{1,0:T(8,128)(2,1)} %get-tuple-element.123.w_ref.refs_1_.refs_5_, f32[512,128]{1,0:T(8,128)} %pad_maximum_fusion.2.cos_ref.refs_6_, ...), custom_call_target="tpu_custom_call" | custom-call | flops 3221225472 | bytes 12091392 | tf_op jit(solution)/shard_map/project/pallas_call | solution.py:117
  69.7 109.9 %attend.1 = (bf16[2,512,512]{2,1,0:T(8,128)(2,1)}, f32[2,512,512]{2,1,0:T(8,128)}, f32[2,512,512]{2,1,0:T(8,128)}, f32[2,256,1024]{2,1,0:T(8,128)}, bf16[2,256,1...) custom-call(bf16[2,512,512]{2,1,0:T(8,128)(2,1)} %get-tuple-element., ...), custom_call_target="tpu_custom_call", output_to_operand_aliasing={{7}: (4, {})} | custom-call | flops 17179869184 | bytes 51380224 | tf_op jit(solution)/shard_map/attend/pallas_call | solution.py:117
  179.6 1.4 slice_bitcast_fusion.9
  181.0 1.6 collective-permute-start
  183.1 1.2 slice.170
  185.6 1.0 slice_bitcast_fusion.10
  186.6 1.6 slice_bitcast_fusion.2
  188.2 7.6 %collective-permute-done.arrived_ref = bf16[256,1024]{1,0:T(8,128)(2,1)S(1)} collective-permute-done((bf16[256,1024]{1,0:T(8,128)(2,1)S(1)}, bf16[256,1024]{1,0:T(8,128)(2,1)S(1)}, u32[]{:S(2)}, u32[]{:S(2)}) %collective-permute-start) | collective-permute-done | bytes 524320 | tf_op jit(solution)/shard_map/ppermute | solution.py:45
  196.6 3.0 second_norm.2
  199.6 1.5 collective-permute-start.1
  201.1 1.0 slice_bitcast_fusion.8
  202.1 1.0 slice_bitcast_fusion.7
  203.2 3.9 collective-permute-done.2.arrived_ref
  207.9 2.8 second_norm.3
  210.7 1.5 collective-permute-start.3
  212.1 6.1 %collective-permute-done.1.refs_1_ = bf16[256,1024]{1,0:T(8,128)(2,1)S(1)} collective-permute-done((bf16[256,1024]{1,0:T(8,128)(2,1)}, bf16[256,1024]{1,0:T(8,128)(2,1)S(1)}, u32[]{:S(2)}, u32[]{:S(2)}) %collective-permute-start.1) | collective-permute-done | bytes 524320 | tf_op jit(solution)/shard_map/ppermute | solution.py:45
  219.1 23.7 %feed.2 = (bf16[512,1024]{1,0:T(8,128)(2,1)}, bf16[512,1024]{1,0:T(8,128)(2,1)}, bf16[512,2048]{1,0:T(8,128)(2,1)}, bf16[512,2048]{1,0:T(8,128)(2,1)}, bf16[512,...) custom-call(f32[1,1]{1,0:T(1,128)} %bitcast.11.factor_ref, ...), custom_call_target="tpu_custom_call" | custom-call | flops 12884901888 | bytes 51380228 | tf_op jit(solution)/shard_map/feed/pallas_call | solution.py:117
  242.8 1.6 collective-permute-start.4
  245.1 23.3 %feed.3 = (bf16[512,1024]{1,0:T(8,128)(2,1)}, bf16[512,1024]{1,0:T(8,128)(2,1)}, bf16[512,2048]{1,0:T(8,128)(2,1)}, bf16[512,2048]{1,0:T(8,128)(2,1)}, bf16[512,...) custom-call(f32[1,1]{1,0:T(1,128)} %bitcast.14.factor_ref, ...), custom_call_target="tpu_custom_call" | custom-call | flops 12884901888 | bytes 51380228 | tf_op jit(solution)/shard_map/feed/pallas_call | solution.py:117
  269.3 4.5 second_norm_back.2
  273.8 22.6 %feed_weights.1 = bf16[1024,6144]{1,0:T(8,128)(2,1)} custom-call(bf16[512,1024]{1,0:T(8,128)(2,1)} %get-tuple-element.139.refs_0_.refs_4_, bf16[512,1024]{1,0:T(8,128)(2,1)} %get-tuple-element.149.refs_1_.refs_5_, bf16[512,2048]{1,0:T(8,128)(2,1)} %get-tuple-element.142.refs_2_, bf16[512,2048]{1,0:T(8,128)(2,1)} %get-tuple-element.150.refs_3_, ...), custom_call_target="tpu_custom_call" | custom-call | flops 12884901888 | bytes 31457280 | tf_op jit(solution)/shard_map/feed_weights/pallas_call | solution.py:117
  297.9 1.5 collective-permute-start.6
  299.4 12.8 %collective-permute-done.5.arrived_ref = bf16[256,1024]{1,0:T(8,128)(2,1)S(1)} collective-permute-done((bf16[256,1024]{1,0:T(8,128)(2,1)S(1)}, bf16[256,1024]{1,0:T(8,128)(2,1)S(1)}, u32[]{:S(2)}, u32[]{:S(2)}) %collective-permute-start.5) | collective-permute-done | bytes 524320 | tf_op jit(solution)/shard_map/ppermute | solution.py:45
  313.1 5.0 second_norm_back.3
  318.5 5.0 collective-permute-done.6.refs_4_
  324.3 17.1 %attend_back_far.2 = (f32[512,512]{1,0:T(8,128)}, bf16[2,512,512]{2,1,0:T(8,128)(2,1)}, bf16[2,512,512]{2,1,0:T(8,128)(2,1)}, bf16[512,512]{1,0:T(8,128)(2,1)}, bf16[512,1024]{1,0:T(8,128)(2,1)}) custom-call(bf16[2,512,512]{2,1,0:T(8,128)(2,1)} %get-tuple-element.177.refs_0_, f32[2,512,512]{2,1,0:T(8,128)} %get-tuple-element.162.refs_1_, ...), custom_call_target="tpu_custom_call" | custom-call | flops 10737418240 | bytes 23592960 | tf_op jit(solution)/shard_map/attend_back_far/pallas_call | solution.py:117
  342.3 16.9 %attend_back_far.3 = (f32[512,512]{1,0:T(8,128)}, bf16[2,512,512]{2,1,0:T(8,128)(2,1)}, bf16[2,512,512]{2,1,0:T(8,128)(2,1)}, bf16[512,512]{1,0:T(8,128)(2,1)}, bf16[512,1024]{1,0:T(8,128)(2,1)}) custom-call(bf16[2,512,512]{2,1,0:T(8,128)(2,1)} %get-tuple-element.177.refs_0_, f32[2,512,512]{2,1,0:T(8,128)} %get-tuple-element.162.refs_1_, ...), custom_call_target="tpu_custom_call" | custom-call | flops 10737418240 | bytes 23592960 | tf_op jit(solution)/shard_map/attend_back_far/pallas_call | solution.py:117
  359.2 15.0 %attend_back_near.2 = (bf16[512,512]{1,0:T(8,128)(2,1)}, bf16[2,512,512]{2,1,0:T(8,128)(2,1)}, bf16[2,512,512]{2,1,0:T(8,128)(2,1)}) custom-call(bf16[2,512,512]{2,1,0:T(8,128)(2,1)} %get-tuple-element.177.refs_0_, f32[2,512,512]{2,1,0:T(8,128)} %get-tuple-element.162.refs_1_, f32[2,512,512]{2,1,0:T(8,128)} %get-tuple-element.163.refs_2_, ...), custom_call_target="tpu_custom_call" | custom-call | flops 10737418240 | bytes 18350080 | tf_op jit(solution)/shard_map/attend_back_near/pallas_call | solution.py:117
  374.9 15.3 %attend_back_near.3 = (bf16[512,512]{1,0:T(8,128)(2,1)}, bf16[2,512,512]{2,1,0:T(8,128)(2,1)}, bf16[2,512,512]{2,1,0:T(8,128)(2,1)}) custom-call(bf16[2,512,512]{2,1,0:T(8,128)(2,1)} %get-tuple-element.177.refs_0_, f32[2,512,512]{2,1,0:T(8,128)} %get-tuple-element.162.refs_1_, f32[2,512,512]{2,1,0:T(8,128)} %get-tuple-element.163.refs_2_, ...), custom_call_target="tpu_custom_call" | custom-call | flops 10737418240 | bytes 18350080 | tf_op jit(solution)/shard_map/attend_back_near/pallas_call | solution.py:117
  392.2 1.2 collective-permute-start.12
  393.4 1.1 slice_bitcast_fusion.5
  394.5 1.5 slice_bitcast_fusion
  396.0 29.4 %collective-permute-done.15.far_ref = bf16[2,512,512]{2,1,0:T(8,128)(2,1)S(1)} collective-permute-done((bf16[2,512,512]{2,1,0:T(8,128)(2,1)S(1)}, bf16[2,512,512]{2,1,0:T(8,128)(2,1)S(1)}, u32[]{:S(2)}, u32[]{:S(2)}) %collective-permute-start.15) | collective-permute-done | bytes 1048608 | tf_op jit(solution)/shard_map/ppermute | solution.py:45
  426.4 6.5 %turn_back.3 = (bf16[512,1536]{1,0:T(8,128)(2,1)}, f32[256,1024]{1,0:T(8,128)}, bf16[256,1024]{1,0:T(8,128)(2,1)}) custom-call(bf16[512,512]{1,0:T(8,128)(2,1)} %get-tuple-element.176.dq_ref, bf16[2,512,512]{2,1,0:T(8,128)(2,1)} %get-tuple-element.186.own_ref, bf16[2,512,512]{2,1,0:T(8,128)(2,1)} %copy-done.10, bf16[2,512,512]{2,1,0:T(8,128)(2,1)} %copy-done.12, ...), custom_call_target="tpu_custom_call" | custom-call | flops 1610612736 | bytes 11534336 | tf_op jit(solution)/shard_map/turn_back/pallas_call | solution.py:117
  433.0 14.1 %collective-permute-done.12.far_ref = bf16[2,512,512]{2,1,0:T(8,128)(2,1)S(1)} collective-permute-done((bf16[2,512,512]{2,1,0:T(8,128)(2,1)S(1)}, bf16[2,512,512]{2,1,0:T(8,128)(2,1)S(1)}, u32[]{:S(2)}, u32[]{:S(2)}) %collective-permute-start.12) | collective-permute-done | bytes 1048608 | tf_op jit(solution)/shard_map/ppermute | solution.py:45
  448.1 6.6 %turn_back.2 = (bf16[512,1536]{1,0:T(8,128)(2,1)}, f32[256,1024]{1,0:T(8,128)}, bf16[256,1024]{1,0:T(8,128)(2,1)}) custom-call(bf16[512,512]{1,0:T(8,128)(2,1)} %get-tuple-element.179.dq_ref, bf16[2,512,512]{2,1,0:T(8,128)(2,1)} %get-tuple-element.180.own_ref, bf16[2,512,512]{2,1,0:T(8,128)(2,1)} %copy-done.9, bf16[2,512,512]{2,1,0:T(8,128)(2,1)} %copy-done.11, ...), custom_call_target="tpu_custom_call" | custom-call | flops 1610612736 | bytes 11534336 | tf_op jit(solution)/shard_map/turn_back/pallas_call | solution.py:117
  454.7 9.6 %attend_weights.1 = bf16[1024,2048]{1,0:T(8,128)(2,1)} custom-call(bf16[512,1024]{1,0:T(8,128)(2,1)} %get-tuple-element.208.refs_0_, bf16[512,1024]{1,0:T(8,128)(2,1)} %get-tuple-element.207.refs_1_, bf16[512,1536]{1,0:T(8,128)(2,1)} %get-tuple-element.190.refs_2_, bf16[512,1536]{1,0:T(8,128)(2,1)} %get-tuple-element.191.refs_3_, ...), custom_call_target="tpu_custom_call" | custom-call | flops 4294967296 | bytes 12582912 | tf_op jit(solution)/shard_map/attend_weights/pallas_call | solution.py:117
  464.3 1.2 convert_element_type.42
  465.6 1.0 copy-done.41
  466.5 1.0 collective-permute-start.17
  467.6 1.0 collective-permute-start.16
  468.6 12.8 %collective-permute-done.17.arrived_ref = bf16[256,1024]{1,0:T(8,128)(2,1)S(1)} collective-permute-done((bf16[256,1024]{1,0:T(8,128)(2,1)S(1)}, bf16[256,1024]{1,0:T(8,128)(2,1)S(1)}, u32[]{:S(2)}, u32[]{:S(2)}) %collective-permute-start.17) | collective-permute-done | bytes 524320 | tf_op jit(solution)/shard_map/ppermute | solution.py:45
  482.2 3.8 first_norm_back.2
  486.0 4.9 collective-permute-done.16.arrived_ref
  491.7 3.7 first_norm_back.3
  496.3 2.6 collective-permute-start.18
  498.9 4.1 collective-permute-done.18
  503.0 1.0 collective-permute-start.19
  504.0 2.9 collective-permute-done.19
  507.0 1.2 collective-permute-start.20
  508.2 1.4 collective-permute-start.8
  510.8 1.1 collective-permute-done.21
  512.0 1.6 collective-permute-start.22
  513.6 9.7 %collective-permute-done.8.refs_5_ = bf16[256,1024]{1,0:T(8,128)(2,1)S(1)} collective-permute-done((bf16[256,1024]{1,0:T(8,128)(2,1)}, bf16[256,1024]{1,0:T(8,128)(2,1)S(1)}, u32[]{:S(2)}, u32[]{:S(2)}) %collective-permute-start.8) | collective-permute-done | bytes 524320 | tf_op jit(solution)/shard_map/ppermute | solution.py:45
  523.3 6.1 %collective-permute-done.7.refs_2_ = bf16[256,1024]{1,0:T(8,128)(2,1)S(1)} collective-permute-done((bf16[256,1024]{1,0:T(8,128)(2,1)S(1)}, bf16[256,1024]{1,0:T(8,128)(2,1)S(1)}, u32[]{:S(2)}, u32[]{:S(2)}) %collective-permute-start.7) | collective-permute-done | bytes 524320 | tf_op jit(solution)/shard_map/ppermute | solution.py:45
  530.1 3.8 results.1
  535.3 1.1 fusion.4
  536.3 2.8 reduce-scatter.5.cloned.1.call-done
  539.2 1.0 convert_element_type.43
  540.8 1.7 fusion.5
  (151 shorter events, 24.8 us)
Async XLA Ops:
  7.2 3.2 copy-start.33
  7.2 3.2 copy-start.32
  7.2 3.4 copy-start.38
  7.2 4.0 copy-start.21
  7.2 4.0 copy-start.23
  7.2 4.0 copy-start.22
  7.2 4.9 copy-start.37
  7.3 4.9 copy-start.36
  7.3 4.9 copy-start.35
  7.3 4.9 copy-start.34
  7.3 5.6 %copy-start.24 = (bf16[512,64]{0,1:T(8,128)(2,1)S(1)}, bf16[512,64]{0,1:T(8,128)(2,1)}, u32[]{:S(2)}) copy-start(bf16[512,64]{0,1:T(8,128)(2,1)} %param.30) | copy-start | bytes 196612
  7.3 5.6 %copy-start.27 = (bf16[64,512]{1,0:T(8,128)(2,1)S(1)}, bf16[64,512]{1,0:T(8,128)(2,1)}, u32[]{:S(2)}) copy-start(bf16[64,512]{1,0:T(8,128)(2,1)} %param.27) | copy-start | bytes 196612
  7.3 5.6 %copy-start.26 = (bf16[64,512]{1,0:T(8,128)(2,1)S(1)}, bf16[64,512]{1,0:T(8,128)(2,1)}, u32[]{:S(2)}) copy-start(bf16[64,512]{1,0:T(8,128)(2,1)} %param.28) | copy-start | bytes 196612
  7.3 5.6 %copy-start.25 = (bf16[64,512]{1,0:T(8,128)(2,1)S(1)}, bf16[64,512]{1,0:T(8,128)(2,1)}, u32[]{:S(2)}) copy-start(bf16[64,512]{1,0:T(8,128)(2,1)} %param.29) | copy-start | bytes 196612
  7.3 456.9 %reduce-scatter.3.cloned.1.call-start = ((), (), s32[]{:S(2)}) async-start(), calls=%async_computation.2 | async-start | bytes 13369344 | tf_op jit(solution)/shard_map/reduce_scatter | solution.py:1150
  179.6 6.0 %copy-start.1 = (bf16[2,256,1024]{2,1,0:T(8,128)(2,1)S(1)}, bf16[2,256,1024]{2,1,0:T(8,128)(2,1)}, u32[]{:S(2)}) copy-start(bf16[2,256,1024]{2,1,0:T(8,128)(2,1)} %refs_0_.1) | copy-start | bytes 3145732
  179.6 7.0 %copy-start.3 = (f32[2,256,1024]{2,1,0:T(8,128)S(1)}, f32[2,256,1024]{2,1,0:T(8,128)}, u32[]{:S(2)}) copy-start(f32[2,256,1024]{2,1,0:T(8,128)} %get-tuple-element.128) | copy-start | bytes 6291460
  181.0 14.8 %collective-permute-start = (bf16[256,1024]{1,0:T(8,128)(2,1)S(1)}, bf16[256,1024]{1,0:T(8,128)(2,1)S(1)}, u32[]{:S(2)}, u32[]{:S(2)}) collective-permute-start(bf16[256,1024]{1,0:T(8,128)(2,1)S(1)} %get-tuple-element.218), channel_id=1, source_target_pairs={{0,1},{1,0},{2,3},{3,2},{4,5},{5,4},{6,7},{7,6},{8,9},{9,8},{10,11... | collective-permute-start | bytes 1572872 | tf_op jit(solution)/shard_map/ppermute | solution.py:45
  182.6 24.5 %collective-permute-start.2 = (bf16[256,1024]{1,0:T(8,128)(2,1)S(1)}, bf16[256,1024]{1,0:T(8,128)(2,1)S(1)}, u32[]{:S(2)}, u32[]{:S(2)}) collective-permute-start(bf16[256,1024]{1,0:T(8,128)(2,1)S(1)} %get-tuple-element.217), channel_id=1, source_target_pairs={{0,1},{1,0},{2,3},{3,2},{4,5},{5,4},{6,7},{7,6},{8,9},{9,8},{10,11... | collective-permute-start | bytes 1572872 | tf_op jit(solution)/shard_map/ppermute | solution.py:45
  188.2 12.9 %copy-start.6 = (bf16[2,256,1024]{2,1,0:T(8,128)(2,1)S(1)}, bf16[2,256,1024]{2,1,0:T(8,128)(2,1)}, u32[]{:S(2)}) copy-start(bf16[2,256,1024]{2,1,0:T(8,128)(2,1)} %refs_3_.1) | copy-start | bytes 3145732
  196.6 5.5 copy-start.8
  199.6 18.7 %collective-permute-start.1 = (bf16[256,1024]{1,0:T(8,128)(2,1)}, bf16[256,1024]{1,0:T(8,128)(2,1)S(1)}, u32[]{:S(2)}, u32[]{:S(2)}) collective-permute-start(bf16[256,1024]{1,0:T(8,128)(2,1)} %get-tuple-element.133.refs_0_), channel_id=1, source_target_pairs={{0,1},{1,0},{2,3},{3,2},{4,5},{5,4},{6,7},{7,6},{8,9},{9,8},{10,11... | collective-permute-start | bytes 1572872 | tf_op jit(solution)/shard_map/ppermute | solution.py:45
  210.7 33.7 %collective-permute-start.3 = (bf16[256,1024]{1,0:T(8,128)(2,1)}, bf16[256,1024]{1,0:T(8,128)(2,1)S(1)}, u32[]{:S(2)}, u32[]{:S(2)}) collective-permute-start(bf16[256,1024]{1,0:T(8,128)(2,1)} %get-tuple-element.146.refs_0_), channel_id=1, source_target_pairs={{0,1},{1,0},{2,3},{3,2},{4,5},{5,4},{6,7},{7,6},{8,9},{9,8},{10,11... | collective-permute-start | bytes 1572872 | tf_op jit(solution)/shard_map/ppermute | solution.py:45
  242.8 25.7 %collective-permute-start.4 = (bf16[256,1024]{1,0:T(8,128)(2,1)}, bf16[256,1024]{1,0:T(8,128)(2,1)S(1)}, u32[]{:S(2)}, u32[]{:S(2)}) collective-permute-start(bf16[256,1024]{1,0:T(8,128)(2,1)} %get-tuple-element.145), channel_id=1, source_target_pairs={{0,1},{1,0},{2,3},{3,2},{4,5},{5,4},{6,7},{7,6},{8,9},{9,8},{10,11... | collective-permute-start | bytes 1572872 | tf_op jit(solution)/shard_map/ppermute | solution.py:45
  244.4 0.8 copy-start.44
  268.5 0.8 copy-start.18
  296.4 1.0 copy-start.43
  296.4 1.6 copy-start.42
  296.4 242.8 %reduce-scatter.5.cloned.1.call-start = ((), (), s32[]{:S(2)}) async-start(), calls=%async_computation.3 | async-start | bytes 4456448 | tf_op jit(solution)/shard_map/reduce_scatter | solution.py:1203
  297.4 14.9 %collective-permute-start.5 = (bf16[256,1024]{1,0:T(8,128)(2,1)S(1)}, bf16[256,1024]{1,0:T(8,128)(2,1)S(1)}, u32[]{:S(2)}, u32[]{:S(2)}) collective-permute-start(bf16[256,1024]{1,0:T(8,128)(2,1)S(1)} %copy-done.43), channel_id=1, source_target_pairs={{0,1},{1,0},{2,3},{3,2},{4,5},{5,4},{6,7},{7,6},{8,9},{9,8},{10,11... | collective-permute-start | bytes 1572872 | tf_op jit(solution)/shard_map/ppermute | solution.py:45
  297.9 25.6 %collective-permute-start.6 = (bf16[256,1024]{1,0:T(8,128)(2,1)S(1)}, bf16[256,1024]{1,0:T(8,128)(2,1)S(1)}, u32[]{:S(2)}, u32[]{:S(2)}) collective-permute-start(bf16[256,1024]{1,0:T(8,128)(2,1)S(1)} %copy-done.42), channel_id=1, source_target_pairs={{0,1},{1,0},{2,3},{3,2},{4,5},{5,4},{6,7},{7,6},{8,9},{9,8},{10,11... | collective-permute-start | bytes 1572872 | tf_op jit(solution)/shard_map/ppermute | solution.py:45
  318.0 23.5 %collective-permute-start.9 = (bf16[256,1024]{1,0:T(8,128)(2,1)}, bf16[256,1024]{1,0:T(8,128)(2,1)S(1)}, u32[]{:S(2)}, u32[]{:S(2)}) collective-permute-start(bf16[256,1024]{1,0:T(8,128)(2,1)} %get-tuple-element.173.refs_3_), channel_id=1, source_target_pairs={{0,1},{1,0},{2,3},{3,2},{4,5},{5,4},{6,7},{7,6},{8,9},{9,8},{10,11... | collective-permute-start | bytes 1572872 | tf_op jit(solution)/shard_map/ppermute | solution.py:45
  341.4 49.2 %collective-permute-start.14 = (bf16[2,512,512]{2,1,0:T(8,128)(2,1)}, bf16[2,512,512]{2,1,0:T(8,128)(2,1)S(1)}, u32[]{:S(2)}, u32[]{:S(2)}) collective-permute-start(bf16[2,512,512]{2,1,0:T(8,128)(2,1)} %get-tuple-element.189), channel_id=1, source_target_pairs={{0,2},{2,0},{4,6},{6,4},{1,3},{3,1},{5,7},{7,5},{8,10},{10,8},{12,... | collective-permute-start | bytes 3145736 | tf_op jit(solution)/shard_map/ppermute | solution.py:45
  341.5 0.8 copy-start.47
  359.2 15.6 %copy-start.39 = (bf16[2,512,512]{2,1,0:T(8,128)(2,1)S(1)}, bf16[2,512,512]{2,1,0:T(8,128)(2,1)}, u32[]{:S(2)}) copy-start(bf16[2,512,512]{2,1,0:T(8,128)(2,1)} %get-tuple-element.183) | copy-start | bytes 3145732
  374.2 21.8 %collective-permute-start.13 = (bf16[2,512,512]{2,1,0:T(8,128)(2,1)}, bf16[2,512,512]{2,1,0:T(8,128)(2,1)S(1)}, u32[]{:S(2)}, u32[]{:S(2)}) collective-permute-start(bf16[2,512,512]{2,1,0:T(8,128)(2,1)} %get-tuple-element.187), channel_id=1, source_target_pairs={{0,2},{2,0},{4,6},{6,4},{1,3},{3,1},{5,7},{7,5},{8,10},{10,8},{12,... | collective-permute-start | bytes 3145736 | tf_op jit(solution)/shard_map/ppermute | solution.py:45
  374.8 17.1 %collective-permute-start.11 = (bf16[2,512,512]{2,1,0:T(8,128)(2,1)S(1)}, bf16[2,512,512]{2,1,0:T(8,128)(2,1)S(1)}, u32[]{:S(2)}, u32[]{:S(2)}) collective-permute-start(bf16[2,512,512]{2,1,0:T(8,128)(2,1)S(1)} %copy-done.39), channel_id=1, source_target_pairs={{0,2},{2,0},{4,6},{6,4},{1,3},{3,1},{5,7},{7,5},{8,10},{10,8},{12,... | collective-permute-start | bytes 3145736 | tf_op jit(solution)/shard_map/ppermute | solution.py:45
  374.9 15.8 %copy-start.4 = (bf16[2,512,512]{2,1,0:T(8,128)(2,1)S(1)}, bf16[2,512,512]{2,1,0:T(8,128)(2,1)}, u32[]{:S(2)}) copy-start(bf16[2,512,512]{2,1,0:T(8,128)(2,1)} %get-tuple-element.188) | copy-start | bytes 3145732
  390.2 1.7 copy-start.5
  390.2 42.8 %collective-permute-start.10 = (bf16[2,512,512]{2,1,0:T(8,128)(2,1)}, bf16[2,512,512]{2,1,0:T(8,128)(2,1)S(1)}, u32[]{:S(2)}, u32[]{:S(2)}) collective-permute-start(bf16[2,512,512]{2,1,0:T(8,128)(2,1)} %get-tuple-element.181), channel_id=1, source_target_pairs={{0,2},{2,0},{4,6},{6,4},{1,3},{3,1},{5,7},{7,5},{8,10},{10,8},{12,... | collective-permute-start | bytes 3145736 | tf_op jit(solution)/shard_map/ppermute | solution.py:45
  391.0 2.5 copy-start.7
  391.0 34.5 %collective-permute-start.15 = (bf16[2,512,512]{2,1,0:T(8,128)(2,1)S(1)}, bf16[2,512,512]{2,1,0:T(8,128)(2,1)S(1)}, u32[]{:S(2)}, u32[]{:S(2)}) collective-permute-start(bf16[2,512,512]{2,1,0:T(8,128)(2,1)S(1)} %add_convert_fusion), channel_id=1, source_target_pairs={{0,4},{2,6},{4,0},{6,2},{1,5},{3,7},{5,1},{7,3},{8,12},{10,14},{12... | collective-permute-start | bytes 3145736 | tf_op jit(solution)/shard_map/ppermute | solution.py:45
  391.9 2.6 copy-start.2
  392.2 54.9 %collective-permute-start.12 = (bf16[2,512,512]{2,1,0:T(8,128)(2,1)S(1)}, bf16[2,512,512]{2,1,0:T(8,128)(2,1)S(1)}, u32[]{:S(2)}, u32[]{:S(2)}) collective-permute-start(bf16[2,512,512]{2,1,0:T(8,128)(2,1)S(1)} %add_convert_fusion.1), channel_id=1, source_target_pairs={{0,4},{2,6},{4,0},{6,2},{1,5},{3,7},{5,1},{7,3},{8,12},{10,14},{12... | collective-permute-start | bytes 3145736 | tf_op jit(solution)/shard_map/ppermute | solution.py:45
  396.0 29.4 %copy-start.10 = (bf16[2,512,512]{2,1,0:T(8,128)(2,1)}, bf16[2,512,512]{2,1,0:T(8,128)(2,1)S(1)}, u32[]{:S(2)}) copy-start(bf16[2,512,512]{2,1,0:T(8,128)(2,1)S(1)} %collective-permute-done.13.near_ref) | copy-start | bytes 3145732
  425.5 1.0 copy-start.12
  433.0 14.1 %copy-start.9 = (bf16[2,512,512]{2,1,0:T(8,128)(2,1)}, bf16[2,512,512]{2,1,0:T(8,128)(2,1)S(1)}, u32[]{:S(2)}) copy-start(bf16[2,512,512]{2,1,0:T(8,128)(2,1)S(1)} %collective-permute-done.10.near_ref) | copy-start | bytes 3145732
  447.1 1.0 copy-start.11
  465.5 1.0 copy-start.41
  465.5 3.1 copy-start.29
  465.5 3.1 copy-start.30
  466.5 14.9 %collective-permute-start.17 = (bf16[256,1024]{1,0:T(8,128)(2,1)S(1)}, bf16[256,1024]{1,0:T(8,128)(2,1)S(1)}, u32[]{:S(2)}, u32[]{:S(2)}) collective-permute-start(bf16[256,1024]{1,0:T(8,128)(2,1)S(1)} %copy-done.41), channel_id=1, source_target_pairs={{0,1},{1,0},{2,3},{3,2},{4,5},{5,4},{6,7},{7,6},{8,9},{9,8},{10,11... | collective-permute-start | bytes 1572872 | tf_op jit(solution)/shard_map/ppermute | solution.py:45
  467.6 23.3 %collective-permute-start.16 = (bf16[256,1024]{1,0:T(8,128)(2,1)}, bf16[256,1024]{1,0:T(8,128)(2,1)S(1)}, u32[]{:S(2)}, u32[]{:S(2)}) collective-permute-start(bf16[256,1024]{1,0:T(8,128)(2,1)} %get-tuple-element.196), channel_id=1, source_target_pairs={{0,1},{1,0},{2,3},{3,2},{4,5},{5,4},{6,7},{7,6},{8,9},{9,8},{10,11... | collective-permute-start | bytes 1572872 | tf_op jit(solution)/shard_map/ppermute | solution.py:45
  491.7 3.7 copy-start.31
  491.7 17.9 %copy-start.40 = (bf16[256,1024]{1,0:T(8,128)(2,1)S(1)}, bf16[256,1024]{1,0:T(8,128)(2,1)}, u32[]{:S(2)}) copy-start(bf16[256,1024]{1,0:T(8,128)(2,1)} %get-tuple-element.168) | copy-start | bytes 1572868
  496.3 6.7 %collective-permute-start.18 = (f32[16,4,32]{2,1,0:T(4,128)S(1)}, f32[16,4,32]{2,1,0:T(4,128)S(1)}, u32[]{:S(2)}, u32[]{:S(2)}) collective-permute-start(f32[16,4,32]{2,1,0:T(4,128)S(1)} %slice_select_fusion), channel_id=1, source_target_pairs={{0,16},{8,24},{16,0},{24,8},{1,17},{9,25},{17,1},{25,9},{2,18},{10... | collective-permute-start | bytes 24584 | tf_op jit(solution)/shard_map/ppermute | solution.py:45
  503.0 3.9 collective-permute-start.19
  507.0 3.7 collective-permute-start.20
  508.2 15.1 %collective-permute-start.8 = (bf16[256,1024]{1,0:T(8,128)(2,1)}, bf16[256,1024]{1,0:T(8,128)(2,1)S(1)}, u32[]{:S(2)}, u32[]{:S(2)}) collective-permute-start(bf16[256,1024]{1,0:T(8,128)(2,1)} %get-tuple-element.171), channel_id=1, source_target_pairs={{0,1},{1,0},{2,3},{3,2},{4,5},{5,4},{6,7},{7,6},{8,9},{9,8},{10,11... | collective-permute-start | bytes 1572872 | tf_op jit(solution)/shard_map/ppermute | solution.py:45
  509.6 19.8 %collective-permute-start.7 = (bf16[256,1024]{1,0:T(8,128)(2,1)S(1)}, bf16[256,1024]{1,0:T(8,128)(2,1)S(1)}, u32[]{:S(2)}, u32[]{:S(2)}) collective-permute-start(bf16[256,1024]{1,0:T(8,128)(2,1)S(1)} %copy-done.40), channel_id=1, source_target_pairs={{0,1},{1,0},{2,3},{3,2},{4,5},{5,4},{6,7},{7,6},{8,9},{9,8},{10,11... | collective-permute-start | bytes 1572872 | tf_op jit(solution)/shard_map/ppermute | solution.py:45
  510.7 1.2 collective-permute-start.21
  512.0 21.9 %collective-permute-start.22 = (f32[1,4,32]{2,1,0:T(4,128)S(1)}, f32[1,4,32]{2,1,0:T(4,128)S(1)}, u32[]{:S(2)}, u32[]{:S(2)}) collective-permute-start(f32[1,4,32]{2,1,0:T(4,128)S(1)} %slice_select_fusion.4), channel_id=1, source_target_pairs={{0,1},{1,0},{2,3},{3,2},{4,5},{5,4},{6,7},{7,6},{8,9},{9,8},{10,11... | collective-permute-start | bytes 1544 | tf_op jit(solution)/shard_map/ppermute | solution.py:45
  523.3 6.1 %copy-start.15 = (bf16[256,1024]{1,0:T(8,128)(2,1)}, bf16[256,1024]{1,0:T(8,128)(2,1)S(1)}, u32[]{:S(2)}) copy-start(bf16[256,1024]{1,0:T(8,128)(2,1)S(1)} %collective-permute-done.8.refs_5_) | copy-start | bytes 1572868
  530.1 5.1 copy-start
  (9 other events, 7.1 us)
Sparse Core Ops, SparseCore 0:
  296.5 140.3 reduce-scatter.2
  465.7 73.4 reduce-scatter.4

commit v5 on v4

--- a/solution.py
+++ b/solution.py
@@ -55,58 +55,21 @@
 
 
 def scatter_pair(kept, sent, axis):
+    return later_pair(kept, swap(sent, axis, lax.axis_size(axis) // 2), axis)
+
+
+def later_pair(kept, arrived, axis):
     bit = lax.axis_size(axis) // 2
     while bit > 1:
-        partial = kept + swap(sent, axis, bit).astype(F32)
+        partial = kept + arrived.astype(F32)
         bit //= 2
         rows = partial.shape[0] // 2
-        kept, sent = partial[:rows], partial[rows:].astype(BF16)
-    return kept, swap(sent, axis, 1)
+        kept, arrived = partial[:rows], swap(partial[rows:].astype(BF16), axis, bit)
+    return kept, arrived
 
 
 def hold(values, *others):
     return lax.optimization_barrier((values, others))[0]
-
-
-def scatter_ordered(array, axes):
-    for axis in axes:
-        bit = lax.axis_size(axis) // 2
-        while bit >= 1:
-            rows = array.shape[0] // 2
-            upper = (lax.axis_index(axis) // bit) % 2 == 1
-            kept = jnp.where(upper, array[rows:], array[:rows])
-            sent = jnp.where(upper, array[:rows], array[rows:])
-            array = kept + swap(sent, axis, bit)
-            bit //= 2
-    return array
-
-
-def gather_ordered(array, axes):
-    for axis in reversed(axes):
-        bit = 1
-        while bit < lax.axis_size(axis):
-            arrived = swap(array, axis, bit)
-            upper = (lax.axis_index(axis) // bit) % 2 == 1
-            array = jnp.where(
-                upper,
-                jnp.concatenate([arrived, array], axis=0),
-                jnp.concatenate([array, arrived], axis=0),
-            )
-            bit *= 2
-    return array
-
-
-def scatter_ordered(array, axes):
-    for axis in axes:
-        bit = lax.axis_size(axis) // 2
-        while bit >= 1:
-            rows = array.shape[0] // 2
-            upper = (lax.axis_index(axis) // bit) % 2 == 1
-            kept = jnp.where(upper, array[rows:], array[:rows])
-            sent = jnp.where(upper, array[:rows], array[rows:])
-            array = kept + swap(sent, axis, bit)
-            bit //= 2
-    return array
 
 
 def run(kernel, name, out_shape, flops, args, collective_id=None, **options):
@@ -250,40 +213,34 @@
 
 
 class Route:
-    PARTS = ((0, 0), (0, 1), (3, 0), (1, 0), (3, 1), (1, 1), (2, 0), (2, 1))
-
-    def __init__(self, whole, rows, send_sem, recv_sem, own=None):
-        self.whole, self.rows = whole, rows
+    PARTS = ((0, 0), (3, 0), (1, 0), (2, 0), (0, 1), (3, 1), (1, 1), (2, 1))
+
+    def __init__(self, whole, rows, send_sem, recv_sem, own):
+        self.whole, self.rows, self.own = whole, rows, own
         self.send_sem, self.recv_sem = send_sem, recv_sem
         self.seq, self.depth = lax.axis_index("seq"), lax.axis_index("dp")
         self.peers = half_chip_peers()
-        self.own = self.part((0, 0)) if own is None else own
-
-    def part(self, place, half=None):
+
+    def part(self, place):
         turn, other = place
         seq = flipped(self.seq, 2) if other else self.seq
         at = (((self.depth + turn) % lax.axis_size("dp")) * lax.axis_size("seq") + seq) * self.rows
-        count = self.rows if half is None else self.rows // 2
-        if half == 1:
-            at = at + count
-        return self.whole.at[pl.ds(pl.multiple_of(at, count), count), :]
+        return self.whole.at[pl.ds(pl.multiple_of(at, self.rows), self.rows), :]
 
     def message(self, number):
-        if number >= 9:
-            place, peer, half = self.PARTS[number - 9], "core", None
+        if number >= 7:
+            place, peer = self.PARTS[number - 7], "core"
         else:
-            place, peer, half = (
-                ((0, 0), "far", None),
-                ((0, 0), "up", None),
-                ((0, 0), "down", None),
-                ((0, 1), "up", None),
-                ((0, 1), "down", None),
-                ((3, 0), "up", 0),
-                ((1, 0), "down", 1),
-                ((3, 1), "up", 0),
-                ((1, 1), "down", 1),
+            place, peer = (
+                ((0, 0), "up"),
+                ((0, 0), "down"),
+                ((3, 0), "up"),
+                ((0, 0), "far"),
+                ((3, 0), "far"),
+                ((1, 0), "far"),
+                ((2, 0), "far"),
             )[number]
-        target = self.part(place, half)
+        target = self.part(place)
         return send(
             self.own if place == (0, 0) else target,
             target,
@@ -305,22 +262,19 @@
             self.message(number).wait_send()
 
 
-MESSAGES = 17
-
-
-def gather_kernel(trades, att_ref, ffn_ref, tile_ref, tokens_ref, *refs):
-    att_all, ffn_all, norms_ref, tokens_all = refs[:4]
-    tiles, pair_of_tiles = refs[4:6]
-    att_send, att_recv, ffn_send, ffn_recv, tile_send, tile_recv = refs[6:12]
-    own_sem, tokens_send, tokens_recv, pair_send, pair_recv = refs[12:]
+MESSAGES = 15
+
+
+def gather_kernel(trades, att_ref, tile_ref, tokens_ref, *refs):
+    att_all, norms_ref, tokens_all = refs[:3]
+    tiles, pair_of_tiles = refs[3:5]
+    att_send, att_recv, tile_send, tile_recv = refs[5:9]
+    own_sem, tokens_send, tokens_recv, pair_send, pair_recv = refs[9:]
     tensor = lax.axis_index("tensor")
     others = [{"tensor": flipped(tensor, other + 1)} for other in range(trades)]
-    rows = att_ref.shape[0]
-    att = Route(att_all, rows, att_send, att_recv, att_ref)
-    ffn = Route(ffn_all, rows, ffn_send, ffn_recv, ffn_ref)
+    att = Route(att_all, att_ref.shape[0], att_send, att_recv, att_ref)
     tile_rows = tile_ref.shape[0]
-    group = pair_of_tiles.shape[0]
-    small = Route(tiles, group, tile_send, tile_recv, pair_of_tiles)
+    small = Route(tiles, pair_of_tiles.shape[0], tile_send, tile_recv, pair_of_tiles)
 
     def tokens_trade(other):
         return send(
@@ -344,43 +298,45 @@
 
     own_copies = [
         pltpu.make_async_copy(att_ref, att.part((0, 0)), own_sem.at[0]),
-        pltpu.make_async_copy(ffn_ref, ffn.part((0, 0)), own_sem.at[1]),
-        pltpu.make_async_copy(tile_ref, pair_of_tiles.at[own_rows, :], own_sem.at[2]),
-        pltpu.make_async_copy(pair_of_tiles, small.part((0, 0)), own_sem.at[3]),
+        pltpu.make_async_copy(tile_ref, pair_of_tiles.at[own_rows, :], own_sem.at[1]),
+        pltpu.make_async_copy(pair_of_tiles, small.part((0, 0)), own_sem.at[2]),
     ]
 
     greet(list(att.peers.values()) + others)
     for other in range(trades):
         pair_trade(other).start()
-    att.start(0, 1, 2, 9)
+    own_copies[1].start()
+    own_copies[1].wait()
+    for other in range(trades):
+        pair_trade(other).wait_recv()
+    for route in (small, att):
+        route.start(0, 1, 3, 7)
+    own_copies[0].start()
     own_copies[2].start()
-    own_copies[0].start()
-    own_copies[1].start()
     for other in range(trades):
         tokens_trade(other).start()
+    for route in (small, att):
+        route.arrived(0)
+        route.start(2, 4, 8)
+    for route in (small, att):
+        route.arrived(3)
+        route.start(11)
+    for route in (small, att):
+        route.arrived(1)
+        route.start(5, 9)
+    for route in (small, att):
+        route.arrived(2)
+        route.start(6, 10)
+    for route in (small, att):
+        route.arrived(4)
+        route.start(12)
+        route.arrived(5)
+        route.start(13)
+        route.arrived(6)
+        route.start(14)
+    for route in (small, att):
+        route.arrived(*range(7, MESSAGES))
     own_copies[2].wait()
-    for other in range(trades):
-        pair_trade(other).wait_recv()
-    own_copies[3].start()
-    small.start(0, 1, 2, 9)
-    ffn.start(0)
-    att.arrived(0)
-    att.start(3, 4, 10)
-    small.arrived(0)
-    small.start(3, 4, 10)
-    for route in (att, small):
-        route.arrived(1, 2)
-        route.start(5, 6, 11, 12)
-    for route in (att, small):
-        route.arrived(3, 4)
-        route.start(7, 8, 13, 14)
-    for route in (small, att):
-        route.arrived(5, 6)
-        route.start(15)
-        route.arrived(7, 8)
-        route.start(16)
-        route.arrived(*range(9, 17))
-    own_copies[3].wait()
     shard = norms_ref.shape[1] // (tiles.shape[0] // tile_rows)
     total = None
     for device in range(tiles.shape[0] // tile_rows):
@@ -393,17 +349,14 @@
     norms_ref[4:5, : total.shape[1]] = total
     for route in (att, small):
         route.sent(*range(MESSAGES))
-    ffn.arrived(0)
-    ffn.sent(0)
     own_copies[0].wait()
-    own_copies[1].wait()
     for other in range(trades):
         pair_trade(other).wait_send()
         tokens_trade(other).wait_recv()
         tokens_trade(other).wait_send()
 
 
-def gather(att, ffn, tile, tokens, trades):
+def gather(att, tile, tokens, trades):
     count = lax.axis_size("dp") * lax.axis_size("seq")
     rows = att.shape[0]
     group = tile.shape[0] * (trades + 1)
@@ -415,28 +368,25 @@
         "gather",
         [
             shaped((count * rows, att.shape[1]), BF16),
-            shaped((count * rows, ffn.shape[1]), BF16),
             shaped((tile.shape[0], count * rows), F32),
             shaped((trades,) + tokens.shape, BF16),
         ],
         0,
-        [att, ffn, tile, tokens],
+        [att, tile, tokens],
         collective_id=1,
-        in_specs=[vmem, vmem, vmem, anywhere],
-        out_specs=[anywhere, anywhere, vmem, anywhere],
+        in_specs=[vmem, vmem, anywhere],
+        out_specs=[anywhere, vmem, anywhere],
         scratch_shapes=[pltpu.VMEM((count * group, 128), F32), pltpu.VMEM((group, 128), F32)]
-        + [dma((MESSAGES,))] * 6
-        + [dma((4,)), dma((trades,)), dma((trades,)), dma((trades,)), dma((trades,))],
+        + [dma((MESSAGES,))] * 4
+        + [dma((3,)), dma((trades,)), dma((trades,)), dma((trades,)), dma((trades,))],
     )
 
 
 def attend_kernel(windows, pairs, trades, exp_scale, *refs):
     q_ref, w_ref, kv_ref, cot_ref = refs[:4]
-    low_ref, wide_ref, log_ref, kept_ref, sent_ref, slots_ref, cots_ref, ffn_ref = refs[5:13]
-    slots, acc_all, top_all, total_all, mixed_rows = refs[13:18]
-    own_sem, send_sem, recv_sem, save_sem, cot_send, cot_recv, ffn_send, ffn_recv = refs[18:]
-    shards = lax.axis_size("dp") * lax.axis_size("seq")
-    ffn = Route(ffn_ref, ffn_ref.shape[0] // shards, ffn_send, ffn_recv)
+    low_ref, wide_ref, log_ref, kept_ref, sent_ref, slots_ref, cots_ref = refs[4:11]
+    slots, acc_all, top_all, total_all, mixed_rows = refs[11:16]
+    own_sem, send_sem, recv_sem, save_sem, cot_send, cot_recv = refs[16:]
     step = pl.program_id(0)
     near_steps = windows * pairs
     steps = 2 * near_steps
@@ -475,8 +425,7 @@
 
     @pl.when(step == 0)
     def _():
-        greet(list(ffn.peers.values()) + cot_peers)
-        ffn.start(1, 2, 3, 4, 9, 10)
+        greet([core_peer, far_peer] + cot_peers)
 
         @pl.loop(0, near_steps)
         def _(number):
@@ -486,16 +435,6 @@
 
         for other in range(trades):
             cot_trade(other).start()
-
-    @pl.when(step == near_steps - 1)
-    def _():
-        ffn.arrived(1, 2)
-        ffn.start(5, 6, 11, 12)
-
-    @pl.when(step == near_steps + near_steps // 2)
-    def _():
-        ffn.arrived(3, 4)
-        ffn.start(7, 8, 13, 14)
 
     relayed = step - (near_steps - 1)
 
@@ -580,11 +519,6 @@
 
     @pl.when(step == steps - 1)
     def _():
-        ffn.arrived(5, 6)
-        ffn.start(15)
-        ffn.arrived(7, 8)
-        ffn.start(16)
-
         @pl.loop(0, near_steps)
         def _(number):
             for slot in range(1, 4):
@@ -595,11 +529,9 @@
         for other in range(trades):
             cot_trade(other).wait_send()
             cot_trade(other).wait_recv()
-        ffn.arrived(*range(9, MESSAGES))
-        ffn.sent(*range(1, MESSAGES))
-
-
-def attend(queries, own_kv, w_att, cotangent, w_ffn, trades):
+
+
+def attend(queries, own_kv, w_att, cotangent, trades):
     windows, rows, cols = queries.shape
     width = w_att.shape[0]
     pairs = cols // PAIR
@@ -625,17 +557,14 @@
             shaped((windows, rows // 2, width), BF16),
             shaped((near, 4, 2, rows, PAIR), BF16),
             shaped((trades,) + cotangent.shape, BF16),
-            shaped(w_ffn.shape, BF16),
         ],
         64 * windows * rows * rows * cols,
-        [queries, w_att, own_kv, cotangent, w_ffn],
+        [queries, w_att, own_kv, cotangent],
         collective_id=0,
-        input_output_aliases={4: 7},
         grid=(2 * near,),
         in_specs=[
             pl.BlockSpec((1, rows, PAIR), lambda i: ((i // pairs) % windows, 0, i % pairs)),
             pl.BlockSpec((width, PAIR), lambda i: (0, out_at + far(i) % pairs)),
-            anywhere,
             anywhere,
             anywhere,
         ],
@@ -645,7 +574,6 @@
             pl.BlockSpec((1, PAIR, rows), lambda i: (far(i) // pairs, far(i) % pairs, 0)),
             half,
             half,
-            anywhere,
             anywhere,
             anywhere,
         ],
@@ -661,124 +589,220 @@
             dma((near, 4)),
             dma((trades,)),
             dma((trades,)),
-            dma((MESSAGES,)),
-            dma((MESSAGES,)),
         ],
     )
 
 
-def attend_back_kernel(slots, first, grad_blocks, exp_scale, score_scale, *refs):
-    refs = list(refs)
-    q_ref, wide_ref, log_ref = [refs.pop(0) for _ in range(3)]
-    if first:
-        grad_refs = [refs.pop(0) for _ in range(grad_blocks)]
-        w_ref = refs.pop(0)
-    else:
-        do_ref = refs.pop(0)
-    slots_ref = refs.pop(0)
-    if not first:
-        dq_in = refs.pop(0)
-        cos_ref, sin_ref = refs.pop(0), refs.pop(0)
-    dq_ref = refs.pop(0)
-    dkv_refs = [refs.pop(0) for _ in range(slots)]
-    query = q_ref[0]
-    if first:
-        do_ref, rows_ref = refs
-
-        @pl.when(pl.program_id(0) == 0)
+def attend_back_kernel(windows, pairs, blocks, exp_scale, score_scale, *refs):
+    q_ref, wide_ref, log_ref, slots_ref, w_ref, cos_ref, sin_ref = refs[:7]
+    grad_refs = refs[7 : 7 + windows * blocks]
+    refs = refs[7 + windows * blocks :]
+    sent_refs, refs = refs[:windows], refs[windows:]
+    gq_ref, gk_ref, gv_ref, rows_ref = refs[:4]
+    arrived_refs, refs = refs[4 : 4 + windows], refs[4 + windows :]
+    dq_all, do_all, far_kept, far_sent, far_core, far_x, near_kept, near_sent, near_core = refs[:9]
+    send_sem, recv_sem, result_send, result_recv = refs[9:]
+    step = pl.program_id(0)
+    count = windows * pairs
+    seq, tensor = lax.axis_index("seq"), lax.axis_index("tensor")
+    core_peer = {"seq": flipped(seq, 1)}
+    far_peer = {"seq": flipped(seq, 2)}
+    result_peer = {"tensor": flipped(tensor, lax.axis_size("tensor") // 2)}
+
+    def trade(kind, number):
+        source, target, peer = (
+            (far_sent, far_core, core_peer),
+            (far_kept, far_x, far_peer),
+            (near_sent, near_core, core_peer),
+        )[kind]
+        return send(
+            source.at[number],
+            target.at[number],
+            send_sem.at[kind, number],
+            recv_sem.at[kind, number],
+            peer,
+        )
+
+    def result_trade(w):
+        return send(
+            sent_refs[w], arrived_refs[w], result_send.at[w], result_recv.at[w], result_peer
+        )
+
+    @pl.when(step == 0)
+    def _():
+        greet([core_peer, far_peer, result_peer])
+        for w in range(windows):
+            result_trade(w).start()
+
+    def at_step(first, body):
+        number = step - first
+
+        @pl.when(jnp.logical_and(number >= 0, number < count))
         def _():
+            body(number)
+
+    def send_far(number):
+        trade(0, number).start()
+
+    def add_far(number):
+        trade(0, number).wait_recv()
+        far_kept[number] = (
+            far_kept[number].astype(F32) + far_core[number].astype(F32)
+        ).astype(BF16)
+
+    def send_x(number):
+        trade(1, number).start()
+
+    def send_near(number):
+        trade(2, number).start()
+
+    def finish(number):
+        trade(2, number).wait_recv()
+        trade(1, number).wait_recv()
+        total = (
+            near_kept[number].astype(F32)
+            + near_core[number].astype(F32)
+            + far_x[number].astype(F32)
+        )
+        key = total[0]
+        gk_ref[0] = (key * cos_ref[...] - swap_halves(key) * sin_ref[...]).astype(BF16)
+        gv_ref[0] = total[1].astype(BF16)
+
+    at_step(1, send_far)
+    at_step(3, send_x)
+    at_step(count + 1, send_near)
+    at_step(2, add_far)
+    at_step(count + 2, finish)
+
+    for w in range(windows):
+
+        @pl.when(step == w * pairs)
+        def _(w=w):
             at_row = 0
-            for grad_ref in grad_refs:
-                rows_ref[at_row : at_row + grad_ref.shape[0], :] = grad_ref[...]
+            for grad_ref in grad_refs[w * blocks : (w + 1) * blocks]:
+                rows_ref[0, at_row : at_row + grad_ref.shape[0], :] = grad_ref[...]
                 at_row += grad_ref.shape[0]
 
-        grad_out = dot_nn(rows_ref[...], w_ref[...]).astype(BF16)
-        do_ref[...] = grad_out
-    else:
-        grad_out = do_ref[...]
-    is_first = first_head(query.shape)
-    overlap = (grad_out.astype(F32) * wide_ref[0]).T
-    logs = log_ref[0]
-    zero = jnp.zeros_like(query)
-    own_q, own_do, row_log, row_sum = [], [], [], []
-    for head in range(2):
-        mine = is_first if head == 0 else jnp.logical_not(is_first)
-        own_q.append(jnp.where(mine, query, zero))
-        own_do.append(jnp.where(mine, grad_out, zero))
-        at = head * HEAD_DIM
-        row_log.append(logs[at : at + 1, :])
-        row_sum.append(jnp.sum(overlap[at : at + HEAD_DIM, :], axis=0, keepdims=True))
-    dq_parts = [None, None]
-    for slot, dkv_ref in enumerate(dkv_refs):
-        key, value = slots_ref[0, slot, 0], slots_ref[0, slot, 1]
-        key_turned = key.T
-        grad_key, grad_value = None, None
+    def gradients(number, grad_out, kept, sent):
+        query = q_ref[0]
+        is_first = first_head(query.shape)
+        overlap = (grad_out.astype(F32) * wide_ref[0]).T
+        logs = log_ref[0]
+        zero = jnp.zeros_like(query)
+        own_q, own_do, row_log, row_sum = [], [], [], []
         for head in range(2):
-            scores = dot_nt(key, own_q[head])
-            probs = jnp.exp2(scores * exp_scale - row_log[head])
-            grad_probs = dot_nt(value, own_do[head])
-            grad_scores = (probs * (grad_probs - row_sum[head])).astype(BF16)
-            term_v = dot_nn(probs.astype(BF16), own_do[head])
-            term_k = dot_nn(grad_scores, own_q[head])
+            mine = is_first if head == 0 else jnp.logical_not(is_first)
+            own_q.append(jnp.where(mine, query, zero))
+            own_do.append(jnp.where(mine, grad_out, zero))
             at = head * HEAD_DIM
-            term_q = dot_nn(key_turned[at : at + HEAD_DIM, :], grad_scores)
-            grad_value = term_v if grad_value is None else grad_value + term_v
-            grad_key = term_k if grad_key is None else grad_key + term_k
-            dq_parts[head] = term_q if dq_parts[head] is None else dq_parts[head] + term_q
-        dkv_ref[0] = (grad_key * score_scale).astype(BF16)
-        dkv_ref[1] = grad_value.astype(BF16)
-    grad_query = jnp.concatenate(dq_parts, axis=0).T * score_scale
-    if not first:
-        grad_query = grad_query + dq_in[...]
-        grad_query = grad_query * cos_ref[...] - swap_halves(grad_query) * sin_ref[...]
-    dq_ref[...] = grad_query.astype(dq_ref.dtype)
-
-
-def attend_back(window, queries, wide, logs, slots_all, grads, w_att, tables):
-    rows, cols = queries.shape[1:]
-    keys = rows
-    slots = slots_all.shape[1] // 2
+            row_log.append(logs[at : at + 1, :])
+            row_sum.append(jnp.sum(overlap[at : at + HEAD_DIM, :], axis=0, keepdims=True))
+        dq_parts = [None, None]
+        for slot, target in enumerate((kept, sent)):
+            key, value = slots_ref[0, slot, 0], slots_ref[0, slot, 1]
+            key_turned = key.T
+            grad_key, grad_value = None, None
+            for head in range(2):
+                scores = dot_nt(key, own_q[head])
+                probs = jnp.exp2(scores * exp_scale - row_log[head])
+                grad_probs = dot_nt(value, own_do[head])
+                grad_scores = (probs * (grad_probs - row_sum[head])).astype(BF16)
+                term_v = dot_nn(probs.astype(BF16), own_do[head])
+                term_k = dot_nn(grad_scores, own_q[head])
+                at = head * HEAD_DIM
+                term_q = dot_nn(key_turned[at : at + HEAD_DIM, :], grad_scores)
+                grad_value = term_v if grad_value is None else grad_value + term_v
+                grad_key = term_k if grad_key is None else grad_key + term_k
+                dq_parts[head] = term_q if dq_parts[head] is None else dq_parts[head] + term_q
+            target[number, 0] = (grad_key * score_scale).astype(BF16)
+            target[number, 1] = grad_value.astype(BF16)
+        return jnp.concatenate(dq_parts, axis=0).T * score_scale
+
+    @pl.when(step < count)
+    def _():
+        grad_out = dot_nn(rows_ref[0], w_ref[...]).astype(BF16)
+        do_all[step] = grad_out
+        dq_all[step] = gradients(step, grad_out, far_kept, far_sent)
+
+    @pl.when(jnp.logical_and(step >= count, step < 2 * count))
+    def _():
+        number = step - count
+        grad_query = dq_all[number] + gradients(number, do_all[number], near_kept, near_sent)
+        gq_ref[0] = (grad_query * cos_ref[...] - swap_halves(grad_query) * sin_ref[...]).astype(
+            BF16
+        )
+
+    @pl.when(step == pl.num_programs(0) - 1)
+    def _():
+        @pl.loop(0, count)
+        def _(number):
+            for kind in range(3):
+                trade(kind, number).wait_send()
+
+        for w in range(windows):
+            result_trade(w).wait_send()
+            result_trade(w).wait_recv()
+
+
+def attend_back(queries, wide, logs, slots_all, grad_blocks, w_att, tables, sent):
+    windows, rows, cols = queries.shape
+    width = w_att.shape[0]
     pairs = cols // PAIR
-    first = tables is None
+    count = windows * pairs
+    out_at = 3 * pairs
     score_scale = 1.0 / math.sqrt(HEAD_DIM)
-    row_spec = pl.BlockSpec((rows, PAIR), lambda i: (0, i))
-    block = pl.BlockSpec((2, keys, PAIR), lambda i: (0, 0, i))
-    stacked = pl.BlockSpec((1, rows, PAIR), lambda i: (window, 0, i))
-    in_specs = [stacked] * 2 + [pl.BlockSpec((1, PAIR, rows), lambda i: (window, i, 0))]
-    args = [queries, wide, logs]
-    out_shape = [shaped((rows, cols), F32 if first else BF16)]
-    out_shape += [shaped((2, keys, cols), BF16)] * slots
-    out_specs = [row_spec] + [block] * slots
-    if first:
-        width = w_att.shape[0]
-        out_at = 3 * cols // PAIR
-        args += [*grads, w_att]
-        in_specs += [pl.BlockSpec(grad.shape, lambda i: (0, 0)) for grad in grads]
-        in_specs += [pl.BlockSpec((width, PAIR), lambda i: (0, out_at + i))]
-        out_shape += [shaped((rows, cols), BF16), shaped((rows, width), BF16)]
-        out_specs += [row_spec, pl.BlockSpec((rows, width), lambda i: (0, 0))]
-    else:
-        args.append(grads[1])
-        in_specs.append(row_spec)
-    args.append(slots_all)
-    half = 1 if first else 0
-    in_specs.append(
-        pl.BlockSpec((1, slots, 2, keys, PAIR), lambda i: (window * pairs + i, half, 0, 0, 0))
-    )
-    if not first:
-        args += [grads[0], *tables]
-        in_specs += [row_spec] + [pl.BlockSpec((rows, PAIR), lambda i: (0, 0))] * 2
+    blocks = len(grad_blocks[0])
+    grads = [block for one in grad_blocks for block in one]
+
+    def spot(lag, last=None):
+        def index(i):
+            number = jnp.clip(i - lag, 0, count - 1)
+            return (number // pairs, 0, number % pairs)
+
+        return pl.BlockSpec((1, rows, PAIR), index)
+
+    def both(i):
+        return jnp.minimum(i, 2 * count - 1) % count
+
+    dma = pltpu.SemaphoreType.DMA
+    piece = pltpu.VMEM((count, 2, rows, PAIR), BF16)
+    anywhere = pl.BlockSpec(memory_space=pl.ANY)
     return run(
         functools.partial(
-            attend_back_kernel, slots, first, len(grads), score_scale * LOG2E, score_scale
+            attend_back_kernel, windows, pairs, blocks, score_scale * LOG2E, score_scale
         ),
-        "attend_back_far" if first else "attend_back_near",
-        out_shape,
-        40 * rows * keys * slots * cols,
-        args,
-        grid=(cols // PAIR,),
-        in_specs=in_specs,
-        out_specs=out_specs,
+        "attend_back",
+        [shaped((windows, rows, cols), BF16)] * 3
+        + [shaped((windows, rows, width), BF16)]
+        + [shaped(one.shape, BF16) for one in sent],
+        160 * windows * rows * rows * cols,
+        [queries, wide, logs, slots_all, w_att, *tables, *grads, *sent],
+        collective_id=2,
+        grid=(2 * count + 2,),
+        in_specs=[
+            pl.BlockSpec((1, rows, PAIR), lambda i: (both(i) // pairs, 0, both(i) % pairs)),
+            pl.BlockSpec((1, rows, PAIR), lambda i: (both(i) // pairs, 0, both(i) % pairs)),
+            pl.BlockSpec((1, PAIR, rows), lambda i: (both(i) // pairs, both(i) % pairs, 0)),
+            pl.BlockSpec(
+                (1, 2, 2, rows, PAIR),
+                lambda i: (both(i), jnp.where(i < count, 1, 0), 0, 0, 0),
+            ),
+            pl.BlockSpec((width, PAIR), lambda i: (0, out_at + jnp.minimum(i, count - 1) % pairs)),
+            pl.BlockSpec((rows, PAIR), lambda i: (0, 0)),
+            pl.BlockSpec((rows, PAIR), lambda i: (0, 0)),
+        ]
+        + [pl.BlockSpec(block.shape, lambda i: (0, 0)) for block in grads]
+        + [anywhere] * windows,
+        out_specs=[
+            spot(count),
+            spot(count + 2),
+            spot(count + 2),
+            pl.BlockSpec((1, rows, width), lambda i: (jnp.minimum(i // pairs, windows - 1), 0, 0)),
+        ]
+        + [anywhere] * windows,
+        scratch_shapes=[pltpu.VMEM((count, rows, PAIR), F32), pltpu.VMEM((count, rows, PAIR), BF16)]
+        + [piece] * 7
+        + [dma((3, count)), dma((3, count)), dma((windows,)), dma((windows,))],
     )
 
 
@@ -800,25 +824,12 @@
     )
 
 
-def feed_kernel(blocks, factor_ref, gate_w_ref, up_w_ref, down_w_ref, *refs):
-    x_refs, cot_refs = refs[:blocks], refs[blocks : 2 * blocks]
-    x_all, gy_all, hidden_ref, grad_gate_ref, grad_up_ref = refs[2 * blocks : 2 * blocks + 5]
-    kept_ref, sent_ref, grad_kept_ref, grad_sent_ref, total, grad_total = refs[2 * blocks + 5 :]
-    step = pl.program_id(0)
-
-    @pl.when(step == 0)
-    def _():
-        at_row = 0
-        for x_ref, cot_ref in zip(x_refs, cot_refs):
-            rows = slice(at_row, at_row + x_ref.shape[0])
-            at_row += x_ref.shape[0]
-            x_all[rows, :] = x_ref[...]
-            gy_all[rows, :] = (cot_ref[...].astype(F32) * factor_ref[0, 0]).astype(BF16)
-
-    x_rows = x_all[...]
+def feed_step(x_rows, gy_rows, w_refs, out_refs):
+    gate_w_ref, up_w_ref, down_w_ref = w_refs
+    hidden_ref, grad_gate_ref, grad_up_ref = out_refs
     gate = dot_nn(x_rows, gate_w_ref[...])
     up = dot_nn(x_rows, up_w_ref[...])
-    grad_hidden = dot_nn(gy_all[...], down_w_ref[...])
+    grad_hidden = dot_nn(gy_rows, down_w_ref[...])
     sig = jax.nn.sigmoid(gate)
     swish = gate * sig
     hidden = (swish * up).astype(BF16)
@@ -828,12 +839,51 @@
     grad_gate_ref[...] = grad_gate
     grad_up_ref[...] = grad_up
     grad_term = dot_nt(grad_gate, gate_w_ref[...]) + dot_nt(grad_up, up_w_ref[...])
-    term = dot_nt(hidden, down_w_ref[...])
+    return dot_nt(hidden, down_w_ref[...]), grad_term
+
+
+def feed_first_kernel(blocks, factor_ref, *refs):
+    w_refs, refs = refs[:3], refs[3:]
+    x_refs, cot_refs = refs[:blocks], refs[blocks : 2 * blocks]
+    x_all, gy_all = refs[2 * blocks : 2 * blocks + 2]
+    total, grad_total = refs[2 * blocks + 5 :]
+    step = pl.program_id(0)
+
+    @pl.when(step == 0)
+    def _():
+        at_row = 0
+        for x_ref, cot_ref in zip(x_refs, cot_refs):
+            rows = slice(at_row, at_row + x_ref.shape[0])
+            at_row += x_ref.shape[0]
+            x_all[rows, :] = x_ref[...]
+            gy_all[rows, :] = (cot_ref[...].astype(F32) * factor_ref[0, 0]).astype(BF16)
+
+    term, grad_term = feed_step(
+        x_all[...], gy_all[...], w_refs, refs[2 * blocks + 2 : 2 * blocks + 5]
+    )
 
     @pl.when(step == 0)
     def _():
         total[...] = term
         grad_total[...] = grad_term
+
+    @pl.when(step > 0)
+    def _():
+        total[...] += term
+        grad_total[...] += grad_term
+
+
+def feed_last_kernel(*refs):
+    w_refs = refs[:3]
+    x_ref, gy_ref, total_in, grad_in = refs[3:7]
+    kept_ref, sent_ref, grad_kept_ref, grad_sent_ref, total, grad_total = refs[13:]
+    step = pl.program_id(0)
+    term, grad_term = feed_step(x_ref[...], gy_ref[...], w_refs, refs[10:13])
+
+    @pl.when(step == 0)
+    def _():
+        total[...] = total_in[...] + term
+        grad_total[...] = grad_in[...] + grad_term
 
     @pl.when(step > 0)
     def _():
@@ -849,32 +899,57 @@
         grad_sent_ref[...] = grad_total[half:].astype(BF16)
 
 
-def feed(x_blocks, cot_blocks, factor, weights):
+def feed_specs(weights):
+    width, part_cols = weights.shape[0], weights.shape[1] // 3
+    step = min(512, part_cols)
+    steps = part_cols // step
+    specs = [
+        pl.BlockSpec((width, step), functools.partial(lambda at, i: (0, at + i), k * steps))
+        for k in range(3)
+    ]
+    return step, steps, specs
+
+
+def feed_first(x_blocks, cot_blocks, factor, weights):
     width = x_blocks[0].shape[1]
     rows = sum(block.shape[0] for block in x_blocks)
-    hidden_cols = weights.shape[1] // 3
-    step = min(512, hidden_cols)
-    steps = hidden_cols // step
+    step, steps, w_specs = feed_specs(weights)
+    hidden_cols = 2 * step * steps
     full = pl.BlockSpec((rows, width), lambda i: (0, 0))
-    half = pl.BlockSpec((rows // 2, width), lambda i: (0, 0))
-    block = pl.BlockSpec((rows, step), lambda i: (0, i))
     return run(
-        functools.partial(feed_kernel, len(x_blocks)),
-        "feed",
+        functools.partial(feed_first_kernel, len(x_blocks)),
+        "feed_first",
         [shaped((rows, width), BF16)] * 2
         + [shaped((rows, hidden_cols), BF16)] * 3
-        + [shaped((rows // 2, width), F32), shaped((rows // 2, width), BF16)] * 2,
-        12 * rows * width * hidden_cols,
+        + [shaped((rows, width), F32)] * 2,
+        6 * rows * width * hidden_cols,
         [factor, weights, weights, weights, *x_blocks, *cot_blocks],
         grid=(steps,),
         in_specs=[SCALAR]
-        + [
-            pl.BlockSpec((width, step), functools.partial(lambda at, i: (0, at + i), k * steps))
-            for k in range(3)
-        ]
+        + w_specs
         + [pl.BlockSpec(array.shape, lambda i: (0, 0)) for array in (*x_blocks, *cot_blocks)],
-        out_specs=[full] * 2 + [block] * 3 + [half] * 4,
+        out_specs=[full] * 2 + [pl.BlockSpec((rows, step), lambda i: (0, i))] * 3 + [full] * 2,
+    )
+
+
+def feed_last(x_rows, gy_rows, totals, earlier, weights):
+    rows, width = x_rows.shape
+    step, steps, w_specs = feed_specs(weights)
+    hidden_cols = 2 * step * steps
+    full = pl.BlockSpec((rows, width), lambda i: (0, 0))
+    half = pl.BlockSpec((rows // 2, width), lambda i: (0, 0))
+    return run(
+        feed_last_kernel,
+        "feed_last",
+        [shaped((rows, hidden_cols), BF16)] * 3
+        + [shaped((rows // 2, width), F32), shaped((rows // 2, width), BF16)] * 2,
+        6 * rows * width * hidden_cols,
+        [weights, weights, weights, x_rows, gy_rows, *totals, *earlier],
+        grid=(steps,),
+        in_specs=w_specs + [full] * 4 + [pl.BlockSpec(memory_space=pl.ANY)] * 3,
+        out_specs=[pl.BlockSpec((rows, step), lambda i: (0, steps + i))] * 3 + [half] * 4,
         scratch_shapes=[pltpu.VMEM((rows, width), F32)] * 2,
+        input_output_aliases={7: 0, 8: 1, 9: 2},
     )
 
 
@@ -893,19 +968,23 @@
             out_ref[...] = total.astype(BF16)
 
 
-def weight_grads(groups, step, name):
+def weight_grads(groups, step, name, first=0, parts=1):
     windows = len(groups[0][0])
     rows, width = groups[0][0][0].shape
     args, in_specs, starts = [], [], []
     at = 0
     for lefts, rights in groups:
-        count = rights[0].shape[1] // step
+        count = rights[0].shape[1] // (step * parts)
         args += [*lefts, *rights]
         in_specs += [pl.BlockSpec((rows, width), lambda i: (0, 0))] * windows
         in_specs += [
             pl.BlockSpec(
                 (rows, step),
-                functools.partial(lambda at, count, i: (0, jnp.clip(i - at, 0, count - 1)), at, count),
+                functools.partial(
+                    lambda at, count, i: (0, first * count + jnp.clip(i - at, 0, count - 1)),
+                    at,
+                    count,
+                ),
             )
         ] * windows
         starts.append((at, at + count))
@@ -956,43 +1035,35 @@
     )
 
 
-def turn_back_kernel(
-    dq_ref, own_ref, near_ref, far_ref, cos_ref, sin_ref, w_ref, out_ref, kept_ref, sent_ref
-):
-    cols = dq_ref.shape[1]
-    cosine, sine = cos_ref[...], sin_ref[...]
-    out_ref[:, :cols] = dq_ref[...]
-    for at in range(0, cols, PAIR):
-        part = slice(at, at + PAIR)
-        key = (
-            own_ref[0, :, part].astype(F32)
-            + near_ref[0, :, part].astype(F32)
-            + far_ref[0, :, part].astype(F32)
-        )
-        out_ref[:, cols + at : cols + at + PAIR] = (
-            key * cosine - swap_halves(key) * sine
-        ).astype(BF16)
-    out_ref[:, 2 * cols :] = (
-        own_ref[1].astype(F32) + near_ref[1].astype(F32) + far_ref[1].astype(F32)
-    ).astype(BF16)
+def turn_back_kernel(gq_ref, gk_ref, gv_ref, w_ref, kept_ref, sent_ref):
+    cols = gq_ref.shape[2]
     half = kept_ref.shape[0]
-    sent_ref[...] = dot_nt(out_ref[half:, :], w_ref[:, : 3 * cols]).astype(BF16)
-    kept_ref[...] = dot_nt(out_ref[:half, :], w_ref[:, : 3 * cols])
-
-
-def turn_back(grad_query, own, near, far, cosine, sine, w_att):
-    rows, cols = grad_query.shape
+
+    def rows_of(part):
+        total = None
+        for at, ref in enumerate((gq_ref, gk_ref, gv_ref)):
+            term = dot_nt(ref[0, part, :], w_ref[:, at * cols : (at + 1) * cols])
+            total = term if total is None else total + term
+        return total
+
+    sent_ref[...] = rows_of(slice(half, 2 * half)).astype(BF16)
+    kept_ref[...] = rows_of(slice(0, half))
+
+
+def turn_back(window, grads, w_att):
+    windows, rows, cols = grads[0].shape
     width = w_att.shape[0]
+    half = pl.BlockSpec((rows // 2, width), lambda i: (0, 0))
     return run(
         turn_back_kernel,
         "turn_back",
-        [
-            shaped((rows, 3 * cols), BF16),
-            shaped((rows // 2, width), F32),
-            shaped((rows // 2, width), BF16),
-        ],
+        [shaped((rows // 2, width), F32), shaped((rows // 2, width), BF16)],
         6 * rows * cols * width,
-        [grad_query, own, near, far, cosine, sine, w_att],
+        [*grads, w_att],
+        grid=(1,),
+        in_specs=[pl.BlockSpec((1, rows, cols), lambda i: (window, 0, 0))] * 3
+        + [pl.BlockSpec((width, 3 * cols), lambda i: (0, 0))],
+        out_specs=[half, half],
     )
 
 
@@ -1020,6 +1091,187 @@
             pl.BlockSpec((2, width), lambda i: (0, 0)),
         ],
         input_output_aliases={} if earlier is None else {5: 0},
+    )
+
+
+class SumRoute:
+    def __init__(self, part, rows, core_in, mine, x_in, z_in, send_sem, recv_sem):
+        self.read, self.rows = part, rows
+        self.core_in, self.mine, self.x_in, self.z_in = core_in, mine, x_in, z_in
+        self.send_sem, self.recv_sem = send_sem, recv_sem
+        self.seq, self.depth = lax.axis_index("seq"), lax.axis_index("dp")
+        self.peers = half_chip_peers()
+
+    def place(self, number, other_core):
+        seq = flipped(self.seq, 2) if number >= 4 else self.seq
+        seq = flipped(seq, 1) if other_core else seq
+        turn = (self.depth + number % 4) % lax.axis_size("dp")
+        return pl.ds(
+            pl.multiple_of((turn * lax.axis_size("seq") + seq) * self.rows, self.rows), self.rows
+        )
+
+    def message(self, number):
+        if number < 8:
+            source, target, peer = self.read.at[self.place(number, True), :], self.core_in, "core"
+            target = target.at[number]
+        elif number < 12:
+            source, target, peer = self.mine.at[number - 4], self.x_in.at[number - 8], "far"
+        else:
+            turn, peer = ((2, "up"), (1, "up"), (3, "down"))[number - 12]
+            source, target = self.mine.at[turn], self.z_in.at[number - 12]
+        return send(
+            source, target, self.send_sem.at[number], self.recv_sem.at[number], self.peers[peer]
+        )
+
+    def start(self, *numbers):
+        for number in numbers:
+            self.message(number).start()
+
+    def add_core(self, number):
+        self.message(number).wait_recv()
+        own = self.read[self.place(number, False), :].astype(F32)
+        self.mine[number] = (own + self.core_in[number].astype(F32)).astype(self.mine.dtype)
+
+    def add_x(self, number):
+        self.message(8 + number).wait_recv()
+        total = self.mine[number].astype(F32) + self.x_in[number].astype(F32)
+        self.mine[number] = total.astype(self.mine.dtype)
+
+    def add_up(self):
+        self.message(12).wait_recv()
+        total = self.mine[1].astype(F32) + self.z_in[0].astype(F32)
+        self.mine[1] = total.astype(self.mine.dtype)
+
+    def total(self):
+        self.message(13).wait_recv()
+        self.message(14).wait_recv()
+        return (
+            self.mine[0].astype(F32) + self.z_in[1].astype(F32) + self.z_in[2].astype(F32)
+        )
+
+    def sent(self):
+        for number in range(SUM_MESSAGES):
+            self.message(number).wait_send()
+
+
+SUM_MESSAGES = 15
+
+
+def reduce_kernel(trades, windows, part_ref, *refs):
+    first_refs, second_refs = refs[:windows], refs[windows : 2 * windows]
+    out_ref, vectors_ref = refs[2 * windows : 2 * windows + 2]
+    refs = refs[2 * windows + 2 :]
+    tiles, own_tiles, arrived_tiles = refs[:3]
+    big = refs[3:9]
+    small = refs[9:15]
+    tile_send, tile_recv = refs[15:]
+    tensor = lax.axis_index("tensor")
+    others = [{"tensor": flipped(tensor, other + 1)} for other in range(trades)]
+    shards = lax.axis_size("dp") * lax.axis_size("seq")
+    devices = shards * (trades + 1)
+    group = tiles.shape[0] // shards
+    routes = (
+        SumRoute(tiles, group, *small),
+        SumRoute(part_ref, part_ref.shape[0] // shards, *big),
+    )
+    small_route, big_route = routes
+    first = sum(ref[...] for ref in first_refs)
+    second = sum(ref[...] for ref in second_refs)
+    span = first.shape[1] // devices
+    tiles[...] = jnp.zeros_like(tiles)
+    for device in range(devices):
+        at = device * 8
+        part = slice(device * span, (device + 1) * span)
+        tiles[at : at + 2, :span] = first[:, part]
+        tiles[at + 2 : at + 4, :span] = second[:, part]
+    greet(list(big_route.peers.values()) + others)
+    small_route.start(6, 5, 7, 4, 2, 1, 3, 0)
+    big_route.start(6, 5, 7, 4, 2, 1, 3, 0)
+    for number in (6, 5, 7, 4, 2, 1, 3, 0):
+        small_route.add_core(number)
+    big_route.add_core(6)
+    small_route.start(10, 9, 11, 8)
+    big_route.add_core(5)
+    big_route.start(10)
+    big_route.add_core(7)
+    big_route.start(9)
+    big_route.add_core(4)
+    big_route.start(11)
+    big_route.add_core(2)
+    big_route.start(8)
+    for number in (2, 1, 3, 0):
+        small_route.add_x(number)
+    big_route.add_core(1)
+    small_route.start(12, 14)
+    big_route.add_core(3)
+    big_route.add_core(0)
+    small_route.add_up()
+    big_route.add_x(2)
+    small_route.start(13)
+    own = small_route.total()
+    big_route.start(12)
+    own_tiles[...] = own
+    big_route.add_x(1)
+    big_route.add_up()
+    out_ref[...] = jnp.zeros_like(out_ref)
+    big_route.start(13)
+    big_route.add_x(3)
+    out_ref[...] = jnp.zeros_like(out_ref)
+    big_route.start(14)
+    big_route.add_x(0)
+    out_ref[...] = big_route.total()
+
+    def tile_trade(other):
+        rows = pl.ds(pl.multiple_of(flipped(tensor, other + 1) * 8, 8), 8)
+        return send(
+            own_tiles.at[rows, :],
+            arrived_tiles.at[other],
+            tile_send.at[other],
+            tile_recv.at[other],
+            others[other],
+        )
+
+    for other in range(trades):
+        tile_trade(other).start()
+    vectors = own_tiles[pl.ds(pl.multiple_of(tensor * 8, 8), 8), :]
+    for other in range(trades):
+        tile_trade(other).wait_recv()
+        vectors = vectors + arrived_tiles[other]
+    vectors_ref[...] = vectors
+    for route in routes:
+        route.sent()
+    for other in range(trades):
+        tile_trade(other).wait_send()
+
+
+def reduce_grads(part, first_sums, second_sums, trades):
+    shards = lax.axis_size("dp") * lax.axis_size("seq")
+    rows, cols = part.shape[0] // shards, part.shape[1]
+    group = 8 * (trades + 1)
+    windows = len(first_sums)
+    dma = pltpu.SemaphoreType.DMA
+
+    def buffers(shape, dtype):
+        return [pltpu.VMEM((count,) + shape, dtype) for count in (8, 8, 4, 3)] + [
+            dma((SUM_MESSAGES,)),
+            dma((SUM_MESSAGES,)),
+        ]
+
+    return run(
+        functools.partial(reduce_kernel, trades, windows),
+        "reduce_grads",
+        [shaped((rows, cols), F32), shaped((8, 128), F32)],
+        0,
+        [part, *first_sums, *second_sums],
+        collective_id=3,
+        scratch_shapes=[
+            pltpu.VMEM((shards * group, 128), F32),
+            pltpu.VMEM((group, 128), F32),
+            pltpu.VMEM((trades, 8, 128), F32),
+        ]
+        + buffers((rows, cols), BF16)
+        + buffers((group, 128), F32)
+        + [dma((trades,)), dma((trades,))],
     )
 
 
@@ -1067,7 +1319,6 @@
     block_rows = own_rows * tensor_size
     head_cols = w_query.shape[1]
     hidden_cols = w_gate.shape[1]
-    every = ("dp", "seq", "tensor")
     shards = ("dp", "seq")
 
     own_at = lax.axis_index("tensor")
@@ -1089,9 +1340,13 @@
     lanes = jnp.zeros((8, 128), F32)
     vectors = jnp.stack([norm1_gain, norm1_bias, norm2_gain, norm2_bias])
     tile = lanes.at[:4, : vectors.shape[1]].set(vectors).at[4, :].set(jnp.sum(weighted))
-    w_att, w_ffn, norms, arrived_tokens = gather(
+    part = hidden_cols // 2
+    turned = w_down.T
+    first_ffn = jnp.concatenate([w_gate[:, :part], w_up[:, :part], turned[:, :part]], axis=1)
+    last_ffn = jnp.concatenate([w_gate[:, part:], w_up[:, part:], turned[:, part:]], axis=1)
+    first_ffn = lax.all_gather(first_ffn, shards, axis=0, tiled=True)
+    w_att, norms, arrived_tokens = gather(
         jnp.concatenate([w_query, w_key, w_value, w_out.T], axis=1),
-        jnp.concatenate([w_gate, w_up, w_down.T], axis=1),
         tile,
         tokens,
         tensor_size - 1,
@@ -1104,9 +1359,10 @@
 
     token_blocks = [tokens] + [arrived_tokens[other] for other in range(tensor_size - 1)]
     normed_rows, queries, own_kv = project(token_blocks, norms, w_att, cosine, sine)
-    attended, wide_attended, logs, kept_all, sent_all, slots_all, cots, w_ffn = attend(
-        queries, own_kv, w_att, cotangent, w_ffn, tensor_size - 1
-    )
+    attended, wide_attended, logs, kept_all, sent_all, slots_all, cots = attend(
+        queries, own_kv, w_att, cotangent, tensor_size - 1
+    )
+    last_ffn = lax.all_gather(hold(last_ffn, kept_all), shards, axis=0, tiled=True)
     cot_blocks = [
         [cotangent[w]] + [cots[other, w] for other in range(tensor_size - 1)] for w in windows
     ]
@@ -1118,13 +1374,32 @@
         middles.append(middle)
         mid_blocks.append(spread(normed_mid, "tensor"))
 
+    begun = []
+    for w in windows:
+        blocks = hold(mid_blocks[w], begun[-1] if begun else ())
+        begun.append(feed_first(blocks, cot_blocks[w], factors[w], first_ffn))
+    step = min(512, part)
+
+    def feed_weights(done, half):
+        return weight_grads(
+            [
+                ([one[0] for one in done], [one[3] for one in done]),
+                ([one[0] for one in done], [one[4] for one in done]),
+                ([one[1] for one in done], [one[2] for one in done]),
+            ],
+            step,
+            "feed_weights",
+            half,
+            2,
+        )
+
+    g_first_part = feed_weights(begun, 0)
+    g_first = lax.psum_scatter(g_first_part, shards, scatter_dimension=0, tiled=True)
     fed = []
     for w in windows:
-        blocks = hold(mid_blocks[w], fed[-1] if fed else ())
-        fed.append(feed(blocks, cot_blocks[w], factors[w], w_ffn))
-    mid_rows, grad_y_rows, hiddens, grad_gates, grad_ups = [
-        [one[at] for one in fed] for at in range(5)
-    ]
+        x_rows, gy_rows, *parts = hold(begun[w], fed[-1] if fed else g_first_part)
+        ended = feed_last(x_rows, gy_rows, parts[3:], parts[:3], last_ffn)
+        fed.append((x_rows, gy_rows, *ended))
     grad_middles, grad_mid_blocks, second_sums = [], [], []
 
     def through_second_norm(w, *after):
@@ -1138,71 +1413,40 @@
 
     for w in windows[:-1]:
         through_second_norm(w)
-    g_ffn_part = weight_grads(
+    g_ffn_part = feed_weights(hold(fed, grad_middles), 1)
+    g_last = lax.psum_scatter(g_ffn_part, shards, scatter_dimension=0, tiled=True)
+    through_second_norm(windows[-1], g_ffn_part)
+
+    grad_q, grad_k, grad_v, grad_mid_rows, *arrived_results = attend_back(
+        hold(queries, g_ffn_part),
+        wide_attended,
+        logs,
+        slots_all,
+        grad_mid_blocks,
+        w_att,
+        (cosine, sine),
+        [fed[w][6] for w in windows],
+    )
+    output = results(
         [
-            (mid_rows, grad_gates),
-            (mid_rows, grad_ups),
-            (grad_y_rows, hold(hiddens, grad_middles)),
-        ],
-        min(512, hidden_cols),
-        "feed_weights",
-    )
-    g_ffn = lax.psum_scatter(g_ffn_part, shards, scatter_dimension=0, tiled=True).astype(F32)
-    through_second_norm(windows[-1], g_ffn_part)
-
-    def fold(blocks, down_to):
-        while len(blocks) > down_to:
-            half = len(blocks) // 2
-            arrived = [swap(block, "seq", half) for block in blocks[half:]]
-            blocks = [
-                (kept.astype(F32) + new.astype(F32)).astype(BF16)
-                for kept, new in zip(blocks[:half], arrived)
-            ]
-        return blocks
-
-    slots = seq_size // 2
-    far_sums, dq_states, grad_mid_rows = [], [], []
+            (middles[w], *later_pair(fed[w][5], arrived_results[w], "tensor"))
+            for w in windows
+        ]
+    )
+
+    first_parts = []
     for w in windows:
-        query = hold(queries, dq_states[-1][0] if dq_states else grad_middles[-1])
-        parts = attend_back(
-            w, query, wide_attended, logs, slots_all, grad_mid_blocks[w], w_att, None
-        )
-        dq_states.append((parts[0], parts[1 + slots]))
-        grad_mid_rows.append(parts[2 + slots])
-        far_sums.append(swap(fold(list(parts[1 : 1 + slots]), 1)[0], "seq", top_bit))
-    result_parts = [
-        (middles[w], *scatter_pair(fed[w][5], hold(fed[w][6], dq_states[0]), "tensor"))
-        for w in windows
-    ]
-    grad_queries, near_pairs = [], []
-    for w in windows:
-        query = hold(queries, grad_queries[-1] if grad_queries else dq_states[-1][0])
-        parts = attend_back(
-            w, query, wide_attended, logs, slots_all, dq_states[w], None, (cosine, sine)
-        )
-        grad_queries.append(parts[0])
-        blocks = fold(list(parts[1:]), 2)
-        near_pairs.append((blocks[0], swap(blocks[1], "seq", 1)))
-    output = results(result_parts)
-
-    grad_qkvs, first_parts = [], []
-    for w in windows:
-        grad_qkv, kept, sent = turn_back(
-            grad_queries[w], *near_pairs[w], far_sums[w], cosine, sine, w_att
-        )
-        grad_qkvs.append(grad_qkv)
+        kept, sent = turn_back(w, (grad_q, grad_k, grad_v), w_att)
         first_parts.append(scatter_pair(kept, sent, "tensor"))
     g_att_part = weight_grads(
         [
-            ([normed_rows[w] for w in windows], grad_qkvs),
-            (grad_mid_rows, [attended[w] for w in windows]),
-        ],
+            ([normed_rows[w] for w in windows], [grad[w] for w in windows])
+            for grad in (grad_q, grad_k, grad_v)
+        ]
+        + [([grad_mid_rows[w] for w in windows], [attended[w] for w in windows])],
         head_cols,
         "attend_weights",
     )
-    g_att = lax.psum_scatter(
-        hold(g_att_part, g_ffn), shards, scatter_dimension=0, tiled=True
-    ).astype(F32)
     input_grad = None
     first_sums = []
     for w in windows:
@@ -1219,10 +1463,15 @@
         )
         first_sums.append(sums)
 
-    norm_sums = jnp.concatenate([sum(first_sums), sum(second_sums)], axis=0)
-    devices = model_width // norm1_gain.shape[0]
-    norm_sums = norm_sums.reshape(4, devices, -1).transpose(1, 0, 2)
-    norm_sums = scatter_ordered(norm_sums, every)[0]
+    g_att, vectors = reduce_grads(g_att_part, first_sums, second_sums, tensor_size - 1)
+    norm_sums = vectors[:4, : norm1_gain.shape[0]]
+    ffn_grads = [
+        jnp.concatenate(
+            [g_first[:, at * part : (at + 1) * part], g_last[:, at * part : (at + 1) * part]],
+            axis=1,
+        ).astype(F32)
+        for at in range(3)
+    ]
 
     return (
         output,
@@ -1235,9 +1484,9 @@
         g_att[:, 3 * head_cols :].T,
         norm_sums[2],
         norm_sums[3],
-        g_ffn[:, :hidden_cols],
-        g_ffn[:, hidden_cols : 2 * hidden_cols],
-        g_ffn[:, 2 * hidden_cols :].T,
+        ffn_grads[0],
+        ffn_grads[1],
+        ffn_grads[2].T,
     )
 
 

time: 559 us -> 501 us (0.90)
  waiting for transfers between devices: 124 us -> 48.9 us
  Pallas kernels: 349 us -> 377 us
  starting transfers between devices: 23.1 us -> 11.3 us
    ppermute x23 -> x10, waiting for transfers between devices: 121 us -> 48.8 us  [swap(): return lax.ppermute(array, axis, [(i, i ^ bit) for i in range(size)])]
    pallas_call x20 -> x21, Pallas kernels: 349 us -> 377 us  [run(): pl.pallas_call(kernel, out_shape=out_shape, compiler_params=pltpu.Compile...]
    ppermute x23 -> x10, starting transfers between devices: 23 us -> 10.5 us  [swap(): return lax.ppermute(array, axis, [(i, i ^ bit) for i in range(size)])]
    unnamed x96 -> x68, local copies, waits for them, and re-layouts: 12.7 us -> 8.29 us
  transfers between devices with their start and end apart: 25 -> 14, of which waited for: 16 -> 5; matrix products, arithmetic and copies ran while one was open for 2% -> 5% of each run, Pallas kernels for 28% -> 77%
where the time goes in v5:
time: 501 us; the launch traced here: 493 us
  Pallas kernels  377 us (75%)
  waiting for transfers between devices  48.9 us (10%)
  local copies, waits for them, and re-layouts  31.7 us (6%)
  between operations  14.6 us (3%)
  starting transfers between devices  11.3 us (2%)
  other arithmetic  9.19 us (2%)
    pallas_call x21, Pallas kernels, run(): pl.pallas_call(kernel, out_shape=out_shape, compiler_params=pltpu.Compile...  377 us
    ppermute x10, waiting for transfers between devices, swap(): return lax.ppermute(array, axis, [(i, i ^ bit) for i in range(size)])  48.8 us
    ppermute x10, starting transfers between devices, swap(): return lax.ppermute(array, axis, [(i, i ^ bit) for i in range(size)])  10.5 us
  transfers between devices with their start and end apart: 14, of which 5 were waited for; matrix products, arithmetic and copies ran while one was open for 5% of the time, Pallas kernels for 77%

profile of v5, /device:TPU:0, one launch (start us, length us, event | category | flops | bytes accessed | tf_op | source)
XLA Modules:
  0.0 492.7 jit_solution(6068992298285735330)
XLA Ops:
  7.3 1.1 fusion.8
  8.4 1.1 fusion.6
  9.5 0.8 pad_maximum_fusion.1
  12.7 52.4 %gather.1 = (bf16[1024,2048]{1,0:T(8,128)(2,1)}, f32[8,1024]{1,0:T(8,128)}, bf16[1,2,256,1024]{3,2,1,0:T(8,128)(2,1)}) custom-call(bf16[64,2048]{1,0:T(8,128)(2,1)} %pad_maximum_fusion.2.att_ref, f32[8,128]{1,0:T(8,128)} %copy-done.20, bf16[2,256,1024]{2,1,0:T(8,128)(2,1)} %refs_0_.1), custom_call_target="tpu_custom_call" | custom-call | bytes 6590464 | tf_op jit(solution)/shard_map/gather/pallas_call | solution.py:80
  65.2 1.0 fusion
  66.2 1.0 pad_maximum_fusion.3.cos_ref.refs_5_
  67.2 1.0 pad_maximum_fusion.4.sin_ref.refs_6_
  68.1 8.4 %project.1 = (bf16[2,512,1024]{2,1,0:T(8,128)(2,1)}, bf16[2,512,512]{2,1,0:T(8,128)(2,1)}, bf16[2,2,512,512]{3,2,1,0:T(8,128)(2,1)}) custom-call(f32[8,1024]{1,0:T(8,128)} %get-tuple-element.137.norms_ref, bf16[1024,2048]{1,0:T(8,128)(2,1)} %get-tuple-element.138.w_ref.refs_1_.refs_4_, f32[512,128]{1,0:T(8,128)} %pad_maximum_fusion.3.cos_ref.refs_5_, ...), custom_call_target="tpu_custom_call" | custom-call | flops 3221225472 | bytes 12091392 | tf_op jit(solution)/shard_map/project/pallas_call | solution.py:80
  77.3 58.7 %attend.1 = (bf16[2,512,512]{2,1,0:T(8,128)(2,1)}, f32[2,512,512]{2,1,0:T(8,128)}, f32[2,512,512]{2,1,0:T(8,128)}, f32[2,256,1024]{2,1,0:T(8,128)}, bf16[2,256,1...) custom-call(bf16[2,512,512]{2,1,0:T(8,128)(2,1)} %get-tuple-element.206.refs_0_, ...), custom_call_target="tpu_custom_call" | custom-call | flops 17179869184 | bytes 26214400 | tf_op jit(solution)/shard_map/attend/pallas_call | solution.py:80
  136.5 1.4 slice_bitcast_fusion.16
  138.0 1.8 collective-permute-start.2
  140.0 1.2 slice.189
  142.5 1.0 slice_bitcast_fusion.17
  143.5 1.6 slice_bitcast_fusion.4
  145.1 17.8 %collective-permute-done.arrived_ref = bf16[256,1024]{1,0:T(8,128)(2,1)S(1)} collective-permute-done((bf16[256,1024]{1,0:T(8,128)(2,1)S(1)}, bf16[256,1024]{1,0:T(8,128)(2,1)S(1)}, u32[]{:S(2)}, u32[]{:S(2)}) %collective-permute-start) | collective-permute-done | bytes 524320 | tf_op jit(solution)/shard_map/ppermute | solution.py:45
  162.8 0.8 copy-done.14
  163.6 3.5 second_norm.2
  167.2 1.6 collective-permute-start.1
  168.8 1.0 slice_bitcast_fusion.15
  169.8 1.1 slice_bitcast_fusion.14
  170.9 0.8 copy-done.12
  171.7 2.9 second_norm.3
  175.0 7.3 %collective-permute-done.1.refs_4_ = bf16[256,1024]{1,0:T(8,128)(2,1)S(1)} collective-permute-done((bf16[256,1024]{1,0:T(8,128)(2,1)}, bf16[256,1024]{1,0:T(8,128)(2,1)S(1)}, u32[]{:S(2)}, u32[]{:S(2)}) %collective-permute-start.1) | collective-permute-done | bytes 524320 | tf_op jit(solution)/shard_map/ppermute | solution.py:45
  182.3 0.8 copy-done.30
  183.0 15.3 %feed_first.2 = (bf16[512,1024]{1,0:T(8,128)(2,1)}, bf16[512,1024]{1,0:T(8,128)(2,1)}, bf16[512,2048]{1,0:T(8,128)(2,1)}, bf16[512,2048]{1,0:T(8,128)(2,1)}, bf1...) custom-call(f32[1,1]{1,0:T(1,128)} %bitcast.11.factor_ref, ...), custom_call_target="tpu_custom_call" | custom-call | flops 6442450944 | bytes 33554436 | tf_op jit(solution)/shard_map/feed_first/pallas_call | solution.py:80
  198.4 0.8 copy-done.32
  199.1 15.0 %feed_first.3 = (bf16[512,1024]{1,0:T(8,128)(2,1)}, bf16[512,1024]{1,0:T(8,128)(2,1)}, bf16[512,2048]{1,0:T(8,128)(2,1)}, bf16[512,2048]{1,0:T(8,128)(2,1)}, bf1...) custom-call(f32[1,1]{1,0:T(1,128)} %bitcast.14.factor_ref, ...), custom_call_target="tpu_custom_call" | custom-call | flops 6442450944 | bytes 33554436 | tf_op jit(solution)/shard_map/feed_first/pallas_call | solution.py:80
  214.2 13.7 %feed_weights.2 = bf16[1024,3072]{1,0:T(8,128)(2,1)} custom-call(bf16[512,1024]{1,0:T(8,128)(2,1)} %get-tuple-element.196.refs_0_.refs_4_.refs_3_, bf16[512,1024]{1,0:T(8,128)(2,1)} %get-tuple-element.197.refs_1_.refs_5_.refs_3_, bf16[512,2048]{1,0:T(8,128)(2,1)} %get-tuple-element.170.refs_2_.refs_8_, bf16[512,2048]{1,0:T(8,128)(2,1)} %get-tuple-element.186.refs_3_.refs_8_, ...), custom_call_target="tpu_custom_call" | custom-call | flops 6442450944 | bytes 25165824 | tf_op jit(solution)/shard_map/feed_weights/pallas_call | solution.py:80
  228.2 15.1 %feed_last.2 = (bf16[512,2048]{1,0:T(8,128)(2,1)}, bf16[512,2048]{1,0:T(8,128)(2,1)}, bf16[512,2048]{1,0:T(8,128)(2,1)}, f32[256,1024]{1,0:T(8,128)}, bf16[256,1...) custom-call(bf16[1024,3072]{1,0:T(8,128)(2,1)} %all-gather.3.cloned., ...), custom_call_target="tpu_custom_call", output_to_operand_aliasing={{0}: (7, {}), {1}: (8, {}), {2}: (9, {})} | custom-call | flops 6442450944 | bytes 40894464 | tf_op jit(solution)/shard_map/feed_last/pallas_call | solution.py:80
  243.3 1.7 collective-permute-start.4
  245.0 15.3 %feed_last.3 = (bf16[512,2048]{1,0:T(8,128)(2,1)}, bf16[512,2048]{1,0:T(8,128)(2,1)}, bf16[512,2048]{1,0:T(8,128)(2,1)}, f32[256,1024]{1,0:T(8,128)}, bf16[256,1...) custom-call(bf16[1024,3072]{1,0:T(8,128)(2,1)} %all-gather.3.cloned., ...), custom_call_target="tpu_custom_call", output_to_operand_aliasing={{0}: (7, {}), {1}: (8, {}), {2}: (9, {})} | custom-call | flops 6442450944 | bytes 40894464 | tf_op jit(solution)/shard_map/feed_last/pallas_call | solution.py:80
  261.1 4.5 second_norm_back.2
  265.6 13.9 %feed_weights.3 = bf16[1024,3072]{1,0:T(8,128)(2,1)} custom-call(bf16[512,1024]{1,0:T(8,128)(2,1)} %get-tuple-element.196.refs_0_.refs_4_.refs_3_, bf16[512,1024]{1,0:T(8,128)(2,1)} %get-tuple-element.197.refs_1_.refs_5_.refs_3_, bf16[512,2048]{1,0:T(8,128)(2,1)} %get-tuple-element.198.refs_2_, bf16[512,2048]{1,0:T(8,128)(2,1)} %get-tuple-element.199.refs_3_, ...), custom_call_target="tpu_custom_call" | custom-call | flops 6442450944 | bytes 25165824 | tf_op jit(solution)/shard_map/feed_weights/pallas_call | solution.py:80
  279.6 1.0 copy-done.29
  281.3 8.5 %collective-permute-done.6.arrived_ref = bf16[256,1024]{1,0:T(8,128)(2,1)S(1)} collective-permute-done((bf16[256,1024]{1,0:T(8,128)(2,1)S(1)}, bf16[256,1024]{1,0:T(8,128)(2,1)S(1)}, u32[]{:S(2)}, u32[]{:S(2)}) %collective-permute-start.6) | collective-permute-done | bytes 524320 | tf_op jit(solution)/shard_map/ppermute | solution.py:45
  289.8 0.8 copy-done.15
  290.6 4.7 second_norm_back.3
  295.9 1.4 collective-permute-start.5
  297.3 1.0 slice_bitcast_fusion.6
  298.3 1.5 slice_bitcast_fusion.2
  299.8 9.6 %collective-permute-done.7.refs_10_ = bf16[256,1024]{1,0:T(8,128)(2,1)S(1)} collective-permute-done((bf16[256,1024]{1,0:T(8,128)(2,1)}, bf16[256,1024]{1,0:T(8,128)(2,1)S(1)}, u32[]{:S(2)}, u32[]{:S(2)}) %collective-permute-start.7) | collective-permute-done | bytes 524320 | tf_op jit(solution)/shard_map/ppermute | solution.py:45
  309.4 5.6 %collective-permute-done.5.refs_8_ = bf16[256,1024]{1,0:T(8,128)(2,1)S(1)} collective-permute-done((bf16[256,1024]{1,0:T(8,128)(2,1)S(1)}, bf16[256,1024]{1,0:T(8,128)(2,1)S(1)}, u32[]{:S(2)}, u32[]{:S(2)}) %collective-permute-start.5) | collective-permute-done | bytes 524320 | tf_op jit(solution)/shard_map/ppermute | solution.py:45
  315.8 80.9 %attend_back.1 = (bf16[2,512,512]{2,1,0:T(8,128)(2,1)}, bf16[2,512,512]{2,1,0:T(8,128)(2,1)}, bf16[2,512,512]{2,1,0:T(8,128)(2,1)}, bf16[2,512,1024]{2,1,0:T(8,1...) custom-call(bf16[2,512,512]{2,1,0:T(8,128)(2,1)} %get-tuple-element.206.refs_0_, ...), custom_call_target="tpu_custom_call" | custom-call | flops 42949672960 | bytes 27787264 | tf_op jit(solution)/shard_map/attend_back/pallas_call | solution.py:80
  396.7 5.2 %turn_back.3 = (f32[256,1024]{1,0:T(8,128)}, bf16[256,1024]{1,0:T(8,128)(2,1)}) custom-call(bf16[2,512,512]{2,1,0:T(8,128)(2,1)} %get-tuple-element.216.gq_ref, bf16[2,512,512]{2,1,0:T(8,128)(2,1)} %get-tuple-element.217.gk_ref, bf16[2,512,512]{2,1,0:T(8,128)(2,1)} %get-tuple-element.218.gv_ref, bf16[1024,2048]{1,0:T(8,128)(2,1)} %get-tuple-element.138.w_ref.refs_1_.refs_4_), custom_call_target="tpu_custom_call" | custom-call | flops 1610612736 | bytes 8912896 | tf_op jit(solution)/shard_map/turn_back/pallas_call | solution.py:80
  402.3 5.2 %turn_back.2 = (f32[256,1024]{1,0:T(8,128)}, bf16[256,1024]{1,0:T(8,128)(2,1)}) custom-call(bf16[2,512,512]{2,1,0:T(8,128)(2,1)} %get-tuple-element.216.gq_ref, bf16[2,512,512]{2,1,0:T(8,128)(2,1)} %get-tuple-element.217.gk_ref, bf16[2,512,512]{2,1,0:T(8,128)(2,1)} %get-tuple-element.218.gv_ref, bf16[1024,2048]{1,0:T(8,128)(2,1)} %get-tuple-element.138.w_ref.refs_1_.refs_4_), custom_call_target="tpu_custom_call" | custom-call | flops 1610612736 | bytes 8912896 | tf_op jit(solution)/shard_map/turn_back/pallas_call | solution.py:80
  407.5 1.7 collective-permute-start.8
  409.1 1.1 slice_bitcast_fusion.12
  410.3 1.1 slice_bitcast_fusion.10
  411.4 1.5 slice_bitcast_fusion
  412.9 1.0 slice_bitcast_fusion.8
  414.0 11.5 %attend_weights.1.part_ref = bf16[1024,2048]{1,0:T(8,128)(2,1)} custom-call(bf16[512,1024]{1,0:T(8,128)(2,1)} %get-tuple-element.240.refs_0_.refs_4_.refs_8_, bf16[512,1024]{1,0:T(8,128)(2,1)} %get-tuple-element.239.refs_1_.refs_5_.refs_9_, bf16[512,512]{1,0:T(8,128)(2,1)} %get-tuple-element.250.refs_2_, bf16[512,512]{1,0:T(8,128)(2,1)} %get-tuple-element.249.refs_3_, ...), custom_call_target="tpu_custom_call" | custom-call | flops 4294967296 | bytes 16777216 | tf_op jit(solution)/shard_map/attend_weights/pallas_call | solution.py:80
  425.5 3.7 results.1
  429.2 0.8 copy-done.11
  430.0 3.6 first_norm_back.2
  433.6 0.8 copy-done.10
  434.4 3.6 first_norm_back.3
  438.1 39.8 %reduce_grads.1 = (f32[64,2048]{1,0:T(8,128)}, f32[8,128]{1,0:T(8,128)}) custom-call(bf16[1024,2048]{1,0:T(8,128)(2,1)} %attend_weights.1.part_ref, f32[2,1024]{1,0:T(2,128)} %get-tuple-element.231.refs_0_, f32[2,1024]{1,0:T(2,128)} %get-tuple-element.232.refs_1_, f32[2,1024]{1,0:T(2,128)} %get-tuple-element.233.refs_2_, f32[2,1024]{1,0:T(2,128)} %get-tuple-element.234.refs_3_), custom_call_target="tpu_custom_call" | custom-call | bytes 4755456 | tf_op jit(solution)/shard_map/reduce_grads/pallas_call | solution.py:80
  477.8 1.4 slice_bitcast_fusion.23
  479.2 1.9 slice_bitcast_fusion.22
  481.1 1.1 fusion.4
  482.2 1.1 fusion.5
  483.2 0.8 convert_bitcast_fusion
  484.1 0.8 maximum_convert_fusion.1
  484.9 0.8 maximum_convert_fusion
  (94 shorter events, 9.3 us)
Async XLA Ops:
  7.2 3.2 copy-start.22
  7.2 3.2 copy-start.23
  7.2 3.2 copy-start.24
  7.2 3.2 copy-start.25
  7.2 3.2 copy-start.21
  7.2 3.2 copy-start.26
  7.2 3.4 copy-start.27
  7.3 4.7 copy-start.16
  7.3 4.7 copy-start.17
  7.3 4.7 copy-start.18
  7.3 4.7 copy-start.19
  7.3 175.0 %all-gather.5.cloned.1.call-start = ((), (), s32[]{:S(2)}) async-start(), calls=%async_computation.3 | async-start | bytes 6684672 | tf_op jit(solution)/shard_map/all_gather | solution.py:1347
  10.4 217.8 %all-gather.3.cloned.1.call-start = ((), (), s32[]{:S(2)}) async-start(), calls=%async_computation.2 | async-start | bytes 6684672 | tf_op jit(solution)/shard_map/all_gather | solution.py:1365
  12.0 0.8 copy-start.20
  136.0 6.5 %copy-start.3 = (bf16[2,256,1024]{2,1,0:T(8,128)(2,1)S(1)}, bf16[2,256,1024]{2,1,0:T(8,128)(2,1)}, u32[]{:S(2)}) copy-start(bf16[2,256,1024]{2,1,0:T(8,128)(2,1)} %refs_0_.1) | copy-start | bytes 3145732
  136.0 345.1 %reduce-scatter.3.cloned.1.call-start = ((), (), s32[]{:S(2)}) async-start(), calls=%async_computation.4 | async-start | bytes 6684672 | tf_op jit(solution)/shard_map/reduce_scatter | solution.py:1397
  136.5 7.0 %copy-start.5 = (f32[2,256,1024]{2,1,0:T(8,128)S(1)}, f32[2,256,1024]{2,1,0:T(8,128)}, u32[]{:S(2)}) copy-start(f32[2,256,1024]{2,1,0:T(8,128)} %get-tuple-element.142) | copy-start | bytes 6291460
  138.0 32.9 %collective-permute-start.2 = (bf16[256,1024]{1,0:T(8,128)(2,1)S(1)}, bf16[256,1024]{1,0:T(8,128)(2,1)S(1)}, u32[]{:S(2)}, u32[]{:S(2)}) collective-permute-start(bf16[256,1024]{1,0:T(8,128)(2,1)S(1)} %get-tuple-element.255), channel_id=1, source_target_pairs={{0,1},{1,0},{2,3},{3,2},{4,5},{5,4},{6,7},{7,6},{8,9},{9,8},{10,11... | collective-permute-start | bytes 1572872 | tf_op jit(solution)/shard_map/ppermute | solution.py:45
  139.8 23.1 %collective-permute-start = (bf16[256,1024]{1,0:T(8,128)(2,1)S(1)}, bf16[256,1024]{1,0:T(8,128)(2,1)S(1)}, u32[]{:S(2)}, u32[]{:S(2)}) collective-permute-start(bf16[256,1024]{1,0:T(8,128)(2,1)S(1)} %get-tuple-element.256), channel_id=1, source_target_pairs={{0,1},{1,0},{2,3},{3,2},{4,5},{5,4},{6,7},{7,6},{8,9},{9,8},{10,11... | collective-permute-start | bytes 1572872 | tf_op jit(solution)/shard_map/ppermute | solution.py:45
  145.1 23.7 %copy-start.7 = (bf16[2,256,1024]{2,1,0:T(8,128)(2,1)S(1)}, bf16[2,256,1024]{2,1,0:T(8,128)(2,1)}, u32[]{:S(2)}) copy-start(bf16[2,256,1024]{2,1,0:T(8,128)(2,1)} %refs_3_.1) | copy-start | bytes 3145732
  162.8 0.8 copy-start.14
  163.6 6.2 %copy-start.9 = (bf16[1,2,256,1024]{3,2,1,0:T(8,128)(2,1)S(1)}, bf16[1,2,256,1024]{3,2,1,0:T(8,128)(2,1)}, u32[]{:S(2)}) copy-start(bf16[1,2,256,1024]{3,2,1,0:T(8,128)(2,1)} %get-tuple-element.149) | copy-start | bytes 3145732
  167.2 15.1 %collective-permute-start.1 = (bf16[256,1024]{1,0:T(8,128)(2,1)}, bf16[256,1024]{1,0:T(8,128)(2,1)S(1)}, u32[]{:S(2)}, u32[]{:S(2)}) collective-permute-start(bf16[256,1024]{1,0:T(8,128)(2,1)} %get-tuple-element.147.refs_3_), channel_id=1, source_target_pairs={{0,1},{1,0},{2,3},{3,2},{4,5},{5,4},{6,7},{7,6},{8,9},{9,8},{10,11... | collective-permute-start | bytes 1572872 | tf_op jit(solution)/shard_map/ppermute | solution.py:45
  170.9 0.8 copy-start.12
  174.6 23.8 %collective-permute-start.3 = (bf16[256,1024]{1,0:T(8,128)(2,1)}, bf16[256,1024]{1,0:T(8,128)(2,1)S(1)}, u32[]{:S(2)}, u32[]{:S(2)}) collective-permute-start(bf16[256,1024]{1,0:T(8,128)(2,1)} %get-tuple-element.158.refs_3_), channel_id=1, source_target_pairs={{0,1},{1,0},{2,3},{3,2},{4,5},{5,4},{6,7},{7,6},{8,9},{9,8},{10,11... | collective-permute-start | bytes 1572872 | tf_op jit(solution)/shard_map/ppermute | solution.py:45
  182.2 0.8 copy-start.30
  198.4 0.8 copy-start.32
  227.9 254.3 %reduce-scatter.5.cloned.1.call-start = ((), (), s32[]{:S(2)}) async-start(), calls=%async_computation.5 | async-start | bytes 6684672 | tf_op jit(solution)/shard_map/reduce_scatter | solution.py:1417
  243.3 17.0 %collective-permute-start.4 = (bf16[256,1024]{1,0:T(8,128)(2,1)}, bf16[256,1024]{1,0:T(8,128)(2,1)S(1)}, u32[]{:S(2)}, u32[]{:S(2)}) collective-permute-start(bf16[256,1024]{1,0:T(8,128)(2,1)} %get-tuple-element.178), channel_id=1, source_target_pairs={{0,1},{1,0},{2,3},{3,2},{4,5},{5,4},{6,7},{7,6},{8,9},{9,8},{10,11... | collective-permute-start | bytes 1572872 | tf_op jit(solution)/shard_map/ppermute | solution.py:45
  260.3 0.8 copy-start.13
  279.5 1.1 copy-start.29
  280.6 15.3 %copy-start.28 = (bf16[256,1024]{1,0:T(8,128)(2,1)S(1)}, bf16[256,1024]{1,0:T(8,128)(2,1)}, u32[]{:S(2)}) copy-start(bf16[256,1024]{1,0:T(8,128)(2,1)} %get-tuple-element.210.refs_7_) | copy-start | bytes 1572868
  280.6 16.7 %copy-start.8 = (bf16[2,512,512]{2,1,0:T(8,128)(2,1)S(1)}, bf16[2,512,512]{2,1,0:T(8,128)(2,1)}, u32[]{:S(2)}) copy-start(bf16[2,512,512]{2,1,0:T(8,128)(2,1)} %get-tuple-element.222) | copy-start | bytes 3145732
  280.6 9.2 %collective-permute-start.6 = (bf16[256,1024]{1,0:T(8,128)(2,1)S(1)}, bf16[256,1024]{1,0:T(8,128)(2,1)S(1)}, u32[]{:S(2)}, u32[]{:S(2)}) collective-permute-start(bf16[256,1024]{1,0:T(8,128)(2,1)S(1)} %copy-done.29), channel_id=1, source_target_pairs={{0,1},{1,0},{2,3},{3,2},{4,5},{5,4},{6,7},{7,6},{8,9},{9,8},{10,11... | collective-permute-start | bytes 1572872 | tf_op jit(solution)/shard_map/ppermute | solution.py:45
  289.8 0.8 copy-start.15
  290.6 7.7 %copy-start.4 = (bf16[2,512,1024]{2,1,0:T(8,128)(2,1)S(1)}, bf16[2,512,1024]{2,1,0:T(8,128)(2,1)}, u32[]{:S(2)}) copy-start(bf16[2,512,1024]{2,1,0:T(8,128)(2,1)} %get-tuple-element.220) | copy-start | bytes 6291460
  295.2 14.2 %collective-permute-start.7 = (bf16[256,1024]{1,0:T(8,128)(2,1)}, bf16[256,1024]{1,0:T(8,128)(2,1)S(1)}, u32[]{:S(2)}, u32[]{:S(2)}) collective-permute-start(bf16[256,1024]{1,0:T(8,128)(2,1)} %get-tuple-element.213.refs_9_), channel_id=1, source_target_pairs={{0,1},{1,0},{2,3},{3,2},{4,5},{5,4},{6,7},{7,6},{8,9},{9,8},{10,11... | collective-permute-start | bytes 1572872 | tf_op jit(solution)/shard_map/ppermute | solution.py:45
  295.9 19.1 %collective-permute-start.5 = (bf16[256,1024]{1,0:T(8,128)(2,1)S(1)}, bf16[256,1024]{1,0:T(8,128)(2,1)S(1)}, u32[]{:S(2)}, u32[]{:S(2)}) collective-permute-start(bf16[256,1024]{1,0:T(8,128)(2,1)S(1)} %copy-done.28), channel_id=1, source_target_pairs={{0,1},{1,0},{2,3},{3,2},{4,5},{5,4},{6,7},{7,6},{8,9},{9,8},{10,11... | collective-permute-start | bytes 1572872 | tf_op jit(solution)/shard_map/ppermute | solution.py:45
  309.4 5.6 %copy-start.31 = (bf16[256,1024]{1,0:T(8,128)(2,1)}, bf16[256,1024]{1,0:T(8,128)(2,1)S(1)}, u32[]{:S(2)}) copy-start(bf16[256,1024]{1,0:T(8,128)(2,1)S(1)} %collective-permute-done.7.refs_10_) | copy-start | bytes 1572868
  315.0 0.8 copy-start.33
  401.9 7.2 %copy-start.2 = (bf16[2,512,512]{2,1,0:T(8,128)(2,1)S(1)}, bf16[2,512,512]{2,1,0:T(8,128)(2,1)}, u32[]{:S(2)}) copy-start(bf16[2,512,512]{2,1,0:T(8,128)(2,1)} %get-tuple-element.216.gq_ref) | copy-start | bytes 3145732
  401.9 27.3 %collective-permute-start.9 = (bf16[256,1024]{1,0:T(8,128)(2,1)}, bf16[256,1024]{1,0:T(8,128)(2,1)S(1)}, u32[]{:S(2)}, u32[]{:S(2)}) collective-permute-start(bf16[256,1024]{1,0:T(8,128)(2,1)} %get-tuple-element.228), channel_id=1, source_target_pairs={{0,1},{1,0},{2,3},{3,2},{4,5},{5,4},{6,7},{7,6},{8,9},{9,8},{10,11... | collective-permute-start | bytes 1572872 | tf_op jit(solution)/shard_map/ppermute | solution.py:45
  407.5 2.8 copy-start.1
  407.5 3.9 copy-start.6
  407.5 26.2 %collective-permute-start.8 = (bf16[256,1024]{1,0:T(8,128)(2,1)}, bf16[256,1024]{1,0:T(8,128)(2,1)S(1)}, u32[]{:S(2)}, u32[]{:S(2)}) collective-permute-start(bf16[256,1024]{1,0:T(8,128)(2,1)} %get-tuple-element.224), channel_id=1, source_target_pairs={{0,1},{1,0},{2,3},{3,2},{4,5},{5,4},{6,7},{7,6},{8,9},{9,8},{10,11... | collective-permute-start | bytes 1572872 | tf_op jit(solution)/shard_map/ppermute | solution.py:45
  411.4 1.6 copy-start
  429.2 0.8 copy-start.11
  433.6 0.8 copy-start.10
Sparse Core Ops, SparseCore 0:
  10.5 77.9 all-gather.4
  136.1 60.7 all-gather.2
  228.0 83.3 reduce-scatter.2
  315.7 101.8 reduce-scatter.4

commit v6 on v5

--- a/solution.py
+++ b/solution.py
@@ -94,6 +94,13 @@
 
 
 SCALAR = pl.BlockSpec(memory_space=pltpu.SMEM)
+
+
+def plane(operand, block=None, index=None):
+    array, at = operand if isinstance(operand, tuple) else (operand, ())
+    shape = array.shape[len(at) :] if block is None else block
+    place = (lambda *i: (0,) * len(shape)) if index is None else index
+    return array, pl.BlockSpec((None,) * len(at) + tuple(shape), lambda *i: at + place(*i))
 
 
 def normalise(stream):
@@ -383,10 +390,14 @@
 
 
 def attend_kernel(windows, pairs, trades, exp_scale, *refs):
-    q_ref, w_ref, kv_ref, cot_ref = refs[:4]
-    low_ref, wide_ref, log_ref, kept_ref, sent_ref, slots_ref, cots_ref = refs[4:11]
-    slots, acc_all, top_all, total_all, mixed_rows = refs[11:16]
-    own_sem, send_sem, recv_sem, save_sem, cot_send, cot_recv = refs[16:]
+    stages = (trades + 1).bit_length() - 1
+    q_ref, w_ref, kv_ref, cot_ref, x_ref, norms_ref = refs[:6]
+    low_ref, wide_ref, log_ref, kept_ref, sent_ref, slots_ref, cots_ref = refs[6:13]
+    middle_ref, normed_ref, others_ref = refs[13:16]
+    slots, acc_all, top_all, total_all, mixed_rows = refs[16:21]
+    own_sem, send_sem, recv_sem, save_sem, cot_send, cot_recv = refs[21:27]
+    early_kept, early_normed, early_sem, early_recv, normed_sem, normed_recv = refs[27:33]
+    early_sent, early_arrived = refs[33 : 33 + stages], refs[33 + stages :]
     step = pl.program_id(0)
     near_steps = windows * pairs
     steps = 2 * near_steps
@@ -418,6 +429,24 @@
             cot_ref, cots_ref.at[other], cot_send.at[other], cot_recv.at[other], cot_peers[other]
         )
 
+    def early_trade(stage):
+        return send(
+            early_sent[stage],
+            early_arrived[stage],
+            early_sem.at[stage],
+            early_recv.at[stage],
+            {"tensor": flipped(tensor, (trades + 1) >> (stage + 1))},
+        )
+
+    def normed_trade(other):
+        return send(
+            early_normed,
+            others_ref.at[other],
+            normed_sem.at[other],
+            normed_recv.at[other],
+            cot_peers[other],
+        )
+
     def save(number, slot):
         return pltpu.make_async_copy(
             slots.at[number, slot], slots_ref.at[number, slot], save_sem.at[number, slot]
@@ -435,6 +464,32 @@
 
         for other in range(trades):
             cot_trade(other).start()
+
+    @pl.when(step == near_steps + pairs)
+    def _():
+        early_trade(0).start()
+
+    @pl.when(step == steps - 2)
+    def _():
+        kept = early_kept[...]
+        for stage in range(stages):
+            early_trade(stage).wait_recv()
+            kept = kept + early_arrived[stage][...].astype(F32)
+            if stage + 1 < stages:
+                half = kept.shape[0] // 2
+                early_sent[stage + 1][...] = kept[half:].astype(BF16)
+                early_trade(stage + 1).start()
+                kept = kept[:half]
+        middle = x_ref[...].astype(F32) + kept
+        middle_ref[...] = middle
+        normed = (normalise(middle)[0] * norms_ref[2:3, :] + norms_ref[3:4, :]).astype(BF16)
+        normed_ref[...] = normed
+        early_normed[...] = normed
+
+    @pl.when(step == steps - 1)
+    def _():
+        for other in range(trades):
+            normed_trade(other).start()
 
     relayed = step - (near_steps - 1)
 
@@ -511,11 +566,17 @@
         def _():
             mixed_rows[...] += term
 
-        @pl.when(pair == pairs - 1)
+        @pl.when(jnp.logical_and(pair == pairs - 1, number >= pairs))
         def _():
             half = kept_ref.shape[1]
             kept_ref[0] = mixed_rows[:half]
             sent_ref[0] = mixed_rows[half:].astype(BF16)
+
+        @pl.when(number == pairs - 1)
+        def _():
+            half = kept_ref.shape[1]
+            early_kept[...] = mixed_rows[:half]
+            early_sent[0][...] = mixed_rows[half:].astype(BF16)
 
     @pl.when(step == steps - 1)
     def _():
@@ -526,12 +587,16 @@
             for slot in range(4):
                 save(number, slot).wait()
 
+        for stage in range(stages):
+            early_trade(stage).wait_send()
         for other in range(trades):
             cot_trade(other).wait_send()
             cot_trade(other).wait_recv()
-
-
-def attend(queries, own_kv, w_att, cotangent, trades):
+            normed_trade(other).wait_send()
+            normed_trade(other).wait_recv()
+
+
+def attend(queries, own_kv, w_att, cotangent, tokens, norms, trades):
     windows, rows, cols = queries.shape
     width = w_att.shape[0]
     pairs = cols // PAIR
@@ -543,7 +608,10 @@
 
     anywhere = pl.BlockSpec(memory_space=pl.ANY)
     wide = pl.BlockSpec((1, rows, PAIR), lambda i: (far(i) // pairs, 0, far(i) % pairs))
-    half = pl.BlockSpec((1, rows // 2, width), lambda i: (far(i) // pairs, 0, 0))
+    half = pl.BlockSpec((1, rows // 2, width), lambda i: (jnp.maximum(far(i) // pairs, 1) - 1, 0, 0))
+    own_rows = tokens.shape[1]
+    own = pl.BlockSpec((own_rows, width), lambda i: (0, 0))
+    stages = [rows >> (stage + 1) for stage in range((trades + 1).bit_length() - 1)]
     state = pltpu.VMEM((near, rows, PAIR), F32)
     dma = pltpu.SemaphoreType.DMA
     return run(
@@ -553,13 +621,16 @@
             shaped((windows, rows, cols), BF16),
             shaped((windows, rows, cols), F32),
             shaped((windows, cols, rows), F32),
-            shaped((windows, rows // 2, width), F32),
-            shaped((windows, rows // 2, width), BF16),
+            shaped((windows - 1, rows // 2, width), F32),
+            shaped((windows - 1, rows // 2, width), BF16),
             shaped((near, 4, 2, rows, PAIR), BF16),
             shaped((trades,) + cotangent.shape, BF16),
+            shaped((own_rows, width), F32),
+            shaped((own_rows, width), BF16),
+            shaped((trades, own_rows, width), BF16),
         ],
         64 * windows * rows * rows * cols,
-        [queries, w_att, own_kv, cotangent],
+        [queries, w_att, own_kv, cotangent, tokens, norms],
         collective_id=0,
         grid=(2 * near,),
         in_specs=[
@@ -567,6 +638,8 @@
             pl.BlockSpec((width, PAIR), lambda i: (0, out_at + far(i) % pairs)),
             anywhere,
             anywhere,
+            pl.BlockSpec((None, own_rows, width), lambda i: (0, 0, 0)),
+            pl.BlockSpec(norms.shape, lambda i: (0, 0)),
         ],
         out_specs=[
             wide,
@@ -575,6 +648,9 @@
             half,
             half,
             anywhere,
+            anywhere,
+            own,
+            own,
             anywhere,
         ],
         scratch_shapes=[
@@ -589,19 +665,29 @@
             dma((near, 4)),
             dma((trades,)),
             dma((trades,)),
-        ],
+            pltpu.VMEM((rows // 2, width), F32),
+            pltpu.VMEM((own_rows, width), BF16),
+            dma((len(stages),)),
+            dma((len(stages),)),
+            dma((trades,)),
+            dma((trades,)),
+        ]
+        + [pltpu.VMEM((count, width), BF16) for count in stages] * 2,
     )
 
 
 def attend_back_kernel(windows, pairs, blocks, exp_scale, score_scale, *refs):
-    q_ref, wide_ref, log_ref, slots_ref, w_ref, cos_ref, sin_ref = refs[:7]
-    grad_refs = refs[7 : 7 + windows * blocks]
-    refs = refs[7 + windows * blocks :]
+    q_ref, wide_ref, log_ref, slots_ref, w_ref, cos_ref, sin_ref, last_ref = refs[:8]
+    trades = blocks - 1
+    known = (windows - 1) * blocks + 1
+    grad_refs = list(refs[8 : 8 + known])
+    refs = refs[8 + known :]
     sent_refs, refs = refs[:windows], refs[windows:]
     gq_ref, gk_ref, gv_ref, rows_ref = refs[:4]
     arrived_refs, refs = refs[4 : 4 + windows], refs[4 + windows :]
     dq_all, do_all, far_kept, far_sent, far_core, far_x, near_kept, near_sent, near_core = refs[:9]
-    send_sem, recv_sem, result_send, result_recv = refs[9:]
+    send_sem, recv_sem, result_send, result_recv, last_send, last_recv, last_others = refs[9:]
+    grad_refs += [last_others.at[other] for other in range(trades)]
     step = pl.program_id(0)
     count = windows * pairs
     seq, tensor = lax.axis_index("seq"), lax.axis_index("tensor")
@@ -628,9 +714,18 @@
             sent_refs[w], arrived_refs[w], result_send.at[w], result_recv.at[w], result_peer
         )
 
+    others = [{"tensor": flipped(tensor, other + 1)} for other in range(trades)]
+
+    def last_trade(other):
+        return send(
+            last_ref, last_others.at[other], last_send.at[other], last_recv.at[other], others[other]
+        )
+
     @pl.when(step == 0)
     def _():
-        greet([core_peer, far_peer, result_peer])
+        greet([core_peer, far_peer] + others)
+        for other in range(trades):
+            last_trade(other).start()
         for w in range(windows):
             result_trade(w).start()
 
@@ -678,6 +773,9 @@
 
         @pl.when(step == w * pairs)
         def _(w=w):
+            if w == windows - 1:
+                for other in range(trades):
+                    last_trade(other).wait_recv()
             at_row = 0
             for grad_ref in grad_refs[w * blocks : (w + 1) * blocks]:
                 rows_ref[0, at_row : at_row + grad_ref.shape[0], :] = grad_ref[...]
@@ -739,6 +837,8 @@
             for kind in range(3):
                 trade(kind, number).wait_send()
 
+        for other in range(trades):
+            last_trade(other).wait_send()
         for w in range(windows):
             result_trade(w).wait_send()
             result_trade(w).wait_recv()
@@ -751,8 +851,9 @@
     count = windows * pairs
     out_at = 3 * pairs
     score_scale = 1.0 / math.sqrt(HEAD_DIM)
-    blocks = len(grad_blocks[0])
+    blocks = lax.axis_size("tensor")
     grads = [block for one in grad_blocks for block in one]
+    last = grads[-1]
 
     def spot(lag, last=None):
         def index(i):
@@ -776,7 +877,7 @@
         + [shaped((windows, rows, width), BF16)]
         + [shaped(one.shape, BF16) for one in sent],
         160 * windows * rows * rows * cols,
-        [queries, wide, logs, slots_all, w_att, *tables, *grads, *sent],
+        [queries, wide, logs, slots_all, w_att, *tables, last, *grads, *sent],
         collective_id=2,
         grid=(2 * count + 2,),
         in_specs=[
@@ -790,6 +891,7 @@
             pl.BlockSpec((width, PAIR), lambda i: (0, out_at + jnp.minimum(i, count - 1) % pairs)),
             pl.BlockSpec((rows, PAIR), lambda i: (0, 0)),
             pl.BlockSpec((rows, PAIR), lambda i: (0, 0)),
+            anywhere,
         ]
         + [pl.BlockSpec(block.shape, lambda i: (0, 0)) for block in grads]
         + [anywhere] * windows,
@@ -802,7 +904,8 @@
         + [anywhere] * windows,
         scratch_shapes=[pltpu.VMEM((count, rows, PAIR), F32), pltpu.VMEM((count, rows, PAIR), BF16)]
         + [piece] * 7
-        + [dma((3, count)), dma((3, count)), dma((windows,)), dma((windows,))],
+        + [dma((3, count)), dma((3, count)), dma((windows,)), dma((windows,))]
+        + [dma((blocks - 1,)), dma((blocks - 1,)), pltpu.VMEM((blocks - 1,) + last.shape, BF16)],
     )
 
 
@@ -815,12 +918,18 @@
 
 
 def second_norm(x_rows, kept, arrived, norms):
+    args, in_specs = zip(*[plane(one) for one in (x_rows, kept, arrived, norms)])
+    rows, width = in_specs[1].block_shape[-2:]
+    full = pl.BlockSpec((rows, width), lambda i: (0, 0))
     return run(
         middle_kernel,
         "second_norm",
-        [shaped(kept.shape, F32), shaped(kept.shape, BF16)],
-        20 * kept.size,
-        [x_rows, kept, arrived, norms],
+        [shaped((rows, width), F32), shaped((rows, width), BF16)],
+        20 * rows * width,
+        args,
+        grid=(1,),
+        in_specs=list(in_specs),
+        out_specs=[full, full],
     )
 
 
@@ -911,6 +1020,7 @@
 
 
 def feed_first(x_blocks, cot_blocks, factor, weights):
+    blocks, block_specs = zip(*[plane(block) for block in (*x_blocks, *cot_blocks)])
     width = x_blocks[0].shape[1]
     rows = sum(block.shape[0] for block in x_blocks)
     step, steps, w_specs = feed_specs(weights)
@@ -923,11 +1033,9 @@
         + [shaped((rows, hidden_cols), BF16)] * 3
         + [shaped((rows, width), F32)] * 2,
         6 * rows * width * hidden_cols,
-        [factor, weights, weights, weights, *x_blocks, *cot_blocks],
+        [factor, weights, weights, weights, *blocks],
         grid=(steps,),
-        in_specs=[SCALAR]
-        + w_specs
-        + [pl.BlockSpec(array.shape, lambda i: (0, 0)) for array in (*x_blocks, *cot_blocks)],
+        in_specs=[SCALAR] + w_specs + list(block_specs),
         out_specs=[full] * 2 + [pl.BlockSpec((rows, step), lambda i: (0, i))] * 3 + [full] * 2,
     )
 
@@ -953,9 +1061,33 @@
     )
 
 
-def weights_kernel(windows, starts, *refs):
-    out_ref = refs[-1]
+def weights_kernel(windows, starts, masks, *refs):
+    inputs = 2 * windows * len(starts)
+    sources = refs[inputs : inputs + len(masks)]
+    out_ref = refs[inputs + len(masks)]
+    targets = refs[inputs + len(masks) + 1 : inputs + 2 * len(masks) + 1]
     at = pl.program_id(0)
+    trades = []
+    if masks:
+        send_sem, recv_sem = refs[inputs + 2 * len(masks) + 1 :]
+        tensor = lax.axis_index("tensor")
+        for source, target, kinds in zip(sources, targets, masks):
+            for number, mask in enumerate(kinds):
+                sems = (send_sem.at[len(trades)], recv_sem.at[len(trades)])
+                peer = {"tensor": flipped(tensor, mask)}
+                trades.append(send(source, target.at[number], *sems, peer))
+
+        @pl.when(at == 0)
+        def _():
+            greet(
+                [
+                    {"tensor": flipped(tensor, mask)}
+                    for mask in sorted({mask for kinds in masks for mask in kinds})
+                ]
+            )
+            for trade in trades:
+                trade.start()
+
     for group, (start, stop) in enumerate(starts):
         pairs = refs[2 * windows * group : 2 * windows * (group + 1)]
 
@@ -967,38 +1099,53 @@
                 total = term if total is None else total + term
             out_ref[...] = total.astype(BF16)
 
-
-def weight_grads(groups, step, name, first=0, parts=1):
+    if masks:
+
+        @pl.when(at == pl.num_programs(0) - 1)
+        def _():
+            for trade in trades:
+                trade.wait()
+
+
+def weight_grads(groups, step, name, first=0, parts=1, swaps=(), collective_id=None):
     windows = len(groups[0][0])
-    rows, width = groups[0][0][0].shape
     args, in_specs, starts = [], [], []
     at = 0
     for lefts, rights in groups:
-        count = rights[0].shape[1] // (step * parts)
-        args += [*lefts, *rights]
-        in_specs += [pl.BlockSpec((rows, width), lambda i: (0, 0))] * windows
-        in_specs += [
-            pl.BlockSpec(
-                (rows, step),
-                functools.partial(
-                    lambda at, count, i: (0, first * count + jnp.clip(i - at, 0, count - 1)),
-                    at,
-                    count,
-                ),
+        for left in lefts:
+            array, spec = plane(left)
+            rows, width = array.shape[-2:]
+            args.append(array)
+            in_specs.append(spec)
+        for right in rights:
+            cols = plane(right)[0].shape[-1]
+            count = cols // (step * parts)
+            place = functools.partial(
+                lambda at, count, i: (0, first * count + jnp.clip(i - at, 0, count - 1)), at, count
             )
-        ] * windows
+            array, spec = plane(right, (rows, step), place)
+            args.append(array)
+            in_specs.append(spec)
         starts.append((at, at + count))
         at += count
-    return run(
-        functools.partial(weights_kernel, windows, starts),
+    masks = [kinds for _, kinds in swaps]
+    anywhere = pl.BlockSpec(memory_space=pl.ANY)
+    out_shape = [shaped((width, at * step), BF16)]
+    out_shape += [shaped((len(kinds),) + array.shape, BF16) for array, kinds in swaps]
+    total = sum(len(kinds) for kinds in masks)
+    outs = run(
+        functools.partial(weights_kernel, windows, starts, masks),
         name,
-        shaped((width, at * step), BF16),
+        out_shape,
         2 * windows * rows * width * at * step,
-        args,
+        args + [array for array, _ in swaps],
+        collective_id=collective_id,
         grid=(at,),
-        in_specs=in_specs,
-        out_specs=pl.BlockSpec((width, step), lambda i: (0, i)),
-    )
+        in_specs=in_specs + [anywhere] * len(swaps),
+        out_specs=[pl.BlockSpec((width, step), lambda i: (0, i))] + [anywhere] * len(swaps),
+        scratch_shapes=[pltpu.SemaphoreType.DMA((total,))] * 2 if total else [],
+    )
+    return outs if swaps else outs[0]
 
 
 def norm_grad(kept_ref, arrived_ref, stream, gain, sums_ref):
@@ -1021,6 +1168,8 @@
 
 
 def second_norm_back(factor, kept, arrived, middle, cot_rows, norms):
+    args, in_specs = zip(*[plane(one) for one in (kept, arrived, middle, cot_rows, norms)])
+    full = pl.BlockSpec(kept.shape, lambda i: (0, 0))
     return run(
         middle_back_kernel,
         "second_norm_back",
@@ -1030,8 +1179,10 @@
             shaped((2, kept.shape[1]), F32),
         ],
         40 * kept.size,
-        [factor, kept, arrived, middle, cot_rows, norms],
-        in_specs=[SCALAR] + [pl.BlockSpec(memory_space=pltpu.VMEM)] * 5,
+        [factor, *args],
+        grid=(1,),
+        in_specs=[SCALAR, *in_specs],
+        out_specs=[full, full, pl.BlockSpec((2, kept.shape[1]), lambda i: (0, 0))],
     )
 
 
@@ -1076,8 +1227,9 @@
 
 def first_norm_back(window, windows, kept, arrived, x_rows, grad_middle, norms, earlier):
     rows, width = kept.shape
-    args = [kept, arrived, x_rows, grad_middle, norms] + ([] if earlier is None else [earlier])
-    whole = [pl.BlockSpec(array.shape, lambda i: (0, 0)) for array in args[:5]]
+    args, whole = zip(*[plane(one) for one in (kept, arrived, x_rows, grad_middle, norms)])
+    args, whole = list(args), list(whole)
+    args += [] if earlier is None else [earlier]
     return run(
         functools.partial(input_back_kernel, window),
         "first_norm_back",
@@ -1359,28 +1511,45 @@
 
     token_blocks = [tokens] + [arrived_tokens[other] for other in range(tensor_size - 1)]
     normed_rows, queries, own_kv = project(token_blocks, norms, w_att, cosine, sine)
-    attended, wide_attended, logs, kept_all, sent_all, slots_all, cots = attend(
-        queries, own_kv, w_att, cotangent, tensor_size - 1
-    )
+    (
+        attended,
+        wide_attended,
+        logs,
+        kept_all,
+        sent_all,
+        slots_all,
+        cots,
+        first_middle,
+        first_normed,
+        first_others,
+    ) = attend(queries, own_kv, w_att, cotangent, tokens, norms, tensor_size - 1)
     last_ffn = lax.all_gather(hold(last_ffn, kept_all), shards, axis=0, tiled=True)
+    others = range(tensor_size - 1)
     cot_blocks = [
-        [cotangent[w]] + [cots[other, w] for other in range(tensor_size - 1)] for w in windows
+        [(cotangent, (w,))] + [(cots, (other, w)) for other in others] for w in windows
     ]
-    middles, mid_blocks = [], []
-    for w in windows:
+    middles = [first_middle]
+
+    begun = [
+        feed_first(
+            [first_normed] + [first_others[other] for other in others],
+            cot_blocks[0],
+            factors[0],
+            first_ffn,
+        )
+    ]
+    for w in windows[1:]:
+        kept, arrived = scatter_pair(kept_all[w - 1], sent_all[w - 1], "tensor")
         middle, normed_mid = second_norm(
-            tokens[w], *scatter_pair(kept_all[w], sent_all[w], "tensor"), norms
+            (tokens, (w,)), hold(kept, begun[-1]), arrived, norms
         )
         middles.append(middle)
-        mid_blocks.append(spread(normed_mid, "tensor"))
-
-    begun = []
-    for w in windows:
-        blocks = hold(mid_blocks[w], begun[-1] if begun else ())
-        begun.append(feed_first(blocks, cot_blocks[w], factors[w], first_ffn))
+        begun.append(
+            feed_first(spread(normed_mid, "tensor"), cot_blocks[w], factors[w], first_ffn)
+        )
     step = min(512, part)
 
-    def feed_weights(done, half):
+    def feed_weights(done, half, swaps, collective_id):
         return weight_grads(
             [
                 ([one[0] for one in done], [one[3] for one in done]),
@@ -1391,34 +1560,47 @@
             "feed_weights",
             half,
             2,
-        )
-
-    g_first_part = feed_weights(begun, 0)
+            swaps,
+            collective_id,
+        )
+
+    g_first_part = feed_weights(begun, 0, (), None)
     g_first = lax.psum_scatter(g_first_part, shards, scatter_dimension=0, tiled=True)
     fed = []
     for w in windows:
         x_rows, gy_rows, *parts = hold(begun[w], fed[-1] if fed else g_first_part)
         ended = feed_last(x_rows, gy_rows, parts[3:], parts[:3], last_ffn)
         fed.append((x_rows, gy_rows, *ended))
-    grad_middles, grad_mid_blocks, second_sums = [], [], []
-
-    def through_second_norm(w, *after):
+    grad_middles, second_sums = [], []
+
+    def through_second_norm(w, kept, arrived):
+        grad_middle, low, sums = second_norm_back(
+            factors[w], kept, arrived, middles[w], (cotangent, (w,)), norms
+        )
+        grad_middles.append(grad_middle)
+        second_sums.append(sums)
+        return low
+
+    lows = []
+    for w in windows[:-1]:
         kept, arrived = scatter_pair(fed[w][7], fed[w][8], "tensor")
-        grad_middle, low, sums = second_norm_back(
-            factors[w], hold(kept, *after), arrived, middles[w], cotangent[w], norms
-        )
-        grad_middles.append(grad_middle)
-        grad_mid_blocks.append(spread(low, "tensor"))
-        second_sums.append(sums)
-
-    for w in windows[:-1]:
-        through_second_norm(w)
-    g_ffn_part = feed_weights(hold(fed, grad_middles), 1)
-    g_last = lax.psum_scatter(g_ffn_part, shards, scatter_dimension=0, tiled=True)
-    through_second_norm(windows[-1], g_ffn_part)
+        lows.append(through_second_norm(w, hold(kept, fed[w + 1]), arrived))
+    masks = [other + 1 for other in others]
+    g_last_part, arrived, *arrived_lows = feed_weights(
+        hold(fed, grad_middles),
+        1,
+        [(fed[-1][8], [tensor_size // 2])] + [(low, masks) for low in lows],
+        4,
+    )
+    g_last = lax.psum_scatter(g_last_part, shards, scatter_dimension=0, tiled=True)
+    kept, arrived = later_pair(fed[-1][7], arrived[0], "tensor")
+    last_low = through_second_norm(windows[-1], hold(kept, g_last_part), arrived)
+    grad_mid_blocks = [
+        [low] + [arrived[other] for other in others] for low, arrived in zip(lows, arrived_lows)
+    ] + [[last_low]]
 
     grad_q, grad_k, grad_v, grad_mid_rows, *arrived_results = attend_back(
-        hold(queries, g_ffn_part),
+        hold(queries, g_last_part),
         wide_attended,
         logs,
         slots_all,
@@ -1440,10 +1622,10 @@
         first_parts.append(scatter_pair(kept, sent, "tensor"))
     g_att_part = weight_grads(
         [
-            ([normed_rows[w] for w in windows], [grad[w] for w in windows])
+            ([(normed_rows, (w,)) for w in windows], [(grad, (w,)) for w in windows])
             for grad in (grad_q, grad_k, grad_v)
         ]
-        + [([grad_mid_rows[w] for w in windows], [attended[w] for w in windows])],
+        + [([(grad_mid_rows, (w,)) for w in windows], [(attended, (w,)) for w in windows])],
         head_cols,
         "attend_weights",
     )
@@ -1456,7 +1638,7 @@
             windows_here,
             hold(kept, g_att_part),
             arrived,
-            tokens[w],
+            (tokens, (w,)),
             grad_middles[w],
             norms,
             input_grad,

time: 501 us -> 458 us (0.914)
  waiting for transfers between devices: 48.9 us -> 11 us
  local copies, waits for them, and re-layouts: 31.7 us -> 14 us
  Pallas kernels: 377 us -> 394 us
    ppermute x10 -> x5, waiting for transfers between devices: 48.8 us -> 10.9 us  [swap(): return lax.ppermute(array, axis, [(i, i ^ bit) for i in range(size)])]
    pallas_call x21 -> x20, Pallas kernels: 377 us -> 394 us  [run(): pl.pallas_call(kernel, out_shape=out_shape, compiler_params=pltpu.Compile...]
    squeeze x11 -> x0, local copies, waits for them, and re-layouts: 13.4 us -> none  [the longest x3 3.24 us: local(): grad[w]]
    ppermute x10 -> x5, starting transfers between devices: 10.5 us -> 5.9 us  [swap(): return lax.ppermute(array, axis, [(i, i ^ bit) for i in range(size)])]
  transfers between devices with their start and end apart: 14 -> 9, of which waited for: 5 -> 1; matrix products, arithmetic and copies ran while one was open for 5% -> 3% of each run, Pallas kernels for 77% -> 88%
where the time goes in v6:
time: 458 us; the launch traced here: 450 us
  Pallas kernels  394 us (86%)
  between operations  14.6 us (3%)
  local copies, waits for them, and re-layouts  14 us (3%)
  waiting for transfers between devices  11 us (2%)
  other arithmetic  9.17 us (2%)
  starting transfers between devices  6.7 us (1%)
    pallas_call x20, Pallas kernels, run(): pl.pallas_call(kernel, out_shape=out_shape, compiler_params=pltpu.Compile...  394 us
    ppermute x5, waiting for transfers between devices, swap(): return lax.ppermute(array, axis, [(i, i ^ bit) for i in range(size)])  10.9 us
  transfers between devices with their start and end apart: 9, of which 1 were waited for; matrix products, arithmetic and copies ran while one was open for 3% of the time, Pallas kernels for 88%

profile of v6, /device:TPU:0, one launch (start us, length us, event | category | flops | bytes accessed | tf_op | source)
XLA Modules:
  0.0 449.7 jit_solution(1114559618217234005)
XLA Ops:
  7.3 0.0 all-gather.5.cloned.1.call-start
  7.3 1.1 fusion.8
  8.4 1.1 fusion.6
  9.5 0.8 pad_maximum_fusion.1
  10.3 0.0 all-gather.5.cloned.1.call-update
  10.3 0.0 all-gather.3.cloned.1.call-start
  10.5 0.2 fusion.1
  10.7 0.6 fusion.3
  11.3 0.6 broadcast.63
  12.0 0.7 pad_maximum_fusion.2.att_ref
  12.7 51.8 %gather.1 = (bf16[1024,2048]{1,0:T(8,128)(2,1)}, f32[8,1024]{1,0:T(8,128)}, bf16[1,2,256,1024]{3,2,1,0:T(8,128)(2,1)}) custom-call(bf16[64,2048]{1,0:T(8,128)(2,1)} %pad_maximum_fusion.2.att_ref, f32[8,128]{1,0:T(8,128)} %copy-done.8, bf16[2,256,1024]{2,1,0:T(8,128)(2,1)} %x_ref.5), custom_call_target="tpu_custom_call" | custom-call | bytes 6590464 | tf_op jit(solution)/shard_map/gather/pallas_call | solution.py:80
  64.6 1.0 fusion
  65.6 1.0 pad_maximum_fusion.3.cos_ref.refs_5_
  66.6 1.0 pad_maximum_fusion.4.sin_ref.refs_6_
  67.5 8.4 %project.1 = (bf16[2,512,1024]{2,1,0:T(8,128)(2,1)}, bf16[2,512,512]{2,1,0:T(8,128)(2,1)}, bf16[2,2,512,512]{3,2,1,0:T(8,128)(2,1)}) custom-call(f32[8,1024]{1,0:T(8,128)} %get-tuple-element.139.norms_ref.refs_5_, bf16[1024,2048]{1,0:T(8,128)(2,1)} %get-tuple-element.140.w_ref.refs_1_.refs_4_, f32[512,128]{1,0:T(8,128)} %pad_maximum_fusion.3.cos_ref.refs_5_, ...), custom_call_target="tpu_custom_call" | custom-call | flops 3221225472 | bytes 12091392 | tf_op jit(solution)/shard_map/project/pallas_call | solution.py:80
  75.9 0.8 pad_maximum_fusion
  76.7 70.0 %attend.1 = (bf16[2,512,512]{2,1,0:T(8,128)(2,1)}, f32[2,512,512]{2,1,0:T(8,128)}, f32[2,512,512]{2,1,0:T(8,128)}, f32[1,256,1024]{2,1,0:T(8,128)}, bf16[1,256,1...) custom-call(bf16[2,512,512]{2,1,0:T(8,128)(2,1)} %get-tuple-element., ...), custom_call_target="tpu_custom_call" | custom-call | flops 17179869184 | bytes 27820032 | tf_op jit(solution)/shard_map/attend/pallas_call | solution.py:80
  146.7 0.0 all-gather.3.cloned.1.call-update
  146.7 0.5 reduce-scatter.3.cloned.1.call-start
  147.2 0.2 collective-permute-start
  147.4 1.2 slice.112
  148.6 0.7 multiply_divide_fusion
  149.2 0.6 fusion.9
  149.8 15.3 %feed_first.2 = (bf16[512,1024]{1,0:T(8,128)(2,1)}, bf16[512,1024]{1,0:T(8,128)(2,1)}, bf16[512,2048]{1,0:T(8,128)(2,1)}, bf16[512,2048]{1,0:T(8,128)(2,1)}, bf1...) custom-call(f32[1,1]{1,0:T(1,128)} %bitcast.8.factor_ref, ...), custom_call_target="tpu_custom_call" | custom-call | flops 6442450944 | bytes 34603012 | tf_op jit(solution)/shard_map/feed_first/pallas_call | solution.py:80
  165.1 0.0 copy-start.1
  165.1 0.8 copy-done.1
  165.9 2.8 second_norm.1
  168.8 2.0 collective-permute-start.1
  170.7 10.9 %collective-permute-done.1.refs_4_ = bf16[256,1024]{1,0:T(8,128)(2,1)S(1)} collective-permute-done((bf16[256,1024]{1,0:T(8,128)(2,1)}, bf16[256,1024]{1,0:T(8,128)(2,1)S(1)}, u32[]{:S(2)}, u32[]{:S(2)}) %collective-permute-start.1) | collective-permute-done | bytes 524320 | tf_op jit(solution)/shard_map/ppermute | solution.py:45
  181.7 0.8 copy-done.16
  182.4 15.1 %feed_first.3 = (bf16[512,1024]{1,0:T(8,128)(2,1)}, bf16[512,1024]{1,0:T(8,128)(2,1)}, bf16[512,2048]{1,0:T(8,128)(2,1)}, bf16[512,2048]{1,0:T(8,128)(2,1)}, bf1...) custom-call(f32[1,1]{1,0:T(1,128)} %bitcast.10.factor_ref, ...), custom_call_target="tpu_custom_call" | custom-call | flops 6442450944 | bytes 34603012 | tf_op jit(solution)/shard_map/feed_first/pallas_call | solution.py:80
  197.6 13.7 %feed_weights.2 = bf16[1024,3072]{1,0:T(8,128)(2,1)} custom-call(bf16[512,1024]{1,0:T(8,128)(2,1)} %get-tuple-element.197.refs_0_.refs_4_.refs_3_, bf16[512,1024]{1,0:T(8,128)(2,1)} %get-tuple-element.198.refs_1_.refs_5_.refs_3_, bf16[512,2048]{1,0:T(8,128)(2,1)} %get-tuple-element.170.refs_2_.refs_8_, bf16[512,2048]{1,0:T(8,128)(2,1)} %get-tuple-element.186.refs_3_.refs_8_, ...), custom_call_target="tpu_custom_call" | custom-call | flops 6442450944 | bytes 25165824 | tf_op jit(solution)/shard_map/feed_weights/pallas_call | solution.py:80
  211.3 0.0 reduce-scatter.3.cloned.1.call-update
  211.3 0.2 reduce-scatter.5.cloned.1.call-start
  211.6 0.0 all-gather.3.cloned.1.call-done.refs_0_.refs_1_.refs_2_
  211.6 14.9 %feed_last.2 = (bf16[512,2048]{1,0:T(8,128)(2,1)}, bf16[512,2048]{1,0:T(8,128)(2,1)}, bf16[512,2048]{1,0:T(8,128)(2,1)}, f32[256,1024]{1,0:T(8,128)}, bf16[256,1...) custom-call(bf16[1024,3072]{1,0:T(8,128)(2,1)} %all-gather.3.cloned., ...), custom_call_target="tpu_custom_call", output_to_operand_aliasing={{0}: (7, {}), {1}: (8, {}), {2}: (9, {})} | custom-call | flops 6442450944 | bytes 40894464 | tf_op jit(solution)/shard_map/feed_last/pallas_call | solution.py:80
  226.5 1.7 collective-permute-start.2
  228.2 15.5 %feed_last.3 = (bf16[512,2048]{1,0:T(8,128)(2,1)}, bf16[512,2048]{1,0:T(8,128)(2,1)}, bf16[512,2048]{1,0:T(8,128)(2,1)}, f32[256,1024]{1,0:T(8,128)}, bf16[256,1...) custom-call(bf16[1024,3072]{1,0:T(8,128)(2,1)} %all-gather.3.cloned., ...), custom_call_target="tpu_custom_call", output_to_operand_aliasing={{0}: (7, {}), {1}: (8, {}), {2}: (9, {})} | custom-call | flops 6442450944 | bytes 40894464 | tf_op jit(solution)/shard_map/feed_last/pallas_call | solution.py:80
  243.8 0.0 copy-start.2
  243.8 0.8 copy-done.2
  244.6 4.5 %second_norm_back.2 = (f32[256,1024]{1,0:T(8,128)}, bf16[256,1024]{1,0:T(8,128)(2,1)}, f32[2,1024]{1,0:T(2,128)}) custom-call(f32[1,1]{1,0:T(1,128)} %bitcast.8.factor_ref, f32[256,1024]{1,0:T(8,128)} %get-tuple-element.195.kept_ref, bf16[256,1024]{1,0:T(8,128)(2,1)} %copy-done.2, f32[256,1024]{1,0:T(8,128)} %get-tuple-element.144.middle_ref.refs_0_, ...), custom_call_target="tpu_custom_call" | custom-call | flops 10485760 | bytes 5283844 | tf_op jit(solution)/shard_map/second_norm_back/pallas_call | solution.py:80
  249.1 28.5 %feed_weights.3 = (bf16[1024,3072]{1,0:T(8,128)(2,1)}, bf16[1,256,1024]{2,1,0:T(8,128)(2,1)}, bf16[1,256,1024]{2,1,0:T(8,128)(2,1)}) custom-call(bf16[512,1024]{1,0:T(8,128)(2,1)} %get-tuple-element.197.refs_0_.refs_4_.refs_3_, bf16[512,1024]{1,0:T(8,128)(2,1)} %get-tuple-element.198.refs_1_.refs_5_.refs_3_, bf16[512,2048]{1,0:T(8,128)(2,1)} %get-tuple-element.199.refs_2_, ...), custom_call_target="tpu_custom_call" | custom-call | flops 6442450944 | bytes 27262976 | tf_op jit(solution)/shard_map/feed_weights/pallas_call | solution.py:80
  277.6 0.0 reduce-scatter.5.cloned.1.call-update
  277.6 4.8 %second_norm_back.3 = (f32[256,1024]{1,0:T(8,128)}, bf16[256,1024]{1,0:T(8,128)(2,1)}, f32[2,1024]{1,0:T(2,128)}) custom-call(f32[1,1]{1,0:T(1,128)} %bitcast.10.factor_ref, f32[256,1024]{1,0:T(8,128)} %get-tuple-element.213.kept_ref, bf16[256,1024]{1,0:T(8,128)(2,1)} %bitcast.28, f32[256,1024]{1,0:T(8,128)} %get-tuple-element.215.middle_ref.refs_3_, ...), custom_call_target="tpu_custom_call" | custom-call | flops 10485760 | bytes 5283844 | tf_op jit(solution)/shard_map/second_norm_back/pallas_call | solution.py:80
  282.4 74.3 %attend_back.1 = (bf16[2,512,512]{2,1,0:T(8,128)(2,1)}, bf16[2,512,512]{2,1,0:T(8,128)(2,1)}, bf16[2,512,512]{2,1,0:T(8,128)(2,1)}, bf16[2,512,1024]{2,1,0:T(8,1...) custom-call(bf16[2,512,512]{2,1,0:T(8,128)(2,1)} %get-tuple-element.209.refs_0_, ...), custom_call_target="tpu_custom_call" | custom-call | flops 42949672960 | bytes 27787264 | tf_op jit(solution)/shard_map/attend_back/pallas_call | solution.py:80
  356.7 5.2 %turn_back.3 = (f32[256,1024]{1,0:T(8,128)}, bf16[256,1024]{1,0:T(8,128)(2,1)}) custom-call(bf16[2,512,512]{2,1,0:T(8,128)(2,1)} %get-tuple-element.220.gq_ref.refs_2_.refs_3_, bf16[2,512,512]{2,1,0:T(8,128)(2,1)} %get-tuple-element.221.gk_ref.refs_6_.refs_7_, bf16[2,512,512]{2,1,0:T(8,128)(2,1)} %get-tuple-element.222.gv_ref.refs_10_.refs_11_, ...), custom_call_target="tpu_custom_call" | custom-call | flops 1610612736 | bytes 8912896 | tf_op jit(solution)/shard_map/turn_back/pallas_call | solution.py:80
  361.9 0.4 collective-permute-start.4
  362.3 5.2 %turn_back.2 = (f32[256,1024]{1,0:T(8,128)}, bf16[256,1024]{1,0:T(8,128)(2,1)}) custom-call(bf16[2,512,512]{2,1,0:T(8,128)(2,1)} %get-tuple-element.220.gq_ref.refs_2_.refs_3_, bf16[2,512,512]{2,1,0:T(8,128)(2,1)} %get-tuple-element.221.gk_ref.refs_6_.refs_7_, bf16[2,512,512]{2,1,0:T(8,128)(2,1)} %get-tuple-element.222.gv_ref.refs_10_.refs_11_, ...), custom_call_target="tpu_custom_call" | custom-call | flops 1610612736 | bytes 8912896 | tf_op jit(solution)/shard_map/turn_back/pallas_call | solution.py:80
  367.5 1.6 collective-permute-start.3
  369.1 11.6 %attend_weights.1.part_ref = bf16[1024,2048]{1,0:T(8,128)(2,1)} custom-call(bf16[2,512,1024]{2,1,0:T(8,128)(2,1)} %get-tuple-element.224.refs_0_.refs_1_.refs_4_.refs_5_.refs_8_.refs_9_, bf16[2,512,1024]{2,1,0:T(8,128)(2,1)} %get-tuple-element.224.refs_0_.refs_1_.refs_4_.refs_5_.refs_8_.refs_9_, ...), custom_call_target="tpu_custom_call" | custom-call | flops 4294967296 | bytes 29360128 | tf_op jit(solution)/shard_map/attend_weights/pallas_call | solution.py:80
  380.8 3.7 results.1
  384.4 0.8 copy-done
  385.2 3.7 first_norm_back.2
  388.9 0.8 copy-done.3
  389.7 3.7 first_norm_back.3
  393.4 41.4 %reduce_grads.1 = (f32[64,2048]{1,0:T(8,128)}, f32[8,128]{1,0:T(8,128)}) custom-call(bf16[1024,2048]{1,0:T(8,128)(2,1)} %attend_weights.1.part_ref, f32[2,1024]{1,0:T(2,128)} %get-tuple-element.235.refs_0_, f32[2,1024]{1,0:T(2,128)} %get-tuple-element.236.refs_1_, f32[2,1024]{1,0:T(2,128)} %get-tuple-element.237.refs_2_, f32[2,1024]{1,0:T(2,128)} %get-tuple-element.238.refs_3_), custom_call_target="tpu_custom_call" | custom-call | bytes 4755456 | tf_op jit(solution)/shard_map/reduce_grads/pallas_call | solution.py:80
  434.8 1.3 slice_bitcast_fusion.1
  436.2 1.9 slice_bitcast_fusion
  438.1 1.1 fusion.4
  439.1 0.0 reduce-scatter.5.cloned.1.call-done
  439.2 1.1 fusion.5
  440.2 0.8 convert_bitcast_fusion
  441.1 0.8 maximum_convert_fusion.1
  441.9 0.8 maximum_convert_fusion
  (38 shorter events, 0.1 us)
Async XLA Ops:
  7.2 3.2 copy-start.10
  7.2 3.2 copy-start.11
  7.2 3.2 copy-start.12
  7.2 3.2 copy-start.13
  7.2 3.2 copy-start.9
  7.2 3.2 copy-start.14
  7.2 3.4 copy-start.15
  7.3 4.7 %copy-start.4 = (bf16[512,64]{0,1:T(8,128)(2,1)S(1)}, bf16[512,64]{0,1:T(8,128)(2,1)}, u32[]{:S(2)}) copy-start(bf16[512,64]{0,1:T(8,128)(2,1)} %param.30) | copy-start | bytes 196612
  7.3 4.7 %copy-start.5 = (bf16[64,512]{1,0:T(8,128)(2,1)S(1)}, bf16[64,512]{1,0:T(8,128)(2,1)}, u32[]{:S(2)}) copy-start(bf16[64,512]{1,0:T(8,128)(2,1)} %param.29) | copy-start | bytes 196612
  7.3 4.7 %copy-start.6 = (bf16[64,512]{1,0:T(8,128)(2,1)S(1)}, bf16[64,512]{1,0:T(8,128)(2,1)}, u32[]{:S(2)}) copy-start(bf16[64,512]{1,0:T(8,128)(2,1)} %param.28) | copy-start | bytes 196612
  7.3 4.7 %copy-start.7 = (bf16[64,512]{1,0:T(8,128)(2,1)S(1)}, bf16[64,512]{1,0:T(8,128)(2,1)}, u32[]{:S(2)}) copy-start(bf16[64,512]{1,0:T(8,128)(2,1)} %param.27) | copy-start | bytes 196612
  7.3 142.5 %all-gather.5.cloned.1.call-start = ((), (), s32[]{:S(2)}) async-start(), calls=%async_computation.3 | async-start | bytes 6684672 | tf_op jit(solution)/shard_map/all_gather | solution.py:1499
  10.3 201.2 %all-gather.3.cloned.1.call-start = ((), (), s32[]{:S(2)}) async-start(), calls=%async_computation.2 | async-start | bytes 6684672 | tf_op jit(solution)/shard_map/all_gather | solution.py:1526
  12.0 0.8 copy-start.8
  146.7 291.4 %reduce-scatter.3.cloned.1.call-start = ((), (), s32[]{:S(2)}) async-start(), calls=%async_computation.4 | async-start | bytes 6684672 | tf_op jit(solution)/shard_map/reduce_scatter | solution.py:1568
  147.2 17.9 %collective-permute-start = (bf16[256,1024]{1,0:T(8,128)(2,1)}, bf16[256,1024]{1,0:T(8,128)(2,1)S(1)}, u32[]{:S(2)}, u32[]{:S(2)}) collective-permute-start(bf16[256,1024]{1,0:T(8,128)(2,1)} %bitcast.36), channel_id=1, source_target_pairs={{0,1},{1,0},{2,3},{3,2},{4,5},{5,4},{6,7},{7,6},{8,9},{9,8},{10,11... | collective-permute-start | bytes 1572872 | tf_op jit(solution)/shard_map/ppermute | solution.py:45
  165.1 0.8 copy-start.1
  168.8 12.9 %collective-permute-start.1 = (bf16[256,1024]{1,0:T(8,128)(2,1)}, bf16[256,1024]{1,0:T(8,128)(2,1)S(1)}, u32[]{:S(2)}, u32[]{:S(2)}) collective-permute-start(bf16[256,1024]{1,0:T(8,128)(2,1)} %get-tuple-element.159.refs_3_), channel_id=1, source_target_pairs={{0,1},{1,0},{2,3},{3,2},{4,5},{5,4},{6,7},{7,6},{8,9},{9,8},{10,11... | collective-permute-start | bytes 1572872 | tf_op jit(solution)/shard_map/ppermute | solution.py:45
  181.7 0.8 copy-start.16
  211.3 227.8 %reduce-scatter.5.cloned.1.call-start = ((), (), s32[]{:S(2)}) async-start(), calls=%async_computation.5 | async-start | bytes 6684672 | tf_op jit(solution)/shard_map/reduce_scatter | solution.py:1595
  226.5 17.3 %collective-permute-start.2 = (bf16[256,1024]{1,0:T(8,128)(2,1)}, bf16[256,1024]{1,0:T(8,128)(2,1)S(1)}, u32[]{:S(2)}, u32[]{:S(2)}) collective-permute-start(bf16[256,1024]{1,0:T(8,128)(2,1)} %get-tuple-element.178), channel_id=1, source_target_pairs={{0,1},{1,0},{2,3},{3,2},{4,5},{5,4},{6,7},{7,6},{8,9},{9,8},{10,11... | collective-permute-start | bytes 1572872 | tf_op jit(solution)/shard_map/ppermute | solution.py:45
  243.8 0.8 copy-start.2
  361.9 22.6 %collective-permute-start.4 = (bf16[256,1024]{1,0:T(8,128)(2,1)}, bf16[256,1024]{1,0:T(8,128)(2,1)S(1)}, u32[]{:S(2)}, u32[]{:S(2)}) collective-permute-start(bf16[256,1024]{1,0:T(8,128)(2,1)} %get-tuple-element.232), channel_id=1, source_target_pairs={{0,1},{1,0},{2,3},{3,2},{4,5},{5,4},{6,7},{7,6},{8,9},{9,8},{10,11... | collective-permute-start | bytes 1572872 | tf_op jit(solution)/shard_map/ppermute | solution.py:45
  367.5 21.4 %collective-permute-start.3 = (bf16[256,1024]{1,0:T(8,128)(2,1)}, bf16[256,1024]{1,0:T(8,128)(2,1)S(1)}, u32[]{:S(2)}, u32[]{:S(2)}) collective-permute-start(bf16[256,1024]{1,0:T(8,128)(2,1)} %get-tuple-element.228), channel_id=1, source_target_pairs={{0,1},{1,0},{2,3},{3,2},{4,5},{5,4},{6,7},{7,6},{8,9},{9,8},{10,11... | collective-permute-start | bytes 1572872 | tf_op jit(solution)/shard_map/ppermute | solution.py:45
  384.4 0.8 copy-start
  388.9 0.8 copy-start.3
Sparse Core Ops, SparseCore 0:
  11.0 77.3 all-gather.4
  146.8 60.2 all-gather.2
  211.5 84.7 reduce-scatter.2
  300.6 94.9 reduce-scatter.4

commit v7 on v6

--- a/solution.py
+++ b/solution.py
@@ -313,11 +313,11 @@
     for other in range(trades):
         pair_trade(other).start()
     own_copies[1].start()
+    att.start(0, 1, 3, 7)
     own_copies[1].wait()
     for other in range(trades):
         pair_trade(other).wait_recv()
-    for route in (small, att):
-        route.start(0, 1, 3, 7)
+    small.start(0, 1, 3, 7)
     own_copies[0].start()
     own_copies[2].start()
     for other in range(trades):
@@ -401,6 +401,9 @@
     step = pl.program_id(0)
     near_steps = windows * pairs
     steps = 2 * near_steps
+    turn = step % (2 * pairs)
+    is_far = turn >= pairs
+    number = step // (2 * pairs) * pairs + turn % pairs
     seq, tensor = lax.axis_index("seq"), lax.axis_index("tensor")
     core_peer = {"seq": flipped(seq, 1)}
     far_peer = {"seq": flipped(seq, 2)}
@@ -465,11 +468,11 @@
         for other in range(trades):
             cot_trade(other).start()
 
-    @pl.when(step == near_steps + pairs)
+    @pl.when(step == 2 * pairs)
     def _():
         early_trade(0).start()
 
-    @pl.when(step == steps - 2)
+    @pl.when(step == min(3 * pairs + 1, steps - 2))
     def _():
         kept = early_kept[...]
         for stage in range(stages):
@@ -486,70 +489,71 @@
         normed_ref[...] = normed
         early_normed[...] = normed
 
-    @pl.when(step == steps - 1)
+    @pl.when(step == min(3 * pairs + 2, steps - 1))
     def _():
         for other in range(trades):
             normed_trade(other).start()
 
-    relayed = step - (near_steps - 1)
-
-    @pl.when(jnp.logical_and(relayed >= 0, relayed < near_steps))
+    relayed = step // (2 * pairs) * pairs + turn - (pairs - 1)
+
+    @pl.when(jnp.logical_and(turn >= pairs - 1, turn < 2 * pairs - 1))
     def _():
         trade(relayed, 2).wait_recv()
         trade(relayed, 3).start()
         save(relayed, 2).start()
 
+    @pl.when(jnp.logical_not(is_far))
+    def _():
+        own_copy(number).wait()
+        trade(number, 1).wait_recv()
+        save(number, 0).start()
+        save(number, 1).start()
+        acc_all[number] = jnp.zeros(acc_all.shape[1:], F32)
+        total_all[number] = jnp.zeros(acc_all.shape[1:], F32)
+        top_all[number] = jnp.full(acc_all.shape[1:], -1e30, F32)
+
+    @pl.when(is_far)
+    def _():
+        trade(number, 3).wait_recv()
+        save(number, 3).start()
+
     query = q_ref[0]
     is_first = first_head(query.shape)
-
-    def partial_of(number, used, carried_top):
-        outs, tops = [], []
-        for head in range(2):
-            mine = is_first if head == 0 else jnp.logical_not(is_first)
-            own_query = jnp.where(mine, query, jnp.zeros_like(query))
-            scores = [dot_nt(own_query, slots[number, slot, 0]) for slot in used]
-            top = scores[0].max(axis=1, keepdims=True)
-            for one in scores[1:]:
-                top = jnp.maximum(top, one.max(axis=1, keepdims=True))
-            if carried_top is not None:
-                at = head * HEAD_DIM
-                top = jnp.maximum(top, carried_top[:, at : at + 1])
-            shift = top * exp_scale
-            mixed = None
-            for one, slot in zip(scores, used):
-                weight = jnp.exp2(one * exp_scale - shift).astype(BF16)
-                value = slots[number, slot, 1]
-                lane_first = first_head(value.shape)
-                lane_mine = lane_first if head == 0 else jnp.logical_not(lane_first)
-                term = dot_nn(weight, jnp.where(lane_mine, value, jnp.ones_like(value)))
-                mixed = term if mixed is None else mixed + term
-            outs.append(mixed)
-            tops.append(jnp.broadcast_to(top, mixed.shape))
-        acc = jnp.where(is_first, outs[0], outs[1])
-        total = pltpu.roll(jnp.where(is_first, outs[1], outs[0]), HEAD_DIM, 1)
-        return acc, jnp.where(is_first, tops[0], tops[1]), total
-
-    @pl.when(step < near_steps)
-    def _():
-        own_copy(step).wait()
-        trade(step, 1).wait_recv()
-        save(step, 0).start()
-        save(step, 1).start()
-        acc, top, total = partial_of(step, (0, 1), None)
-        acc_all[step] = acc
-        top_all[step] = top
-        total_all[step] = total
-
-    @pl.when(step >= near_steps)
-    def _():
-        number = step - near_steps
-        trade(number, 3).wait_recv()
-        save(number, 3).start()
-        carried_top = top_all[number]
-        acc, top, total = partial_of(number, (2, 3), carried_top)
-        fade = jnp.exp2((carried_top - top) * exp_scale)
-        acc = acc + acc_all[number] * fade
-        total = total + total_all[number] * fade
+    base = jnp.where(is_far, 2, 0)
+    carried_top = top_all[number]
+    outs, tops = [], []
+    for head in range(2):
+        mine = is_first if head == 0 else jnp.logical_not(is_first)
+        own_query = jnp.where(mine, query, jnp.zeros_like(query))
+        scores = [dot_nt(own_query, slots[number, base + slot, 0]) for slot in range(2)]
+        at = head * HEAD_DIM
+        top = carried_top[:, at : at + 1]
+        for one in scores:
+            top = jnp.maximum(top, one.max(axis=1, keepdims=True))
+        shift = top * exp_scale
+        mixed = None
+        for slot, one in enumerate(scores):
+            weight = jnp.exp2(one * exp_scale - shift).astype(BF16)
+            value = slots[number, base + slot, 1]
+            lane_first = first_head(value.shape)
+            lane_mine = lane_first if head == 0 else jnp.logical_not(lane_first)
+            term = dot_nn(weight, jnp.where(lane_mine, value, jnp.ones_like(value)))
+            mixed = term if mixed is None else mixed + term
+        outs.append(mixed)
+        tops.append(jnp.broadcast_to(top, mixed.shape))
+    top = jnp.where(is_first, tops[0], tops[1])
+    fade = jnp.exp2((carried_top - top) * exp_scale)
+    acc = jnp.where(is_first, outs[0], outs[1]) + acc_all[number] * fade
+    total = pltpu.roll(jnp.where(is_first, outs[1], outs[0]), HEAD_DIM, 1) + total_all[number] * fade
+
+    @pl.when(jnp.logical_not(is_far))
+    def _():
+        acc_all[number] = acc
+        top_all[number] = top
+        total_all[number] = total
+
+    @pl.when(is_far)
+    def _():
         attended = acc / total
         low = attended.astype(BF16)
         low_ref[0] = low
@@ -604,11 +608,15 @@
     out_at = 3 * pairs
 
     def far(i):
-        return jnp.maximum(i - near, 0)
+        turn = i % (2 * pairs)
+        done = i // (2 * pairs) * pairs
+        return jnp.where(turn >= pairs, done + turn - pairs, jnp.maximum(done - 1, 0))
 
     anywhere = pl.BlockSpec(memory_space=pl.ANY)
     wide = pl.BlockSpec((1, rows, PAIR), lambda i: (far(i) // pairs, 0, far(i) % pairs))
-    half = pl.BlockSpec((1, rows // 2, width), lambda i: (jnp.maximum(far(i) // pairs, 1) - 1, 0, 0))
+    half = pl.BlockSpec(
+        (1, rows // 2, width), lambda i: (jnp.maximum(far(i) // pairs, 1) - 1, 0, 0)
+    )
     own_rows = tokens.shape[1]
     own = pl.BlockSpec((own_rows, width), lambda i: (0, 0))
     stages = [rows >> (stage + 1) for stage in range((trades + 1).bit_length() - 1)]
@@ -634,7 +642,7 @@
         collective_id=0,
         grid=(2 * near,),
         in_specs=[
-            pl.BlockSpec((1, rows, PAIR), lambda i: ((i // pairs) % windows, 0, i % pairs)),
+            pl.BlockSpec((1, rows, PAIR), lambda i: (i // (2 * pairs), 0, i % pairs)),
             pl.BlockSpec((width, PAIR), lambda i: (0, out_at + far(i) % pairs)),
             anywhere,
             anywhere,
@@ -1186,66 +1194,6 @@
     )
 
 
-def turn_back_kernel(gq_ref, gk_ref, gv_ref, w_ref, kept_ref, sent_ref):
-    cols = gq_ref.shape[2]
-    half = kept_ref.shape[0]
-
-    def rows_of(part):
-        total = None
-        for at, ref in enumerate((gq_ref, gk_ref, gv_ref)):
-            term = dot_nt(ref[0, part, :], w_ref[:, at * cols : (at + 1) * cols])
-            total = term if total is None else total + term
-        return total
-
-    sent_ref[...] = rows_of(slice(half, 2 * half)).astype(BF16)
-    kept_ref[...] = rows_of(slice(0, half))
-
-
-def turn_back(window, grads, w_att):
-    windows, rows, cols = grads[0].shape
-    width = w_att.shape[0]
-    half = pl.BlockSpec((rows // 2, width), lambda i: (0, 0))
-    return run(
-        turn_back_kernel,
-        "turn_back",
-        [shaped((rows // 2, width), F32), shaped((rows // 2, width), BF16)],
-        6 * rows * cols * width,
-        [*grads, w_att],
-        grid=(1,),
-        in_specs=[pl.BlockSpec((1, rows, cols), lambda i: (window, 0, 0))] * 3
-        + [pl.BlockSpec((width, 3 * cols), lambda i: (0, 0))],
-        out_specs=[half, half],
-    )
-
-
-def input_back_kernel(window, kept_ref, arrived_ref, x_ref, grad_ref, norms_ref, *refs):
-    out_ref, sums_ref = refs[-2:]
-    out_ref[0] = grad_ref[...] + norm_grad(
-        kept_ref, arrived_ref, x_ref[...].astype(F32), norms_ref[0:1, :], sums_ref
-    )
-
-
-def first_norm_back(window, windows, kept, arrived, x_rows, grad_middle, norms, earlier):
-    rows, width = kept.shape
-    args, whole = zip(*[plane(one) for one in (kept, arrived, x_rows, grad_middle, norms)])
-    args, whole = list(args), list(whole)
-    args += [] if earlier is None else [earlier]
-    return run(
-        functools.partial(input_back_kernel, window),
-        "first_norm_back",
-        [shaped((windows, rows, width), F32), shaped((2, width), F32)],
-        40 * rows * width,
-        args,
-        grid=(1,),
-        in_specs=whole + ([] if earlier is None else [pl.BlockSpec(memory_space=pl.ANY)]),
-        out_specs=[
-            pl.BlockSpec((1, rows, width), lambda i: (window, 0, 0)),
-            pl.BlockSpec((2, width), lambda i: (0, 0)),
-        ],
-        input_output_aliases={} if earlier is None else {5: 0},
-    )
-
-
 class SumRoute:
     def __init__(self, part, rows, core_in, mine, x_in, z_in, send_sem, recv_sem):
         self.read, self.rows = part, rows
@@ -1309,80 +1257,217 @@
 SUM_MESSAGES = 15
 
 
-def reduce_kernel(trades, windows, part_ref, *refs):
-    first_refs, second_refs = refs[:windows], refs[windows : 2 * windows]
-    out_ref, vectors_ref = refs[2 * windows : 2 * windows + 2]
-    refs = refs[2 * windows + 2 :]
-    tiles, own_tiles, arrived_tiles = refs[:3]
-    big = refs[3:9]
-    small = refs[9:15]
-    tile_send, tile_recv = refs[15:]
+def finish_kernel(windows, trades, score_cols, *refs):
+    stages = (trades + 1).bit_length() - 1
+    refs = list(refs)
+
+    def take(count):
+        taken = refs[:count]
+        del refs[:count]
+        return taken
+
+    far_inputs = take(8)
+    norms_ref = take(1)[0]
+    second_refs = take(windows)
+    grad_refs = take(windows)
+    part_refs = take(3 * windows)
+    weights_ref, vectors_ref, input_ref, output_ref = take(4)
+    loads = take(8)
+    grad_loads = take(windows)
+    part_loads = take(3 * windows)
+    part, core_in, mine, x_in, z_in = take(5)
+    tiles, own_tiles, arrived_tiles = take(3)
+    small_core, small_mine, small_x, small_z = take(4)
+    kept_all = take(windows)
+    stage_sent = [take(stages) for _ in range(windows)]
+    stage_arrived = [take(stages) for _ in range(windows)]
+    load_sem, big_send, big_recv, small_send, small_recv = take(5)
+    y_send, y_recv, tile_send, tile_recv = take(4)
+    assert not refs
+    (grad_q, grad_k, grad_v, normed, grad_mid, attended, w_qkv, tokens) = loads[:8]
     tensor = lax.axis_index("tensor")
     others = [{"tensor": flipped(tensor, other + 1)} for other in range(trades)]
     shards = lax.axis_size("dp") * lax.axis_size("seq")
     devices = shards * (trades + 1)
     group = tiles.shape[0] // shards
-    routes = (
-        SumRoute(tiles, group, *small),
-        SumRoute(part_ref, part_ref.shape[0] // shards, *big),
-    )
-    small_route, big_route = routes
-    first = sum(ref[...] for ref in first_refs)
+    width = part.shape[1]
+    cols = score_cols
+    rows = width // shards
+
+    w_source = far_inputs[6].at[:, pl.ds(0, 3 * cols)]
+    sources = [*far_inputs[:6], w_source, far_inputs[7]]
+    sources += [*grad_refs, *part_refs]
+    targets = [*loads, *grad_loads, *part_loads]
+    copies = [
+        pltpu.make_async_copy(source, target, load_sem.at[at])
+        for at, (source, target) in enumerate(zip(sources, targets))
+    ]
+    order = [4, 5, 6, 0, 1, 2, 3, 7] + list(range(8, len(copies)))
+    for at in order:
+        copies[at].start()
+
+    def block_route(block):
+        return SumRoute(
+            part.at[block],
+            rows,
+            core_in.at[block],
+            mine.at[block],
+            x_in.at[block],
+            z_in.at[block],
+            big_send.at[block],
+            big_recv.at[block],
+        )
+
+    routes = [block_route(block) for block in range(4)]
+    small = SumRoute(
+        tiles, group, small_core, small_mine, small_x, small_z, small_send, small_recv
+    )
+    greet(list(small.peers.values()) + others)
+    everything = (6, 7, 5, 4, 2, 3, 1, 0)
+
+    def product(block, left, right):
+        total = None
+        for w in range(windows):
+            term = dot_tn(left[w], right[w])
+            total = term if total is None else total + term
+        part[block] = total.astype(BF16)
+
+    def y_trade(w, stage):
+        return send(
+            stage_sent[w][stage],
+            stage_arrived[w][stage],
+            y_send.at[w, stage],
+            y_recv.at[w, stage],
+            {"tensor": flipped(tensor, (trades + 1) >> (stage + 1))},
+        )
+
+    def turn_back(w):
+        total = None
+        for at, grad in enumerate((grad_q, grad_k, grad_v)):
+            term = dot_nt(grad[w], w_qkv[:, at * cols : (at + 1) * cols])
+            total = term if total is None else total + term
+        half = total.shape[0] // 2
+        kept_all[w][...] = total[:half]
+        stage_sent[w][0][...] = total[half:].astype(BF16)
+
+    def add_cores(route):
+        for number in everything:
+            route.add_core(number)
+
+    def across(route):
+        route.start(10, 11, 9, 8)
+
+    def add_across(route):
+        for number in (2, 3, 1, 0):
+            route.add_x(number)
+
+    copies[4].wait()
+    copies[5].wait()
+    product(3, grad_mid, attended)
+    for at in (6, 0, 1, 2):
+        copies[at].wait()
+    routes[3].start(*everything)
+    turn_back(0)
+    add_cores(routes[3])
+    y_trade(0, 0).start()
+    across(routes[3])
+    for w in range(1, windows):
+        turn_back(w)
+    copies[3].wait()
+    product(0, normed, grad_q)
+    for w in range(1, windows):
+        y_trade(w, 0).start()
+    routes[0].start(*everything)
+    product(1, normed, grad_k)
+    add_cores(routes[0])
+    routes[1].start(*everything)
+    across(routes[0])
+    product(2, normed, grad_v)
+    add_cores(routes[1])
+    routes[2].start(*everything)
+    across(routes[1])
+    add_across(routes[3])
+    add_cores(routes[2])
+    routes[3].start(12, 14)
+    across(routes[2])
+    for at in range(8 + windows, len(copies)):
+        copies[at].wait()
+    for w in range(windows):
+        middle_ref, kept_ref, arrived_ref = part_loads[3 * w : 3 * w + 3]
+        output_ref[w] = (
+            middle_ref[...] + (kept_ref[...] + arrived_ref[...].astype(F32))
+        ).astype(BF16)
+    routes[3].add_up()
+    for at in range(7, 8 + windows):
+        copies[at].wait()
+    sums = [None, None]
+
+    def first_norm(w):
+        kept = kept_all[w][...]
+        for stage in range(stages):
+            y_trade(w, stage).wait_recv()
+            kept = kept + stage_arrived[w][stage][...].astype(F32)
+            if stage + 1 < stages:
+                half = kept.shape[0] // 2
+                stage_sent[w][stage + 1][...] = kept[half:].astype(BF16)
+                y_trade(w, stage + 1).start()
+                kept = kept[:half]
+        normed_rows, inv_std = normalise(tokens[w].astype(F32))
+        for at, one in enumerate((kept * normed_rows, kept)):
+            one = jnp.sum(one, axis=0, keepdims=True)
+            sums[at] = one if sums[at] is None else sums[at] + one
+        input_ref[w] = grad_loads[w][...] + norm_back(
+            kept, normed_rows, inv_std, norms_ref[0:1, :]
+        )
+
+    first_norm(0)
+    routes[3].start(13)
+    add_across(routes[0])
+    for w in range(1, windows):
+        first_norm(w)
+    routes[0].start(12, 14)
+    first = jnp.concatenate(sums, axis=0)
     second = sum(ref[...] for ref in second_refs)
-    span = first.shape[1] // devices
+    span = width // devices
     tiles[...] = jnp.zeros_like(tiles)
     for device in range(devices):
         at = device * 8
-        part = slice(device * span, (device + 1) * span)
-        tiles[at : at + 2, :span] = first[:, part]
-        tiles[at + 2 : at + 4, :span] = second[:, part]
-    greet(list(big_route.peers.values()) + others)
-    small_route.start(6, 5, 7, 4, 2, 1, 3, 0)
-    big_route.start(6, 5, 7, 4, 2, 1, 3, 0)
-    for number in (6, 5, 7, 4, 2, 1, 3, 0):
-        small_route.add_core(number)
-    big_route.add_core(6)
-    small_route.start(10, 9, 11, 8)
-    big_route.add_core(5)
-    big_route.start(10)
-    big_route.add_core(7)
-    big_route.start(9)
-    big_route.add_core(4)
-    big_route.start(11)
-    big_route.add_core(2)
-    big_route.start(8)
-    for number in (2, 1, 3, 0):
-        small_route.add_x(number)
-    big_route.add_core(1)
-    small_route.start(12, 14)
-    big_route.add_core(3)
-    big_route.add_core(0)
-    small_route.add_up()
-    big_route.add_x(2)
-    small_route.start(13)
-    own = small_route.total()
-    big_route.start(12)
-    own_tiles[...] = own
-    big_route.add_x(1)
-    big_route.add_up()
-    out_ref[...] = jnp.zeros_like(out_ref)
-    big_route.start(13)
-    big_route.add_x(3)
-    out_ref[...] = jnp.zeros_like(out_ref)
-    big_route.start(14)
-    big_route.add_x(0)
-    out_ref[...] = big_route.total()
+        columns = slice(device * span, (device + 1) * span)
+        tiles[at : at + 2, :span] = first[:, columns]
+        tiles[at + 2 : at + 4, :span] = second[:, columns]
+    add_across(routes[1])
+    small.start(*everything)
+    routes[0].add_up()
+    routes[1].start(12, 14)
+    add_cores(small)
+    routes[0].start(13)
+    across(small)
+    add_across(routes[2])
+    routes[1].add_up()
+    routes[2].start(12, 14)
+    add_across(small)
+    routes[1].start(13)
+    small.start(12, 14)
+    for block in (3, 0):
+        weights_ref[:, block * cols : (block + 1) * cols] = routes[block].total()
+    small.add_up()
+    routes[2].add_up()
+    small.start(13)
+    weights_ref[:, cols : 2 * cols] = routes[1].total()
+    routes[2].start(13)
+    own_tiles[...] = small.total()
 
     def tile_trade(other):
-        rows = pl.ds(pl.multiple_of(flipped(tensor, other + 1) * 8, 8), 8)
+        place = pl.ds(pl.multiple_of(flipped(tensor, other + 1) * 8, 8), 8)
         return send(
-            own_tiles.at[rows, :],
+            own_tiles.at[place, :],
             arrived_tiles.at[other],
             tile_send.at[other],
             tile_recv.at[other],
             others[other],
         )
 
+    weights_ref[:, 2 * cols : 3 * cols] = routes[2].total()
     for other in range(trades):
         tile_trade(other).start()
     vectors = own_tiles[pl.ds(pl.multiple_of(tensor * 8, 8), 8), :]
@@ -1390,60 +1475,77 @@
         tile_trade(other).wait_recv()
         vectors = vectors + arrived_tiles[other]
     vectors_ref[...] = vectors
-    for route in routes:
+    for route in (*routes, small):
         route.sent()
+    for w in range(windows):
+        for stage in range(stages):
+            y_trade(w, stage).wait_send()
     for other in range(trades):
         tile_trade(other).wait_send()
 
 
-def reduce_grads(part, first_sums, second_sums, trades):
+def finish(
+    grads, normed, grad_mid, attended, w_att, tokens, norms, second_sums, grad_middles, parts, trades
+):
+    windows, rows, cols = grads[0].shape
+    width = w_att.shape[0]
+    own_rows = tokens.shape[1]
     shards = lax.axis_size("dp") * lax.axis_size("seq")
-    rows, cols = part.shape[0] // shards, part.shape[1]
+    shard = width // shards
     group = 8 * (trades + 1)
-    windows = len(first_sums)
+    stages = [rows >> (stage + 1) for stage in range((trades + 1).bit_length() - 1)]
     dma = pltpu.SemaphoreType.DMA
-
-    def buffers(shape, dtype):
-        return [pltpu.VMEM((count,) + shape, dtype) for count in (8, 8, 4, 3)] + [
-            dma((SUM_MESSAGES,)),
-            dma((SUM_MESSAGES,)),
-        ]
-
+    anywhere = pl.BlockSpec(memory_space=pl.ANY)
+    vmem = pl.BlockSpec(memory_space=pltpu.VMEM)
+    far_inputs = [*grads, normed, grad_mid, attended, w_att, tokens]
+    flat = [array for one in parts for array in one]
+    kinds = (8, 8, 4, 3)
+
+    def like(array):
+        return pltpu.VMEM(array.shape, array.dtype)
+
+    loads = [like(array) for array in far_inputs]
+    loads[6] = pltpu.VMEM((width, 3 * cols), BF16)
     return run(
-        functools.partial(reduce_kernel, trades, windows),
-        "reduce_grads",
-        [shaped((rows, cols), F32), shaped((8, 128), F32)],
-        0,
-        [part, *first_sums, *second_sums],
+        functools.partial(finish_kernel, windows, trades, cols),
+        "finish",
+        [
+            shaped((shard, 4 * cols), F32),
+            shaped((8, 128), F32),
+            shaped((windows, own_rows, width), F32),
+            shaped((windows, own_rows, width), BF16),
+        ],
+        8 * windows * rows * width * cols + 6 * windows * rows * width * cols,
+        [*far_inputs, norms, *second_sums, *grad_middles, *flat],
         collective_id=3,
-        scratch_shapes=[
+        in_specs=[anywhere] * 8
+        + [vmem] * (1 + windows)
+        + [anywhere] * (windows + len(flat)),
+        out_specs=[vmem] * 4,
+        scratch_shapes=loads
+        + [like(array) for array in grad_middles]
+        + [like(array) for array in flat]
+        + [pltpu.VMEM((4, width, cols), BF16)]
+        + [pltpu.VMEM((4, count, shard, cols), BF16) for count in kinds]
+        + [
             pltpu.VMEM((shards * group, 128), F32),
             pltpu.VMEM((group, 128), F32),
             pltpu.VMEM((trades, 8, 128), F32),
         ]
-        + buffers((rows, cols), BF16)
-        + buffers((group, 128), F32)
-        + [dma((trades,)), dma((trades,))],
-    )
-
-
-def result_kernel(windows, *refs):
-    out_ref = refs[-1]
-    for w in range(windows):
-        middle_ref, kept_ref, arrived_ref = refs[3 * w : 3 * w + 3]
-        out_ref[w] = (
-            middle_ref[...] + (kept_ref[...] + arrived_ref[...].astype(F32))
-        ).astype(BF16)
-
-
-def results(parts):
-    rows, width = parts[0][0].shape
-    return run(
-        functools.partial(result_kernel, len(parts)),
-        "results",
-        shaped((len(parts), rows, width), BF16),
-        2 * len(parts) * rows * width,
-        [array for part in parts for array in part],
+        + [pltpu.VMEM((count, group, 128), F32) for count in kinds]
+        + [pltpu.VMEM((rows // 2, width), F32)] * windows
+        + [pltpu.VMEM((count, width), BF16) for count in stages] * (2 * windows)
+        + [
+            dma((8 + windows + len(flat),)),
+            dma((4, SUM_MESSAGES)),
+            dma((4, SUM_MESSAGES)),
+            dma((SUM_MESSAGES,)),
+            dma((SUM_MESSAGES,)),
+            dma((windows, len(stages))),
+            dma((windows, len(stages))),
+            dma((trades,)),
+            dma((trades,)),
+        ],
     )
 
 
@@ -1609,43 +1711,23 @@
         (cosine, sine),
         [fed[w][6] for w in windows],
     )
-    output = results(
-        [
-            (middles[w], *later_pair(fed[w][5], arrived_results[w], "tensor"))
-            for w in windows
-        ]
-    )
-
-    first_parts = []
-    for w in windows:
-        kept, sent = turn_back(w, (grad_q, grad_k, grad_v), w_att)
-        first_parts.append(scatter_pair(kept, sent, "tensor"))
-    g_att_part = weight_grads(
-        [
-            ([(normed_rows, (w,)) for w in windows], [(grad, (w,)) for w in windows])
-            for grad in (grad_q, grad_k, grad_v)
-        ]
-        + [([(grad_mid_rows, (w,)) for w in windows], [(attended, (w,)) for w in windows])],
-        head_cols,
-        "attend_weights",
-    )
-    input_grad = None
-    first_sums = []
-    for w in windows:
-        kept, arrived = first_parts[w]
-        input_grad, sums = first_norm_back(
-            w,
-            windows_here,
-            hold(kept, g_att_part),
-            arrived,
-            (tokens, (w,)),
-            grad_middles[w],
-            norms,
-            input_grad,
-        )
-        first_sums.append(sums)
-
-    g_att, vectors = reduce_grads(g_att_part, first_sums, second_sums, tensor_size - 1)
+    parts = [
+        (middles[w], *later_pair(fed[w][5], arrived_results[w], "tensor")) for w in windows
+    ]
+
+    g_att, vectors, input_grad, output = finish(
+        (grad_q, grad_k, grad_v),
+        normed_rows,
+        grad_mid_rows,
+        attended,
+        w_att,
+        tokens,
+        norms,
+        second_sums,
+        grad_middles,
+        parts,
+        tensor_size - 1,
+    )
     norm_sums = vectors[:4, : norm1_gain.shape[0]]
     ffn_grads = [
         jnp.concatenate(

time: 458 us -> 435 us (0.950)
  Pallas kernels: 394 us -> 373 us
    pallas_call x20 -> x14, Pallas kernels: 394 us -> 373 us  [run(): pl.pallas_call(kernel, out_shape=out_shape, compiler_params=pltpu.Compile...]
    ppermute x5 -> x3, waiting for transfers between devices: 10.9 us -> 11.7 us  [swap(): return lax.ppermute(array, axis, [(i, i ^ bit) for i in range(size)])]
  transfers between devices with their start and end apart: 9 -> 7, of which waited for: 1 -> 1; matrix products, arithmetic and copies ran while one was open for 3% -> 3% of each run, Pallas kernels for 88% -> 87%
where the time goes in v7:
time: 435 us; the launch traced here: 427 us
  Pallas kernels  373 us (86%)
  local copies, waits for them, and re-layouts  14.9 us (3%)
  between operations  14.6 us (3%)
  waiting for transfers between devices  11.8 us (3%)
  other arithmetic  9.23 us (2%)
    pallas_call x14, Pallas kernels, run(): pl.pallas_call(kernel, out_shape=out_shape, compiler_params=pltpu.Compile...  373 us
    ppermute x3, waiting for transfers between devices, swap(): return lax.ppermute(array, axis, [(i, i ^ bit) for i in range(size)])  11.7 us
  transfers between devices with their start and end apart: 7, of which 1 were waited for; matrix products, arithmetic and copies ran while one was open for 3% of the time, Pallas kernels for 87%

profile of v7, /device:TPU:0, one launch (start us, length us, event | category | flops | bytes accessed | tf_op | source)
XLA Modules:
  0.0 427.3 jit_solution(14651856962082897081)
XLA Ops:
  7.3 0.0 all-gather.3.cloned.1.call-start
  7.3 1.1 fusion.8
  8.4 1.1 fusion.6
  9.5 0.8 pad_maximum_fusion
  10.3 0.0 all-gather.3.cloned.1.call-update
  10.3 0.0 all-gather.5.cloned.1.call-start
  10.5 0.0 copy-done.9
  10.5 0.0 copy-done.14
  10.5 0.2 fusion.1
  10.7 0.6 fusion.3
  11.3 0.6 broadcast.63
  12.0 0.0 copy-start.8
  12.0 0.0 copy-done.4
  12.0 0.0 copy-done.5
  12.0 0.0 copy-done.6
  12.0 0.0 copy-done.7
  12.0 0.7 pad_maximum_fusion.2.att_ref
  12.7 46.6 %gather.1 = (bf16[1024,2048]{1,0:T(8,128)(2,1)}, f32[8,1024]{1,0:T(8,128)}, bf16[1,2,256,1024]{3,2,1,0:T(8,128)(2,1)}) custom-call(bf16[64,2048]{1,0:T(8,128)(2,1)} %pad_maximum_fusion.2.att_ref, f32[8,128]{1,0:T(8,128)} %copy-done.8, bf16[2,256,1024]{2,1,0:T(8,128)(2,1)} %refs_7_.1), custom_call_target="tpu_custom_call" | custom-call | bytes 6590464 | tf_op jit(solution)/shard_map/gather/pallas_call | solution.py:80
  59.4 1.0 fusion
  60.4 1.0 pad_maximum_fusion.3.cos_ref.refs_5_
  61.4 1.0 pad_maximum_fusion.4.sin_ref.refs_6_
  62.4 8.4 %project.1 = (bf16[2,512,1024]{2,1,0:T(8,128)(2,1)}, bf16[2,512,512]{2,1,0:T(8,128)(2,1)}, bf16[2,2,512,512]{3,2,1,0:T(8,128)(2,1)}) custom-call(f32[8,1024]{1,0:T(8,128)} %get-tuple-element.131.norms_ref.refs_5_.refs_8_, bf16[1024,2048]{1,0:T(8,128)(2,1)} %get-tuple-element.132.w_ref.refs_1_.refs_4_.refs_6_, f32[512,128]{1,0:T(8,128)} %pad_maximum_fusion.3.cos_ref.refs_5_, ...), custom_call_target="tpu_custom_call" | custom-call | flops 3221225472 | bytes 12091392 | tf_op jit(solution)/shard_map/project/pallas_call | solution.py:80
  70.8 0.8 pad_maximum_fusion.1
  71.6 66.9 %attend.1 = (bf16[2,512,512]{2,1,0:T(8,128)(2,1)}, f32[2,512,512]{2,1,0:T(8,128)}, f32[2,512,512]{2,1,0:T(8,128)}, f32[1,256,1024]{2,1,0:T(8,128)}, bf16[1,256,1...) custom-call(bf16[2,512,512]{2,1,0:T(8,128)(2,1)} %get-tuple-element., ...), custom_call_target="tpu_custom_call" | custom-call | flops 17179869184 | bytes 27820032 | tf_op jit(solution)/shard_map/attend/pallas_call | solution.py:80
  138.5 0.0 all-gather.5.cloned.1.call-update
  138.5 0.5 reduce-scatter.3.cloned.1.call-start
  139.0 1.4 collective-permute-start
  140.4 1.2 slice.109
  141.6 0.7 multiply_divide_fusion
  142.2 0.6 fusion.9
  142.8 15.2 %feed_first.2 = (bf16[512,1024]{1,0:T(8,128)(2,1)}, bf16[512,1024]{1,0:T(8,128)(2,1)}, bf16[512,2048]{1,0:T(8,128)(2,1)}, bf16[512,2048]{1,0:T(8,128)(2,1)}, bf1...) custom-call(f32[1,1]{1,0:T(1,128)} %bitcast.7.factor_ref, ...), custom_call_target="tpu_custom_call" | custom-call | flops 6442450944 | bytes 34603012 | tf_op jit(solution)/shard_map/feed_first/pallas_call | solution.py:80
  158.1 0.0 collective-permute-done.arrived_ref
  158.1 0.0 copy-start.2
  158.1 0.8 copy-done.2
  158.9 2.8 second_norm.1
  161.7 0.6 collective-permute-start.1
  162.2 11.7 %collective-permute-done.1.refs_4_ = bf16[256,1024]{1,0:T(8,128)(2,1)S(1)} collective-permute-done((bf16[256,1024]{1,0:T(8,128)(2,1)}, bf16[256,1024]{1,0:T(8,128)(2,1)S(1)}, u32[]{:S(2)}, u32[]{:S(2)}) %collective-permute-start.1) | collective-permute-done | bytes 524320 | tf_op jit(solution)/shard_map/ppermute | solution.py:45
  174.0 0.8 copy-done.16
  174.8 15.2 %feed_first.3 = (bf16[512,1024]{1,0:T(8,128)(2,1)}, bf16[512,1024]{1,0:T(8,128)(2,1)}, bf16[512,2048]{1,0:T(8,128)(2,1)}, bf16[512,2048]{1,0:T(8,128)(2,1)}, bf1...) custom-call(f32[1,1]{1,0:T(1,128)} %bitcast.10.factor_ref, ...), custom_call_target="tpu_custom_call" | custom-call | flops 6442450944 | bytes 34603012 | tf_op jit(solution)/shard_map/feed_first/pallas_call | solution.py:80
  189.9 13.7 %feed_weights.2 = bf16[1024,3072]{1,0:T(8,128)(2,1)} custom-call(bf16[512,1024]{1,0:T(8,128)(2,1)} %get-tuple-element.189.refs_0_.refs_4_.refs_3_, bf16[512,1024]{1,0:T(8,128)(2,1)} %get-tuple-element.190.refs_1_.refs_5_.refs_3_, bf16[512,2048]{1,0:T(8,128)(2,1)} %get-tuple-element.161.refs_2_.refs_8_, bf16[512,2048]{1,0:T(8,128)(2,1)} %get-tuple-element.177.refs_3_.refs_8_, ...), custom_call_target="tpu_custom_call" | custom-call | flops 6442450944 | bytes 25165824 | tf_op jit(solution)/shard_map/feed_weights/pallas_call | solution.py:80
  203.7 0.0 reduce-scatter.3.cloned.1.call-update
  203.7 0.2 reduce-scatter.5.cloned.1.call-start
  203.9 0.0 all-gather.5.cloned.1.call-done.refs_0_.refs_1_.refs_2_
  203.9 14.9 %feed_last.2 = (bf16[512,2048]{1,0:T(8,128)(2,1)}, bf16[512,2048]{1,0:T(8,128)(2,1)}, bf16[512,2048]{1,0:T(8,128)(2,1)}, f32[256,1024]{1,0:T(8,128)}, bf16[256,1...) custom-call(bf16[1024,3072]{1,0:T(8,128)(2,1)} %all-gather.5.cloned., ...), custom_call_target="tpu_custom_call", output_to_operand_aliasing={{0}: (7, {}), {1}: (8, {}), {2}: (9, {})} | custom-call | flops 6442450944 | bytes 40894464 | tf_op jit(solution)/shard_map/feed_last/pallas_call | solution.py:80
  218.8 0.8 collective-permute-start.2
  219.6 15.6 %feed_last.3 = (bf16[512,2048]{1,0:T(8,128)(2,1)}, bf16[512,2048]{1,0:T(8,128)(2,1)}, bf16[512,2048]{1,0:T(8,128)(2,1)}, f32[256,1024]{1,0:T(8,128)}, bf16[256,1...) custom-call(bf16[1024,3072]{1,0:T(8,128)(2,1)} %all-gather.5.cloned., ...), custom_call_target="tpu_custom_call", output_to_operand_aliasing={{0}: (7, {}), {1}: (8, {}), {2}: (9, {})} | custom-call | flops 6442450944 | bytes 40894464 | tf_op jit(solution)/shard_map/feed_last/pallas_call | solution.py:80
  235.3 0.0 collective-permute-done.2.arrived_ref
  235.3 0.8 copy-done.3
  236.1 4.5 %second_norm_back.2 = (f32[256,1024]{1,0:T(8,128)}, bf16[256,1024]{1,0:T(8,128)(2,1)}, f32[2,1024]{1,0:T(2,128)}) custom-call(f32[1,1]{1,0:T(1,128)} %bitcast.7.factor_ref, f32[256,1024]{1,0:T(8,128)} %get-tuple-element.186.kept_ref, bf16[256,1024]{1,0:T(8,128)(2,1)} %copy-done.3, f32[256,1024]{1,0:T(8,128)} %get-tuple-element.187.middle_ref.refs_13_, ...), custom_call_target="tpu_custom_call" | custom-call | flops 10485760 | bytes 5283844 | tf_op jit(solution)/shard_map/second_norm_back/pallas_call | solution.py:80
  240.6 28.2 %feed_weights.3 = (bf16[1024,3072]{1,0:T(8,128)(2,1)}, bf16[1,256,1024]{2,1,0:T(8,128)(2,1)}, bf16[1,256,1024]{2,1,0:T(8,128)(2,1)}) custom-call(bf16[512,1024]{1,0:T(8,128)(2,1)} %get-tuple-element.189.refs_0_.refs_4_.refs_3_, bf16[512,1024]{1,0:T(8,128)(2,1)} %get-tuple-element.190.refs_1_.refs_5_.refs_3_, bf16[512,2048]{1,0:T(8,128)(2,1)} %get-tuple-element.191.refs_2_, ...), custom_call_target="tpu_custom_call" | custom-call | flops 6442450944 | bytes 27262976 | tf_op jit(solution)/shard_map/feed_weights/pallas_call | solution.py:80
  268.8 0.0 reduce-scatter.5.cloned.1.call-update
  268.8 4.5 %second_norm_back.3 = (f32[256,1024]{1,0:T(8,128)}, bf16[256,1024]{1,0:T(8,128)(2,1)}, f32[2,1024]{1,0:T(2,128)}) custom-call(f32[1,1]{1,0:T(1,128)} %bitcast.10.factor_ref, f32[256,1024]{1,0:T(8,128)} %get-tuple-element.205.kept_ref, bf16[256,1024]{1,0:T(8,128)(2,1)} %bitcast.28, f32[256,1024]{1,0:T(8,128)} %get-tuple-element.207.middle_ref.refs_16_, ...), custom_call_target="tpu_custom_call" | custom-call | flops 10485760 | bytes 5283844 | tf_op jit(solution)/shard_map/second_norm_back/pallas_call | solution.py:80
  273.3 74.8 %attend_back.1 = (bf16[2,512,512]{2,1,0:T(8,128)(2,1)}, bf16[2,512,512]{2,1,0:T(8,128)(2,1)}, bf16[2,512,512]{2,1,0:T(8,128)(2,1)}, bf16[2,512,1024]{2,1,0:T(8,1...) custom-call(bf16[2,512,512]{2,1,0:T(8,128)(2,1)} %get-tuple-element.201.refs_0_, ...), custom_call_target="tpu_custom_call" | custom-call | flops 42949672960 | bytes 27787264 | tf_op jit(solution)/shard_map/attend_back/pallas_call | solution.py:80
  348.1 61.9 %finish.1 = (f32[64,2048]{1,0:T(8,128)}, f32[8,128]{1,0:T(8,128)}, f32[2,256,1024]{2,1,0:T(8,128)}, bf16[2,256,1024]{2,1,0:T(8,128)(2,1)}) custom-call(bf16[2,512,512]{2,1,0:T(8,128)(2,1)} %get-tuple-element.210.refs_0_, bf16[2,512,512]{2,1,0:T(8,128)(2,1)} %get-tuple-element.211.refs_1_, bf16[2,512,512]{2,1,0:T(8,128)(2,1)} %get-tuple-element.212.refs_2_, ...), custom_call_target="tpu_custom_call" | custom-call | flops 7516192768 | bytes 24694784 | tf_op jit(solution)/shard_map/finish/pallas_call | solution.py:80
  410.1 1.4 slice_bitcast_fusion.1
  411.4 1.9 slice_bitcast_fusion
  413.3 1.1 fusion.4
  414.5 0.0 reduce-scatter.5.cloned.1.call-done
  414.5 1.1 fusion.5
  415.6 0.8 convert_bitcast_fusion
  416.4 0.8 maximum_convert_fusion.1
  417.2 0.8 maximum_convert_fusion
  418.1 1.0 copy.45
  419.0 1.3 copy.46
  (30 shorter events, 0.1 us)
Async XLA Ops:
  7.2 3.2 copy-start.10
  7.2 3.2 copy-start.11
  7.2 3.2 copy-start.12
  7.2 3.2 copy-start.13
  7.2 3.2 copy-start.9
  7.2 3.2 copy-start.14
  7.2 3.4 copy-start.15
  7.3 4.7 %copy-start.4 = (bf16[512,64]{0,1:T(8,128)(2,1)S(1)}, bf16[512,64]{0,1:T(8,128)(2,1)}, u32[]{:S(2)}) copy-start(bf16[512,64]{0,1:T(8,128)(2,1)} %param.30) | copy-start | bytes 196612
  7.3 4.7 %copy-start.5 = (bf16[64,512]{1,0:T(8,128)(2,1)S(1)}, bf16[64,512]{1,0:T(8,128)(2,1)}, u32[]{:S(2)}) copy-start(bf16[64,512]{1,0:T(8,128)(2,1)} %param.29) | copy-start | bytes 196612
  7.3 4.7 %copy-start.6 = (bf16[64,512]{1,0:T(8,128)(2,1)S(1)}, bf16[64,512]{1,0:T(8,128)(2,1)}, u32[]{:S(2)}) copy-start(bf16[64,512]{1,0:T(8,128)(2,1)} %param.28) | copy-start | bytes 196612
  7.3 4.7 %copy-start.7 = (bf16[64,512]{1,0:T(8,128)(2,1)S(1)}, bf16[64,512]{1,0:T(8,128)(2,1)}, u32[]{:S(2)}) copy-start(bf16[64,512]{1,0:T(8,128)(2,1)} %param.27) | copy-start | bytes 196612
  7.3 135.5 %all-gather.3.cloned.1.call-start = ((), (), s32[]{:S(2)}) async-start(), calls=%async_computation.2 | async-start | bytes 6684672 | tf_op jit(solution)/shard_map/all_gather | solution.py:1601
  10.3 193.6 %all-gather.5.cloned.1.call-start = ((), (), s32[]{:S(2)}) async-start(), calls=%async_computation.3 | async-start | bytes 6684672 | tf_op jit(solution)/shard_map/all_gather | solution.py:1628
  12.0 0.8 copy-start.8
  138.5 274.8 %reduce-scatter.3.cloned.1.call-start = ((), (), s32[]{:S(2)}) async-start(), calls=%async_computation.4 | async-start | bytes 6684672 | tf_op jit(solution)/shard_map/reduce_scatter | solution.py:1670
  139.0 19.0 %collective-permute-start = (bf16[256,1024]{1,0:T(8,128)(2,1)}, bf16[256,1024]{1,0:T(8,128)(2,1)S(1)}, u32[]{:S(2)}, u32[]{:S(2)}) collective-permute-start(bf16[256,1024]{1,0:T(8,128)(2,1)} %bitcast.36), channel_id=1, source_target_pairs={{0,1},{1,0},{2,3},{3,2},{4,5},{5,4},{6,7},{7,6},{8,9},{9,8},{10,11... | collective-permute-start | bytes 1572872 | tf_op jit(solution)/shard_map/ppermute | solution.py:45
  158.1 0.8 copy-start.2
  161.7 12.3 %collective-permute-start.1 = (bf16[256,1024]{1,0:T(8,128)(2,1)}, bf16[256,1024]{1,0:T(8,128)(2,1)S(1)}, u32[]{:S(2)}, u32[]{:S(2)}) collective-permute-start(bf16[256,1024]{1,0:T(8,128)(2,1)} %get-tuple-element.149.refs_3_), channel_id=1, source_target_pairs={{0,1},{1,0},{2,3},{3,2},{4,5},{5,4},{6,7},{7,6},{8,9},{9,8},{10,11... | collective-permute-start | bytes 1572872 | tf_op jit(solution)/shard_map/ppermute | solution.py:45
  174.0 0.8 copy-start.16
  203.7 210.8 %reduce-scatter.5.cloned.1.call-start = ((), (), s32[]{:S(2)}) async-start(), calls=%async_computation.5 | async-start | bytes 6684672 | tf_op jit(solution)/shard_map/reduce_scatter | solution.py:1697
  218.8 16.4 %collective-permute-start.2 = (bf16[256,1024]{1,0:T(8,128)(2,1)}, bf16[256,1024]{1,0:T(8,128)(2,1)S(1)}, u32[]{:S(2)}, u32[]{:S(2)}) collective-permute-start(bf16[256,1024]{1,0:T(8,128)(2,1)} %get-tuple-element.169), channel_id=1, source_target_pairs={{0,1},{1,0},{2,3},{3,2},{4,5},{5,4},{6,7},{7,6},{8,9},{9,8},{10,11... | collective-permute-start | bytes 1572872 | tf_op jit(solution)/shard_map/ppermute | solution.py:45
  235.3 0.8 copy-start.3
  413.3 4.7 %copy-start.1 = (bf16[2,256,1024]{2,1,0:T(8,128)(2,1)S(1)}, bf16[2,256,1024]{2,1,0:T(8,128)(2,1)}, u32[]{:S(2)}) copy-start(bf16[2,256,1024]{2,1,0:T(8,128)(2,1)} %get-tuple-element.267) | copy-start | bytes 3145732
  415.6 3.5 copy-start
Sparse Core Ops, SparseCore 0:
  11.0 75.9 all-gather.2
  138.6 61.6 all-gather.4
  204.3 84.0 reduce-scatter.2
  292.7 104.5 reduce-scatter.4

commit v8 on v7

--- a/solution.py
+++ b/solution.py
@@ -66,6 +66,14 @@
         rows = partial.shape[0] // 2
         kept, arrived = partial[:rows], swap(partial[rows:].astype(BF16), axis, bit)
     return kept, arrived
+
+
+def seq_size():
+    return lax.axis_size("x") * lax.axis_size("core")
+
+
+def seq_index():
+    return lax.axis_index("x") * lax.axis_size("core") + lax.axis_index("core")
 
 
 def hold(values, *others):
@@ -209,13 +217,13 @@
 
 
 def half_chip_peers():
-    seq, depth = lax.axis_index("seq"), lax.axis_index("dp")
+    depth = lax.axis_index("dp")
     size = lax.axis_size("dp")
     return {
-        "far": {"seq": flipped(seq, 2)},
+        "far": {"x": 1 - lax.axis_index("x")},
         "up": {"dp": (depth + 1) % size},
         "down": {"dp": (depth + size - 1) % size},
-        "core": {"seq": flipped(seq, 1)},
+        "core": {"core": 1 - lax.axis_index("core")},
     }
 
 
@@ -225,13 +233,13 @@
     def __init__(self, whole, rows, send_sem, recv_sem, own):
         self.whole, self.rows, self.own = whole, rows, own
         self.send_sem, self.recv_sem = send_sem, recv_sem
-        self.seq, self.depth = lax.axis_index("seq"), lax.axis_index("dp")
+        self.seq, self.depth = seq_index(), lax.axis_index("dp")
         self.peers = half_chip_peers()
 
     def part(self, place):
         turn, other = place
         seq = flipped(self.seq, 2) if other else self.seq
-        at = (((self.depth + turn) % lax.axis_size("dp")) * lax.axis_size("seq") + seq) * self.rows
+        at = (((self.depth + turn) % lax.axis_size("dp")) * seq_size() + seq) * self.rows
         return self.whole.at[pl.ds(pl.multiple_of(at, self.rows), self.rows), :]
 
     def message(self, number):
@@ -364,7 +372,7 @@
 
 
 def gather(att, tile, tokens, trades):
-    count = lax.axis_size("dp") * lax.axis_size("seq")
+    count = lax.axis_size("dp") * seq_size()
     rows = att.shape[0]
     group = tile.shape[0] * (trades + 1)
     anywhere = pl.BlockSpec(memory_space=pl.ANY)
@@ -404,9 +412,9 @@
     turn = step % (2 * pairs)
     is_far = turn >= pairs
     number = step // (2 * pairs) * pairs + turn % pairs
-    seq, tensor = lax.axis_index("seq"), lax.axis_index("tensor")
-    core_peer = {"seq": flipped(seq, 1)}
-    far_peer = {"seq": flipped(seq, 2)}
+    tensor = lax.axis_index("tensor")
+    core_peer = {"core": 1 - lax.axis_index("core")}
+    far_peer = {"x": 1 - lax.axis_index("x")}
     cot_peers = [{"tensor": flipped(tensor, other + 1)} for other in range(trades)]
 
     def piece(number):
@@ -690,17 +698,18 @@
     known = (windows - 1) * blocks + 1
     grad_refs = list(refs[8 : 8 + known])
     refs = refs[8 + known :]
-    sent_refs, refs = refs[:windows], refs[windows:]
+    sent_refs, shard_ref, refs = refs[:windows], refs[windows], refs[windows + 1 :]
     gq_ref, gk_ref, gv_ref, rows_ref = refs[:4]
-    arrived_refs, refs = refs[4 : 4 + windows], refs[4 + windows :]
+    arrived_refs, shard_arrived = refs[4 : 4 + windows], refs[4 + windows]
+    refs = refs[5 + windows :]
     dq_all, do_all, far_kept, far_sent, far_core, far_x, near_kept, near_sent, near_core = refs[:9]
-    send_sem, recv_sem, result_send, result_recv, last_send, last_recv, last_others = refs[9:]
+    send_sem, recv_sem, result_send, result_recv, last_send, last_recv, last_others, shard_sem = refs[9:]
     grad_refs += [last_others.at[other] for other in range(trades)]
     step = pl.program_id(0)
     count = windows * pairs
-    seq, tensor = lax.axis_index("seq"), lax.axis_index("tensor")
-    core_peer = {"seq": flipped(seq, 1)}
-    far_peer = {"seq": flipped(seq, 2)}
+    tensor = lax.axis_index("tensor")
+    core_peer = {"core": 1 - lax.axis_index("core")}
+    far_peer = {"x": 1 - lax.axis_index("x")}
     result_peer = {"tensor": flipped(tensor, lax.axis_size("tensor") // 2)}
 
     def trade(kind, number):
@@ -729,9 +738,13 @@
             last_ref, last_others.at[other], last_send.at[other], last_recv.at[other], others[other]
         )
 
+    def shard_trade():
+        return send(shard_ref, shard_arrived, shard_sem.at[0], shard_sem.at[1], far_peer)
+
     @pl.when(step == 0)
     def _():
         greet([core_peer, far_peer] + others)
+        shard_trade().start()
         for other in range(trades):
             last_trade(other).start()
         for w in range(windows):
@@ -845,6 +858,7 @@
             for kind in range(3):
                 trade(kind, number).wait_send()
 
+        shard_trade().wait()
         for other in range(trades):
             last_trade(other).wait_send()
         for w in range(windows):
@@ -852,7 +866,7 @@
             result_trade(w).wait_recv()
 
 
-def attend_back(queries, wide, logs, slots_all, grad_blocks, w_att, tables, sent):
+def attend_back(queries, wide, logs, slots_all, grad_blocks, w_att, tables, sent, shard):
     windows, rows, cols = queries.shape
     width = w_att.shape[0]
     pairs = cols // PAIR
@@ -883,9 +897,9 @@
         "attend_back",
         [shaped((windows, rows, cols), BF16)] * 3
         + [shaped((windows, rows, width), BF16)]
-        + [shaped(one.shape, BF16) for one in sent],
+        + [shaped(one.shape, BF16) for one in (*sent, shard)],
         160 * windows * rows * rows * cols,
-        [queries, wide, logs, slots_all, w_att, *tables, last, *grads, *sent],
+        [queries, wide, logs, slots_all, w_att, *tables, last, *grads, *sent, shard],
         collective_id=2,
         grid=(2 * count + 2,),
         in_specs=[
@@ -902,210 +916,272 @@
             anywhere,
         ]
         + [pl.BlockSpec(block.shape, lambda i: (0, 0)) for block in grads]
-        + [anywhere] * windows,
+        + [anywhere] * (windows + 1),
         out_specs=[
             spot(count),
             spot(count + 2),
             spot(count + 2),
             pl.BlockSpec((1, rows, width), lambda i: (jnp.minimum(i // pairs, windows - 1), 0, 0)),
         ]
-        + [anywhere] * windows,
+        + [anywhere] * (windows + 1),
         scratch_shapes=[pltpu.VMEM((count, rows, PAIR), F32), pltpu.VMEM((count, rows, PAIR), BF16)]
         + [piece] * 7
         + [dma((3, count)), dma((3, count)), dma((windows,)), dma((windows,))]
-        + [dma((blocks - 1,)), dma((blocks - 1,)), pltpu.VMEM((blocks - 1,) + last.shape, BF16)],
-    )
-
-
-def middle_kernel(x_ref, kept_ref, arrived_ref, norms_ref, middle_ref, normed_ref):
-    middle = x_ref[...].astype(F32) + (kept_ref[...] + arrived_ref[...].astype(F32))
-    middle_ref[...] = middle
-    normed_ref[...] = (
-        normalise(middle)[0] * norms_ref[2:3, :] + norms_ref[3:4, :]
-    ).astype(BF16)
-
-
-def second_norm(x_rows, kept, arrived, norms):
-    args, in_specs = zip(*[plane(one) for one in (x_rows, kept, arrived, norms)])
-    rows, width = in_specs[1].block_shape[-2:]
-    full = pl.BlockSpec((rows, width), lambda i: (0, 0))
-    return run(
-        middle_kernel,
-        "second_norm",
-        [shaped((rows, width), F32), shaped((rows, width), BF16)],
-        20 * rows * width,
-        args,
-        grid=(1,),
-        in_specs=list(in_specs),
-        out_specs=[full, full],
-    )
-
-
-def feed_step(x_rows, gy_rows, w_refs, out_refs):
-    gate_w_ref, up_w_ref, down_w_ref = w_refs
-    hidden_ref, grad_gate_ref, grad_up_ref = out_refs
-    gate = dot_nn(x_rows, gate_w_ref[...])
-    up = dot_nn(x_rows, up_w_ref[...])
-    grad_hidden = dot_nn(gy_rows, down_w_ref[...])
+        + [dma((blocks - 1,)), dma((blocks - 1,)), pltpu.VMEM((blocks - 1,) + last.shape, BF16)]
+        + [dma((2,))],
+    )
+
+
+def feed_kernel(blocks, trades, chained, *refs):
+    stages = (trades + 1).bit_length() - 1
+    refs = list(refs)
+
+    def take(count):
+        taken = refs[:count]
+        del refs[:count]
+        return taken
+
+    first = blocks > 0
+    w_refs = take(3)
+    if first:
+        factor_ref = take(1)[0]
+        x_refs, cot_refs = take(blocks), take(blocks)
+    else:
+        both_ref, total_in, grad_in, _ = take(4)
+    if chained:
+        next_kept, next_sent, next_x, norms_ref = take(4)
+    if first:
+        both_ref, wide_ref, total, grad_total = take(4)
+    else:
+        wide_ref, kept_ref, sent_ref, grad_kept_ref, grad_sent_ref = take(5)
+    if chained:
+        middle_ref, normed_ref, others_ref = take(3)
+    if not first:
+        total, grad_total = take(2)
+    step, steps = pl.program_id(0), pl.num_programs(0)
+
+    gate_w, up_w, down_w = [ref[...] for ref in w_refs]
+    if chained:
+        normed, sum_send, sum_recv, normed_send, normed_recv = take(5)
+        later_sent, arrived = take(stages - 1), take(stages)
+        tensor = lax.axis_index("tensor")
+        others = [{"tensor": flipped(tensor, other + 1)} for other in range(trades)]
+
+        def sum_trade(stage):
+            return send(
+                next_sent if stage == 0 else later_sent[stage - 1],
+                arrived[stage],
+                sum_send.at[stage],
+                sum_recv.at[stage],
+                {"tensor": flipped(tensor, (trades + 1) >> (stage + 1))},
+            )
+
+        def normed_trade(other):
+            return send(
+                normed,
+                others_ref.at[other],
+                normed_send.at[other],
+                normed_recv.at[other],
+                others[other],
+            )
+
+    @pl.when(step == 0)
+    def _():
+        if chained:
+            greet(others)
+            sum_trade(0).start()
+        if first:
+            at_row = 0
+            for x_ref, cot_ref in zip(x_refs, cot_refs):
+                rows = slice(at_row, at_row + x_ref.shape[0])
+                at_row += x_ref.shape[0]
+                both_ref[0, rows, :] = x_ref[...]
+                both_ref[1, rows, :] = (cot_ref[...].astype(F32) * factor_ref[0, 0]).astype(BF16)
+
+    x_rows = both_ref[0]
+    gate = dot_nn(x_rows, gate_w)
+    up = dot_nn(x_rows, up_w)
+    grad_hidden = dot_nn(both_ref[1], down_w)
     sig = jax.nn.sigmoid(gate)
     swish = gate * sig
     hidden = (swish * up).astype(BF16)
     grad_gate = (grad_hidden * up * sig * (1.0 + gate * (1.0 - sig))).astype(BF16)
     grad_up = (grad_hidden * swish).astype(BF16)
-    hidden_ref[...] = hidden
-    grad_gate_ref[...] = grad_gate
-    grad_up_ref[...] = grad_up
-    grad_term = dot_nt(grad_gate, gate_w_ref[...]) + dot_nt(grad_up, up_w_ref[...])
-    return dot_nt(hidden, down_w_ref[...]), grad_term
-
-
-def feed_first_kernel(blocks, factor_ref, *refs):
-    w_refs, refs = refs[:3], refs[3:]
-    x_refs, cot_refs = refs[:blocks], refs[blocks : 2 * blocks]
-    x_all, gy_all = refs[2 * blocks : 2 * blocks + 2]
-    total, grad_total = refs[2 * blocks + 5 :]
-    step = pl.program_id(0)
+    wide_ref[0] = grad_gate
+    wide_ref[1] = grad_up
+    wide_ref[2] = hidden
+    grad_term = dot_nt(grad_gate, gate_w) + dot_nt(grad_up, up_w)
+    term = dot_nt(hidden, down_w)
 
     @pl.when(step == 0)
     def _():
-        at_row = 0
-        for x_ref, cot_ref in zip(x_refs, cot_refs):
-            rows = slice(at_row, at_row + x_ref.shape[0])
-            at_row += x_ref.shape[0]
-            x_all[rows, :] = x_ref[...]
-            gy_all[rows, :] = (cot_ref[...].astype(F32) * factor_ref[0, 0]).astype(BF16)
-
-    term, grad_term = feed_step(
-        x_all[...], gy_all[...], w_refs, refs[2 * blocks + 2 : 2 * blocks + 5]
-    )
-
-    @pl.when(step == 0)
-    def _():
-        total[...] = term
-        grad_total[...] = grad_term
+        total[...] = term if first else total_in[...] + term
+        grad_total[...] = grad_term if first else grad_in[...] + grad_term
 
     @pl.when(step > 0)
     def _():
         total[...] += term
         grad_total[...] += grad_term
 
-
-def feed_last_kernel(*refs):
-    w_refs = refs[:3]
-    x_ref, gy_ref, total_in, grad_in = refs[3:7]
-    kept_ref, sent_ref, grad_kept_ref, grad_sent_ref, total, grad_total = refs[13:]
-    step = pl.program_id(0)
-    term, grad_term = feed_step(x_ref[...], gy_ref[...], w_refs, refs[10:13])
-
-    @pl.when(step == 0)
+    if chained:
+
+        @pl.when(step == steps - 1)
+        def _():
+            kept = next_kept[...]
+            for stage in range(stages):
+                sum_trade(stage).wait_recv()
+                kept = kept + arrived[stage][...].astype(F32)
+                if stage + 1 < stages:
+                    half = kept.shape[0] // 2
+                    later_sent[stage][...] = kept[half:].astype(BF16)
+                    sum_trade(stage + 1).start()
+                    kept = kept[:half]
+            middle = next_x[...].astype(F32) + kept
+            low = (normalise(middle)[0] * norms_ref[2:3, :] + norms_ref[3:4, :]).astype(BF16)
+            normed[...] = low
+            normed_ref[...] = low
+            middle_ref[...] = middle
+
+    @pl.when(step == steps - 1)
     def _():
-        total[...] = total_in[...] + term
-        grad_total[...] = grad_in[...] + grad_term
-
-    @pl.when(step > 0)
-    def _():
-        total[...] += term
-        grad_total[...] += grad_term
-
-    @pl.when(step == pl.num_programs(0) - 1)
-    def _():
-        half = kept_ref.shape[0]
-        kept_ref[...] = total[:half]
-        sent_ref[...] = total[half:].astype(BF16)
-        grad_kept_ref[...] = grad_total[:half]
-        grad_sent_ref[...] = grad_total[half:].astype(BF16)
+        if not first:
+            half = kept_ref.shape[0]
+            kept_ref[...] = total[:half]
+            sent_ref[...] = total[half:].astype(BF16)
+            grad_kept_ref[...] = grad_total[:half]
+            grad_sent_ref[...] = grad_total[half:].astype(BF16)
+        if chained:
+            for other in range(trades):
+                normed_trade(other).start()
+            for stage in range(stages):
+                sum_trade(stage).wait_send()
+            for other in range(trades):
+                normed_trade(other).wait_recv()
+                normed_trade(other).wait_send()
 
 
 def feed_specs(weights):
-    width, part_cols = weights.shape[0], weights.shape[1] // 3
+    lead = weights.shape[:-1]
+    part_cols = weights.shape[-1] // 3
     step = min(512, part_cols)
     steps = part_cols // step
+    zeros = (0,) * len(lead)
     specs = [
-        pl.BlockSpec((width, step), functools.partial(lambda at, i: (0, at + i), k * steps))
+        pl.BlockSpec(
+            lead + (step,), functools.partial(lambda at, i: zeros + (at + i,), k * steps)
+        )
         for k in range(3)
     ]
     return step, steps, specs
 
 
-def feed_first(x_blocks, cot_blocks, factor, weights):
+def full(*shape):
+    return pl.BlockSpec(shape, lambda i: (0,) * len(shape))
+
+
+def feed_first(x_blocks, cot_blocks, factor, weights, trades, chain=None):
     blocks, block_specs = zip(*[plane(block) for block in (*x_blocks, *cot_blocks)])
-    width = x_blocks[0].shape[1]
-    rows = sum(block.shape[0] for block in x_blocks)
+    width = weights.shape[0]
+    rows = sum(spec.block_shape[-2] for spec in block_specs[: len(x_blocks)])
     step, steps, w_specs = feed_specs(weights)
     hidden_cols = 2 * step * steps
-    full = pl.BlockSpec((rows, width), lambda i: (0, 0))
+    anywhere = pl.BlockSpec(memory_space=pl.ANY)
+    args = [weights, weights, weights, factor, *blocks]
+    in_specs = w_specs + [SCALAR] + list(block_specs)
+    out_shape = [shaped((2, rows, width), BF16), shaped((3, rows, hidden_cols), BF16)]
+    out_shape += [shaped((rows, width), F32)] * 2
+    out_specs = [full(2, rows, width), pl.BlockSpec((3, rows, step), lambda i: (0, 0, i))]
+    out_specs += [full(rows, width)] * 2
+    scratch = []
+    if chain is not None:
+        kept, sent, x_rows, norms = chain
+        for one in (kept, None, x_rows, norms):
+            array, spec = (sent, anywhere) if one is None else plane(one)
+            args.append(array)
+            in_specs.append(spec)
+        own = in_specs[-2].block_shape[-2]
+        out_shape += [
+            shaped((own, width), F32),
+            shaped((own, width), BF16),
+            shaped((trades, own, width), BF16),
+        ]
+        out_specs += [full(own, width), full(own, width), anywhere]
+        dma = pltpu.SemaphoreType.DMA
+        stages = [rows >> (stage + 1) for stage in range((trades + 1).bit_length() - 1)]
+        scratch += [pltpu.VMEM((own, width), BF16)]
+        scratch += [dma((len(stages),))] * 2 + [dma((trades,))] * 2
+        scratch += [pltpu.VMEM((count, width), BF16) for count in stages[1:] + stages]
     return run(
-        functools.partial(feed_first_kernel, len(x_blocks)),
+        functools.partial(feed_kernel, len(x_blocks), trades, chain is not None),
         "feed_first",
-        [shaped((rows, width), BF16)] * 2
-        + [shaped((rows, hidden_cols), BF16)] * 3
-        + [shaped((rows, width), F32)] * 2,
+        out_shape,
         6 * rows * width * hidden_cols,
-        [factor, weights, weights, weights, *blocks],
+        args,
+        collective_id=None if chain is None else 5,
         grid=(steps,),
-        in_specs=[SCALAR] + w_specs + list(block_specs),
-        out_specs=[full] * 2 + [pl.BlockSpec((rows, step), lambda i: (0, i))] * 3 + [full] * 2,
-    )
-
-
-def feed_last(x_rows, gy_rows, totals, earlier, weights):
-    rows, width = x_rows.shape
+        in_specs=in_specs,
+        out_specs=out_specs,
+        scratch_shapes=scratch,
+    )
+
+
+def feed_last(both, wide, totals, weights):
+    rows, width = both.shape[1:]
     step, steps, w_specs = feed_specs(weights)
     hidden_cols = 2 * step * steps
-    full = pl.BlockSpec((rows, width), lambda i: (0, 0))
-    half = pl.BlockSpec((rows // 2, width), lambda i: (0, 0))
+    half = full(rows // 2, width)
     return run(
-        feed_last_kernel,
+        functools.partial(feed_kernel, 0, 0, False),
         "feed_last",
-        [shaped((rows, hidden_cols), BF16)] * 3
+        [shaped((3, rows, hidden_cols), BF16)]
         + [shaped((rows // 2, width), F32), shaped((rows // 2, width), BF16)] * 2,
         6 * rows * width * hidden_cols,
-        [weights, weights, weights, x_rows, gy_rows, *totals, *earlier],
+        [weights, weights, weights, both, *totals, wide],
         grid=(steps,),
-        in_specs=w_specs + [full] * 4 + [pl.BlockSpec(memory_space=pl.ANY)] * 3,
-        out_specs=[pl.BlockSpec((rows, step), lambda i: (0, steps + i))] * 3 + [half] * 4,
+        in_specs=w_specs
+        + [full(2, rows, width), full(rows, width), full(rows, width)]
+        + [pl.BlockSpec(memory_space=pl.ANY)],
+        out_specs=[pl.BlockSpec((3, rows, step), lambda i: (0, 0, steps + i))] + [half] * 4,
         scratch_shapes=[pltpu.VMEM((rows, width), F32)] * 2,
-        input_output_aliases={7: 0, 8: 1, 9: 2},
-    )
-
-
-def weights_kernel(windows, starts, masks, *refs):
-    inputs = 2 * windows * len(starts)
-    sources = refs[inputs : inputs + len(masks)]
-    out_ref = refs[inputs + len(masks)]
-    targets = refs[inputs + len(masks) + 1 : inputs + 2 * len(masks) + 1]
+        input_output_aliases={6: 0},
+    )
+
+
+def weights_kernel(windows, masks, *refs):
+    lefts, rights = refs[:windows], refs[windows : 2 * windows]
+    refs = refs[2 * windows :]
+    sources, out_ref, targets = refs[: len(masks)], refs[len(masks)], refs[len(masks) + 1 :]
     at = pl.program_id(0)
+    tensor = lax.axis_index("tensor")
     trades = []
     if masks:
-        send_sem, recv_sem = refs[inputs + 2 * len(masks) + 1 :]
-        tensor = lax.axis_index("tensor")
-        for source, target, kinds in zip(sources, targets, masks):
-            for number, mask in enumerate(kinds):
-                sems = (send_sem.at[len(trades)], recv_sem.at[len(trades)])
-                peer = {"tensor": flipped(tensor, mask)}
-                trades.append(send(source, target.at[number], *sems, peer))
+        targets, (send_sem, recv_sem) = targets[: len(masks)], targets[len(masks) :]
+    for source, target, kinds in zip(sources, targets, masks):
+        for number, mask in enumerate(kinds):
+            sems = (send_sem.at[len(trades)], recv_sem.at[len(trades)])
+            peer = {"tensor": flipped(tensor, mask)}
+            trades.append(send(source, target.at[number], *sems, peer))
+
+    if masks:
 
         @pl.when(at == 0)
         def _():
-            greet(
-                [
-                    {"tensor": flipped(tensor, mask)}
-                    for mask in sorted({mask for kinds in masks for mask in kinds})
-                ]
-            )
+            peers = sorted({mask for kinds in masks for mask in kinds})
+            greet([{"tensor": flipped(tensor, mask)} for mask in peers])
             for trade in trades:
                 trade.start()
 
-    for group, (start, stop) in enumerate(starts):
-        pairs = refs[2 * windows * group : 2 * windows * (group + 1)]
-
-        @pl.when(jnp.logical_and(at >= start, at < stop))
-        def _(pairs=pairs):
-            total = None
-            for left, right in zip(pairs[:windows], pairs[windows:]):
-                term = dot_tn(left[...], right[...])
-                total = term if total is None else total + term
-            out_ref[...] = total.astype(BF16)
+    total = None
+    for left, right in zip(lefts, rights):
+        term = dot_tn(left[...], right[...])
+        total = term if total is None else total + term
+    total = total.astype(BF16)
+    depths, cores, halves, shard = out_ref.shape[:4]
+    for depth in range(depths):
+        for half in range(halves):
+            for core in range(cores):
+                start = ((depth * halves + half) * cores + core) * shard
+                out_ref[depth, core, half] = total[start : start + shard]
 
     if masks:
 
@@ -1115,45 +1191,33 @@
                 trade.wait()
 
 
-def weight_grads(groups, step, name, first=0, parts=1, swaps=(), collective_id=None):
-    windows = len(groups[0][0])
-    args, in_specs, starts = [], [], []
-    at = 0
-    for lefts, rights in groups:
-        for left in lefts:
-            array, spec = plane(left)
-            rows, width = array.shape[-2:]
-            args.append(array)
-            in_specs.append(spec)
-        for right in rights:
-            cols = plane(right)[0].shape[-1]
-            count = cols // (step * parts)
-            place = functools.partial(
-                lambda at, count, i: (0, first * count + jnp.clip(i - at, 0, count - 1)), at, count
-            )
-            array, spec = plane(right, (rows, step), place)
-            args.append(array)
-            in_specs.append(spec)
-        starts.append((at, at + count))
-        at += count
+def feed_weights(boths, wides, part, swaps):
+    windows = len(boths)
+    rows, width = boths[0].shape[1:]
+    hidden_cols = wides[0].shape[2] // 2
+    step = min(512, hidden_cols)
+    steps = hidden_cols // step
+    lead = (lax.axis_size("dp"), lax.axis_size("core"), lax.axis_size("x"))
+    lead += (width // math.prod(lead),)
     masks = [kinds for _, kinds in swaps]
     anywhere = pl.BlockSpec(memory_space=pl.ANY)
-    out_shape = [shaped((width, at * step), BF16)]
-    out_shape += [shaped((len(kinds),) + array.shape, BF16) for array, kinds in swaps]
+    left = pl.BlockSpec((None, rows, width), lambda i: (i // (2 * steps), 0, 0))
+    right = pl.BlockSpec((None, rows, step), lambda i: (i // steps, 0, part * steps + i % steps))
     total = sum(len(kinds) for kinds in masks)
-    outs = run(
-        functools.partial(weights_kernel, windows, starts, masks),
-        name,
-        out_shape,
-        2 * windows * rows * width * at * step,
-        args + [array for array, _ in swaps],
-        collective_id=collective_id,
-        grid=(at,),
-        in_specs=in_specs + [anywhere] * len(swaps),
-        out_specs=[pl.BlockSpec((width, step), lambda i: (0, i))] + [anywhere] * len(swaps),
-        scratch_shapes=[pltpu.SemaphoreType.DMA((total,))] * 2 if total else [],
-    )
-    return outs if swaps else outs[0]
+    return run(
+        functools.partial(weights_kernel, windows, masks),
+        "feed_weights",
+        [shaped(lead + (3 * hidden_cols,), BF16)]
+        + [shaped((len(kinds),) + array.shape, BF16) for array, kinds in swaps],
+        6 * windows * rows * width * hidden_cols,
+        [*boths, *wides] + [array for array, _ in swaps],
+        collective_id=4 if swaps else None,
+        grid=(3 * steps,),
+        in_specs=[left] * windows + [right] * windows + [anywhere] * len(swaps),
+        out_specs=[pl.BlockSpec(lead + (step,), lambda i: (0, 0, 0, 0, i))]
+        + [anywhere] * len(swaps),
+        scratch_shapes=[pltpu.SemaphoreType.DMA((total,))] * 2 if swaps else [],
+    )
 
 
 def norm_grad(kept_ref, arrived_ref, stream, gain, sums_ref):
@@ -1199,7 +1263,7 @@
         self.read, self.rows = part, rows
         self.core_in, self.mine, self.x_in, self.z_in = core_in, mine, x_in, z_in
         self.send_sem, self.recv_sem = send_sem, recv_sem
-        self.seq, self.depth = lax.axis_index("seq"), lax.axis_index("dp")
+        self.seq, self.depth = seq_index(), lax.axis_index("dp")
         self.peers = half_chip_peers()
 
     def place(self, number, other_core):
@@ -1207,7 +1271,7 @@
         seq = flipped(seq, 1) if other_core else seq
         turn = (self.depth + number % 4) % lax.axis_size("dp")
         return pl.ds(
-            pl.multiple_of((turn * lax.axis_size("seq") + seq) * self.rows, self.rows), self.rows
+            pl.multiple_of((turn * seq_size() + seq) * self.rows, self.rows), self.rows
         )
 
     def message(self, number):
@@ -1267,11 +1331,12 @@
         return taken
 
     far_inputs = take(8)
+    shard_ref = take(1)[0]
     norms_ref = take(1)[0]
     second_refs = take(windows)
     grad_refs = take(windows)
     part_refs = take(3 * windows)
-    weights_ref, vectors_ref, input_ref, output_ref = take(4)
+    weights_ref, vectors_ref, input_ref, output_ref, shard_arrived = take(5)
     loads = take(8)
     grad_loads = take(windows)
     part_loads = take(3 * windows)
@@ -1282,12 +1347,12 @@
     stage_sent = [take(stages) for _ in range(windows)]
     stage_arrived = [take(stages) for _ in range(windows)]
     load_sem, big_send, big_recv, small_send, small_recv = take(5)
-    y_send, y_recv, tile_send, tile_recv = take(4)
+    y_send, y_recv, tile_send, tile_recv, shard_sem = take(5)
     assert not refs
     (grad_q, grad_k, grad_v, normed, grad_mid, attended, w_qkv, tokens) = loads[:8]
     tensor = lax.axis_index("tensor")
     others = [{"tensor": flipped(tensor, other + 1)} for other in range(trades)]
-    shards = lax.axis_size("dp") * lax.axis_size("seq")
+    shards = lax.axis_size("dp") * seq_size()
     devices = shards * (trades + 1)
     group = tiles.shape[0] // shards
     width = part.shape[1]
@@ -1361,6 +1426,10 @@
         for number in (2, 3, 1, 0):
             route.add_x(number)
 
+    shard_trade = send(
+        shard_ref, shard_arrived, shard_sem.at[0], shard_sem.at[1], small.peers["far"]
+    )
+    shard_trade.start()
     copies[4].wait()
     copies[5].wait()
     product(3, grad_mid, attended)
@@ -1475,6 +1544,7 @@
         tile_trade(other).wait_recv()
         vectors = vectors + arrived_tiles[other]
     vectors_ref[...] = vectors
+    shard_trade.wait()
     for route in (*routes, small):
         route.sent()
     for w in range(windows):
@@ -1485,12 +1555,23 @@
 
 
 def finish(
-    grads, normed, grad_mid, attended, w_att, tokens, norms, second_sums, grad_middles, parts, trades
+    grads,
+    normed,
+    grad_mid,
+    attended,
+    w_att,
+    tokens,
+    ffn_shard,
+    norms,
+    second_sums,
+    grad_middles,
+    parts,
+    trades,
 ):
     windows, rows, cols = grads[0].shape
     width = w_att.shape[0]
     own_rows = tokens.shape[1]
-    shards = lax.axis_size("dp") * lax.axis_size("seq")
+    shards = lax.axis_size("dp") * seq_size()
     shard = width // shards
     group = 8 * (trades + 1)
     stages = [rows >> (stage + 1) for stage in range((trades + 1).bit_length() - 1)]
@@ -1514,14 +1595,15 @@
             shaped((8, 128), F32),
             shaped((windows, own_rows, width), F32),
             shaped((windows, own_rows, width), BF16),
+            shaped(ffn_shard.shape, BF16),
         ],
         8 * windows * rows * width * cols + 6 * windows * rows * width * cols,
-        [*far_inputs, norms, *second_sums, *grad_middles, *flat],
+        [*far_inputs, ffn_shard, norms, *second_sums, *grad_middles, *flat],
         collective_id=3,
-        in_specs=[anywhere] * 8
+        in_specs=[anywhere] * 9
         + [vmem] * (1 + windows)
         + [anywhere] * (windows + len(flat)),
-        out_specs=[vmem] * 4,
+        out_specs=[vmem] * 4 + [anywhere],
         scratch_shapes=loads
         + [like(array) for array in grad_middles]
         + [like(array) for array in flat]
@@ -1545,6 +1627,7 @@
             dma((windows, len(stages))),
             dma((trades,)),
             dma((trades,)),
+            dma((2,)),
         ],
     )
 
@@ -1569,11 +1652,10 @@
 ):
     windows_here, own_rows, model_width = tokens.shape
     tensor_size = lax.axis_size("tensor")
-    seq_size = lax.axis_size("seq")
     block_rows = own_rows * tensor_size
     head_cols = w_query.shape[1]
     hidden_cols = w_gate.shape[1]
-    shards = ("dp", "seq")
+    shards = ("dp", "x", "core")
 
     own_at = lax.axis_index("tensor")
     starts = jnp.concatenate(
@@ -1582,7 +1664,7 @@
             for other in range(tensor_size)
         ]
     )
-    positions = (lax.axis_index("seq") * block_rows + starts).astype(F32)
+    positions = (seq_index() * block_rows + starts).astype(F32)
     cos_half, sin_half = angles(positions, HEAD_DIM)
     cosine = jnp.concatenate([cos_half] * 4, axis=1)
     sine = jnp.concatenate([-sin_half, sin_half] * 2, axis=1)
@@ -1599,6 +1681,7 @@
     first_ffn = jnp.concatenate([w_gate[:, :part], w_up[:, :part], turned[:, :part]], axis=1)
     last_ffn = jnp.concatenate([w_gate[:, part:], w_up[:, part:], turned[:, part:]], axis=1)
     first_ffn = lax.all_gather(first_ffn, shards, axis=0, tiled=True)
+    upper = lax.axis_index("x") == 1
     w_att, norms, arrived_tokens = gather(
         jnp.concatenate([w_query, w_key, w_value, w_out.T], axis=1),
         tile,
@@ -1609,7 +1692,6 @@
 
     windows = range(windows_here)
     factors = [factor[w].reshape(1, 1) for w in windows]
-    top_bit = seq_size // 2
 
     token_blocks = [tokens] + [arrived_tokens[other] for other in range(tensor_size - 1)]
     normed_rows, queries, own_kv = project(token_blocks, norms, w_att, cosine, sine)
@@ -1632,47 +1714,35 @@
     ]
     middles = [first_middle]
 
-    begun = [
-        feed_first(
-            [first_normed] + [first_others[other] for other in others],
-            cot_blocks[0],
-            factors[0],
-            first_ffn,
-        )
-    ]
-    for w in windows[1:]:
-        kept, arrived = scatter_pair(kept_all[w - 1], sent_all[w - 1], "tensor")
-        middle, normed_mid = second_norm(
-            (tokens, (w,)), hold(kept, begun[-1]), arrived, norms
-        )
-        middles.append(middle)
+    begun = []
+    blocks = [first_normed] + [first_others[other] for other in others]
+    for w in windows:
+        chain = None
+        if w + 1 < windows_here:
+            chain = ((kept_all, (w,)), sent_all[w], (tokens, (w + 1,)), norms)
         begun.append(
-            feed_first(spread(normed_mid, "tensor"), cot_blocks[w], factors[w], first_ffn)
-        )
-    step = min(512, part)
-
-    def feed_weights(done, half, swaps, collective_id):
-        return weight_grads(
-            [
-                ([one[0] for one in done], [one[3] for one in done]),
-                ([one[0] for one in done], [one[4] for one in done]),
-                ([one[1] for one in done], [one[2] for one in done]),
-            ],
-            step,
-            "feed_weights",
-            half,
-            2,
-            swaps,
-            collective_id,
-        )
-
-    g_first_part = feed_weights(begun, 0, (), None)
-    g_first = lax.psum_scatter(g_first_part, shards, scatter_dimension=0, tiled=True)
+            feed_first(blocks, cot_blocks[w], factors[w], first_ffn, tensor_size - 1, chain)
+        )
+        if chain is not None:
+            middle, normed_mid, arrived = begun[-1][4:]
+            middles.append(middle)
+            blocks = [normed_mid] + [arrived[other] for other in others]
+
+    def reduce_ffn(partial):
+        partial = partial.reshape(-1, partial.shape[-1])
+        mine = lax.psum_scatter(partial, ("dp", "core"), scatter_dimension=0, tiled=True)
+        count = mine.shape[0] // 2
+        kept = jnp.where(upper, mine[count:], mine[:count])
+        sent = jnp.where(upper, mine[:count], mine[count:])
+        return kept, sent
+
+    boths = [one[0] for one in begun]
+    g_first_part = feed_weights(boths, [one[1] for one in begun], 0, ())[0]
+    first_kept, first_sent = reduce_ffn(g_first_part)
     fed = []
     for w in windows:
-        x_rows, gy_rows, *parts = hold(begun[w], fed[-1] if fed else g_first_part)
-        ended = feed_last(x_rows, gy_rows, parts[3:], parts[:3], last_ffn)
-        fed.append((x_rows, gy_rows, *ended))
+        both, wide, *totals = hold(begun[w][:4], fed[-1] if fed else g_first_part)
+        fed.append(feed_last(both, wide, totals, last_ffn))
     grad_middles, second_sums = [], []
 
     def through_second_norm(w, kept, arrived):
@@ -1685,55 +1755,59 @@
 
     lows = []
     for w in windows[:-1]:
-        kept, arrived = scatter_pair(fed[w][7], fed[w][8], "tensor")
+        kept, arrived = scatter_pair(fed[w][3], fed[w][4], "tensor")
         lows.append(through_second_norm(w, hold(kept, fed[w + 1]), arrived))
     masks = [other + 1 for other in others]
-    g_last_part, arrived, *arrived_lows = feed_weights(
-        hold(fed, grad_middles),
+    g_ffn_part, arrived, *arrived_lows = feed_weights(
+        boths,
+        [one[0] for one in hold(fed, grad_middles)],
         1,
-        [(fed[-1][8], [tensor_size // 2])] + [(low, masks) for low in lows],
-        4,
-    )
-    g_last = lax.psum_scatter(g_last_part, shards, scatter_dimension=0, tiled=True)
-    kept, arrived = later_pair(fed[-1][7], arrived[0], "tensor")
-    last_low = through_second_norm(windows[-1], hold(kept, g_last_part), arrived)
+        [(fed[-1][4], [tensor_size // 2])] + [(low, masks) for low in lows],
+    )
+    last_kept, last_sent = reduce_ffn(g_ffn_part)
+    kept, arrived = later_pair(fed[-1][3], arrived[0], "tensor")
+    last_low = through_second_norm(windows[-1], hold(kept, g_ffn_part), arrived)
     grad_mid_blocks = [
         [low] + [arrived[other] for other in others] for low, arrived in zip(lows, arrived_lows)
     ] + [[last_low]]
 
-    grad_q, grad_k, grad_v, grad_mid_rows, *arrived_results = attend_back(
-        hold(queries, g_last_part),
+    grad_q, grad_k, grad_v, grad_mid_rows, *arrived_results, first_arrived = attend_back(
+        hold(queries, g_ffn_part),
         wide_attended,
         logs,
         slots_all,
         grad_mid_blocks,
         w_att,
         (cosine, sine),
-        [fed[w][6] for w in windows],
+        [fed[w][2] for w in windows],
+        first_sent,
     )
     parts = [
-        (middles[w], *later_pair(fed[w][5], arrived_results[w], "tensor")) for w in windows
+        (middles[w], *later_pair(fed[w][1], arrived_results[w], "tensor")) for w in windows
     ]
 
-    g_att, vectors, input_grad, output = finish(
+    g_att, vectors, input_grad, output, last_arrived = finish(
         (grad_q, grad_k, grad_v),
         normed_rows,
         grad_mid_rows,
         attended,
         w_att,
         tokens,
+        last_sent,
         norms,
         second_sums,
         grad_middles,
         parts,
         tensor_size - 1,
     )
+    g_first = first_kept.astype(F32) + first_arrived.astype(F32)
+    g_last = last_kept.astype(F32) + last_arrived.astype(F32)
     norm_sums = vectors[:4, : norm1_gain.shape[0]]
     ffn_grads = [
         jnp.concatenate(
             [g_first[:, at * part : (at + 1) * part], g_last[:, at * part : (at + 1) * part]],
             axis=1,
-        ).astype(F32)
+        )
         for at in range(3)
     ]
 
@@ -1755,13 +1829,17 @@
 
 
 def solution(mesh):
-    rows = P("dp", ("seq", "tensor"), None)
-    vector = P(("dp", "seq", "tensor"))
-    tall = P(("dp", "seq"), "tensor")
-    flat = P("tensor", ("dp", "seq"))
+    depth, seq, tensor = mesh.devices.shape
+    finer = jax.sharding.Mesh(
+        mesh.devices.reshape(depth, seq // 2, 2, tensor), ("dp", "x", "core", "tensor")
+    )
+    rows = P("dp", ("x", "core", "tensor"), None)
+    vector = P(("dp", "x", "core", "tensor"))
+    tall = P(("dp", "x", "core"), "tensor")
+    flat = P("tensor", ("dp", "x", "core"))
     return jax.shard_map(
         local,
-        mesh=mesh,
+        mesh=finer,
         in_specs=(
             rows, rows, P("dp"), P("dp"), P(), vector, vector,
             tall, tall, tall, flat, vector, vector, tall, tall, flat,

time: 435 us -> 421 us (0.968)
  waiting for transfers between devices: 11.8 us -> 2.93 us
  other arithmetic: 9.23 us -> 15.3 us
  local copies, waits for them, and re-layouts: 14.9 us -> 9.26 us
    ppermute x3 -> x1, waiting for transfers between devices: 11.7 us -> 0.01 us  [swap(): return lax.ppermute(array, axis, [(i, i ^ bit) for i in range(size)])]
    pallas_call x14 -> x13, Pallas kernels: 373 us -> 369 us  [run(): pl.pallas_call(kernel, out_shape=out_shape, compiler_params=pltpu.Compile...]
  transfers between devices with their start and end apart: 7 -> 5, of which waited for: 1 -> 3; matrix products, arithmetic and copies ran while one was open for 3% -> 3% of each run, Pallas kernels for 87% -> 76%
where the time goes in v8:
time: 421 us; the launch traced here: 413 us
  Pallas kernels  369 us (88%)
  other arithmetic  15.3 us (4%)
  between operations  14.3 us (3%)
  local copies, waits for them, and re-layouts  9.26 us (2%)
    pallas_call x13, Pallas kernels, run(): pl.pallas_call(kernel, out_shape=out_shape, compiler_params=pltpu.Compile...  369 us
  transfers between devices with their start and end apart: 5, of which 3 were waited for; matrix products, arithmetic and copies ran while one was open for 3% of the time, Pallas kernels for 76%

profile of v8, /device:TPU:0, one launch (start us, length us, event | category | flops | bytes accessed | tf_op | source)
XLA Modules:
  0.0 413.4 jit_solution(6633231483168738120)
XLA Ops:
  7.3 0.0 all-gather.3.cloned.1.call-start
  7.3 1.1 fusion.8
  8.4 1.1 fusion.6
  9.5 0.8 pad_maximum_fusion.2
  10.3 0.0 all-gather.3.cloned.1.call-update
  10.3 0.0 all-gather.5.cloned.1.call-start
  10.4 0.0 copy-done.13
  10.4 0.0 copy-done.14
  10.4 0.0 copy-done.15
  10.4 0.0 copy-done.16
  10.5 0.2 fusion.1
  10.7 0.6 fusion.3
  11.3 0.6 broadcast.63
  12.0 0.0 copy-start.10
  12.0 0.7 pad_maximum_fusion.4.att_ref
  12.7 0.0 copy-done.10
  12.7 46.6 %gather.1 = (bf16[1024,2048]{1,0:T(8,128)(2,1)}, f32[8,1024]{1,0:T(8,128)}, bf16[1,2,256,1024]{3,2,1,0:T(8,128)(2,1)}) custom-call(bf16[64,2048]{1,0:T(8,128)(2,1)} %pad_maximum_fusion.4.att_ref, f32[8,128]{1,0:T(8,128)} %copy-done.10, bf16[2,256,1024]{2,1,0:T(8,128)(2,1)} %refs_7_.1), custom_call_target="tpu_custom_call" | custom-call | bytes 6590464 | tf_op jit(solution)/shard_map/gather/pallas_call | solution.py:88
  59.4 1.0 fusion
  60.4 1.0 pad_maximum_fusion.5.cos_ref.refs_5_
  61.4 1.0 pad_maximum_fusion.6.sin_ref.refs_6_
  62.4 8.4 %project.1 = (bf16[2,512,1024]{2,1,0:T(8,128)(2,1)}, bf16[2,512,512]{2,1,0:T(8,128)(2,1)}, bf16[2,2,512,512]{3,2,1,0:T(8,128)(2,1)}) custom-call(f32[8,1024]{1,0:T(8,128)} %get-tuple-element.109.norms_ref.refs_5_.refs_11_.refs_9_, bf16[1024,2048]{1,0:T(8,128)(2,1)} %get-tuple-element.110.w_ref.refs_1_.refs_4_.refs_6_, ...), custom_call_target="tpu_custom_call" | custom-call | flops 3221225472 | bytes 12091392 | tf_op jit(solution)/shard_map/project/pallas_call | solution.py:88
  70.8 0.8 pad_maximum_fusion.3
  71.5 67.1 %attend.1 = (bf16[2,512,512]{2,1,0:T(8,128)(2,1)}, f32[2,512,512]{2,1,0:T(8,128)}, f32[2,512,512]{2,1,0:T(8,128)}, f32[1,256,1024]{2,1,0:T(8,128)}, bf16[1,256,1...) custom-call(bf16[2,512,512]{2,1,0:T(8,128)(2,1)} %get-tuple-element., ...), custom_call_target="tpu_custom_call" | custom-call | flops 17179869184 | bytes 27820032 | tf_op jit(solution)/shard_map/attend/pallas_call | solution.py:88
  138.6 0.0 all-gather.5.cloned.1.call-update
  138.7 0.2 reduce-scatter.3.cloned.1.call-start
  138.9 1.2 slice.128
  140.1 0.7 multiply_divide_fusion
  140.7 0.6 fusion.9
  141.3 32.2 %feed_first.2 = (bf16[2,512,1024]{2,1,0:T(8,128)(2,1)}, bf16[3,512,2048]{2,1,0:T(8,128)(2,1)}, f32[512,1024]{1,0:T(8,128)}, f32[512,1024]{1,0:T(8,128)}, f32[256...) custom-call(bf16[1024,3072]{1,0:T(8,128)(2,1)} %all-gather.3.cloned.1.call-done.refs_0_.refs_1_.refs_2_, ...), custom_call_target="tpu_custom_call" | custom-call | flops 6442450944 | bytes 39354372 | tf_op jit(solution)/shard_map/feed_first/pallas_call | solution.py:88
  173.5 15.5 %feed_first.3 = (bf16[2,512,1024]{2,1,0:T(8,128)(2,1)}, bf16[3,512,2048]{2,1,0:T(8,128)(2,1)}, f32[512,1024]{1,0:T(8,128)}, f32[512,1024]{1,0:T(8,128)}) custom-call(bf16[1024,3072]{1,0:T(8,128)(2,1)} %all-gather.3.cloned.1.call-done.refs_0_.refs_1_.refs_2_, bf16[1024,3072]{1,0:T(8,128)(2,1)} %all-gather.3.cloned.1.call-done.refs_0_.refs_1_.refs_2_, ...), custom_call_target="tpu_custom_call" | custom-call | flops 6442450944 | bytes 34603012 | tf_op jit(solution)/shard_map/feed_first/pallas_call | solution.py:88
  189.0 12.2 %feed_weights.2 = bf16[4,2,2,64,3072]{4,3,2,1,0:T(8,128)(2,1)} custom-call(bf16[2,512,1024]{2,1,0:T(8,128)(2,1)} %get-tuple-element.128.refs_0_.refs_3_, bf16[2,512,1024]{2,1,0:T(8,128)(2,1)} %get-tuple-element.139.refs_1_.refs_3_, bf16[3,512,2048]{2,1,0:T(8,128)(2,1)} %get-tuple-element.131.refs_2_.refs_6_, ...), custom_call_target="tpu_custom_call" | custom-call | flops 6442450944 | bytes 23068672 | tf_op jit(solution)/shard_map/feed_weights/pallas_call | solution.py:88
  201.2 0.0 reduce-scatter.3.cloned.1.call-update
  201.2 0.4 reduce-scatter.5.cloned.1.call-start
  201.7 0.3 all-gather.5.cloned.1.call-done.refs_0_.refs_1_.refs_2_
  202.0 14.8 %feed_last.2 = (bf16[3,512,2048]{2,1,0:T(8,128)(2,1)}, f32[256,1024]{1,0:T(8,128)}, bf16[256,1024]{1,0:T(8,128)(2,1)}, f32[256,1024]{1,0:T(8,128)}, bf16[256,1024]{1,0:T(8,128)(2,1)}) custom-call(bf16[1024,3072]{1,0:T(8,128)(2,1)} %all-gather.5.cloned.1.call-done.refs_0_.refs_1_.refs_2_, ...), custom_call_target="tpu_custom_call", output_to_operand_aliasing={{0}: (6, {})} | custom-call | flops 6442450944 | bytes 40894464 | tf_op jit(solution)/shard_map/feed_last/pallas_call | solution.py:88
  216.7 1.5 collective-permute-start
  218.2 14.9 %feed_last.3 = (bf16[3,512,2048]{2,1,0:T(8,128)(2,1)}, f32[256,1024]{1,0:T(8,128)}, bf16[256,1024]{1,0:T(8,128)(2,1)}, f32[256,1024]{1,0:T(8,128)}, bf16[256,1024]{1,0:T(8,128)(2,1)}) custom-call(bf16[1024,3072]{1,0:T(8,128)(2,1)} %all-gather.5.cloned.1.call-done.refs_0_.refs_1_.refs_2_, ...), custom_call_target="tpu_custom_call", output_to_operand_aliasing={{0}: (6, {})} | custom-call | flops 6442450944 | bytes 40894464 | tf_op jit(solution)/shard_map/feed_last/pallas_call | solution.py:88
  233.1 0.0 collective-permute-done.arrived_ref
  233.1 0.0 copy-start.5
  233.1 0.8 copy-done.5
  233.9 4.5 %second_norm_back.2 = (f32[256,1024]{1,0:T(8,128)}, bf16[256,1024]{1,0:T(8,128)(2,1)}, f32[2,1024]{1,0:T(2,128)}) custom-call(f32[1,1]{1,0:T(1,128)} %bitcast.8.refs_3_.factor_ref, f32[256,1024]{1,0:T(8,128)} %get-tuple-element.148.kept_ref, bf16[256,1024]{1,0:T(8,128)(2,1)} %copy-done.5, f32[256,1024]{1,0:T(8,128)} %get-tuple-element.149.middle_ref.refs_14_, ...), custom_call_target="tpu_custom_call" | custom-call | flops 10485760 | bytes 5283844 | tf_op jit(solution)/shard_map/second_norm_back/pallas_call | solution.py:88
  238.4 28.4 %feed_weights.3 = (bf16[4,2,2,64,3072]{4,3,2,1,0:T(8,128)(2,1)}, bf16[1,256,1024]{2,1,0:T(8,128)(2,1)}, bf16[1,256,1024]{2,1,0:T(8,128)(2,1)}) custom-call(bf16[2,512,1024]{2,1,0:T(8,128)(2,1)} %get-tuple-element.128.refs_0_.refs_3_, bf16[2,512,1024]{2,1,0:T(8,128)(2,1)} %get-tuple-element.139.refs_1_.refs_3_, ...), custom_call_target="tpu_custom_call" | custom-call | flops 6442450944 | bytes 25165824 | tf_op jit(solution)/shard_map/feed_weights/pallas_call | solution.py:88
  266.8 0.0 reduce-scatter.5.cloned.1.call-update
  266.8 4.6 %second_norm_back.3 = (f32[256,1024]{1,0:T(8,128)}, bf16[256,1024]{1,0:T(8,128)(2,1)}, f32[2,1024]{1,0:T(2,128)}) custom-call(f32[1,1]{1,0:T(1,128)} %bitcast.11.refs_3_.factor_ref, f32[256,1024]{1,0:T(8,128)} %get-tuple-element.159.kept_ref, bf16[256,1024]{1,0:T(8,128)(2,1)} %bitcast.33, f32[256,1024]{1,0:T(8,128)} %get-tuple-element.161.middle_ref.refs_17_, ...), custom_call_target="tpu_custom_call" | custom-call | flops 10485760 | bytes 5283844 | tf_op jit(solution)/shard_map/second_norm_back/pallas_call | solution.py:88
  271.4 1.3 reduce-scatter.3.cloned.1.call-done
  272.7 1.9 broadcast_select_fusion.1.refs_13_
  274.6 66.0 %attend_back.1 = (bf16[2,512,512]{2,1,0:T(8,128)(2,1)}, bf16[2,512,512]{2,1,0:T(8,128)(2,1)}, bf16[2,512,512]{2,1,0:T(8,128)(2,1)}, bf16[2,512,1024]{2,1,0:T(8,1...) custom-call(bf16[2,512,512]{2,1,0:T(8,128)(2,1)} %get-tuple-element.155.refs_0_, ...), custom_call_target="tpu_custom_call" | custom-call | flops 42949672960 | bytes 28573696 | tf_op jit(solution)/shard_map/attend_back/pallas_call | solution.py:88
  340.6 0.0 copy-done
  340.6 1.1 convert_add_fusion.1
  341.7 0.1 fusion.4
  341.8 1.3 reduce-scatter.5.cloned.1.call-done
  343.1 1.9 broadcast_select_fusion.refs_8_
  345.0 54.2 %finish.1 = (f32[64,2048]{1,0:T(8,128)}, f32[8,128]{1,0:T(8,128)}, f32[2,256,1024]{2,1,0:T(8,128)}, bf16[2,256,1024]{2,1,0:T(8,128)(2,1)}, bf16[64,3072]{1,0:T(8,128)(2,1)}) custom-call(bf16[2,512,512]{2,1,0:T(8,128)(2,1)} %get-tuple-element.164.refs_0_, bf16[2,512,512]{2,1,0:T(8,128)(2,1)} %get-tuple-element.165.refs_1_, ...), custom_call_target="tpu_custom_call" | custom-call | flops 7516192768 | bytes 25481216 | tf_op jit(solution)/shard_map/finish/pallas_call | solution.py:88
  399.2 0.0 copy-start.12
  399.2 0.0 copy-start.4
  399.3 1.2 convert_add_fusion
  400.5 0.1 fusion.5
  400.5 0.5 slice_bitcast_fusion.1
  401.1 0.8 slice_bitcast_fusion
  401.9 0.8 maximum_bitcast_fusion
  402.7 0.8 pad_maximum_fusion.1
  403.5 0.8 pad_maximum_fusion
  404.4 1.0 copy.37
  405.3 1.3 copy.38
  (33 shorter events, 0.1 us)
Async XLA Ops:
  7.2 3.2 copy-start.13
  7.2 3.2 copy-start.14
  7.2 3.2 copy-start.15
  7.2 3.2 copy-start.16
  7.2 3.2 copy-start.11
  7.2 3.2 copy-start.17
  7.2 3.4 copy-start.18
  7.3 4.7 %copy-start.6 = (bf16[512,64]{0,1:T(8,128)(2,1)S(1)}, bf16[512,64]{0,1:T(8,128)(2,1)}, u32[]{:S(2)}) copy-start(bf16[512,64]{0,1:T(8,128)(2,1)} %param.30) | copy-start | bytes 196612
  7.3 4.7 %copy-start.7 = (bf16[64,512]{1,0:T(8,128)(2,1)S(1)}, bf16[64,512]{1,0:T(8,128)(2,1)}, u32[]{:S(2)}) copy-start(bf16[64,512]{1,0:T(8,128)(2,1)} %param.29) | copy-start | bytes 196612
  7.3 4.7 %copy-start.8 = (bf16[64,512]{1,0:T(8,128)(2,1)S(1)}, bf16[64,512]{1,0:T(8,128)(2,1)}, u32[]{:S(2)}) copy-start(bf16[64,512]{1,0:T(8,128)(2,1)} %param.28) | copy-start | bytes 196612
  7.3 4.7 %copy-start.9 = (bf16[64,512]{1,0:T(8,128)(2,1)S(1)}, bf16[64,512]{1,0:T(8,128)(2,1)}, u32[]{:S(2)}) copy-start(bf16[64,512]{1,0:T(8,128)(2,1)} %param.27) | copy-start | bytes 196612
  7.3 134.0 %all-gather.3.cloned.1.call-start = ((), (), s32[]{:S(2)}) async-start(), calls=%async_computation.2 | async-start | bytes 6684672 | tf_op jit(solution)/shard_map/all_gather | solution.py:1683
  10.3 191.6 %all-gather.5.cloned.1.call-start = ((), (), s32[]{:S(2)}) async-start(), calls=%async_computation.3 | async-start | bytes 6684672 | tf_op jit(solution)/shard_map/all_gather | solution.py:1710
  12.0 0.8 copy-start.10
  138.7 134.1 %reduce-scatter.3.cloned.1.call-start = ((), (), s32[]{:S(2)}) async-start(), calls=%async_computation.4 | async-start | bytes 7077888 | tf_op jit(solution)/shard_map/reduce_scatter | solution.py:1733
  201.2 141.9 %reduce-scatter.5.cloned.1.call-start = ((), (), s32[]{:S(2)}) async-start(), calls=%async_computation.5 | async-start | bytes 7077888 | tf_op jit(solution)/shard_map/reduce_scatter | solution.py:1733
  216.7 16.4 %collective-permute-start = (bf16[256,1024]{1,0:T(8,128)(2,1)}, bf16[256,1024]{1,0:T(8,128)(2,1)S(1)}, u32[]{:S(2)}, u32[]{:S(2)}) collective-permute-start(bf16[256,1024]{1,0:T(8,128)(2,1)} %get-tuple-element.136), channel_id=1, source_target_pairs={{0,1},{1,0},{2,3},{3,2},{4,5},{5,4},{6,7},{7,6},{8,9},{9,8},{10,11... | collective-permute-start | bytes 1572872 | tf_op jit(solution)/shard_map/ppermute | solution.py:45
  233.1 0.8 copy-start.5
  274.6 66.0 %copy-start = (bf16[128,3072]{1,0:T(8,128)(2,1)S(1)}, bf16[128,3072]{1,0:T(8,128)(2,1)}, u32[]{:S(2)}) copy-start(bf16[128,3072]{1,0:T(8,128)(2,1)} %reduce-scatter.3.cloned.1.call-done) | copy-start | bytes 2359300
  345.0 54.3 %copy-start.1 = (bf16[128,3072]{1,0:T(8,128)(2,1)S(1)}, bf16[128,3072]{1,0:T(8,128)(2,1)}, u32[]{:S(2)}) copy-start(bf16[128,3072]{1,0:T(8,128)(2,1)} %reduce-scatter.5.cloned.1.call-done) | copy-start | bytes 2359300
  399.2 1.3 copy-start.12
  399.2 1.8 copy-start.4
  401.1 3.3 copy-start.3
  402.7 2.6 copy-start.2
Sparse Core Ops, SparseCore 0:
  11.0 75.9 all-gather.2
  138.8 63.1 all-gather.4
  204.3 68.3 reduce-scatter.2
  274.9 68.1 reduce-scatter.4

commit v9 on v8

--- a/solution.py
+++ b/solution.py
@@ -154,19 +154,21 @@
         cosine, sine = cos_ref[rows, :], sin_ref[rows, :]
         query = dot_nn(normed, w_ref[:, :cols])
         key = dot_nn(normed, w_ref[:, cols : 2 * cols])
+        value = dot_nn(normed, w_ref[:, 2 * cols : 3 * cols]).astype(BF16)
         for at in range(0, cols, PAIR):
-            part = slice(at, at + PAIR)
+            part, pair = slice(at, at + PAIR), at // PAIR
             one = query[:, part]
             q_ref[0, rows, part] = (one * cosine + swap_halves(one) * sine).astype(BF16)
             one = key[:, part]
-            kv_ref[0, 0, rows, part] = (one * cosine + swap_halves(one) * sine).astype(BF16)
-        kv_ref[0, 1, rows, :] = dot_nn(normed, w_ref[:, 2 * cols : 3 * cols]).astype(BF16)
+            kv_ref[0, pair, 0, rows, :] = (one * cosine + swap_halves(one) * sine).astype(BF16)
+            kv_ref[0, pair, 1, rows, :] = value[:, part]
 
 
 def project(x_blocks, norms, w_att, cosine, sine):
     windows = x_blocks[0].shape[0]
     width, cols = w_att.shape[0], w_att.shape[1] // 4
     rows = sum(block.shape[1] for block in x_blocks)
+    pieces = (cols // PAIR, 2, rows, PAIR)
     args = [norms, w_att, cosine, sine, *x_blocks]
     return run(
         functools.partial(project_kernel, len(x_blocks)),
@@ -174,7 +176,7 @@
         [
             shaped((windows, rows, width), BF16),
             shaped((windows, rows, cols), BF16),
-            shaped((windows, 2, rows, cols), BF16),
+            shaped((windows,) + pieces, BF16),
         ],
         6 * windows * rows * width * cols,
         args,
@@ -184,7 +186,7 @@
         out_specs=[
             pl.BlockSpec((1, rows, width), lambda i: (i, 0, 0)),
             pl.BlockSpec((1, rows, cols), lambda i: (i, 0, 0)),
-            pl.BlockSpec((1, 2, rows, cols), lambda i: (i, 0, 0, 0)),
+            pl.BlockSpec((1,) + pieces, lambda i: (i, 0, 0, 0, 0)),
         ],
     )
 
@@ -418,8 +420,7 @@
     cot_peers = [{"tensor": flipped(tensor, other + 1)} for other in range(trades)]
 
     def piece(number):
-        columns = pl.ds(pl.multiple_of((number % pairs) * PAIR, PAIR), PAIR)
-        return kv_ref.at[number // pairs, :, :, columns]
+        return kv_ref.at[number // pairs, number % pairs]
 
     def own_copy(number):
         return pltpu.make_async_copy(piece(number), slots.at[number, 0], own_sem.at[number])
@@ -698,12 +699,11 @@
     known = (windows - 1) * blocks + 1
     grad_refs = list(refs[8 : 8 + known])
     refs = refs[8 + known :]
-    sent_refs, shard_ref, refs = refs[:windows], refs[windows], refs[windows + 1 :]
+    sent_refs, refs = refs[:windows], refs[windows:]
     gq_ref, gk_ref, gv_ref, rows_ref = refs[:4]
-    arrived_refs, shard_arrived = refs[4 : 4 + windows], refs[4 + windows]
-    refs = refs[5 + windows :]
+    arrived_refs, refs = refs[4 : 4 + windows], refs[4 + windows :]
     dq_all, do_all, far_kept, far_sent, far_core, far_x, near_kept, near_sent, near_core = refs[:9]
-    send_sem, recv_sem, result_send, result_recv, last_send, last_recv, last_others, shard_sem = refs[9:]
+    send_sem, recv_sem, result_send, result_recv, last_send, last_recv, last_others = refs[9:]
     grad_refs += [last_others.at[other] for other in range(trades)]
     step = pl.program_id(0)
     count = windows * pairs
@@ -738,13 +738,9 @@
             last_ref, last_others.at[other], last_send.at[other], last_recv.at[other], others[other]
         )
 
-    def shard_trade():
-        return send(shard_ref, shard_arrived, shard_sem.at[0], shard_sem.at[1], far_peer)
-
     @pl.when(step == 0)
     def _():
         greet([core_peer, far_peer] + others)
-        shard_trade().start()
         for other in range(trades):
             last_trade(other).start()
         for w in range(windows):
@@ -858,7 +854,6 @@
             for kind in range(3):
                 trade(kind, number).wait_send()
 
-        shard_trade().wait()
         for other in range(trades):
             last_trade(other).wait_send()
         for w in range(windows):
@@ -866,7 +861,7 @@
             result_trade(w).wait_recv()
 
 
-def attend_back(queries, wide, logs, slots_all, grad_blocks, w_att, tables, sent, shard):
+def attend_back(queries, wide, logs, slots_all, grad_blocks, w_att, tables, sent):
     windows, rows, cols = queries.shape
     width = w_att.shape[0]
     pairs = cols // PAIR
@@ -897,9 +892,9 @@
         "attend_back",
         [shaped((windows, rows, cols), BF16)] * 3
         + [shaped((windows, rows, width), BF16)]
-        + [shaped(one.shape, BF16) for one in (*sent, shard)],
+        + [shaped(one.shape, BF16) for one in sent],
         160 * windows * rows * rows * cols,
-        [queries, wide, logs, slots_all, w_att, *tables, last, *grads, *sent, shard],
+        [queries, wide, logs, slots_all, w_att, *tables, last, *grads, *sent],
         collective_id=2,
         grid=(2 * count + 2,),
         in_specs=[
@@ -916,24 +911,46 @@
             anywhere,
         ]
         + [pl.BlockSpec(block.shape, lambda i: (0, 0)) for block in grads]
-        + [anywhere] * (windows + 1),
+        + [anywhere] * windows,
         out_specs=[
             spot(count),
             spot(count + 2),
             spot(count + 2),
             pl.BlockSpec((1, rows, width), lambda i: (jnp.minimum(i // pairs, windows - 1), 0, 0)),
         ]
-        + [anywhere] * (windows + 1),
+        + [anywhere] * windows,
         scratch_shapes=[pltpu.VMEM((count, rows, PAIR), F32), pltpu.VMEM((count, rows, PAIR), BF16)]
         + [piece] * 7
         + [dma((3, count)), dma((3, count)), dma((windows,)), dma((windows,))]
-        + [dma((blocks - 1,)), dma((blocks - 1,)), pltpu.VMEM((blocks - 1,) + last.shape, BF16)]
-        + [dma((2,))],
-    )
-
-
-def feed_kernel(blocks, trades, chained, *refs):
-    stages = (trades + 1).bit_length() - 1
+        + [dma((blocks - 1,)), dma((blocks - 1,)), pltpu.VMEM((blocks - 1,) + last.shape, BF16)],
+    )
+
+
+def middle_kernel(x_ref, kept_ref, arrived_ref, norms_ref, middle_ref, normed_ref):
+    middle = x_ref[...].astype(F32) + (kept_ref[...] + arrived_ref[...].astype(F32))
+    middle_ref[...] = middle
+    normed_ref[...] = (
+        normalise(middle)[0] * norms_ref[2:3, :] + norms_ref[3:4, :]
+    ).astype(BF16)
+
+
+def second_norm(x_rows, kept, arrived, norms):
+    args, in_specs = zip(*[plane(one) for one in (x_rows, kept, arrived, norms)])
+    rows, width = in_specs[1].block_shape[-2:]
+    full = pl.BlockSpec((rows, width), lambda i: (0, 0))
+    return run(
+        middle_kernel,
+        "second_norm",
+        [shaped((rows, width), F32), shaped((rows, width), BF16)],
+        20 * rows * width,
+        args,
+        grid=(1,),
+        in_specs=list(in_specs),
+        out_specs=[full, full],
+    )
+
+
+def feed_kernel(blocks, swaps, first, *refs):
     refs = list(refs)
 
     def take(count):
@@ -941,62 +958,46 @@
         del refs[:count]
         return taken
 
-    first = blocks > 0
     w_refs = take(3)
     if first:
         factor_ref = take(1)[0]
         x_refs, cot_refs = take(blocks), take(blocks)
+        sources = take(len(swaps))
+        both_ref, wide_ref, total_ref, grad_ref = take(4)
     else:
         both_ref, total_in, grad_in, _ = take(4)
-    if chained:
-        next_kept, next_sent, next_x, norms_ref = take(4)
+        sources = take(len(swaps))
+        wide_ref, kept_ref, sent_ref, grad_kept_ref, grad_sent_ref = take(5)
+    trades = tensor_trades(sources, take(len(swaps)), swaps, *take(2 if swaps else 0))
+    block = pl.program_id(0)
+
+    def weights_of(ref):
+        if len(ref.shape) == 2:
+            return ref[...]
+        depths, cores, halves = ref.shape[:3]
+        return jnp.concatenate(
+            [
+                ref[depth, core, half]
+                for depth in range(depths)
+                for half in range(halves)
+                for core in range(cores)
+            ],
+            axis=0,
+        )
+
+    gate_w, up_w, down_w = [weights_of(ref) for ref in w_refs]
+
+    @pl.when(block == 0)
+    def _():
+        start_trades(trades, swaps)
+
     if first:
-        both_ref, wide_ref, total, grad_total = take(4)
-    else:
-        wide_ref, kept_ref, sent_ref, grad_kept_ref, grad_sent_ref = take(5)
-    if chained:
-        middle_ref, normed_ref, others_ref = take(3)
-    if not first:
-        total, grad_total = take(2)
-    step, steps = pl.program_id(0), pl.num_programs(0)
-
-    gate_w, up_w, down_w = [ref[...] for ref in w_refs]
-    if chained:
-        normed, sum_send, sum_recv, normed_send, normed_recv = take(5)
-        later_sent, arrived = take(stages - 1), take(stages)
-        tensor = lax.axis_index("tensor")
-        others = [{"tensor": flipped(tensor, other + 1)} for other in range(trades)]
-
-        def sum_trade(stage):
-            return send(
-                next_sent if stage == 0 else later_sent[stage - 1],
-                arrived[stage],
-                sum_send.at[stage],
-                sum_recv.at[stage],
-                {"tensor": flipped(tensor, (trades + 1) >> (stage + 1))},
-            )
-
-        def normed_trade(other):
-            return send(
-                normed,
-                others_ref.at[other],
-                normed_send.at[other],
-                normed_recv.at[other],
-                others[other],
-            )
-
-    @pl.when(step == 0)
-    def _():
-        if chained:
-            greet(others)
-            sum_trade(0).start()
-        if first:
-            at_row = 0
-            for x_ref, cot_ref in zip(x_refs, cot_refs):
-                rows = slice(at_row, at_row + x_ref.shape[0])
-                at_row += x_ref.shape[0]
-                both_ref[0, rows, :] = x_ref[...]
-                both_ref[1, rows, :] = (cot_ref[...].astype(F32) * factor_ref[0, 0]).astype(BF16)
+        for at in range(blocks):
+
+            @pl.when(block == at)
+            def _(at=at):
+                both_ref[0] = x_refs[at][...]
+                both_ref[1] = (cot_refs[at][...].astype(F32) * factor_ref[0, 0]).astype(BF16)
 
     x_rows = both_ref[0]
     gate = dot_nn(x_rows, gate_w)
@@ -1010,139 +1011,137 @@
     wide_ref[0] = grad_gate
     wide_ref[1] = grad_up
     wide_ref[2] = hidden
-    grad_term = dot_nt(grad_gate, gate_w) + dot_nt(grad_up, up_w)
-    term = dot_nt(hidden, down_w)
-
-    @pl.when(step == 0)
+    grad_total = dot_nt(grad_gate, gate_w) + dot_nt(grad_up, up_w)
+    total = dot_nt(hidden, down_w)
+    if first:
+        total_ref[...] = total
+        grad_ref[...] = grad_total
+    else:
+        total = total + total_in[...]
+        grad_total = grad_total + grad_in[...]
+        rows = total.shape[0]
+        for at in range(blocks):
+
+            @pl.when(block == at)
+            def _(at=at):
+                start = (at % (blocks // 2)) * rows
+                if at < blocks // 2:
+                    kept_ref[start : start + rows] = total
+                    grad_kept_ref[start : start + rows] = grad_total
+                else:
+                    sent_ref[start : start + rows] = total.astype(BF16)
+                    grad_sent_ref[start : start + rows] = grad_total.astype(BF16)
+
+    @pl.when(block == blocks - 1)
     def _():
-        total[...] = term if first else total_in[...] + term
-        grad_total[...] = grad_term if first else grad_in[...] + grad_term
-
-    @pl.when(step > 0)
-    def _():
-        total[...] += term
-        grad_total[...] += grad_term
-
-    if chained:
-
-        @pl.when(step == steps - 1)
-        def _():
-            kept = next_kept[...]
-            for stage in range(stages):
-                sum_trade(stage).wait_recv()
-                kept = kept + arrived[stage][...].astype(F32)
-                if stage + 1 < stages:
-                    half = kept.shape[0] // 2
-                    later_sent[stage][...] = kept[half:].astype(BF16)
-                    sum_trade(stage + 1).start()
-                    kept = kept[:half]
-            middle = next_x[...].astype(F32) + kept
-            low = (normalise(middle)[0] * norms_ref[2:3, :] + norms_ref[3:4, :]).astype(BF16)
-            normed[...] = low
-            normed_ref[...] = low
-            middle_ref[...] = middle
-
-    @pl.when(step == steps - 1)
-    def _():
-        if not first:
-            half = kept_ref.shape[0]
-            kept_ref[...] = total[:half]
-            sent_ref[...] = total[half:].astype(BF16)
-            grad_kept_ref[...] = grad_total[:half]
-            grad_sent_ref[...] = grad_total[half:].astype(BF16)
-        if chained:
-            for other in range(trades):
-                normed_trade(other).start()
-            for stage in range(stages):
-                sum_trade(stage).wait_send()
-            for other in range(trades):
-                normed_trade(other).wait_recv()
-                normed_trade(other).wait_send()
+        for trade in trades:
+            trade.wait()
+
+
+def tensor_trades(sources, targets, masks, send_sem=None, recv_sem=None):
+    tensor = lax.axis_index("tensor")
+    trades = []
+    for source, target, kinds in zip(sources, targets, masks):
+        for number, mask in enumerate(kinds):
+            sems = (send_sem.at[len(trades)], recv_sem.at[len(trades)])
+            peer = {"tensor": flipped(tensor, mask)}
+            trades.append(send(source, target.at[number], *sems, peer))
+    return trades
+
+
+def start_trades(trades, masks):
+    if trades:
+        tensor = lax.axis_index("tensor")
+        peers = sorted({mask for kinds in masks for mask in kinds})
+        greet([{"tensor": flipped(tensor, mask)} for mask in peers])
+        for trade in trades:
+            trade.start()
 
 
 def feed_specs(weights):
     lead = weights.shape[:-1]
     part_cols = weights.shape[-1] // 3
-    step = min(512, part_cols)
-    steps = part_cols // step
     zeros = (0,) * len(lead)
-    specs = [
-        pl.BlockSpec(
-            lead + (step,), functools.partial(lambda at, i: zeros + (at + i,), k * steps)
-        )
+    return part_cols, [
+        pl.BlockSpec(lead + (part_cols,), functools.partial(lambda at, i: zeros + (at,), k))
         for k in range(3)
     ]
-    return step, steps, specs
 
 
 def full(*shape):
     return pl.BlockSpec(shape, lambda i: (0,) * len(shape))
 
 
-def feed_first(x_blocks, cot_blocks, factor, weights, trades, chain=None):
-    blocks, block_specs = zip(*[plane(block) for block in (*x_blocks, *cot_blocks)])
-    width = weights.shape[0]
-    rows = sum(spec.block_shape[-2] for spec in block_specs[: len(x_blocks)])
-    step, steps, w_specs = feed_specs(weights)
-    hidden_cols = 2 * step * steps
+def feed_call(name, collective_id, blocks, rows, width, part_cols, out, args, swaps, **options):
+    masks = [kinds for _, kinds in swaps]
     anywhere = pl.BlockSpec(memory_space=pl.ANY)
-    args = [weights, weights, weights, factor, *blocks]
-    in_specs = w_specs + [SCALAR] + list(block_specs)
-    out_shape = [shaped((2, rows, width), BF16), shaped((3, rows, hidden_cols), BF16)]
+    total = sum(len(kinds) for kinds in masks)
+    out_shape, out_specs = out
+    return run(
+        functools.partial(feed_kernel, blocks, masks, name == "feed_first"),
+        name,
+        out_shape + [shaped((len(kinds),) + array.shape, BF16) for array, kinds in swaps],
+        12 * rows * width * part_cols,
+        args + [array for array, _ in swaps],
+        collective_id=collective_id if swaps else None,
+        grid=(blocks,),
+        in_specs=options.pop("in_specs") + [anywhere] * len(swaps),
+        out_specs=out_specs + [anywhere] * len(swaps),
+        scratch_shapes=[pltpu.SemaphoreType.DMA((total,))] * 2 if swaps else [],
+        **options,
+    )
+
+
+def feed_first(x_blocks, cot_blocks, factor, weights, swaps=()):
+    operands, specs = zip(*[plane(block) for block in (*x_blocks, *cot_blocks)])
+    width = math.prod(weights.shape[:-1])
+    blocks, own = len(x_blocks), specs[0].block_shape[-2]
+    rows = blocks * own
+    part_cols, w_specs = feed_specs(weights)
+    row_block = pl.BlockSpec((own, width), lambda i: (i, 0))
+    out_shape = [shaped((2, rows, width), BF16), shaped((3, rows, 2 * part_cols), BF16)]
     out_shape += [shaped((rows, width), F32)] * 2
-    out_specs = [full(2, rows, width), pl.BlockSpec((3, rows, step), lambda i: (0, 0, i))]
-    out_specs += [full(rows, width)] * 2
-    scratch = []
-    if chain is not None:
-        kept, sent, x_rows, norms = chain
-        for one in (kept, None, x_rows, norms):
-            array, spec = (sent, anywhere) if one is None else plane(one)
-            args.append(array)
-            in_specs.append(spec)
-        own = in_specs[-2].block_shape[-2]
-        out_shape += [
-            shaped((own, width), F32),
-            shaped((own, width), BF16),
-            shaped((trades, own, width), BF16),
-        ]
-        out_specs += [full(own, width), full(own, width), anywhere]
-        dma = pltpu.SemaphoreType.DMA
-        stages = [rows >> (stage + 1) for stage in range((trades + 1).bit_length() - 1)]
-        scratch += [pltpu.VMEM((own, width), BF16)]
-        scratch += [dma((len(stages),))] * 2 + [dma((trades,))] * 2
-        scratch += [pltpu.VMEM((count, width), BF16) for count in stages[1:] + stages]
-    return run(
-        functools.partial(feed_kernel, len(x_blocks), trades, chain is not None),
+    out_specs = [
+        pl.BlockSpec((2, own, width), lambda i: (0, i, 0)),
+        pl.BlockSpec((3, own, part_cols), lambda i: (0, i, 0)),
+        row_block,
+        row_block,
+    ]
+    return feed_call(
         "feed_first",
-        out_shape,
-        6 * rows * width * hidden_cols,
-        args,
-        collective_id=None if chain is None else 5,
-        grid=(steps,),
-        in_specs=in_specs,
-        out_specs=out_specs,
-        scratch_shapes=scratch,
-    )
-
-
-def feed_last(both, wide, totals, weights):
+        6,
+        blocks,
+        rows,
+        width,
+        part_cols,
+        (out_shape, out_specs),
+        [weights, weights, weights, factor, *operands],
+        swaps,
+        in_specs=w_specs + [SCALAR] + list(specs),
+    )
+
+
+def feed_last(both, wide, totals, weights, blocks, swaps=()):
     rows, width = both.shape[1:]
-    step, steps, w_specs = feed_specs(weights)
-    hidden_cols = 2 * step * steps
+    own = rows // blocks
+    part_cols, w_specs = feed_specs(weights)
     half = full(rows // 2, width)
-    return run(
-        functools.partial(feed_kernel, 0, 0, False),
+    row_block = pl.BlockSpec((own, width), lambda i: (i, 0))
+    out_shape = [shaped(wide.shape, BF16)]
+    out_shape += [shaped((rows // 2, width), F32), shaped((rows // 2, width), BF16)] * 2
+    return feed_call(
         "feed_last",
-        [shaped((3, rows, hidden_cols), BF16)]
-        + [shaped((rows // 2, width), F32), shaped((rows // 2, width), BF16)] * 2,
-        6 * rows * width * hidden_cols,
+        5,
+        blocks,
+        rows,
+        width,
+        part_cols,
+        (out_shape, [pl.BlockSpec((3, own, part_cols), lambda i: (0, i, 1))] + [half] * 4),
         [weights, weights, weights, both, *totals, wide],
-        grid=(steps,),
+        swaps,
         in_specs=w_specs
-        + [full(2, rows, width), full(rows, width), full(rows, width)]
+        + [pl.BlockSpec((2, own, width), lambda i: (0, i, 0)), row_block, row_block]
         + [pl.BlockSpec(memory_space=pl.ANY)],
-        out_specs=[pl.BlockSpec((3, rows, step), lambda i: (0, 0, steps + i))] + [half] * 4,
-        scratch_shapes=[pltpu.VMEM((rows, width), F32)] * 2,
         input_output_aliases={6: 0},
     )
 
@@ -1152,24 +1151,11 @@
     refs = refs[2 * windows :]
     sources, out_ref, targets = refs[: len(masks)], refs[len(masks)], refs[len(masks) + 1 :]
     at = pl.program_id(0)
-    tensor = lax.axis_index("tensor")
-    trades = []
-    if masks:
-        targets, (send_sem, recv_sem) = targets[: len(masks)], targets[len(masks) :]
-    for source, target, kinds in zip(sources, targets, masks):
-        for number, mask in enumerate(kinds):
-            sems = (send_sem.at[len(trades)], recv_sem.at[len(trades)])
-            peer = {"tensor": flipped(tensor, mask)}
-            trades.append(send(source, target.at[number], *sems, peer))
-
-    if masks:
-
-        @pl.when(at == 0)
-        def _():
-            peers = sorted({mask for kinds in masks for mask in kinds})
-            greet([{"tensor": flipped(tensor, mask)} for mask in peers])
-            for trade in trades:
-                trade.start()
+    trades = tensor_trades(refs[: len(masks)], targets[: len(masks)], masks, *targets[len(masks) :])
+
+    @pl.when(at == 0)
+    def _():
+        start_trades(trades, masks)
 
     total = None
     for left, right in zip(lefts, rights):
@@ -1426,8 +1412,14 @@
         for number in (2, 3, 1, 0):
             route.add_x(number)
 
+    count = shard_ref.shape[0] // 2
+    far_rows = pl.ds(pl.multiple_of((1 - lax.axis_index("x")) * count, count), count)
     shard_trade = send(
-        shard_ref, shard_arrived, shard_sem.at[0], shard_sem.at[1], small.peers["far"]
+        shard_ref.at[far_rows, :],
+        shard_arrived,
+        shard_sem.at[0],
+        shard_sem.at[1],
+        small.peers["far"],
     )
     shard_trade.start()
     copies[4].wait()
@@ -1595,7 +1587,7 @@
             shaped((8, 128), F32),
             shaped((windows, own_rows, width), F32),
             shaped((windows, own_rows, width), BF16),
-            shaped(ffn_shard.shape, BF16),
+            shaped((ffn_shard.shape[0] // 2, ffn_shard.shape[1]), BF16),
         ],
         8 * windows * rows * width * cols + 6 * windows * rows * width * cols,
         [*far_inputs, ffn_shard, norms, *second_sums, *grad_middles, *flat],
@@ -1680,8 +1672,21 @@
     turned = w_down.T
     first_ffn = jnp.concatenate([w_gate[:, :part], w_up[:, :part], turned[:, :part]], axis=1)
     last_ffn = jnp.concatenate([w_gate[:, part:], w_up[:, part:], turned[:, part:]], axis=1)
+    upper = lax.axis_index("x") == 1
+
+    def gather_ffn(own, across):
+        pair = jnp.where(
+            upper,
+            jnp.concatenate([across, own], axis=0),
+            jnp.concatenate([own, across], axis=0),
+        )
+        whole = lax.all_gather(pair, ("dp", "core"), axis=0, tiled=True)
+        return whole.reshape(
+            lax.axis_size("dp"), lax.axis_size("core"), lax.axis_size("x"), -1, whole.shape[1]
+        )
+
     first_ffn = lax.all_gather(first_ffn, shards, axis=0, tiled=True)
-    upper = lax.axis_index("x") == 1
+    last_across = swap(last_ffn, "x", 1)
     w_att, norms, arrived_tokens = gather(
         jnp.concatenate([w_query, w_key, w_value, w_out.T], axis=1),
         tile,
@@ -1695,6 +1700,7 @@
 
     token_blocks = [tokens] + [arrived_tokens[other] for other in range(tensor_size - 1)]
     normed_rows, queries, own_kv = project(token_blocks, norms, w_att, cosine, sine)
+    last_ffn = gather_ffn(last_ffn, hold(last_across, w_att))
     (
         attended,
         wide_attended,
@@ -1707,43 +1713,23 @@
         first_normed,
         first_others,
     ) = attend(queries, own_kv, w_att, cotangent, tokens, norms, tensor_size - 1)
-    last_ffn = lax.all_gather(hold(last_ffn, kept_all), shards, axis=0, tiled=True)
     others = range(tensor_size - 1)
     cot_blocks = [
         [(cotangent, (w,))] + [(cots, (other, w)) for other in others] for w in windows
     ]
     middles = [first_middle]
 
-    begun = []
-    blocks = [first_normed] + [first_others[other] for other in others]
-    for w in windows:
-        chain = None
-        if w + 1 < windows_here:
-            chain = ((kept_all, (w,)), sent_all[w], (tokens, (w + 1,)), norms)
-        begun.append(
-            feed_first(blocks, cot_blocks[w], factors[w], first_ffn, tensor_size - 1, chain)
-        )
-        if chain is not None:
-            middle, normed_mid, arrived = begun[-1][4:]
-            middles.append(middle)
-            blocks = [normed_mid] + [arrived[other] for other in others]
-
     def reduce_ffn(partial):
         partial = partial.reshape(-1, partial.shape[-1])
         mine = lax.psum_scatter(partial, ("dp", "core"), scatter_dimension=0, tiled=True)
         count = mine.shape[0] // 2
         kept = jnp.where(upper, mine[count:], mine[:count])
-        sent = jnp.where(upper, mine[:count], mine[count:])
-        return kept, sent
-
-    boths = [one[0] for one in begun]
-    g_first_part = feed_weights(boths, [one[1] for one in begun], 0, ())[0]
-    first_kept, first_sent = reduce_ffn(g_first_part)
-    fed = []
-    for w in windows:
-        both, wide, *totals = hold(begun[w][:4], fed[-1] if fed else g_first_part)
-        fed.append(feed_last(both, wide, totals, last_ffn))
+        return kept, mine
+
+    blocks = [first_normed] + [first_others[other] for other in others]
+    begun, fed, lows, arrived_lows = [], [], [], []
     grad_middles, second_sums = [], []
+    masks = [other + 1 for other in others]
 
     def through_second_norm(w, kept, arrived):
         grad_middle, low, sums = second_norm_back(
@@ -1753,16 +1739,45 @@
         second_sums.append(sums)
         return low
 
-    lows = []
-    for w in windows[:-1]:
-        kept, arrived = scatter_pair(fed[w][3], fed[w][4], "tensor")
-        lows.append(through_second_norm(w, hold(kept, fed[w + 1]), arrived))
-    masks = [other + 1 for other in others]
-    g_ffn_part, arrived, *arrived_lows = feed_weights(
-        boths,
-        [one[0] for one in hold(fed, grad_middles)],
+    for w in windows:
+        swaps = [(fed[-1][4], [tensor_size // 2])] if fed else []
+        started = feed_first(blocks, cot_blocks[w], factors[w], first_ffn, swaps)
+        begun.append(started[:4])
+        if w + 1 < windows_here:
+            kept, arrived = scatter_pair(kept_all[w], sent_all[w], "tensor")
+            middle, normed_mid = second_norm(
+                (tokens, (w + 1,)), hold(kept, begun[-1]), arrived, norms
+            )
+            middles.append(middle)
+            blocks = hold(spread(normed_mid, "tensor"), fed)
+            after = normed_mid
+        else:
+            g_first_part = feed_weights(
+                [one[0] for one in begun],
+                [one[0] for one in fed] + [one[1] for one in begun[len(fed) :]],
+                0,
+                (),
+            )[0]
+            first_kept, first_sent = reduce_ffn(g_first_part)
+            after = g_first_part
+        swaps = ()
+        if w > 0:
+            kept, arrived = later_pair(fed[-1][3], started[4][0], "tensor")
+            low = through_second_norm(w - 1, hold(kept, g_first_part), arrived)
+            lows.append(low)
+            swaps = [(low, masks)]
+            after = low
+        both, wide, *totals = hold(begun[w], after)
+        ended = feed_last(both, wide, totals, last_ffn, tensor_size, swaps)
+        fed.append(ended[:5])
+        arrived_lows += ended[5:]
+        if w + 1 < windows_here:
+            blocks = hold(blocks, ended[3])
+    g_ffn_part, arrived = feed_weights(
+        [one[0] for one in begun],
+        [one[0] for one in fed],
         1,
-        [(fed[-1][4], [tensor_size // 2])] + [(low, masks) for low in lows],
+        [(fed[-1][4], [tensor_size // 2])],
     )
     last_kept, last_sent = reduce_ffn(g_ffn_part)
     kept, arrived = later_pair(fed[-1][3], arrived[0], "tensor")
@@ -1771,7 +1786,7 @@
         [low] + [arrived[other] for other in others] for low, arrived in zip(lows, arrived_lows)
     ] + [[last_low]]
 
-    grad_q, grad_k, grad_v, grad_mid_rows, *arrived_results, first_arrived = attend_back(
+    grad_q, grad_k, grad_v, grad_mid_rows, *arrived_results = attend_back(
         hold(queries, g_ffn_part),
         wide_attended,
         logs,
@@ -1780,20 +1795,19 @@
         w_att,
         (cosine, sine),
         [fed[w][2] for w in windows],
-        first_sent,
     )
     parts = [
         (middles[w], *later_pair(fed[w][1], arrived_results[w], "tensor")) for w in windows
     ]
 
-    g_att, vectors, input_grad, output, last_arrived = finish(
+    g_att, vectors, input_grad, output, first_arrived = finish(
         (grad_q, grad_k, grad_v),
         normed_rows,
         grad_mid_rows,
         attended,
         w_att,
         tokens,
-        last_sent,
+        first_sent,
         norms,
         second_sums,
         grad_middles,
@@ -1801,6 +1815,10 @@
         tensor_size - 1,
     )
     g_first = first_kept.astype(F32) + first_arrived.astype(F32)
+    last_sent = hold(last_sent, output)
+    count = last_sent.shape[0] // 2
+    last_sent = jnp.where(upper, last_sent[:count], last_sent[count:])
+    last_arrived = swap(last_sent, "x", 1)
     g_last = last_kept.astype(F32) + last_arrived.astype(F32)
     norm_sums = vectors[:4, : norm1_gain.shape[0]]
     ffn_grads = [

time: 421 us -> 402 us (0.955)
  Pallas kernels: 369 us -> 350 us
  starting transfers between devices: 2.24 us -> 7.68 us
  other arithmetic: 15.3 us -> 11 us
    pallas_call x13 -> x14, Pallas kernels: 369 us -> 350 us  [run(): pl.pallas_call(kernel, out_shape=out_shape, compiler_params=pltpu.Compile...]
    ppermute x1 -> x4, starting transfers between devices: 1.49 us -> 7.51 us  [swap(): return lax.ppermute(array, axis, [(i, i ^ bit) for i in range(size)])]
  transfers between devices with their start and end apart: 5 -> 8, of which waited for: 3 -> 1; matrix products, arithmetic and copies ran while one was open for 3% -> 3% of each run, Pallas kernels for 76% -> 80%
where the time goes in v9:
time: 402 us; the launch traced here: 398 us
  Pallas kernels  350 us (87%)
  between operations  14.4 us (4%)
  local copies, waits for them, and re-layouts  11.2 us (3%)
  other arithmetic  11 us (3%)
  starting transfers between devices  7.68 us (2%)
    pallas_call x14, Pallas kernels, run(): pl.pallas_call(kernel, out_shape=out_shape, compiler_params=pltpu.Compile...  350 us
  transfers between devices with their start and end apart: 8, of which 1 were waited for; matrix products, arithmetic and copies ran while one was open for 3% of the time, Pallas kernels for 80%

profile of v9, /device:TPU:0, one launch (start us, length us, event | category | flops | bytes accessed | tf_op | source)
XLA Modules:
  0.0 398.2 jit_solution(17012984559028435504)
XLA Ops:
  7.2 0.0 copy-start.11
  7.3 0.0 all-gather.3.cloned.1.call-start
  7.3 1.1 fusion.8
  8.4 1.1 fusion.6
  9.5 0.8 pad_maximum_fusion.2
  10.3 0.0 all-gather.3.cloned.1.call-update
  10.3 0.0 all-gather.5.cloned.1.call-start
  10.4 3.0 collective-permute-start.2
  13.4 0.2 fusion.1
  13.7 0.6 fusion.3
  14.3 0.6 broadcast.63
  15.0 0.0 copy-start.10
  15.0 0.7 pad_maximum_fusion.4.att_ref
  15.8 44.4 %gather.1 = (bf16[1024,2048]{1,0:T(8,128)(2,1)}, f32[8,1024]{1,0:T(8,128)}, bf16[1,2,256,1024]{3,2,1,0:T(8,128)(2,1)}) custom-call(bf16[64,2048]{1,0:T(8,128)(2,1)} %pad_maximum_fusion.4.att_ref, f32[8,128]{1,0:T(8,128)} %copy-done.10, bf16[2,256,1024]{2,1,0:T(8,128)(2,1)} %refs_7_.1), custom_call_target="tpu_custom_call" | custom-call | bytes 6590464 | tf_op jit(solution)/shard_map/gather/pallas_call | solution.py:88
  60.2 0.0 collective-permute-done.2
  60.2 1.1 maximum_select_fusion
  61.3 0.0 all-gather.5.cloned.1.call-update
  61.3 0.0 reduce-scatter.3.cloned.1.call-start
  61.4 1.0 fusion
  62.4 1.0 pad_maximum_fusion.5.cos_ref.refs_5_
  63.4 1.0 pad_maximum_fusion.6.sin_ref.refs_6_
  64.4 8.6 %project.1 = (bf16[2,512,1024]{2,1,0:T(8,128)(2,1)}, bf16[2,512,512]{2,1,0:T(8,128)(2,1)}, bf16[2,4,2,512,128]{4,3,2,1,0:T(8,128)(2,1)}) custom-call(f32[8,1024]{1,0:T(8,128)} %get-tuple-element.112.norms_ref.refs_5_.refs_9_, bf16[1024,2048]{1,0:T(8,128)(2,1)} %get-tuple-element.113.w_ref.refs_1_.refs_4_.refs_6_, ...), custom_call_target="tpu_custom_call" | custom-call | flops 3221225472 | bytes 12091392 | tf_op jit(solution)/shard_map/project/pallas_call | solution.py:88
  73.0 70.7 %attend.1 = (bf16[2,512,512]{2,1,0:T(8,128)(2,1)}, f32[2,512,512]{2,1,0:T(8,128)}, f32[2,512,512]{2,1,0:T(8,128)}, f32[1,256,1024]{2,1,0:T(8,128)}, bf16[1,256,1...) custom-call(bf16[2,512,512]{2,1,0:T(8,128)(2,1)} %get-tuple-element., ...), custom_call_target="tpu_custom_call" | custom-call | flops 17179869184 | bytes 27820032 | tf_op jit(solution)/shard_map/attend/pallas_call | solution.py:88
  143.7 2.0 collective-permute-start
  145.7 1.2 slice.130
  146.9 0.7 multiply_divide_fusion
  147.5 0.6 fusion.9
  148.1 14.9 %feed_first.2 = (bf16[2,512,1024]{2,1,0:T(8,128)(2,1)}, bf16[3,512,2048]{2,1,0:T(8,128)(2,1)}, f32[512,1024]{1,0:T(8,128)}, f32[512,1024]{1,0:T(8,128)}) custom-call(bf16[1024,3072]{1,0:T(8,128)(2,1)} %all-gather.3.cloned.1.call-done.refs_0_.refs_1_.refs_2_, bf16[1024,3072]{1,0:T(8,128)(2,1)} %all-gather.3.cloned.1.call-done.refs_0_.refs_1_.refs_2_, ...), custom_call_target="tpu_custom_call" | custom-call | flops 6442450944 | bytes 34603012 | tf_op jit(solution)/shard_map/feed_first/pallas_call | solution.py:88
  163.1 0.0 collective-permute-done.arrived_ref
  163.1 0.8 copy-done.4
  163.9 2.8 second_norm.1
  166.7 0.1 collective-permute-start.1
  166.8 14.0 %feed_last.2 = (bf16[3,512,2048]{2,1,0:T(8,128)(2,1)}, f32[256,1024]{1,0:T(8,128)}, bf16[256,1024]{1,0:T(8,128)(2,1)}, f32[256,1024]{1,0:T(8,128)}, bf16[256,1024]{1,0:T(8,128)(2,1)}) custom-call(bf16[4,2,2,64,3072]{4,3,2,1,0:T(8,128)(2,1)} %bitcast.31, bf16[4,2,2,64,3072]{4,3,2,1,0:T(8,128)(2,1)} %bitcast.32, ...), custom_call_target="tpu_custom_call", output_to_operand_aliasing={{0}: (6, {})} | custom-call | flops 6442450944 | bytes 40894464 | tf_op jit(solution)/shard_map/feed_last/pallas_call | solution.py:88
  180.8 0.0 collective-permute-done.1.refs_5_
  180.8 0.0 copy-start.19
  180.8 0.8 copy-done.19
  181.6 19.3 %feed_first.3 = (bf16[2,512,1024]{2,1,0:T(8,128)(2,1)}, bf16[3,512,2048]{2,1,0:T(8,128)(2,1)}, f32[512,1024]{1,0:T(8,128)}, f32[512,1024]{1,0:T(8,128)}, bf16[1,256,1024]{2,1,0:T(8,128)(2,1)}) custom-call(bf16[1024,3072]{1,0:T(8,128)(2,1)} %all-gather.3.cloned.1.call-done.refs_0_.refs_1_.refs_2_, ...), custom_call_target="tpu_custom_call" | custom-call | flops 6442450944 | bytes 35651588 | tf_op jit(solution)/shard_map/feed_first/pallas_call | solution.py:88
  200.9 12.0 %feed_weights.2 = bf16[4,2,2,64,3072]{4,3,2,1,0:T(8,128)(2,1)} custom-call(bf16[2,512,1024]{2,1,0:T(8,128)(2,1)} %get-tuple-element.131.refs_3_.refs_0_, bf16[2,512,1024]{2,1,0:T(8,128)(2,1)} %get-tuple-element.148.refs_1_.refs_3_, bf16[3,512,2048]{2,1,0:T(8,128)(2,1)} %get-tuple-element.140.refs_2_, bf16[3,512,2048]{2,1,0:T(8,128)(2,1)} %get-tuple-element.151.refs_3_.refs_6_), custom_call_target="tpu_custom_call" | custom-call | flops 6442450944 | bytes 23068672 | tf_op jit(solution)/shard_map/feed_weights/pallas_call | solution.py:88
  212.8 0.0 reduce-scatter.3.cloned.1.call-update
  212.9 0.0 reduce-scatter.5.cloned.1.call-start
  212.9 4.5 %second_norm_back.2 = (f32[256,1024]{1,0:T(8,128)}, bf16[256,1024]{1,0:T(8,128)(2,1)}, f32[2,1024]{1,0:T(2,128)}) custom-call(f32[1,1]{1,0:T(1,128)} %bitcast.8.refs_3_.factor_ref, f32[256,1024]{1,0:T(8,128)} %get-tuple-element.144.kept_ref, bf16[256,1024]{1,0:T(8,128)(2,1)} %bitcast.40, f32[256,1024]{1,0:T(8,128)} %get-tuple-element.146.middle_ref.refs_14_, ...), custom_call_target="tpu_custom_call" | custom-call | flops 10485760 | bytes 5283844 | tf_op jit(solution)/shard_map/second_norm_back/pallas_call | solution.py:88
  217.4 19.1 %feed_last.3 = (bf16[3,512,2048]{2,1,0:T(8,128)(2,1)}, f32[256,1024]{1,0:T(8,128)}, bf16[256,1024]{1,0:T(8,128)(2,1)}, f32[256,1024]{1,0:T(8,128)}, bf16[256,102...) custom-call(bf16[4,2,2,64,3072]{4,3,2,1,0:T(8,128)(2,1)} %bitcast.34, ...), custom_call_target="tpu_custom_call", output_to_operand_aliasing={{0}: (6, {})} | custom-call | flops 6442450944 | bytes 41943040 | tf_op jit(solution)/shard_map/feed_last/pallas_call | solution.py:88
  236.6 14.4 %feed_weights.3 = (bf16[4,2,2,64,3072]{4,3,2,1,0:T(8,128)(2,1)}, bf16[1,256,1024]{2,1,0:T(8,128)(2,1)}) custom-call(bf16[2,512,1024]{2,1,0:T(8,128)(2,1)} %get-tuple-element.131.refs_3_.refs_0_, bf16[2,512,1024]{2,1,0:T(8,128)(2,1)} %get-tuple-element.148.refs_1_.refs_3_, bf16[3,512,2048]{2,1,0:T(8,128)(2,1)} %get-tuple-element.140.refs_2_, ...), custom_call_target="tpu_custom_call" | custom-call | flops 6442450944 | bytes 24117248 | tf_op jit(solution)/shard_map/feed_weights/pallas_call | solution.py:88
  251.0 0.0 reduce-scatter.5.cloned.1.call-update
  251.0 4.5 %second_norm_back.3 = (f32[256,1024]{1,0:T(8,128)}, bf16[256,1024]{1,0:T(8,128)(2,1)}, f32[2,1024]{1,0:T(2,128)}) custom-call(f32[1,1]{1,0:T(1,128)} %bitcast.10.refs_3_.factor_ref, f32[256,1024]{1,0:T(8,128)} %get-tuple-element.160.kept_ref, bf16[256,1024]{1,0:T(8,128)(2,1)} %bitcast.41, f32[256,1024]{1,0:T(8,128)} %get-tuple-element.162.middle_ref.refs_17_, ...), custom_call_target="tpu_custom_call" | custom-call | flops 10485760 | bytes 5283844 | tf_op jit(solution)/shard_map/second_norm_back/pallas_call | solution.py:88
  255.5 65.8 %attend_back.1 = (bf16[2,512,512]{2,1,0:T(8,128)(2,1)}, bf16[2,512,512]{2,1,0:T(8,128)(2,1)}, bf16[2,512,512]{2,1,0:T(8,128)(2,1)}, bf16[2,512,1024]{2,1,0:T(8,1...) custom-call(bf16[2,512,512]{2,1,0:T(8,128)(2,1)} %get-tuple-element.155.refs_0_, ...), custom_call_target="tpu_custom_call" | custom-call | flops 42949672960 | bytes 27787264 | tf_op jit(solution)/shard_map/attend_back/pallas_call | solution.py:88
  321.3 0.0 reduce-scatter.3.cloned.1.call-done.refs_8_
  321.3 55.4 %finish.1 = (f32[64,2048]{1,0:T(8,128)}, f32[8,128]{1,0:T(8,128)}, f32[2,256,1024]{2,1,0:T(8,128)}, bf16[2,256,1024]{2,1,0:T(8,128)(2,1)}, bf16[64,3072]{1,0:T(8,128)(2,1)}) custom-call(bf16[2,512,512]{2,1,0:T(8,128)(2,1)} %get-tuple-element.167.refs_0_, bf16[2,512,512]{2,1,0:T(8,128)(2,1)} %get-tuple-element.168.refs_1_, ...), custom_call_target="tpu_custom_call" | custom-call | flops 7516192768 | bytes 25874432 | tf_op jit(solution)/shard_map/finish/pallas_call | solution.py:88
  376.7 0.0 reduce-scatter.5.cloned.1.call-done
  376.8 1.2 slice_select_fusion.2
  378.0 2.4 collective-permute-start.3
  380.4 2.0 slice_bitcast_fusion
  382.4 0.1 convert_add_fusion.1
  382.5 0.5 slice_bitcast_fusion.1
  383.1 0.1 fusion.4
  383.1 3.4 collective-permute-done.3
  386.5 0.0 copy-done
  386.5 0.1 convert_add_fusion
  386.7 0.1 fusion.5
  386.7 0.8 maximum_bitcast_fusion
  387.6 0.8 pad_maximum_fusion.1
  388.4 0.8 pad_maximum_fusion
  389.2 1.0 copy.37
  390.2 1.3 copy.38
  (42 shorter events, 0.2 us)
Async XLA Ops:
  7.2 6.2 %copy-start.11 = (f32[850]{0:T(1024)S(1)}, f32[850]{0:T(1024)}, u32[]{:S(2)}) copy-start(f32[850]{0:T(1024)} %param.24) | copy-start | bytes 10204
  7.2 6.2 %copy-start.13 = (s32[2]{0:T(128)S(1)}, s32[2]{0:T(128)}, u32[]{:S(2)}) copy-start(s32[2]{0:T(128)} %param.22) | copy-start | bytes 28
  7.2 6.4 %copy-start.14 = (f32[32]{0:T(128)S(1)}, f32[32]{0:T(128)}, u32[]{:S(2)}) copy-start(f32[32]{0:T(128)} %param.32) | copy-start | bytes 388
  7.2 6.4 %copy-start.15 = (f32[32]{0:T(128)S(1)}, f32[32]{0:T(128)}, u32[]{:S(2)}) copy-start(f32[32]{0:T(128)} %param.31) | copy-start | bytes 388
  7.2 6.4 %copy-start.16 = (f32[32]{0:T(128)S(1)}, f32[32]{0:T(128)}, u32[]{:S(2)}) copy-start(f32[32]{0:T(128)} %param.26) | copy-start | bytes 388
  7.2 6.4 %copy-start.17 = (f32[32]{0:T(128)S(1)}, f32[32]{0:T(128)}, u32[]{:S(2)}) copy-start(f32[32]{0:T(128)} %param.25) | copy-start | bytes 388
  7.2 6.4 %copy-start.18 = (s32[2]{0:T(128)S(1)}, s32[2]{0:T(128)}, u32[]{:S(2)}) copy-start(s32[2]{0:T(128)} %param.23) | copy-start | bytes 28
  7.3 7.7 %copy-start.6 = (bf16[512,64]{0,1:T(8,128)(2,1)S(1)}, bf16[512,64]{0,1:T(8,128)(2,1)}, u32[]{:S(2)}) copy-start(bf16[512,64]{0,1:T(8,128)(2,1)} %param.30) | copy-start | bytes 196612
  7.3 7.7 %copy-start.7 = (bf16[64,512]{1,0:T(8,128)(2,1)S(1)}, bf16[64,512]{1,0:T(8,128)(2,1)}, u32[]{:S(2)}) copy-start(bf16[64,512]{1,0:T(8,128)(2,1)} %param.29) | copy-start | bytes 196612
  7.3 7.7 %copy-start.8 = (bf16[64,512]{1,0:T(8,128)(2,1)S(1)}, bf16[64,512]{1,0:T(8,128)(2,1)}, u32[]{:S(2)}) copy-start(bf16[64,512]{1,0:T(8,128)(2,1)} %param.28) | copy-start | bytes 196612
  7.3 7.7 %copy-start.9 = (bf16[64,512]{1,0:T(8,128)(2,1)S(1)}, bf16[64,512]{1,0:T(8,128)(2,1)}, u32[]{:S(2)}) copy-start(bf16[64,512]{1,0:T(8,128)(2,1)} %param.27) | copy-start | bytes 196612
  7.3 140.8 %all-gather.3.cloned.1.call-start = ((), (), s32[]{:S(2)}) async-start(), calls=%async_computation.2 | async-start | bytes 6684672 | tf_op jit(solution)/shard_map/all_gather | solution.py:1688
  10.3 156.4 %all-gather.5.cloned.1.call-start = ((), (), s32[]{:S(2)}) async-start(), calls=%async_computation.3 | async-start | bytes 7077888 | tf_op jit(solution)/shard_map/all_gather | solution.py:1683
  10.4 49.8 %collective-permute-start.2 = (bf16[64,3072]{1,0:T(8,128)(2,1)S(1)}, bf16[64,3072]{1,0:T(8,128)(2,1)S(1)}, u32[]{:S(2)}, u32[]{:S(2)}) collective-permute-start(bf16[64,3072]{1,0:T(8,128)(2,1)S(1)} %pad_maximum_fusion.3), channel_id=1, source_target_pairs={{0,4},{4,0},{1,5},{5,1},{2,6},{6,2},{3,7},{7,3},{8,12},{12,8},{9,1... | collective-permute-start | bytes 1179656 | tf_op jit(solution)/shard_map/ppermute | solution.py:45
  15.0 0.8 copy-start.10
  61.3 260.0 %reduce-scatter.3.cloned.1.call-start = ((), (), s32[]{:S(2)}) async-start(), calls=%async_computation.4 | async-start | bytes 7077888 | tf_op jit(solution)/shard_map/reduce_scatter | solution.py:1724
  143.7 19.4 %collective-permute-start = (bf16[256,1024]{1,0:T(8,128)(2,1)}, bf16[256,1024]{1,0:T(8,128)(2,1)S(1)}, u32[]{:S(2)}, u32[]{:S(2)}) collective-permute-start(bf16[256,1024]{1,0:T(8,128)(2,1)} %bitcast.50), channel_id=1, source_target_pairs={{0,1},{1,0},{2,3},{3,2},{4,5},{5,4},{6,7},{7,6},{8,9},{9,8},{10,11... | collective-permute-start | bytes 1572872 | tf_op jit(solution)/shard_map/ppermute | solution.py:45
  163.1 0.8 copy-start.4
  166.7 14.1 %collective-permute-start.1 = (bf16[256,1024]{1,0:T(8,128)(2,1)}, bf16[256,1024]{1,0:T(8,128)(2,1)S(1)}, u32[]{:S(2)}, u32[]{:S(2)}) collective-permute-start(bf16[256,1024]{1,0:T(8,128)(2,1)} %get-tuple-element.136.refs_4_), channel_id=1, source_target_pairs={{0,1},{1,0},{2,3},{3,2},{4,5},{5,4},{6,7},{7,6},{8,9},{9,8},{10,11... | collective-permute-start | bytes 1572872 | tf_op jit(solution)/shard_map/ppermute | solution.py:45
  180.8 0.8 copy-start.19
  212.9 163.9 %reduce-scatter.5.cloned.1.call-start = ((), (), s32[]{:S(2)}) async-start(), calls=%async_computation.5 | async-start | bytes 7077888 | tf_op jit(solution)/shard_map/reduce_scatter | solution.py:1724
  376.7 5.7 %copy-start.3 = (bf16[128,3072]{1,0:T(8,128)(2,1)S(1)}, bf16[128,3072]{1,0:T(8,128)(2,1)}, u32[]{:S(2)}) copy-start(bf16[128,3072]{1,0:T(8,128)(2,1)} %reduce-scatter.3.cloned.1.call-done.refs_8_) | copy-start | bytes 2359300
  376.7 5.7 %copy-start.5 = (bf16[64,3072]{1,0:T(8,128)(2,1)S(1)}, bf16[64,3072]{1,0:T(8,128)(2,1)}, u32[]{:S(2)}) copy-start(bf16[64,3072]{1,0:T(8,128)(2,1)} %get-tuple-element.185) | copy-start | bytes 1179652
  376.7 5.8 %copy-start.12 = (f32[8,128]{1,0:T(8,128)S(1)}, f32[8,128]{1,0:T(8,128)}, u32[]{:S(2)}) copy-start(f32[8,128]{1,0:T(8,128)} %get-tuple-element.183) | copy-start | bytes 12292
  378.0 8.5 %collective-permute-start.3 = (bf16[64,3072]{1,0:T(8,128)(2,1)S(1)}, bf16[64,3072]{1,0:T(8,128)(2,1)S(1)}, u32[]{:S(2)}, u32[]{:S(2)}) collective-permute-start(bf16[64,3072]{1,0:T(8,128)(2,1)S(1)} %slice_select_fusion.2), channel_id=1, source_target_pairs={{0,4},{4,0},{1,5},{5,1},{2,6},{6,2},{3,7},{7,3},{8,12},{12,8},{9,1... | collective-permute-start | bytes 1179656 | tf_op jit(solution)/shard_map/ppermute | solution.py:45
  380.4 6.1 %copy-start = (bf16[128,3072]{1,0:T(8,128)(2,1)S(1)}, bf16[128,3072]{1,0:T(8,128)(2,1)}, u32[]{:S(2)}) copy-start(bf16[128,3072]{1,0:T(8,128)(2,1)} %reduce-scatter.5.cloned.1.call-done) | copy-start | bytes 2359300
  386.7 2.6 copy-start.2
  387.6 2.6 copy-start.1
Sparse Core Ops, SparseCore 0:
  11.0 76.2 all-gather.2
  88.9 64.8 all-gather.4
  213.0 67.9 reduce-scatter.2
  283.1 72.3 reduce-scatter.4

commit v10 on v9

--- a/solution.py
+++ b/solution.py
@@ -17,15 +17,6 @@
 F32 = jnp.float32
 VMEM_BYTES = 56 * 1024 * 1024
 MESH = pl.DeviceIdType.MESH
-
-
-def angles(positions, head_dim):
-    half_dim = head_dim // 2
-    inverse = jnp.exp(
-        -(math.log(ROPE_BASE) * 2.0 / head_dim) * jnp.arange(half_dim, dtype=F32)
-    )
-    phase_angle = positions[:, None] * inverse[None, :]
-    return (jnp.cos(phase_angle), jnp.sin(phase_angle))
 
 
 def dot_nn(left, right):
@@ -126,6 +117,10 @@
         - jnp.mean(scaled_grad, axis=-1, keepdims=True)
         - normed * jnp.mean(scaled_grad * normed, axis=-1, keepdims=True)
     )
+
+
+def factor_of(weight_ref, norms_ref, slots):
+    return weight_ref[0, 0] * slots / norms_ref[4:5, 0:1]
 
 
 def first_head(shape):
@@ -282,11 +277,29 @@
 MESSAGES = 15
 
 
+def tables(cos_ref, sin_ref, trades):
+    own_rows = cos_ref.shape[0] // (trades + 1)
+    tensor = lax.axis_index("tensor")
+    half = HEAD_DIM // 2
+    shape = (own_rows, PAIR)
+    lane = lax.broadcasted_iota(jnp.int32, shape, 1)
+    exponent = -(math.log(ROPE_BASE) * 2.0 / HEAD_DIM) * (lane % half).astype(F32)
+    inverse = jnp.exp(exponent)
+    row = lax.broadcasted_iota(jnp.int32, shape, 0)
+    for other in range(trades + 1):
+        start = (seq_index() * (trades + 1) + flipped(tensor, other)) * own_rows
+        phase = (row + start).astype(F32) * inverse
+        rows = slice(other * own_rows, (other + 1) * own_rows)
+        cos_ref[rows, :] = jnp.cos(phase)
+        sine = jnp.sin(phase)
+        sin_ref[rows, :] = jnp.where(lane % HEAD_DIM < half, -sine, sine)
+
+
 def gather_kernel(trades, att_ref, tile_ref, tokens_ref, *refs):
-    att_all, norms_ref, tokens_all = refs[:3]
-    tiles, pair_of_tiles = refs[3:5]
-    att_send, att_recv, tile_send, tile_recv = refs[5:9]
-    own_sem, tokens_send, tokens_recv, pair_send, pair_recv = refs[9:]
+    att_all, norms_ref, tokens_all, cos_ref, sin_ref = refs[:5]
+    tiles, pair_of_tiles = refs[5:7]
+    att_send, att_recv, tile_send, tile_recv = refs[7:11]
+    own_sem, tokens_send, tokens_recv, pair_send, pair_recv = refs[11:]
     tensor = lax.axis_index("tensor")
     others = [{"tensor": flipped(tensor, other + 1)} for other in range(trades)]
     att = Route(att_all, att_ref.shape[0], att_send, att_recv, att_ref)
@@ -332,6 +345,7 @@
     own_copies[2].start()
     for other in range(trades):
         tokens_trade(other).start()
+    tables(cos_ref, sin_ref, trades)
     for route in (small, att):
         route.arrived(0)
         route.start(2, 4, 8)
@@ -387,12 +401,13 @@
             shaped((count * rows, att.shape[1]), BF16),
             shaped((tile.shape[0], count * rows), F32),
             shaped((trades,) + tokens.shape, BF16),
-        ],
+        ]
+        + [shaped((tokens.shape[1] * (trades + 1), PAIR), F32)] * 2,
         0,
         [att, tile, tokens],
         collective_id=1,
         in_specs=[vmem, vmem, anywhere],
-        out_specs=[anywhere, vmem, anywhere],
+        out_specs=[anywhere, vmem, anywhere, vmem, vmem],
         scratch_shapes=[pltpu.VMEM((count * group, 128), F32), pltpu.VMEM((group, 128), F32)]
         + [dma((MESSAGES,))] * 4
         + [dma((3,)), dma((trades,)), dma((trades,)), dma((trades,)), dma((trades,))],
@@ -481,7 +496,7 @@
     def _():
         early_trade(0).start()
 
-    @pl.when(step == min(3 * pairs + 1, steps - 2))
+    @pl.when(step == 3 * pairs)
     def _():
         kept = early_kept[...]
         for stage in range(stages):
@@ -498,7 +513,7 @@
         normed_ref[...] = normed
         early_normed[...] = normed
 
-    @pl.when(step == min(3 * pairs + 2, steps - 1))
+    @pl.when(step == 3 * pairs + 1)
     def _():
         for other in range(trades):
             normed_trade(other).start()
@@ -935,22 +950,22 @@
 
 
 def second_norm(x_rows, kept, arrived, norms):
-    args, in_specs = zip(*[plane(one) for one in (x_rows, kept, arrived, norms)])
-    rows, width = in_specs[1].block_shape[-2:]
-    full = pl.BlockSpec((rows, width), lambda i: (0, 0))
+    args, in_specs = row_planes((x_rows, kept, arrived))
+    rows, width = arrived.shape
+    block = pl.BlockSpec((rows // NORM_BLOCKS, width), lambda i: (i, 0))
     return run(
         middle_kernel,
         "second_norm",
         [shaped((rows, width), F32), shaped((rows, width), BF16)],
         20 * rows * width,
-        args,
-        grid=(1,),
-        in_specs=list(in_specs),
-        out_specs=[full, full],
-    )
-
-
-def feed_kernel(blocks, swaps, first, *refs):
+        [*args, norms],
+        grid=(NORM_BLOCKS,),
+        in_specs=[*in_specs, full(*norms.shape)],
+        out_specs=[block, block],
+    )
+
+
+def feed_kernel(blocks, swaps, first, slots, *refs):
     refs = list(refs)
 
     def take(count):
@@ -960,7 +975,7 @@
 
     w_refs = take(3)
     if first:
-        factor_ref = take(1)[0]
+        weight_ref, norms_ref = take(2)
         x_refs, cot_refs = take(blocks), take(blocks)
         sources = take(len(swaps))
         both_ref, wide_ref, total_ref, grad_ref = take(4)
@@ -992,12 +1007,13 @@
         start_trades(trades, swaps)
 
     if first:
+        factor = factor_of(weight_ref, norms_ref, slots)
         for at in range(blocks):
 
             @pl.when(block == at)
             def _(at=at):
                 both_ref[0] = x_refs[at][...]
-                both_ref[1] = (cot_refs[at][...].astype(F32) * factor_ref[0, 0]).astype(BF16)
+                both_ref[1] = (cot_refs[at][...].astype(F32) * factor).astype(BF16)
 
     x_rows = both_ref[0]
     gate = dot_nn(x_rows, gate_w)
@@ -1078,7 +1094,9 @@
     total = sum(len(kinds) for kinds in masks)
     out_shape, out_specs = out
     return run(
-        functools.partial(feed_kernel, blocks, masks, name == "feed_first"),
+        functools.partial(
+            feed_kernel, blocks, masks, name == "feed_first", options.pop("slots", None)
+        ),
         name,
         out_shape + [shaped((len(kinds),) + array.shape, BF16) for array, kinds in swaps],
         12 * rows * width * part_cols,
@@ -1092,7 +1110,7 @@
     )
 
 
-def feed_first(x_blocks, cot_blocks, factor, weights, swaps=()):
+def feed_first(x_blocks, cot_blocks, weight, norms, slots, weights, swaps=()):
     operands, specs = zip(*[plane(block) for block in (*x_blocks, *cot_blocks)])
     width = math.prod(weights.shape[:-1])
     blocks, own = len(x_blocks), specs[0].block_shape[-2]
@@ -1115,9 +1133,10 @@
         width,
         part_cols,
         (out_shape, out_specs),
-        [weights, weights, weights, factor, *operands],
+        [weights, weights, weights, weight, norms, *operands],
         swaps,
-        in_specs=w_specs + [SCALAR] + list(specs),
+        in_specs=w_specs + [SCALAR, full(*norms.shape)] + list(specs),
+        slots=slots,
     )
 
 
@@ -1197,7 +1216,7 @@
         + [shaped((len(kinds),) + array.shape, BF16) for array, kinds in swaps],
         6 * windows * rows * width * hidden_cols,
         [*boths, *wides] + [array for array, _ in swaps],
-        collective_id=4 if swaps else None,
+        collective_id=(6 if part else 4) if swaps else None,
         grid=(3 * steps,),
         in_specs=[left] * windows + [right] * windows + [anywhere] * len(swaps),
         out_specs=[pl.BlockSpec(lead + (step,), lambda i: (0, 0, 0, 0, i))]
@@ -1209,15 +1228,27 @@
 def norm_grad(kept_ref, arrived_ref, stream, gain, sums_ref):
     grad_normed = kept_ref[...] + arrived_ref[...].astype(F32)
     normed, inv_std = normalise(stream)
-    sums_ref[0:1, :] = jnp.sum(grad_normed * normed, axis=0, keepdims=True)
-    sums_ref[1:2, :] = jnp.sum(grad_normed, axis=0, keepdims=True)
+    sums = [
+        jnp.sum(one, axis=0, keepdims=True) for one in (grad_normed * normed, grad_normed)
+    ]
+
+    @pl.when(pl.program_id(0) == 0)
+    def _():
+        for at, one in enumerate(sums):
+            sums_ref[at : at + 1, :] = one
+
+    @pl.when(pl.program_id(0) > 0)
+    def _():
+        for at, one in enumerate(sums):
+            sums_ref[at : at + 1, :] += one
+
     return norm_back(grad_normed, normed, inv_std, gain)
 
 
 def middle_back_kernel(
-    factor_ref, kept_ref, arrived_ref, middle_ref, cot_ref, norms_ref, grad_ref, low_ref, sums_ref
+    slots, weight_ref, kept_ref, arrived_ref, middle_ref, cot_ref, norms_ref, grad_ref, low_ref, sums_ref
 ):
-    grad_y = cot_ref[...].astype(F32) * factor_ref[0, 0]
+    grad_y = cot_ref[...].astype(F32) * factor_of(weight_ref, norms_ref, slots)
     grad = grad_y + norm_grad(
         kept_ref, arrived_ref, middle_ref[...], norms_ref[2:3, :], sums_ref
     )
@@ -1225,22 +1256,31 @@
     low_ref[...] = grad.astype(BF16)
 
 
-def second_norm_back(factor, kept, arrived, middle, cot_rows, norms):
-    args, in_specs = zip(*[plane(one) for one in (kept, arrived, middle, cot_rows, norms)])
-    full = pl.BlockSpec(kept.shape, lambda i: (0, 0))
+NORM_BLOCKS = 1
+
+
+def row_planes(operands):
+    pairs = []
+    for one in operands:
+        array, at = one if isinstance(one, tuple) else (one, ())
+        rows, width = array.shape[len(at) :]
+        pairs.append(plane(one, (rows // NORM_BLOCKS, width), lambda i: (i, 0)))
+    return [list(part) for part in zip(*pairs)]
+
+
+def second_norm_back(weight, slots, kept, arrived, middle, cot_rows, norms):
+    args, in_specs = row_planes((kept, arrived, middle, cot_rows))
+    rows, width = kept.shape
+    block = pl.BlockSpec((rows // NORM_BLOCKS, width), lambda i: (i, 0))
     return run(
-        middle_back_kernel,
+        functools.partial(middle_back_kernel, slots),
         "second_norm_back",
-        [
-            shaped(kept.shape, F32),
-            shaped(kept.shape, BF16),
-            shaped((2, kept.shape[1]), F32),
-        ],
+        [shaped(kept.shape, F32), shaped(kept.shape, BF16), shaped((2, width), F32)],
         40 * kept.size,
-        [factor, *args],
-        grid=(1,),
-        in_specs=[SCALAR, *in_specs],
-        out_specs=[full, full, pl.BlockSpec((2, kept.shape[1]), lambda i: (0, 0))],
+        [weight, *args, norms],
+        grid=(NORM_BLOCKS,),
+        in_specs=[SCALAR, *in_specs, full(*norms.shape)],
+        out_specs=[block, block, full(2, width)],
     )
 
 
@@ -1321,11 +1361,9 @@
     norms_ref = take(1)[0]
     second_refs = take(windows)
     grad_refs = take(windows)
-    part_refs = take(3 * windows)
-    weights_ref, vectors_ref, input_ref, output_ref, shard_arrived = take(5)
+    weights_ref, vectors_ref, input_ref, shard_arrived = take(4)
     loads = take(8)
     grad_loads = take(windows)
-    part_loads = take(3 * windows)
     part, core_in, mine, x_in, z_in = take(5)
     tiles, own_tiles, arrived_tiles = take(3)
     small_core, small_mine, small_x, small_z = take(4)
@@ -1347,8 +1385,8 @@
 
     w_source = far_inputs[6].at[:, pl.ds(0, 3 * cols)]
     sources = [*far_inputs[:6], w_source, far_inputs[7]]
-    sources += [*grad_refs, *part_refs]
-    targets = [*loads, *grad_loads, *part_loads]
+    sources += [*grad_refs]
+    targets = [*loads, *grad_loads]
     copies = [
         pltpu.make_async_copy(source, target, load_sem.at[at])
         for at, (source, target) in enumerate(zip(sources, targets))
@@ -1451,13 +1489,6 @@
     add_cores(routes[2])
     routes[3].start(12, 14)
     across(routes[2])
-    for at in range(8 + windows, len(copies)):
-        copies[at].wait()
-    for w in range(windows):
-        middle_ref, kept_ref, arrived_ref = part_loads[3 * w : 3 * w + 3]
-        output_ref[w] = (
-            middle_ref[...] + (kept_ref[...] + arrived_ref[...].astype(F32))
-        ).astype(BF16)
     routes[3].add_up()
     for at in range(7, 8 + windows):
         copies[at].wait()
@@ -1557,7 +1588,6 @@
     norms,
     second_sums,
     grad_middles,
-    parts,
     trades,
 ):
     windows, rows, cols = grads[0].shape
@@ -1571,7 +1601,6 @@
     anywhere = pl.BlockSpec(memory_space=pl.ANY)
     vmem = pl.BlockSpec(memory_space=pltpu.VMEM)
     far_inputs = [*grads, normed, grad_mid, attended, w_att, tokens]
-    flat = [array for one in parts for array in one]
     kinds = (8, 8, 4, 3)
 
     def like(array):
@@ -1586,19 +1615,17 @@
             shaped((shard, 4 * cols), F32),
             shaped((8, 128), F32),
             shaped((windows, own_rows, width), F32),
-            shaped((windows, own_rows, width), BF16),
             shaped((ffn_shard.shape[0] // 2, ffn_shard.shape[1]), BF16),
         ],
         8 * windows * rows * width * cols + 6 * windows * rows * width * cols,
-        [*far_inputs, ffn_shard, norms, *second_sums, *grad_middles, *flat],
+        [*far_inputs, ffn_shard, norms, *second_sums, *grad_middles],
         collective_id=3,
         in_specs=[anywhere] * 9
         + [vmem] * (1 + windows)
-        + [anywhere] * (windows + len(flat)),
-        out_specs=[vmem] * 4 + [anywhere],
+        + [anywhere] * windows,
+        out_specs=[vmem] * 3 + [anywhere],
         scratch_shapes=loads
         + [like(array) for array in grad_middles]
-        + [like(array) for array in flat]
         + [pltpu.VMEM((4, width, cols), BF16)]
         + [pltpu.VMEM((4, count, shard, cols), BF16) for count in kinds]
         + [
@@ -1610,7 +1637,7 @@
         + [pltpu.VMEM((rows // 2, width), F32)] * windows
         + [pltpu.VMEM((count, width), BF16) for count in stages] * (2 * windows)
         + [
-            dma((8 + windows + len(flat),)),
+            dma((8 + windows,)),
             dma((4, SUM_MESSAGES)),
             dma((4, SUM_MESSAGES)),
             dma((SUM_MESSAGES,)),
@@ -1621,6 +1648,26 @@
             dma((trades,)),
             dma((2,)),
         ],
+    )
+
+
+def result_kernel(windows, *refs):
+    out_ref = refs[-1]
+    for w in range(windows):
+        middle_ref, kept_ref, arrived_ref = refs[3 * w : 3 * w + 3]
+        out_ref[w] = (
+            middle_ref[...] + (kept_ref[...] + arrived_ref[...].astype(F32))
+        ).astype(BF16)
+
+
+def results(parts):
+    rows, width = parts[0][0].shape
+    return run(
+        functools.partial(result_kernel, len(parts)),
+        "results",
+        shaped((len(parts), rows, width), BF16),
+        2 * len(parts) * rows * width,
+        [array for part in parts for array in part],
     )
 
 
@@ -1649,18 +1696,6 @@
     hidden_cols = w_gate.shape[1]
     shards = ("dp", "x", "core")
 
-    own_at = lax.axis_index("tensor")
-    starts = jnp.concatenate(
-        [
-            lax.iota(jnp.int32, own_rows) + (own_at ^ other) * own_rows
-            for other in range(tensor_size)
-        ]
-    )
-    positions = (seq_index() * block_rows + starts).astype(F32)
-    cos_half, sin_half = angles(positions, HEAD_DIM)
-    cosine = jnp.concatenate([cos_half] * 4, axis=1)
-    sine = jnp.concatenate([-sin_half, sin_half] * 2, axis=1)
-
     labels = lax.broadcasted_iota(jnp.int32, (windows_here, species_scale.shape[0]), 1)
     chosen = jnp.sum(jnp.where(species[:, None] == labels, species_scale[None, :], 0.0), axis=1)
     weighted = counts.astype(F32) * chosen
@@ -1687,16 +1722,16 @@
 
     first_ffn = lax.all_gather(first_ffn, shards, axis=0, tiled=True)
     last_across = swap(last_ffn, "x", 1)
-    w_att, norms, arrived_tokens = gather(
+    w_att, norms, arrived_tokens, cosine, sine = gather(
         jnp.concatenate([w_query, w_key, w_value, w_out.T], axis=1),
         tile,
         tokens,
         tensor_size - 1,
     )
-    factor = weighted * float(windows_here * lax.axis_size("dp")) / norms[4, 0]
+    slots = float(windows_here * lax.axis_size("dp"))
 
     windows = range(windows_here)
-    factors = [factor[w].reshape(1, 1) for w in windows]
+    weights = [weighted[w].reshape(1, 1) for w in windows]
 
     token_blocks = [tokens] + [arrived_tokens[other] for other in range(tensor_size - 1)]
     normed_rows, queries, own_kv = project(token_blocks, norms, w_att, cosine, sine)
@@ -1733,16 +1768,16 @@
 
     def through_second_norm(w, kept, arrived):
         grad_middle, low, sums = second_norm_back(
-            factors[w], kept, arrived, middles[w], (cotangent, (w,)), norms
+            weights[w], slots, kept, arrived, middles[w], (cotangent, (w,)), norms
         )
         grad_middles.append(grad_middle)
         second_sums.append(sums)
         return low
 
     for w in windows:
-        swaps = [(fed[-1][4], [tensor_size // 2])] if fed else []
-        started = feed_first(blocks, cot_blocks[w], factors[w], first_ffn, swaps)
-        begun.append(started[:4])
+        begun.append(
+            feed_first(blocks, cot_blocks[w], weights[w], norms, slots, first_ffn)
+        )
         if w + 1 < windows_here:
             kept, arrived = scatter_pair(kept_all[w], sent_all[w], "tensor")
             middle, normed_mid = second_norm(
@@ -1752,17 +1787,17 @@
             blocks = hold(spread(normed_mid, "tensor"), fed)
             after = normed_mid
         else:
-            g_first_part = feed_weights(
+            g_first_part, *arrived = feed_weights(
                 [one[0] for one in begun],
                 [one[0] for one in fed] + [one[1] for one in begun[len(fed) :]],
                 0,
-                (),
-            )[0]
+                [(one[4], [tensor_size // 2]) for one in fed],
+            )
             first_kept, first_sent = reduce_ffn(g_first_part)
             after = g_first_part
         swaps = ()
         if w > 0:
-            kept, arrived = later_pair(fed[-1][3], started[4][0], "tensor")
+            kept, arrived = later_pair(fed[-1][3], arrived[-1][0], "tensor")
             low = through_second_norm(w - 1, hold(kept, g_first_part), arrived)
             lows.append(low)
             swaps = [(low, masks)]
@@ -1800,7 +1835,7 @@
         (middles[w], *later_pair(fed[w][1], arrived_results[w], "tensor")) for w in windows
     ]
 
-    g_att, vectors, input_grad, output, first_arrived = finish(
+    g_att, vectors, input_grad, first_arrived = finish(
         (grad_q, grad_k, grad_v),
         normed_rows,
         grad_mid_rows,
@@ -1811,11 +1846,11 @@
         norms,
         second_sums,
         grad_middles,
-        parts,
         tensor_size - 1,
     )
+    output = results(hold(parts, input_grad))
     g_first = first_kept.astype(F32) + first_arrived.astype(F32)
-    last_sent = hold(last_sent, output)
+    last_sent = hold(last_sent, input_grad)
     count = last_sent.shape[0] // 2
     last_sent = jnp.where(upper, last_sent[:count], last_sent[count:])
     last_arrived = swap(last_sent, "x", 1)

time: 402 us -> 393 us (0.978)
    pallas_call x14 -> x15, Pallas kernels: 350 us -> 352 us  [run(): pl.pallas_call(kernel, out_shape=out_shape, compiler_params=pltpu.Compile...]
  transfers between devices with their start and end apart: 8 -> 8, of which waited for: 1 -> 1; matrix products, arithmetic and copies ran while one was open for 3% -> 2% of each run, Pallas kernels for 80% -> 83%
where the time goes in v10:
time: 393 us; the launch traced here: 390 us
  Pallas kernels  352 us (90%)
  between operations  14.3 us (4%)
  local copies, waits for them, and re-layouts  8.95 us (2%)
  other arithmetic  7.31 us (2%)
  starting transfers between devices  5.46 us (1%)
    pallas_call x15, Pallas kernels, run(): pl.pallas_call(kernel, out_shape=out_shape, compiler_params=pltpu.Compile...  352 us
  transfers between devices with their start and end apart: 8, of which 1 were waited for; matrix products, arithmetic and copies ran while one was open for 2% of the time, Pallas kernels for 83%

profile of v10, /device:TPU:0, one launch (start us, length us, event | category | flops | bytes accessed | tf_op | source)
XLA Modules:
  0.0 389.6 jit_solution(17361789560131607617)
XLA Ops:
  7.3 0.0 all-gather.5.cloned.1.call-start
  7.3 1.1 fusion.6
  8.4 1.1 fusion.4
  9.5 0.8 pad_maximum_fusion.3
  10.3 0.0 all-gather.5.cloned.1.call-update
  10.3 0.0 all-gather.3.cloned.1.call-start
  10.4 3.0 collective-permute-start
  13.4 0.0 copy-done.10
  13.4 0.2 fusion
  13.6 0.6 fusion.1
  14.2 0.0 copy-done.13
  14.2 0.0 copy-done.15
  14.3 0.6 broadcast.48
  15.0 0.0 copy-start.9
  15.0 0.0 copy-done.5
  15.0 0.0 copy-done.6
  15.0 0.0 copy-done.7
  15.0 0.0 copy-done.8
  15.0 0.7 pad_maximum_fusion.4.att_ref
  15.7 44.6 %gather.1 = (bf16[1024,2048]{1,0:T(8,128)(2,1)}, f32[8,1024]{1,0:T(8,128)}, bf16[1,2,256,1024]{3,2,1,0:T(8,128)(2,1)}, f32[512,128]{1,0:T(8,128)}, f32[512,128]{1,0:T(8,128)}) custom-call(bf16[64,2048]{1,0:T(8,128)(2,1)} %pad_maximum_fusion.4.att_ref, f32[8,128]{1,0:T(8,128)} %copy-done.9, bf16[2,256,1024]{2,1,0:T(8,128)(2,1)} %refs_7_.5), custom_call_target="tpu_custom_call" | custom-call | bytes 7114752 | tf_op jit(solution)/shard_map/gather/pallas_call | solution.py:79
  60.4 0.0 collective-permute-done
  60.4 1.1 maximum_select_fusion
  61.5 0.0 all-gather.3.cloned.1.call-update
  61.5 0.2 reduce-scatter.3.cloned.1.call-start
  61.7 8.5 %project.1 = (bf16[2,512,1024]{2,1,0:T(8,128)(2,1)}, bf16[2,512,512]{2,1,0:T(8,128)(2,1)}, bf16[2,4,2,512,128]{4,3,2,1,0:T(8,128)(2,1)}) custom-call(f32[8,1024]{1,0:T(8,128)} %get-tuple-element.120.norms_ref.refs_5_.refs_4_.refs_9_, bf16[1024,2048]{1,0:T(8,128)(2,1)} %get-tuple-element.121.w_ref.refs_1_.refs_4_.refs_6_, ...), custom_call_target="tpu_custom_call" | custom-call | flops 3221225472 | bytes 12091392 | tf_op jit(solution)/shard_map/project/pallas_call | solution.py:79
  70.2 69.5 %attend.1 = (bf16[2,512,512]{2,1,0:T(8,128)(2,1)}, f32[2,512,512]{2,1,0:T(8,128)}, f32[2,512,512]{2,1,0:T(8,128)}, f32[1,256,1024]{2,1,0:T(8,128)}, bf16[1,256,1...) custom-call(bf16[2,512,512]{2,1,0:T(8,128)(2,1)} %get-tuple-element., ...), custom_call_target="tpu_custom_call" | custom-call | flops 17179869184 | bytes 27820032 | tf_op jit(solution)/shard_map/attend/pallas_call | solution.py:79
  139.7 0.1 collective-permute-start.1
  139.7 0.6 fusion.7
  140.3 15.2 %feed_first.2 = (bf16[2,512,1024]{2,1,0:T(8,128)(2,1)}, bf16[3,512,2048]{2,1,0:T(8,128)(2,1)}, f32[512,1024]{1,0:T(8,128)}, f32[512,1024]{1,0:T(8,128)}) custom-call(bf16[1024,3072]{1,0:T(8,128)(2,1)} %all-gather.5.cloned.1.call-done.refs_0_.refs_1_.refs_2_, bf16[1024,3072]{1,0:T(8,128)(2,1)} %all-gather.5.cloned.1.call-done.refs_0_.refs_1_.refs_2_, ...), custom_call_target="tpu_custom_call" | custom-call | flops 6442450944 | bytes 34635780 | tf_op jit(solution)/shard_map/feed_first/pallas_call | solution.py:79
  155.5 0.0 collective-permute-done.1.arrived_ref
  155.5 0.0 copy-start.3
  155.5 0.8 copy-done.3
  156.3 2.8 second_norm.1
  159.1 2.0 collective-permute-start.2
  161.1 14.0 %feed_last.2 = (bf16[3,512,2048]{2,1,0:T(8,128)(2,1)}, f32[256,1024]{1,0:T(8,128)}, bf16[256,1024]{1,0:T(8,128)(2,1)}, f32[256,1024]{1,0:T(8,128)}, bf16[256,1024]{1,0:T(8,128)(2,1)}) custom-call(bf16[4,2,2,64,3072]{4,3,2,1,0:T(8,128)(2,1)} %bitcast.30, bf16[4,2,2,64,3072]{4,3,2,1,0:T(8,128)(2,1)} %bitcast.31, ...), custom_call_target="tpu_custom_call", output_to_operand_aliasing={{0}: (6, {})} | custom-call | flops 6442450944 | bytes 40894464 | tf_op jit(solution)/shard_map/feed_last/pallas_call | solution.py:79
  175.1 0.0 collective-permute-done.2.refs_6_
  175.1 0.8 copy-done.18
  175.9 15.1 %feed_first.3 = (bf16[2,512,1024]{2,1,0:T(8,128)(2,1)}, bf16[3,512,2048]{2,1,0:T(8,128)(2,1)}, f32[512,1024]{1,0:T(8,128)}, f32[512,1024]{1,0:T(8,128)}) custom-call(bf16[1024,3072]{1,0:T(8,128)(2,1)} %all-gather.5.cloned.1.call-done.refs_0_.refs_1_.refs_2_, bf16[1024,3072]{1,0:T(8,128)(2,1)} %all-gather.5.cloned.1.call-done.refs_0_.refs_1_.refs_2_, ...), custom_call_target="tpu_custom_call" | custom-call | flops 6442450944 | bytes 34635780 | tf_op jit(solution)/shard_map/feed_first/pallas_call | solution.py:79
  190.9 14.8 %feed_weights.2 = (bf16[4,2,2,64,3072]{4,3,2,1,0:T(8,128)(2,1)}, bf16[1,256,1024]{2,1,0:T(8,128)(2,1)}) custom-call(bf16[2,512,1024]{2,1,0:T(8,128)(2,1)} %get-tuple-element.140.refs_3_.refs_0_, bf16[2,512,1024]{2,1,0:T(8,128)(2,1)} %get-tuple-element.160.refs_1_.refs_3_, bf16[3,512,2048]{2,1,0:T(8,128)(2,1)} %get-tuple-element.151.refs_2_, ...), custom_call_target="tpu_custom_call" | custom-call | flops 6442450944 | bytes 24117248 | tf_op jit(solution)/shard_map/feed_weights/pallas_call | solution.py:79
  205.8 0.0 reduce-scatter.3.cloned.1.call-update
  205.8 0.0 reduce-scatter.5.cloned.1.call-start
  205.9 4.5 %second_norm_back.2 = (f32[256,1024]{1,0:T(8,128)}, bf16[256,1024]{1,0:T(8,128)(2,1)}, f32[2,1024]{1,0:T(2,128)}) custom-call(f32[1,1]{1,0:T(1,128)} %bitcast.8.refs_3_.weight_ref, f32[256,1024]{1,0:T(8,128)} %get-tuple-element.157.kept_ref, bf16[256,1024]{1,0:T(8,128)(2,1)} %bitcast.40, f32[256,1024]{1,0:T(8,128)} %get-tuple-element.193.middle_ref.refs_0_, ...), custom_call_target="tpu_custom_call" | custom-call | flops 10485760 | bytes 5283844 | tf_op jit(solution)/shard_map/second_norm_back/pallas_call | solution.py:79
  210.4 18.5 %feed_last.3 = (bf16[3,512,2048]{2,1,0:T(8,128)(2,1)}, f32[256,1024]{1,0:T(8,128)}, bf16[256,1024]{1,0:T(8,128)(2,1)}, f32[256,1024]{1,0:T(8,128)}, bf16[256,102...) custom-call(bf16[4,2,2,64,3072]{4,3,2,1,0:T(8,128)(2,1)} %bitcast.33, ...), custom_call_target="tpu_custom_call", output_to_operand_aliasing={{0}: (6, {})} | custom-call | flops 6442450944 | bytes 41943040 | tf_op jit(solution)/shard_map/feed_last/pallas_call | solution.py:79
  228.8 13.6 %feed_weights.3 = (bf16[4,2,2,64,3072]{4,3,2,1,0:T(8,128)(2,1)}, bf16[1,256,1024]{2,1,0:T(8,128)(2,1)}) custom-call(bf16[2,512,1024]{2,1,0:T(8,128)(2,1)} %get-tuple-element.140.refs_3_.refs_0_, bf16[2,512,1024]{2,1,0:T(8,128)(2,1)} %get-tuple-element.160.refs_1_.refs_3_, bf16[3,512,2048]{2,1,0:T(8,128)(2,1)} %get-tuple-element.151.refs_2_, ...), custom_call_target="tpu_custom_call" | custom-call | flops 6442450944 | bytes 24117248 | tf_op jit(solution)/shard_map/feed_weights/pallas_call | solution.py:79
  242.5 0.0 reduce-scatter.5.cloned.1.call-update
  242.5 4.5 %second_norm_back.3 = (f32[256,1024]{1,0:T(8,128)}, bf16[256,1024]{1,0:T(8,128)(2,1)}, f32[2,1024]{1,0:T(2,128)}) custom-call(f32[1,1]{1,0:T(1,128)} %bitcast.12.refs_3_.weight_ref, f32[256,1024]{1,0:T(8,128)} %get-tuple-element.172.kept_ref, bf16[256,1024]{1,0:T(8,128)(2,1)} %bitcast.39, f32[256,1024]{1,0:T(8,128)} %get-tuple-element.196.middle_ref.refs_3_, ...), custom_call_target="tpu_custom_call" | custom-call | flops 10485760 | bytes 5283844 | tf_op jit(solution)/shard_map/second_norm_back/pallas_call | solution.py:79
  247.0 65.2 %attend_back.1 = (bf16[2,512,512]{2,1,0:T(8,128)(2,1)}, bf16[2,512,512]{2,1,0:T(8,128)(2,1)}, bf16[2,512,512]{2,1,0:T(8,128)(2,1)}, bf16[2,512,1024]{2,1,0:T(8,1...) custom-call(bf16[2,512,512]{2,1,0:T(8,128)(2,1)} %get-tuple-element.167.refs_0_, ...), custom_call_target="tpu_custom_call" | custom-call | flops 42949672960 | bytes 27787264 | tf_op jit(solution)/shard_map/attend_back/pallas_call | solution.py:79
  312.3 0.0 reduce-scatter.3.cloned.1.call-done.refs_8_
  312.3 57.5 %finish.1 = (f32[64,2048]{1,0:T(8,128)}, f32[8,128]{1,0:T(8,128)}, f32[2,256,1024]{2,1,0:T(8,128)}, bf16[64,3072]{1,0:T(8,128)(2,1)}) custom-call(bf16[2,512,512]{2,1,0:T(8,128)(2,1)} %get-tuple-element.182.refs_0_, bf16[2,512,512]{2,1,0:T(8,128)(2,1)} %get-tuple-element.183.refs_1_, bf16[2,512,512]{2,1,0:T(8,128)(2,1)} %get-tuple-element.184.refs_2_, ...), custom_call_target="tpu_custom_call" | custom-call | flops 7516192768 | bytes 19582976 | tf_op jit(solution)/shard_map/finish/pallas_call | solution.py:79
  369.9 0.0 reduce-scatter.5.cloned.1.call-done
  369.9 1.2 slice_select_fusion.2
  371.0 0.1 collective-permute-start.3
  371.1 1.9 slice_bitcast_fusion
  373.0 3.8 results.1
  376.8 0.1 convert_add_fusion.1
  377.0 0.5 slice_bitcast_fusion.1
  377.5 0.1 fusion.2
  377.6 1.3 collective-permute-done.3
  378.9 0.1 convert_add_fusion
  379.0 0.1 fusion.3
  379.1 0.8 maximum_bitcast_fusion
  379.9 0.8 pad_maximum_fusion.1
  380.8 0.8 pad_maximum_fusion
  381.6 1.3 copy.35
  (32 shorter events, 0.1 us)
Async XLA Ops:
  7.2 6.2 %copy-start.10 = (f32[850]{0:T(1024)S(1)}, f32[850]{0:T(1024)}, u32[]{:S(2)}) copy-start(f32[850]{0:T(1024)} %param.24) | copy-start | bytes 10204
  7.2 6.2 %copy-start.12 = (s32[2]{0:T(128)S(1)}, s32[2]{0:T(128)}, u32[]{:S(2)}) copy-start(s32[2]{0:T(128)} %param.22) | copy-start | bytes 28
  7.2 6.4 %copy-start.17 = (s32[2]{0:T(128)S(1)}, s32[2]{0:T(128)}, u32[]{:S(2)}) copy-start(s32[2]{0:T(128)} %param.23) | copy-start | bytes 28
  7.2 7.0 %copy-start.13 = (f32[32]{0:T(128)S(1)}, f32[32]{0:T(128)}, u32[]{:S(2)}) copy-start(f32[32]{0:T(128)} %param.32) | copy-start | bytes 388
  7.2 7.0 %copy-start.14 = (f32[32]{0:T(128)S(1)}, f32[32]{0:T(128)}, u32[]{:S(2)}) copy-start(f32[32]{0:T(128)} %param.31) | copy-start | bytes 388
  7.2 7.0 %copy-start.15 = (f32[32]{0:T(128)S(1)}, f32[32]{0:T(128)}, u32[]{:S(2)}) copy-start(f32[32]{0:T(128)} %param.26) | copy-start | bytes 388
  7.2 7.0 %copy-start.16 = (f32[32]{0:T(128)S(1)}, f32[32]{0:T(128)}, u32[]{:S(2)}) copy-start(f32[32]{0:T(128)} %param.25) | copy-start | bytes 388
  7.3 7.7 %copy-start.5 = (bf16[512,64]{0,1:T(8,128)(2,1)S(1)}, bf16[512,64]{0,1:T(8,128)(2,1)}, u32[]{:S(2)}) copy-start(bf16[512,64]{0,1:T(8,128)(2,1)} %param.30) | copy-start | bytes 196612
  7.3 7.7 %copy-start.6 = (bf16[64,512]{1,0:T(8,128)(2,1)S(1)}, bf16[64,512]{1,0:T(8,128)(2,1)}, u32[]{:S(2)}) copy-start(bf16[64,512]{1,0:T(8,128)(2,1)} %param.29) | copy-start | bytes 196612
  7.3 7.7 %copy-start.7 = (bf16[64,512]{1,0:T(8,128)(2,1)S(1)}, bf16[64,512]{1,0:T(8,128)(2,1)}, u32[]{:S(2)}) copy-start(bf16[64,512]{1,0:T(8,128)(2,1)} %param.28) | copy-start | bytes 196612
  7.3 7.7 %copy-start.8 = (bf16[64,512]{1,0:T(8,128)(2,1)S(1)}, bf16[64,512]{1,0:T(8,128)(2,1)}, u32[]{:S(2)}) copy-start(bf16[64,512]{1,0:T(8,128)(2,1)} %param.27) | copy-start | bytes 196612
  7.3 133.0 %all-gather.5.cloned.1.call-start = ((), (), s32[]{:S(2)}) async-start(), calls=%async_computation.3 | async-start | bytes 6684672 | tf_op jit(solution)/shard_map/all_gather | solution.py:1723
  10.3 150.8 %all-gather.3.cloned.1.call-start = ((), (), s32[]{:S(2)}) async-start(), calls=%async_computation.2 | async-start | bytes 7077888 | tf_op jit(solution)/shard_map/all_gather | solution.py:1718
  10.4 49.9 %collective-permute-start = (bf16[64,3072]{1,0:T(8,128)(2,1)S(1)}, bf16[64,3072]{1,0:T(8,128)(2,1)S(1)}, u32[]{:S(2)}, u32[]{:S(2)}) collective-permute-start(bf16[64,3072]{1,0:T(8,128)(2,1)S(1)} %pad_maximum_fusion.2), channel_id=1, source_target_pairs={{0,4},{4,0},{1,5},{5,1},{2,6},{6,2},{3,7},{7,3},{8,12},{12,8},{9,1... | collective-permute-start | bytes 1179656 | tf_op jit(solution)/shard_map/ppermute | solution.py:36
  15.0 0.8 copy-start.9
  61.5 250.8 %reduce-scatter.3.cloned.1.call-start = ((), (), s32[]{:S(2)}) async-start(), calls=%async_computation.4 | async-start | bytes 7077888 | tf_op jit(solution)/shard_map/reduce_scatter | solution.py:1759
  139.7 15.8 %collective-permute-start.1 = (bf16[256,1024]{1,0:T(8,128)(2,1)}, bf16[256,1024]{1,0:T(8,128)(2,1)S(1)}, u32[]{:S(2)}, u32[]{:S(2)}) collective-permute-start(bf16[256,1024]{1,0:T(8,128)(2,1)} %bitcast.49), channel_id=1, source_target_pairs={{0,1},{1,0},{2,3},{3,2},{4,5},{5,4},{6,7},{7,6},{8,9},{9,8},{10,11... | collective-permute-start | bytes 1572872 | tf_op jit(solution)/shard_map/ppermute | solution.py:36
  155.5 0.8 copy-start.3
  159.1 16.0 %collective-permute-start.2 = (bf16[256,1024]{1,0:T(8,128)(2,1)}, bf16[256,1024]{1,0:T(8,128)(2,1)S(1)}, u32[]{:S(2)}, u32[]{:S(2)}) collective-permute-start(bf16[256,1024]{1,0:T(8,128)(2,1)} %get-tuple-element.148.refs_5_), channel_id=1, source_target_pairs={{0,1},{1,0},{2,3},{3,2},{4,5},{5,4},{6,7},{7,6},{8,9},{9,8},{10,11... | collective-permute-start | bytes 1572872 | tf_op jit(solution)/shard_map/ppermute | solution.py:36
  175.1 0.8 copy-start.18
  205.8 164.1 %reduce-scatter.5.cloned.1.call-start = ((), (), s32[]{:S(2)}) async-start(), calls=%async_computation.5 | async-start | bytes 7077888 | tf_op jit(solution)/shard_map/reduce_scatter | solution.py:1759
  371.0 7.8 %collective-permute-start.3 = (bf16[64,3072]{1,0:T(8,128)(2,1)S(1)}, bf16[64,3072]{1,0:T(8,128)(2,1)S(1)}, u32[]{:S(2)}, u32[]{:S(2)}) collective-permute-start(bf16[64,3072]{1,0:T(8,128)(2,1)S(1)} %slice_select_fusion.2), channel_id=1, source_target_pairs={{0,4},{4,0},{1,5},{5,1},{2,6},{6,2},{3,7},{7,3},{8,12},{12,8},{9,1... | collective-permute-start | bytes 1179656 | tf_op jit(solution)/shard_map/ppermute | solution.py:36
  373.0 3.8 copy-start.2
  373.0 3.8 copy-start.4
  373.0 3.9 %copy-start.11 = (f32[8,128]{1,0:T(8,128)S(1)}, f32[8,128]{1,0:T(8,128)}, u32[]{:S(2)}) copy-start(f32[8,128]{1,0:T(8,128)} %get-tuple-element.199) | copy-start | bytes 12292
  376.8 2.1 copy-start
  379.0 2.6 copy-start.1
Sparse Core Ops, SparseCore 0:
  11.0 76.2 all-gather.4
  88.9 65.0 all-gather.2
  205.9 67.2 reduce-scatter.2
  275.4 72.3 reduce-scatter.4

commit v11 on v10

--- a/solution.py
+++ b/solution.py
@@ -1460,36 +1460,32 @@
         small.peers["far"],
     )
     shard_trade.start()
+    for at in (6, 0, 1, 2):
+        copies[at].wait()
+    turn_back(0)
     copies[4].wait()
     copies[5].wait()
     product(3, grad_mid, attended)
-    for at in (6, 0, 1, 2):
-        copies[at].wait()
+    y_trade(0, 0).start()
+    copies[3].wait()
     routes[3].start(*everything)
-    turn_back(0)
+    product(0, normed, grad_q)
     add_cores(routes[3])
-    y_trade(0, 0).start()
+    routes[0].start(*everything)
     across(routes[3])
     for w in range(1, windows):
         turn_back(w)
-    copies[3].wait()
-    product(0, normed, grad_q)
+    add_cores(routes[0])
+    across(routes[0])
     for w in range(1, windows):
         y_trade(w, 0).start()
-    routes[0].start(*everything)
     product(1, normed, grad_k)
-    add_cores(routes[0])
+    add_across(routes[3])
     routes[1].start(*everything)
-    across(routes[0])
     product(2, normed, grad_v)
+    routes[3].start(12, 14)
     add_cores(routes[1])
-    routes[2].start(*everything)
     across(routes[1])
-    add_across(routes[3])
-    add_cores(routes[2])
-    routes[3].start(12, 14)
-    across(routes[2])
-    routes[3].add_up()
     for at in range(7, 8 + windows):
         copies[at].wait()
     sums = [None, None]
@@ -1513,11 +1509,15 @@
         )
 
     first_norm(0)
+    routes[2].start(*everything)
+    add_across(routes[0])
+    add_cores(routes[2])
+    across(routes[2])
+    routes[3].add_up()
+    routes[0].start(12, 14)
     routes[3].start(13)
-    add_across(routes[0])
     for w in range(1, windows):
         first_norm(w)
-    routes[0].start(12, 14)
     first = jnp.concatenate(sums, axis=0)
     second = sum(ref[...] for ref in second_refs)
     span = width // devices

time: 393 us -> 391 us (level)
  transfers between devices with their start and end apart: 8 -> 8, of which waited for: 1 -> 1; matrix products, arithmetic and copies ran while one was open for 2% -> 2% of each run, Pallas kernels for 83% -> 82%
where the time goes in v11:
time: 391 us; the launch traced here: 388 us
  Pallas kernels  349 us (89%)
  between operations  14.3 us (4%)
  local copies, waits for them, and re-layouts  8.95 us (2%)
  other arithmetic  7.31 us (2%)
  starting transfers between devices  6.96 us (2%)
    pallas_call x15, Pallas kernels, run(): pl.pallas_call(kernel, out_shape=out_shape, compiler_params=pltpu.Compile...  349 us
  transfers between devices with their start and end apart: 8, of which 1 were waited for; matrix products, arithmetic and copies ran while one was open for 2% of the time, Pallas kernels for 82%

profile of v11, /device:TPU:0, one launch (start us, length us, event | category | flops | bytes accessed | tf_op | source)
XLA Modules:
  0.0 387.9 jit_solution(3558895845293873226)
XLA Ops:
  7.2 0.0 copy-start.10
  7.2 0.0 copy-start.12
  7.2 0.0 copy-start.17
  7.3 0.0 all-gather.5.cloned.1.call-start
  7.3 1.1 fusion.6
  8.4 1.1 fusion.4
  9.5 0.8 pad_maximum_fusion.3
  10.3 0.0 all-gather.5.cloned.1.call-update
  10.3 0.0 all-gather.3.cloned.1.call-start
  10.4 3.0 collective-permute-start
  13.4 0.0 copy-done.10
  13.4 0.2 fusion
  13.6 0.0 copy-done.17
  13.6 0.6 fusion.1
  14.2 0.0 copy-done.13
  14.3 0.6 broadcast.48
  15.0 0.0 copy-start.9
  15.0 0.7 pad_maximum_fusion.4.att_ref
  15.7 44.6 %gather.1 = (bf16[1024,2048]{1,0:T(8,128)(2,1)}, f32[8,1024]{1,0:T(8,128)}, bf16[1,2,256,1024]{3,2,1,0:T(8,128)(2,1)}, f32[512,128]{1,0:T(8,128)}, f32[512,128]{1,0:T(8,128)}) custom-call(bf16[64,2048]{1,0:T(8,128)(2,1)} %pad_maximum_fusion.4.att_ref, f32[8,128]{1,0:T(8,128)} %copy-done.9, bf16[2,256,1024]{2,1,0:T(8,128)(2,1)} %refs_7_.5), custom_call_target="tpu_custom_call" | custom-call | bytes 7114752 | tf_op jit(solution)/shard_map/gather/pallas_call | solution.py:79
  60.4 0.0 collective-permute-done
  60.4 1.1 maximum_select_fusion
  61.5 0.0 all-gather.3.cloned.1.call-update
  61.5 0.2 reduce-scatter.3.cloned.1.call-start
  61.7 8.5 %project.1 = (bf16[2,512,1024]{2,1,0:T(8,128)(2,1)}, bf16[2,512,512]{2,1,0:T(8,128)(2,1)}, bf16[2,4,2,512,128]{4,3,2,1,0:T(8,128)(2,1)}) custom-call(f32[8,1024]{1,0:T(8,128)} %get-tuple-element.120.norms_ref.refs_5_.refs_4_.refs_9_, bf16[1024,2048]{1,0:T(8,128)(2,1)} %get-tuple-element.121.w_ref.refs_1_.refs_4_.refs_6_, ...), custom_call_target="tpu_custom_call" | custom-call | flops 3221225472 | bytes 12091392 | tf_op jit(solution)/shard_map/project/pallas_call | solution.py:79
  70.2 69.5 %attend.1 = (bf16[2,512,512]{2,1,0:T(8,128)(2,1)}, f32[2,512,512]{2,1,0:T(8,128)}, f32[2,512,512]{2,1,0:T(8,128)}, f32[1,256,1024]{2,1,0:T(8,128)}, bf16[1,256,1...) custom-call(bf16[2,512,512]{2,1,0:T(8,128)(2,1)} %get-tuple-element., ...), custom_call_target="tpu_custom_call" | custom-call | flops 17179869184 | bytes 27820032 | tf_op jit(solution)/shard_map/attend/pallas_call | solution.py:79
  139.7 0.1 collective-permute-start.1
  139.7 0.6 fusion.7
  140.3 15.2 %feed_first.2 = (bf16[2,512,1024]{2,1,0:T(8,128)(2,1)}, bf16[3,512,2048]{2,1,0:T(8,128)(2,1)}, f32[512,1024]{1,0:T(8,128)}, f32[512,1024]{1,0:T(8,128)}) custom-call(bf16[1024,3072]{1,0:T(8,128)(2,1)} %all-gather.5.cloned.1.call-done.refs_0_.refs_1_.refs_2_, bf16[1024,3072]{1,0:T(8,128)(2,1)} %all-gather.5.cloned.1.call-done.refs_0_.refs_1_.refs_2_, ...), custom_call_target="tpu_custom_call" | custom-call | flops 6442450944 | bytes 34635780 | tf_op jit(solution)/shard_map/feed_first/pallas_call | solution.py:79
  155.5 0.0 collective-permute-done.1.arrived_ref
  155.5 0.0 copy-start.3
  155.5 0.8 copy-done.3
  156.3 2.8 second_norm.1
  159.1 2.0 collective-permute-start.2
  161.1 14.0 %feed_last.2 = (bf16[3,512,2048]{2,1,0:T(8,128)(2,1)}, f32[256,1024]{1,0:T(8,128)}, bf16[256,1024]{1,0:T(8,128)(2,1)}, f32[256,1024]{1,0:T(8,128)}, bf16[256,1024]{1,0:T(8,128)(2,1)}) custom-call(bf16[4,2,2,64,3072]{4,3,2,1,0:T(8,128)(2,1)} %bitcast.30, bf16[4,2,2,64,3072]{4,3,2,1,0:T(8,128)(2,1)} %bitcast.31, ...), custom_call_target="tpu_custom_call", output_to_operand_aliasing={{0}: (6, {})} | custom-call | flops 6442450944 | bytes 40894464 | tf_op jit(solution)/shard_map/feed_last/pallas_call | solution.py:79
  175.1 0.0 collective-permute-done.2.refs_6_
  175.1 0.8 copy-done.18
  175.9 15.1 %feed_first.3 = (bf16[2,512,1024]{2,1,0:T(8,128)(2,1)}, bf16[3,512,2048]{2,1,0:T(8,128)(2,1)}, f32[512,1024]{1,0:T(8,128)}, f32[512,1024]{1,0:T(8,128)}) custom-call(bf16[1024,3072]{1,0:T(8,128)(2,1)} %all-gather.5.cloned.1.call-done.refs_0_.refs_1_.refs_2_, bf16[1024,3072]{1,0:T(8,128)(2,1)} %all-gather.5.cloned.1.call-done.refs_0_.refs_1_.refs_2_, ...), custom_call_target="tpu_custom_call" | custom-call | flops 6442450944 | bytes 34635780 | tf_op jit(solution)/shard_map/feed_first/pallas_call | solution.py:79
  190.9 14.8 %feed_weights.2 = (bf16[4,2,2,64,3072]{4,3,2,1,0:T(8,128)(2,1)}, bf16[1,256,1024]{2,1,0:T(8,128)(2,1)}) custom-call(bf16[2,512,1024]{2,1,0:T(8,128)(2,1)} %get-tuple-element.140.refs_3_.refs_0_, bf16[2,512,1024]{2,1,0:T(8,128)(2,1)} %get-tuple-element.160.refs_1_.refs_3_, bf16[3,512,2048]{2,1,0:T(8,128)(2,1)} %get-tuple-element.151.refs_2_, ...), custom_call_target="tpu_custom_call" | custom-call | flops 6442450944 | bytes 24117248 | tf_op jit(solution)/shard_map/feed_weights/pallas_call | solution.py:79
  205.8 0.0 reduce-scatter.3.cloned.1.call-update
  205.8 0.0 reduce-scatter.5.cloned.1.call-start
  205.9 4.5 %second_norm_back.2 = (f32[256,1024]{1,0:T(8,128)}, bf16[256,1024]{1,0:T(8,128)(2,1)}, f32[2,1024]{1,0:T(2,128)}) custom-call(f32[1,1]{1,0:T(1,128)} %bitcast.8.refs_3_.weight_ref, f32[256,1024]{1,0:T(8,128)} %get-tuple-element.157.kept_ref, bf16[256,1024]{1,0:T(8,128)(2,1)} %bitcast.40, f32[256,1024]{1,0:T(8,128)} %get-tuple-element.193.middle_ref.refs_0_, ...), custom_call_target="tpu_custom_call" | custom-call | flops 10485760 | bytes 5283844 | tf_op jit(solution)/shard_map/second_norm_back/pallas_call | solution.py:79
  210.4 18.5 %feed_last.3 = (bf16[3,512,2048]{2,1,0:T(8,128)(2,1)}, f32[256,1024]{1,0:T(8,128)}, bf16[256,1024]{1,0:T(8,128)(2,1)}, f32[256,1024]{1,0:T(8,128)}, bf16[256,102...) custom-call(bf16[4,2,2,64,3072]{4,3,2,1,0:T(8,128)(2,1)} %bitcast.33, ...), custom_call_target="tpu_custom_call", output_to_operand_aliasing={{0}: (6, {})} | custom-call | flops 6442450944 | bytes 41943040 | tf_op jit(solution)/shard_map/feed_last/pallas_call | solution.py:79
  228.8 13.6 %feed_weights.3 = (bf16[4,2,2,64,3072]{4,3,2,1,0:T(8,128)(2,1)}, bf16[1,256,1024]{2,1,0:T(8,128)(2,1)}) custom-call(bf16[2,512,1024]{2,1,0:T(8,128)(2,1)} %get-tuple-element.140.refs_3_.refs_0_, bf16[2,512,1024]{2,1,0:T(8,128)(2,1)} %get-tuple-element.160.refs_1_.refs_3_, bf16[3,512,2048]{2,1,0:T(8,128)(2,1)} %get-tuple-element.151.refs_2_, ...), custom_call_target="tpu_custom_call" | custom-call | flops 6442450944 | bytes 24117248 | tf_op jit(solution)/shard_map/feed_weights/pallas_call | solution.py:79
  242.5 0.0 reduce-scatter.5.cloned.1.call-update
  242.5 4.5 %second_norm_back.3 = (f32[256,1024]{1,0:T(8,128)}, bf16[256,1024]{1,0:T(8,128)(2,1)}, f32[2,1024]{1,0:T(2,128)}) custom-call(f32[1,1]{1,0:T(1,128)} %bitcast.12.refs_3_.weight_ref, f32[256,1024]{1,0:T(8,128)} %get-tuple-element.172.kept_ref, bf16[256,1024]{1,0:T(8,128)(2,1)} %bitcast.39, f32[256,1024]{1,0:T(8,128)} %get-tuple-element.196.middle_ref.refs_3_, ...), custom_call_target="tpu_custom_call" | custom-call | flops 10485760 | bytes 5283844 | tf_op jit(solution)/shard_map/second_norm_back/pallas_call | solution.py:79
  247.0 65.2 %attend_back.1 = (bf16[2,512,512]{2,1,0:T(8,128)(2,1)}, bf16[2,512,512]{2,1,0:T(8,128)(2,1)}, bf16[2,512,512]{2,1,0:T(8,128)(2,1)}, bf16[2,512,1024]{2,1,0:T(8,1...) custom-call(bf16[2,512,512]{2,1,0:T(8,128)(2,1)} %get-tuple-element.167.refs_0_, ...), custom_call_target="tpu_custom_call" | custom-call | flops 42949672960 | bytes 27787264 | tf_op jit(solution)/shard_map/attend_back/pallas_call | solution.py:79
  312.3 0.0 reduce-scatter.3.cloned.1.call-done.refs_8_
  312.3 54.2 %finish.1 = (f32[64,2048]{1,0:T(8,128)}, f32[8,128]{1,0:T(8,128)}, f32[2,256,1024]{2,1,0:T(8,128)}, bf16[64,3072]{1,0:T(8,128)(2,1)}) custom-call(bf16[2,512,512]{2,1,0:T(8,128)(2,1)} %get-tuple-element.182.refs_0_, bf16[2,512,512]{2,1,0:T(8,128)(2,1)} %get-tuple-element.183.refs_1_, bf16[2,512,512]{2,1,0:T(8,128)(2,1)} %get-tuple-element.184.refs_2_, ...), custom_call_target="tpu_custom_call" | custom-call | flops 7516192768 | bytes 19582976 | tf_op jit(solution)/shard_map/finish/pallas_call | solution.py:79
  366.6 0.0 reduce-scatter.5.cloned.1.call-done
  366.6 1.2 slice_select_fusion.2
  367.8 1.6 collective-permute-start.3
  369.3 1.9 slice_bitcast_fusion
  371.2 3.8 results.1
  375.0 0.1 convert_add_fusion.1
  375.2 0.5 slice_bitcast_fusion.1
  375.7 0.1 fusion.2
  375.8 1.4 collective-permute-done.3
  377.1 0.1 convert_add_fusion
  377.3 0.0 copy-start.1
  377.3 0.1 fusion.3
  377.3 0.8 maximum_bitcast_fusion
  378.2 0.8 pad_maximum_fusion.1
  379.0 0.8 pad_maximum_fusion
  379.8 1.3 copy.35
  (32 shorter events, 0.1 us)
Async XLA Ops:
  7.2 6.2 %copy-start.10 = (f32[850]{0:T(1024)S(1)}, f32[850]{0:T(1024)}, u32[]{:S(2)}) copy-start(f32[850]{0:T(1024)} %param.24) | copy-start | bytes 10204
  7.2 6.2 %copy-start.12 = (s32[2]{0:T(128)S(1)}, s32[2]{0:T(128)}, u32[]{:S(2)}) copy-start(s32[2]{0:T(128)} %param.22) | copy-start | bytes 28
  7.2 6.4 %copy-start.17 = (s32[2]{0:T(128)S(1)}, s32[2]{0:T(128)}, u32[]{:S(2)}) copy-start(s32[2]{0:T(128)} %param.23) | copy-start | bytes 28
  7.2 7.0 %copy-start.13 = (f32[32]{0:T(128)S(1)}, f32[32]{0:T(128)}, u32[]{:S(2)}) copy-start(f32[32]{0:T(128)} %param.32) | copy-start | bytes 388
  7.2 7.0 %copy-start.14 = (f32[32]{0:T(128)S(1)}, f32[32]{0:T(128)}, u32[]{:S(2)}) copy-start(f32[32]{0:T(128)} %param.31) | copy-start | bytes 388
  7.2 7.0 %copy-start.15 = (f32[32]{0:T(128)S(1)}, f32[32]{0:T(128)}, u32[]{:S(2)}) copy-start(f32[32]{0:T(128)} %param.26) | copy-start | bytes 388
  7.2 7.0 %copy-start.16 = (f32[32]{0:T(128)S(1)}, f32[32]{0:T(128)}, u32[]{:S(2)}) copy-start(f32[32]{0:T(128)} %param.25) | copy-start | bytes 388
  7.3 7.7 %copy-start.5 = (bf16[512,64]{0,1:T(8,128)(2,1)S(1)}, bf16[512,64]{0,1:T(8,128)(2,1)}, u32[]{:S(2)}) copy-start(bf16[512,64]{0,1:T(8,128)(2,1)} %param.30) | copy-start | bytes 196612
  7.3 7.7 %copy-start.6 = (bf16[64,512]{1,0:T(8,128)(2,1)S(1)}, bf16[64,512]{1,0:T(8,128)(2,1)}, u32[]{:S(2)}) copy-start(bf16[64,512]{1,0:T(8,128)(2,1)} %param.29) | copy-start | bytes 196612
  7.3 7.7 %copy-start.7 = (bf16[64,512]{1,0:T(8,128)(2,1)S(1)}, bf16[64,512]{1,0:T(8,128)(2,1)}, u32[]{:S(2)}) copy-start(bf16[64,512]{1,0:T(8,128)(2,1)} %param.28) | copy-start | bytes 196612
  7.3 7.7 %copy-start.8 = (bf16[64,512]{1,0:T(8,128)(2,1)S(1)}, bf16[64,512]{1,0:T(8,128)(2,1)}, u32[]{:S(2)}) copy-start(bf16[64,512]{1,0:T(8,128)(2,1)} %param.27) | copy-start | bytes 196612
  7.3 133.0 %all-gather.5.cloned.1.call-start = ((), (), s32[]{:S(2)}) async-start(), calls=%async_computation.3 | async-start | bytes 6684672 | tf_op jit(solution)/shard_map/all_gather | solution.py:1723
  10.3 150.8 %all-gather.3.cloned.1.call-start = ((), (), s32[]{:S(2)}) async-start(), calls=%async_computation.2 | async-start | bytes 7077888 | tf_op jit(solution)/shard_map/all_gather | solution.py:1718
  10.4 49.9 %collective-permute-start = (bf16[64,3072]{1,0:T(8,128)(2,1)S(1)}, bf16[64,3072]{1,0:T(8,128)(2,1)S(1)}, u32[]{:S(2)}, u32[]{:S(2)}) collective-permute-start(bf16[64,3072]{1,0:T(8,128)(2,1)S(1)} %pad_maximum_fusion.2), channel_id=1, source_target_pairs={{0,4},{4,0},{1,5},{5,1},{2,6},{6,2},{3,7},{7,3},{8,12},{12,8},{9,1... | collective-permute-start | bytes 1179656 | tf_op jit(solution)/shard_map/ppermute | solution.py:36
  15.0 0.8 copy-start.9
  61.5 250.8 %reduce-scatter.3.cloned.1.call-start = ((), (), s32[]{:S(2)}) async-start(), calls=%async_computation.4 | async-start | bytes 7077888 | tf_op jit(solution)/shard_map/reduce_scatter | solution.py:1759
  139.7 15.8 %collective-permute-start.1 = (bf16[256,1024]{1,0:T(8,128)(2,1)}, bf16[256,1024]{1,0:T(8,128)(2,1)S(1)}, u32[]{:S(2)}, u32[]{:S(2)}) collective-permute-start(bf16[256,1024]{1,0:T(8,128)(2,1)} %bitcast.49), channel_id=1, source_target_pairs={{0,1},{1,0},{2,3},{3,2},{4,5},{5,4},{6,7},{7,6},{8,9},{9,8},{10,11... | collective-permute-start | bytes 1572872 | tf_op jit(solution)/shard_map/ppermute | solution.py:36
  155.5 0.8 copy-start.3
  159.1 16.0 %collective-permute-start.2 = (bf16[256,1024]{1,0:T(8,128)(2,1)}, bf16[256,1024]{1,0:T(8,128)(2,1)S(1)}, u32[]{:S(2)}, u32[]{:S(2)}) collective-permute-start(bf16[256,1024]{1,0:T(8,128)(2,1)} %get-tuple-element.148.refs_5_), channel_id=1, source_target_pairs={{0,1},{1,0},{2,3},{3,2},{4,5},{5,4},{6,7},{7,6},{8,9},{9,8},{10,11... | collective-permute-start | bytes 1572872 | tf_op jit(solution)/shard_map/ppermute | solution.py:36
  175.1 0.8 copy-start.18
  205.8 160.8 %reduce-scatter.5.cloned.1.call-start = ((), (), s32[]{:S(2)}) async-start(), calls=%async_computation.5 | async-start | bytes 7077888 | tf_op jit(solution)/shard_map/reduce_scatter | solution.py:1759
  367.8 9.4 %collective-permute-start.3 = (bf16[64,3072]{1,0:T(8,128)(2,1)S(1)}, bf16[64,3072]{1,0:T(8,128)(2,1)S(1)}, u32[]{:S(2)}, u32[]{:S(2)}) collective-permute-start(bf16[64,3072]{1,0:T(8,128)(2,1)S(1)} %slice_select_fusion.2), channel_id=1, source_target_pairs={{0,4},{4,0},{1,5},{5,1},{2,6},{6,2},{3,7},{7,3},{8,12},{12,8},{9,1... | collective-permute-start | bytes 1179656 | tf_op jit(solution)/shard_map/ppermute | solution.py:36
  371.2 3.8 copy-start.2
  371.2 3.8 copy-start.4
  371.2 3.9 %copy-start.11 = (f32[8,128]{1,0:T(8,128)S(1)}, f32[8,128]{1,0:T(8,128)}, u32[]{:S(2)}) copy-start(f32[8,128]{1,0:T(8,128)} %get-tuple-element.199) | copy-start | bytes 12292
  375.0 2.1 copy-start
  377.3 2.6 copy-start.1
Sparse Core Ops, SparseCore 0:
  11.0 76.2 all-gather.4
  88.9 65.0 all-gather.2
  205.9 67.2 reduce-scatter.2
  275.4 74.0 reduce-scatter.4

commit v12 on v11

--- a/solution.py
+++ b/solution.py
@@ -1439,6 +1439,12 @@
         kept_all[w][...] = total[:half]
         stage_sent[w][0][...] = total[half:].astype(BF16)
 
+    def fill_tiles(row, values):
+        span = width // devices
+        for device in range(devices):
+            at = device * 8 + row
+            tiles[at : at + 2, :span] = values[:, device * span : (device + 1) * span]
+
     def add_cores(route):
         for number in everything:
             route.add_core(number)
@@ -1467,6 +1473,8 @@
     copies[5].wait()
     product(3, grad_mid, attended)
     y_trade(0, 0).start()
+    tiles[...] = jnp.zeros_like(tiles)
+    fill_tiles(2, sum(ref[...] for ref in second_refs))
     copies[3].wait()
     routes[3].start(*everything)
     product(0, normed, grad_q)
@@ -1518,15 +1526,7 @@
     routes[3].start(13)
     for w in range(1, windows):
         first_norm(w)
-    first = jnp.concatenate(sums, axis=0)
-    second = sum(ref[...] for ref in second_refs)
-    span = width // devices
-    tiles[...] = jnp.zeros_like(tiles)
-    for device in range(devices):
-        at = device * 8
-        columns = slice(device * span, (device + 1) * span)
-        tiles[at : at + 2, :span] = first[:, columns]
-        tiles[at + 2 : at + 4, :span] = second[:, columns]
+    fill_tiles(0, jnp.concatenate(sums, axis=0))
     add_across(routes[1])
     small.start(*everything)
     routes[0].add_up()

time: 391 us -> 391 us (level)
  no operation moved by 1% of the time
where the time goes in v12:
time: 391 us; the launch traced here: 388 us
  Pallas kernels  349 us (89%)
  between operations  14.3 us (4%)
  local copies, waits for them, and re-layouts  8.95 us (2%)
  other arithmetic  7.31 us (2%)
  starting transfers between devices  6.96 us (2%)
    pallas_call x15, Pallas kernels, run(): pl.pallas_call(kernel, out_shape=out_shape, compiler_params=pltpu.Compile...  349 us
  transfers between devices with their start and end apart: 8, of which 1 were waited for; matrix products, arithmetic and copies ran while one was open for 2% of the time, Pallas kernels for 82%

profile of v12, /device:TPU:0, one launch (start us, length us, event | category | flops | bytes accessed | tf_op | source)
XLA Modules:
  0.0 387.9 jit_solution(17646798402396196852)
XLA Ops:
  7.2 0.0 copy-start.10
  7.2 0.0 copy-start.12
  7.2 0.0 copy-start.17
  7.3 0.0 all-gather.5.cloned.1.call-start
  7.3 1.1 fusion.6
  8.4 1.1 fusion.4
  9.5 0.8 pad_maximum_fusion.3
  10.3 0.0 all-gather.5.cloned.1.call-update
  10.3 0.0 all-gather.3.cloned.1.call-start
  10.4 3.0 collective-permute-start
  13.4 0.0 copy-done.10
  13.4 0.2 fusion
  13.6 0.0 copy-done.17
  13.6 0.6 fusion.1
  14.2 0.0 copy-done.13
  14.3 0.6 broadcast.48
  15.0 0.0 copy-start.9
  15.0 0.7 pad_maximum_fusion.4.att_ref
  15.7 44.6 %gather.1 = (bf16[1024,2048]{1,0:T(8,128)(2,1)}, f32[8,1024]{1,0:T(8,128)}, bf16[1,2,256,1024]{3,2,1,0:T(8,128)(2,1)}, f32[512,128]{1,0:T(8,128)}, f32[512,128]{1,0:T(8,128)}) custom-call(bf16[64,2048]{1,0:T(8,128)(2,1)} %pad_maximum_fusion.4.att_ref, f32[8,128]{1,0:T(8,128)} %copy-done.9, bf16[2,256,1024]{2,1,0:T(8,128)(2,1)} %refs_7_.5), custom_call_target="tpu_custom_call" | custom-call | bytes 7114752 | tf_op jit(solution)/shard_map/gather/pallas_call | solution.py:79
  60.4 0.0 collective-permute-done
  60.4 1.1 maximum_select_fusion
  61.5 0.0 all-gather.3.cloned.1.call-update
  61.5 0.2 reduce-scatter.3.cloned.1.call-start
  61.7 8.5 %project.1 = (bf16[2,512,1024]{2,1,0:T(8,128)(2,1)}, bf16[2,512,512]{2,1,0:T(8,128)(2,1)}, bf16[2,4,2,512,128]{4,3,2,1,0:T(8,128)(2,1)}) custom-call(f32[8,1024]{1,0:T(8,128)} %get-tuple-element.120.norms_ref.refs_5_.refs_4_.refs_9_, bf16[1024,2048]{1,0:T(8,128)(2,1)} %get-tuple-element.121.w_ref.refs_1_.refs_4_.refs_6_, ...), custom_call_target="tpu_custom_call" | custom-call | flops 3221225472 | bytes 12091392 | tf_op jit(solution)/shard_map/project/pallas_call | solution.py:79
  70.2 69.5 %attend.1 = (bf16[2,512,512]{2,1,0:T(8,128)(2,1)}, f32[2,512,512]{2,1,0:T(8,128)}, f32[2,512,512]{2,1,0:T(8,128)}, f32[1,256,1024]{2,1,0:T(8,128)}, bf16[1,256,1...) custom-call(bf16[2,512,512]{2,1,0:T(8,128)(2,1)} %get-tuple-element., ...), custom_call_target="tpu_custom_call" | custom-call | flops 17179869184 | bytes 27820032 | tf_op jit(solution)/shard_map/attend/pallas_call | solution.py:79
  139.7 0.1 collective-permute-start.1
  139.7 0.6 fusion.7
  140.3 15.2 %feed_first.2 = (bf16[2,512,1024]{2,1,0:T(8,128)(2,1)}, bf16[3,512,2048]{2,1,0:T(8,128)(2,1)}, f32[512,1024]{1,0:T(8,128)}, f32[512,1024]{1,0:T(8,128)}) custom-call(bf16[1024,3072]{1,0:T(8,128)(2,1)} %all-gather.5.cloned.1.call-done.refs_0_.refs_1_.refs_2_, bf16[1024,3072]{1,0:T(8,128)(2,1)} %all-gather.5.cloned.1.call-done.refs_0_.refs_1_.refs_2_, ...), custom_call_target="tpu_custom_call" | custom-call | flops 6442450944 | bytes 34635780 | tf_op jit(solution)/shard_map/feed_first/pallas_call | solution.py:79
  155.5 0.0 collective-permute-done.1.arrived_ref
  155.5 0.0 copy-start.3
  155.5 0.8 copy-done.3
  156.3 2.8 second_norm.1
  159.1 2.0 collective-permute-start.2
  161.1 14.0 %feed_last.2 = (bf16[3,512,2048]{2,1,0:T(8,128)(2,1)}, f32[256,1024]{1,0:T(8,128)}, bf16[256,1024]{1,0:T(8,128)(2,1)}, f32[256,1024]{1,0:T(8,128)}, bf16[256,1024]{1,0:T(8,128)(2,1)}) custom-call(bf16[4,2,2,64,3072]{4,3,2,1,0:T(8,128)(2,1)} %bitcast.30, bf16[4,2,2,64,3072]{4,3,2,1,0:T(8,128)(2,1)} %bitcast.31, ...), custom_call_target="tpu_custom_call", output_to_operand_aliasing={{0}: (6, {})} | custom-call | flops 6442450944 | bytes 40894464 | tf_op jit(solution)/shard_map/feed_last/pallas_call | solution.py:79
  175.1 0.0 collective-permute-done.2.refs_6_
  175.1 0.8 copy-done.18
  175.9 15.1 %feed_first.3 = (bf16[2,512,1024]{2,1,0:T(8,128)(2,1)}, bf16[3,512,2048]{2,1,0:T(8,128)(2,1)}, f32[512,1024]{1,0:T(8,128)}, f32[512,1024]{1,0:T(8,128)}) custom-call(bf16[1024,3072]{1,0:T(8,128)(2,1)} %all-gather.5.cloned.1.call-done.refs_0_.refs_1_.refs_2_, bf16[1024,3072]{1,0:T(8,128)(2,1)} %all-gather.5.cloned.1.call-done.refs_0_.refs_1_.refs_2_, ...), custom_call_target="tpu_custom_call" | custom-call | flops 6442450944 | bytes 34635780 | tf_op jit(solution)/shard_map/feed_first/pallas_call | solution.py:79
  190.9 14.8 %feed_weights.2 = (bf16[4,2,2,64,3072]{4,3,2,1,0:T(8,128)(2,1)}, bf16[1,256,1024]{2,1,0:T(8,128)(2,1)}) custom-call(bf16[2,512,1024]{2,1,0:T(8,128)(2,1)} %get-tuple-element.140.refs_3_.refs_0_, bf16[2,512,1024]{2,1,0:T(8,128)(2,1)} %get-tuple-element.160.refs_1_.refs_3_, bf16[3,512,2048]{2,1,0:T(8,128)(2,1)} %get-tuple-element.151.refs_2_, ...), custom_call_target="tpu_custom_call" | custom-call | flops 6442450944 | bytes 24117248 | tf_op jit(solution)/shard_map/feed_weights/pallas_call | solution.py:79
  205.8 0.0 reduce-scatter.3.cloned.1.call-update
  205.8 0.0 reduce-scatter.5.cloned.1.call-start
  205.9 4.5 %second_norm_back.2 = (f32[256,1024]{1,0:T(8,128)}, bf16[256,1024]{1,0:T(8,128)(2,1)}, f32[2,1024]{1,0:T(2,128)}) custom-call(f32[1,1]{1,0:T(1,128)} %bitcast.8.refs_3_.weight_ref, f32[256,1024]{1,0:T(8,128)} %get-tuple-element.157.kept_ref, bf16[256,1024]{1,0:T(8,128)(2,1)} %bitcast.40, f32[256,1024]{1,0:T(8,128)} %get-tuple-element.193.middle_ref.refs_0_, ...), custom_call_target="tpu_custom_call" | custom-call | flops 10485760 | bytes 5283844 | tf_op jit(solution)/shard_map/second_norm_back/pallas_call | solution.py:79
  210.4 18.5 %feed_last.3 = (bf16[3,512,2048]{2,1,0:T(8,128)(2,1)}, f32[256,1024]{1,0:T(8,128)}, bf16[256,1024]{1,0:T(8,128)(2,1)}, f32[256,1024]{1,0:T(8,128)}, bf16[256,102...) custom-call(bf16[4,2,2,64,3072]{4,3,2,1,0:T(8,128)(2,1)} %bitcast.33, ...), custom_call_target="tpu_custom_call", output_to_operand_aliasing={{0}: (6, {})} | custom-call | flops 6442450944 | bytes 41943040 | tf_op jit(solution)/shard_map/feed_last/pallas_call | solution.py:79
  228.8 13.6 %feed_weights.3 = (bf16[4,2,2,64,3072]{4,3,2,1,0:T(8,128)(2,1)}, bf16[1,256,1024]{2,1,0:T(8,128)(2,1)}) custom-call(bf16[2,512,1024]{2,1,0:T(8,128)(2,1)} %get-tuple-element.140.refs_3_.refs_0_, bf16[2,512,1024]{2,1,0:T(8,128)(2,1)} %get-tuple-element.160.refs_1_.refs_3_, bf16[3,512,2048]{2,1,0:T(8,128)(2,1)} %get-tuple-element.151.refs_2_, ...), custom_call_target="tpu_custom_call" | custom-call | flops 6442450944 | bytes 24117248 | tf_op jit(solution)/shard_map/feed_weights/pallas_call | solution.py:79
  242.5 0.0 reduce-scatter.5.cloned.1.call-update
  242.5 4.5 %second_norm_back.3 = (f32[256,1024]{1,0:T(8,128)}, bf16[256,1024]{1,0:T(8,128)(2,1)}, f32[2,1024]{1,0:T(2,128)}) custom-call(f32[1,1]{1,0:T(1,128)} %bitcast.12.refs_3_.weight_ref, f32[256,1024]{1,0:T(8,128)} %get-tuple-element.172.kept_ref, bf16[256,1024]{1,0:T(8,128)(2,1)} %bitcast.39, f32[256,1024]{1,0:T(8,128)} %get-tuple-element.196.middle_ref.refs_3_, ...), custom_call_target="tpu_custom_call" | custom-call | flops 10485760 | bytes 5283844 | tf_op jit(solution)/shard_map/second_norm_back/pallas_call | solution.py:79
  247.0 65.2 %attend_back.1 = (bf16[2,512,512]{2,1,0:T(8,128)(2,1)}, bf16[2,512,512]{2,1,0:T(8,128)(2,1)}, bf16[2,512,512]{2,1,0:T(8,128)(2,1)}, bf16[2,512,1024]{2,1,0:T(8,1...) custom-call(bf16[2,512,512]{2,1,0:T(8,128)(2,1)} %get-tuple-element.167.refs_0_, ...), custom_call_target="tpu_custom_call" | custom-call | flops 42949672960 | bytes 27787264 | tf_op jit(solution)/shard_map/attend_back/pallas_call | solution.py:79
  312.3 0.0 reduce-scatter.3.cloned.1.call-done.refs_8_
  312.3 54.2 %finish.1 = (f32[64,2048]{1,0:T(8,128)}, f32[8,128]{1,0:T(8,128)}, f32[2,256,1024]{2,1,0:T(8,128)}, bf16[64,3072]{1,0:T(8,128)(2,1)}) custom-call(bf16[2,512,512]{2,1,0:T(8,128)(2,1)} %get-tuple-element.182.refs_0_, bf16[2,512,512]{2,1,0:T(8,128)(2,1)} %get-tuple-element.183.refs_1_, bf16[2,512,512]{2,1,0:T(8,128)(2,1)} %get-tuple-element.184.refs_2_, ...), custom_call_target="tpu_custom_call" | custom-call | flops 7516192768 | bytes 19582976 | tf_op jit(solution)/shard_map/finish/pallas_call | solution.py:79
  366.6 0.0 reduce-scatter.5.cloned.1.call-done
  366.6 1.2 slice_select_fusion.2
  367.8 1.6 collective-permute-start.3
  369.3 1.9 slice_bitcast_fusion
  371.2 3.8 results.1
  375.0 0.1 convert_add_fusion.1
  375.2 0.5 slice_bitcast_fusion.1
  375.7 0.1 fusion.2
  375.8 1.4 collective-permute-done.3
  377.1 0.0 copy-done
  377.1 0.1 convert_add_fusion
  377.3 0.1 fusion.3
  377.3 0.8 maximum_bitcast_fusion
  378.2 0.8 pad_maximum_fusion.1
  379.0 0.8 pad_maximum_fusion
  379.8 1.3 copy.35
  (32 shorter events, 0.1 us)
Async XLA Ops:
  7.2 6.2 %copy-start.10 = (f32[850]{0:T(1024)S(1)}, f32[850]{0:T(1024)}, u32[]{:S(2)}) copy-start(f32[850]{0:T(1024)} %param.24) | copy-start | bytes 10204
  7.2 6.2 %copy-start.12 = (s32[2]{0:T(128)S(1)}, s32[2]{0:T(128)}, u32[]{:S(2)}) copy-start(s32[2]{0:T(128)} %param.22) | copy-start | bytes 28
  7.2 6.4 %copy-start.17 = (s32[2]{0:T(128)S(1)}, s32[2]{0:T(128)}, u32[]{:S(2)}) copy-start(s32[2]{0:T(128)} %param.23) | copy-start | bytes 28
  7.2 7.0 %copy-start.13 = (f32[32]{0:T(128)S(1)}, f32[32]{0:T(128)}, u32[]{:S(2)}) copy-start(f32[32]{0:T(128)} %param.32) | copy-start | bytes 388
  7.2 7.0 %copy-start.14 = (f32[32]{0:T(128)S(1)}, f32[32]{0:T(128)}, u32[]{:S(2)}) copy-start(f32[32]{0:T(128)} %param.31) | copy-start | bytes 388
  7.2 7.0 %copy-start.15 = (f32[32]{0:T(128)S(1)}, f32[32]{0:T(128)}, u32[]{:S(2)}) copy-start(f32[32]{0:T(128)} %param.26) | copy-start | bytes 388
  7.2 7.0 %copy-start.16 = (f32[32]{0:T(128)S(1)}, f32[32]{0:T(128)}, u32[]{:S(2)}) copy-start(f32[32]{0:T(128)} %param.25) | copy-start | bytes 388
  7.3 7.7 %copy-start.5 = (bf16[512,64]{0,1:T(8,128)(2,1)S(1)}, bf16[512,64]{0,1:T(8,128)(2,1)}, u32[]{:S(2)}) copy-start(bf16[512,64]{0,1:T(8,128)(2,1)} %param.30) | copy-start | bytes 196612
  7.3 7.7 %copy-start.6 = (bf16[64,512]{1,0:T(8,128)(2,1)S(1)}, bf16[64,512]{1,0:T(8,128)(2,1)}, u32[]{:S(2)}) copy-start(bf16[64,512]{1,0:T(8,128)(2,1)} %param.29) | copy-start | bytes 196612
  7.3 7.7 %copy-start.7 = (bf16[64,512]{1,0:T(8,128)(2,1)S(1)}, bf16[64,512]{1,0:T(8,128)(2,1)}, u32[]{:S(2)}) copy-start(bf16[64,512]{1,0:T(8,128)(2,1)} %param.28) | copy-start | bytes 196612
  7.3 7.7 %copy-start.8 = (bf16[64,512]{1,0:T(8,128)(2,1)S(1)}, bf16[64,512]{1,0:T(8,128)(2,1)}, u32[]{:S(2)}) copy-start(bf16[64,512]{1,0:T(8,128)(2,1)} %param.27) | copy-start | bytes 196612
  7.3 133.0 %all-gather.5.cloned.1.call-start = ((), (), s32[]{:S(2)}) async-start(), calls=%async_computation.3 | async-start | bytes 6684672 | tf_op jit(solution)/shard_map/all_gather | solution.py:1723
  10.3 150.8 %all-gather.3.cloned.1.call-start = ((), (), s32[]{:S(2)}) async-start(), calls=%async_computation.2 | async-start | bytes 7077888 | tf_op jit(solution)/shard_map/all_gather | solution.py:1718
  10.4 49.9 %collective-permute-start = (bf16[64,3072]{1,0:T(8,128)(2,1)S(1)}, bf16[64,3072]{1,0:T(8,128)(2,1)S(1)}, u32[]{:S(2)}, u32[]{:S(2)}) collective-permute-start(bf16[64,3072]{1,0:T(8,128)(2,1)S(1)} %pad_maximum_fusion.2), channel_id=1, source_target_pairs={{0,4},{4,0},{1,5},{5,1},{2,6},{6,2},{3,7},{7,3},{8,12},{12,8},{9,1... | collective-permute-start | bytes 1179656 | tf_op jit(solution)/shard_map/ppermute | solution.py:36
  15.0 0.8 copy-start.9
  61.5 250.8 %reduce-scatter.3.cloned.1.call-start = ((), (), s32[]{:S(2)}) async-start(), calls=%async_computation.4 | async-start | bytes 7077888 | tf_op jit(solution)/shard_map/reduce_scatter | solution.py:1759
  139.7 15.8 %collective-permute-start.1 = (bf16[256,1024]{1,0:T(8,128)(2,1)}, bf16[256,1024]{1,0:T(8,128)(2,1)S(1)}, u32[]{:S(2)}, u32[]{:S(2)}) collective-permute-start(bf16[256,1024]{1,0:T(8,128)(2,1)} %bitcast.49), channel_id=1, source_target_pairs={{0,1},{1,0},{2,3},{3,2},{4,5},{5,4},{6,7},{7,6},{8,9},{9,8},{10,11... | collective-permute-start | bytes 1572872 | tf_op jit(solution)/shard_map/ppermute | solution.py:36
  155.5 0.8 copy-start.3
  159.1 16.0 %collective-permute-start.2 = (bf16[256,1024]{1,0:T(8,128)(2,1)}, bf16[256,1024]{1,0:T(8,128)(2,1)S(1)}, u32[]{:S(2)}, u32[]{:S(2)}) collective-permute-start(bf16[256,1024]{1,0:T(8,128)(2,1)} %get-tuple-element.148.refs_5_), channel_id=1, source_target_pairs={{0,1},{1,0},{2,3},{3,2},{4,5},{5,4},{6,7},{7,6},{8,9},{9,8},{10,11... | collective-permute-start | bytes 1572872 | tf_op jit(solution)/shard_map/ppermute | solution.py:36
  175.1 0.8 copy-start.18
  205.8 160.8 %reduce-scatter.5.cloned.1.call-start = ((), (), s32[]{:S(2)}) async-start(), calls=%async_computation.5 | async-start | bytes 7077888 | tf_op jit(solution)/shard_map/reduce_scatter | solution.py:1759
  367.8 9.4 %collective-permute-start.3 = (bf16[64,3072]{1,0:T(8,128)(2,1)S(1)}, bf16[64,3072]{1,0:T(8,128)(2,1)S(1)}, u32[]{:S(2)}, u32[]{:S(2)}) collective-permute-start(bf16[64,3072]{1,0:T(8,128)(2,1)S(1)} %slice_select_fusion.2), channel_id=1, source_target_pairs={{0,4},{4,0},{1,5},{5,1},{2,6},{6,2},{3,7},{7,3},{8,12},{12,8},{9,1... | collective-permute-start | bytes 1179656 | tf_op jit(solution)/shard_map/ppermute | solution.py:36
  371.2 3.8 copy-start.2
  371.2 3.8 copy-start.4
  371.2 3.9 %copy-start.11 = (f32[8,128]{1,0:T(8,128)S(1)}, f32[8,128]{1,0:T(8,128)}, u32[]{:S(2)}) copy-start(f32[8,128]{1,0:T(8,128)} %get-tuple-element.199) | copy-start | bytes 12292
  375.0 2.1 copy-start
  377.3 2.6 copy-start.1
Sparse Core Ops, SparseCore 0:
  11.0 76.2 all-gather.4
  88.9 65.0 all-gather.2
  205.9 67.2 reduce-scatter.2
  275.4 74.0 reduce-scatter.4

commit v13 on v12

--- a/solution.py
+++ b/solution.py
@@ -1200,7 +1200,7 @@
     windows = len(boths)
     rows, width = boths[0].shape[1:]
     hidden_cols = wides[0].shape[2] // 2
-    step = min(512, hidden_cols)
+    step = min(1024, hidden_cols)
     steps = hidden_cols // step
     lead = (lax.axis_size("dp"), lax.axis_size("core"), lax.axis_size("x"))
     lead += (width // math.prod(lead),)
@@ -1465,7 +1465,6 @@
         shard_sem.at[1],
         small.peers["far"],
     )
-    shard_trade.start()
     for at in (6, 0, 1, 2):
         copies[at].wait()
     turn_back(0)
@@ -1521,6 +1520,7 @@
     add_across(routes[0])
     add_cores(routes[2])
     across(routes[2])
+    shard_trade.start()
     routes[3].add_up()
     routes[0].start(12, 14)
     routes[3].start(13)

time: 391 us -> 393 us (level)
  no operation moved by 1% of the time
where the time goes in v13:
time: 393 us; the launch traced here: 389 us
  Pallas kernels  351 us (89%)
  between operations  14.3 us (4%)
  local copies, waits for them, and re-layouts  8.95 us (2%)
  other arithmetic  7.31 us (2%)
  starting transfers between devices  7.14 us (2%)
    pallas_call x15, Pallas kernels, run(): pl.pallas_call(kernel, out_shape=out_shape, compiler_params=pltpu.Compile...  351 us
  transfers between devices with their start and end apart: 8, of which 1 were waited for; matrix products, arithmetic and copies ran while one was open for 2% of the time, Pallas kernels for 82%

profile of v13, /device:TPU:0, one launch (start us, length us, event | category | flops | bytes accessed | tf_op | source)
XLA Modules:
  0.0 389.4 jit_solution(11268107952447516217)
XLA Ops:
  7.2 0.0 copy-start.10
  7.2 0.0 copy-start.12
  7.2 0.0 copy-start.17
  7.2 0.0 copy-start.13
  7.3 0.0 all-gather.5.cloned.1.call-start
  7.3 1.1 fusion.6
  8.4 1.1 fusion.4
  9.5 0.8 pad_maximum_fusion.3
  10.3 0.0 all-gather.5.cloned.1.call-update
  10.3 0.0 all-gather.3.cloned.1.call-start
  10.4 3.0 collective-permute-start
  13.4 0.0 copy-done.10
  13.4 0.2 fusion
  13.6 0.0 copy-done.17
  13.6 0.6 fusion.1
  14.2 0.0 copy-done.13
  14.3 0.6 broadcast.48
  15.0 0.0 copy-start.9
  15.0 0.7 pad_maximum_fusion.4.att_ref
  15.7 44.6 %gather.1 = (bf16[1024,2048]{1,0:T(8,128)(2,1)}, f32[8,1024]{1,0:T(8,128)}, bf16[1,2,256,1024]{3,2,1,0:T(8,128)(2,1)}, f32[512,128]{1,0:T(8,128)}, f32[512,128]{1,0:T(8,128)}) custom-call(bf16[64,2048]{1,0:T(8,128)(2,1)} %pad_maximum_fusion.4.att_ref, f32[8,128]{1,0:T(8,128)} %copy-done.9, bf16[2,256,1024]{2,1,0:T(8,128)(2,1)} %refs_7_.5), custom_call_target="tpu_custom_call" | custom-call | bytes 7114752 | tf_op jit(solution)/shard_map/gather/pallas_call | solution.py:79
  60.4 0.0 collective-permute-done
  60.4 1.1 maximum_select_fusion
  61.5 0.0 all-gather.3.cloned.1.call-update
  61.5 0.3 reduce-scatter.3.cloned.1.call-start
  61.8 8.5 %project.1 = (bf16[2,512,1024]{2,1,0:T(8,128)(2,1)}, bf16[2,512,512]{2,1,0:T(8,128)(2,1)}, bf16[2,4,2,512,128]{4,3,2,1,0:T(8,128)(2,1)}) custom-call(f32[8,1024]{1,0:T(8,128)} %get-tuple-element.120.norms_ref.refs_5_.refs_4_.refs_9_, bf16[1024,2048]{1,0:T(8,128)(2,1)} %get-tuple-element.121.w_ref.refs_1_.refs_4_.refs_6_, ...), custom_call_target="tpu_custom_call" | custom-call | flops 3221225472 | bytes 12091392 | tf_op jit(solution)/shard_map/project/pallas_call | solution.py:79
  70.3 69.4 %attend.1 = (bf16[2,512,512]{2,1,0:T(8,128)(2,1)}, f32[2,512,512]{2,1,0:T(8,128)}, f32[2,512,512]{2,1,0:T(8,128)}, f32[1,256,1024]{2,1,0:T(8,128)}, bf16[1,256,1...) custom-call(bf16[2,512,512]{2,1,0:T(8,128)(2,1)} %get-tuple-element., ...), custom_call_target="tpu_custom_call" | custom-call | flops 17179869184 | bytes 27820032 | tf_op jit(solution)/shard_map/attend/pallas_call | solution.py:79
  139.7 0.1 collective-permute-start.1
  139.8 0.6 fusion.7
  140.4 15.2 %feed_first.2 = (bf16[2,512,1024]{2,1,0:T(8,128)(2,1)}, bf16[3,512,2048]{2,1,0:T(8,128)(2,1)}, f32[512,1024]{1,0:T(8,128)}, f32[512,1024]{1,0:T(8,128)}) custom-call(bf16[1024,3072]{1,0:T(8,128)(2,1)} %all-gather.5.cloned.1.call-done.refs_0_.refs_1_.refs_2_, bf16[1024,3072]{1,0:T(8,128)(2,1)} %all-gather.5.cloned.1.call-done.refs_0_.refs_1_.refs_2_, ...), custom_call_target="tpu_custom_call" | custom-call | flops 6442450944 | bytes 34635780 | tf_op jit(solution)/shard_map/feed_first/pallas_call | solution.py:79
  155.6 0.0 collective-permute-done.1.arrived_ref
  155.6 0.0 copy-start.3
  155.6 0.8 copy-done.3
  156.4 2.8 second_norm.1
  159.2 2.0 collective-permute-start.2
  161.2 14.3 %feed_last.2 = (bf16[3,512,2048]{2,1,0:T(8,128)(2,1)}, f32[256,1024]{1,0:T(8,128)}, bf16[256,1024]{1,0:T(8,128)(2,1)}, f32[256,1024]{1,0:T(8,128)}, bf16[256,1024]{1,0:T(8,128)(2,1)}) custom-call(bf16[4,2,2,64,3072]{4,3,2,1,0:T(8,128)(2,1)} %bitcast.30, bf16[4,2,2,64,3072]{4,3,2,1,0:T(8,128)(2,1)} %bitcast.31, ...), custom_call_target="tpu_custom_call", output_to_operand_aliasing={{0}: (6, {})} | custom-call | flops 6442450944 | bytes 40894464 | tf_op jit(solution)/shard_map/feed_last/pallas_call | solution.py:79
  175.5 0.0 collective-permute-done.2.refs_6_
  175.5 0.8 copy-done.18
  176.3 15.1 %feed_first.3 = (bf16[2,512,1024]{2,1,0:T(8,128)(2,1)}, bf16[3,512,2048]{2,1,0:T(8,128)(2,1)}, f32[512,1024]{1,0:T(8,128)}, f32[512,1024]{1,0:T(8,128)}) custom-call(bf16[1024,3072]{1,0:T(8,128)(2,1)} %all-gather.5.cloned.1.call-done.refs_0_.refs_1_.refs_2_, bf16[1024,3072]{1,0:T(8,128)(2,1)} %all-gather.5.cloned.1.call-done.refs_0_.refs_1_.refs_2_, ...), custom_call_target="tpu_custom_call" | custom-call | flops 6442450944 | bytes 34635780 | tf_op jit(solution)/shard_map/feed_first/pallas_call | solution.py:79
  191.3 15.6 %feed_weights.2 = (bf16[4,2,2,64,3072]{4,3,2,1,0:T(8,128)(2,1)}, bf16[1,256,1024]{2,1,0:T(8,128)(2,1)}) custom-call(bf16[2,512,1024]{2,1,0:T(8,128)(2,1)} %get-tuple-element.140.refs_3_.refs_0_, bf16[2,512,1024]{2,1,0:T(8,128)(2,1)} %get-tuple-element.160.refs_1_.refs_3_, bf16[3,512,2048]{2,1,0:T(8,128)(2,1)} %get-tuple-element.151.refs_2_, ...), custom_call_target="tpu_custom_call" | custom-call | flops 6442450944 | bytes 24117248 | tf_op jit(solution)/shard_map/feed_weights/pallas_call | solution.py:79
  206.9 0.0 reduce-scatter.3.cloned.1.call-update
  206.9 0.0 reduce-scatter.5.cloned.1.call-start
  207.0 4.5 %second_norm_back.2 = (f32[256,1024]{1,0:T(8,128)}, bf16[256,1024]{1,0:T(8,128)(2,1)}, f32[2,1024]{1,0:T(2,128)}) custom-call(f32[1,1]{1,0:T(1,128)} %bitcast.8.refs_3_.weight_ref, f32[256,1024]{1,0:T(8,128)} %get-tuple-element.157.kept_ref, bf16[256,1024]{1,0:T(8,128)(2,1)} %bitcast.40, f32[256,1024]{1,0:T(8,128)} %get-tuple-element.193.middle_ref.refs_0_, ...), custom_call_target="tpu_custom_call" | custom-call | flops 10485760 | bytes 5283844 | tf_op jit(solution)/shard_map/second_norm_back/pallas_call | solution.py:79
  211.5 18.2 %feed_last.3 = (bf16[3,512,2048]{2,1,0:T(8,128)(2,1)}, f32[256,1024]{1,0:T(8,128)}, bf16[256,1024]{1,0:T(8,128)(2,1)}, f32[256,1024]{1,0:T(8,128)}, bf16[256,102...) custom-call(bf16[4,2,2,64,3072]{4,3,2,1,0:T(8,128)(2,1)} %bitcast.33, ...), custom_call_target="tpu_custom_call", output_to_operand_aliasing={{0}: (6, {})} | custom-call | flops 6442450944 | bytes 41943040 | tf_op jit(solution)/shard_map/feed_last/pallas_call | solution.py:79
  229.7 14.2 %feed_weights.3 = (bf16[4,2,2,64,3072]{4,3,2,1,0:T(8,128)(2,1)}, bf16[1,256,1024]{2,1,0:T(8,128)(2,1)}) custom-call(bf16[2,512,1024]{2,1,0:T(8,128)(2,1)} %get-tuple-element.140.refs_3_.refs_0_, bf16[2,512,1024]{2,1,0:T(8,128)(2,1)} %get-tuple-element.160.refs_1_.refs_3_, bf16[3,512,2048]{2,1,0:T(8,128)(2,1)} %get-tuple-element.151.refs_2_, ...), custom_call_target="tpu_custom_call" | custom-call | flops 6442450944 | bytes 24117248 | tf_op jit(solution)/shard_map/feed_weights/pallas_call | solution.py:79
  243.9 0.0 reduce-scatter.5.cloned.1.call-update
  244.0 4.5 %second_norm_back.3 = (f32[256,1024]{1,0:T(8,128)}, bf16[256,1024]{1,0:T(8,128)(2,1)}, f32[2,1024]{1,0:T(2,128)}) custom-call(f32[1,1]{1,0:T(1,128)} %bitcast.12.refs_3_.weight_ref, f32[256,1024]{1,0:T(8,128)} %get-tuple-element.172.kept_ref, bf16[256,1024]{1,0:T(8,128)(2,1)} %bitcast.39, f32[256,1024]{1,0:T(8,128)} %get-tuple-element.196.middle_ref.refs_3_, ...), custom_call_target="tpu_custom_call" | custom-call | flops 10485760 | bytes 5283844 | tf_op jit(solution)/shard_map/second_norm_back/pallas_call | solution.py:79
  248.5 65.3 %attend_back.1 = (bf16[2,512,512]{2,1,0:T(8,128)(2,1)}, bf16[2,512,512]{2,1,0:T(8,128)(2,1)}, bf16[2,512,512]{2,1,0:T(8,128)(2,1)}, bf16[2,512,1024]{2,1,0:T(8,1...) custom-call(bf16[2,512,512]{2,1,0:T(8,128)(2,1)} %get-tuple-element.167.refs_0_, ...), custom_call_target="tpu_custom_call" | custom-call | flops 42949672960 | bytes 27787264 | tf_op jit(solution)/shard_map/attend_back/pallas_call | solution.py:79
  313.8 0.0 reduce-scatter.3.cloned.1.call-done.refs_8_
  313.8 54.6 %finish.1 = (f32[64,2048]{1,0:T(8,128)}, f32[8,128]{1,0:T(8,128)}, f32[2,256,1024]{2,1,0:T(8,128)}, bf16[64,3072]{1,0:T(8,128)(2,1)}) custom-call(bf16[2,512,512]{2,1,0:T(8,128)(2,1)} %get-tuple-element.182.refs_0_, bf16[2,512,512]{2,1,0:T(8,128)(2,1)} %get-tuple-element.183.refs_1_, bf16[2,512,512]{2,1,0:T(8,128)(2,1)} %get-tuple-element.184.refs_2_, ...), custom_call_target="tpu_custom_call" | custom-call | flops 7516192768 | bytes 19582976 | tf_op jit(solution)/shard_map/finish/pallas_call | solution.py:79
  368.4 0.0 reduce-scatter.5.cloned.1.call-done
  368.5 1.2 slice_select_fusion.2
  369.6 1.6 collective-permute-start.3
  371.3 1.9 slice_bitcast_fusion
  373.2 3.8 results.1
  376.9 0.1 convert_add_fusion.1
  377.1 0.5 slice_bitcast_fusion.1
  377.6 0.1 fusion.2
  377.7 0.9 collective-permute-done.3
  378.6 0.1 convert_add_fusion
  378.8 0.1 fusion.3
  378.8 0.8 maximum_bitcast_fusion
  379.6 0.8 pad_maximum_fusion.1
  380.5 0.8 pad_maximum_fusion
  381.3 1.3 copy.35
  (32 shorter events, 0.1 us)
Async XLA Ops:
  7.2 6.2 %copy-start.10 = (f32[850]{0:T(1024)S(1)}, f32[850]{0:T(1024)}, u32[]{:S(2)}) copy-start(f32[850]{0:T(1024)} %param.24) | copy-start | bytes 10204
  7.2 6.2 %copy-start.12 = (s32[2]{0:T(128)S(1)}, s32[2]{0:T(128)}, u32[]{:S(2)}) copy-start(s32[2]{0:T(128)} %param.22) | copy-start | bytes 28
  7.2 6.4 %copy-start.17 = (s32[2]{0:T(128)S(1)}, s32[2]{0:T(128)}, u32[]{:S(2)}) copy-start(s32[2]{0:T(128)} %param.23) | copy-start | bytes 28
  7.2 7.0 %copy-start.13 = (f32[32]{0:T(128)S(1)}, f32[32]{0:T(128)}, u32[]{:S(2)}) copy-start(f32[32]{0:T(128)} %param.32) | copy-start | bytes 388
  7.2 7.0 %copy-start.14 = (f32[32]{0:T(128)S(1)}, f32[32]{0:T(128)}, u32[]{:S(2)}) copy-start(f32[32]{0:T(128)} %param.31) | copy-start | bytes 388
  7.2 7.0 %copy-start.15 = (f32[32]{0:T(128)S(1)}, f32[32]{0:T(128)}, u32[]{:S(2)}) copy-start(f32[32]{0:T(128)} %param.26) | copy-start | bytes 388
  7.2 7.0 %copy-start.16 = (f32[32]{0:T(128)S(1)}, f32[32]{0:T(128)}, u32[]{:S(2)}) copy-start(f32[32]{0:T(128)} %param.25) | copy-start | bytes 388
  7.3 7.7 %copy-start.5 = (bf16[512,64]{0,1:T(8,128)(2,1)S(1)}, bf16[512,64]{0,1:T(8,128)(2,1)}, u32[]{:S(2)}) copy-start(bf16[512,64]{0,1:T(8,128)(2,1)} %param.30) | copy-start | bytes 196612
  7.3 7.7 %copy-start.6 = (bf16[64,512]{1,0:T(8,128)(2,1)S(1)}, bf16[64,512]{1,0:T(8,128)(2,1)}, u32[]{:S(2)}) copy-start(bf16[64,512]{1,0:T(8,128)(2,1)} %param.29) | copy-start | bytes 196612
  7.3 7.7 %copy-start.7 = (bf16[64,512]{1,0:T(8,128)(2,1)S(1)}, bf16[64,512]{1,0:T(8,128)(2,1)}, u32[]{:S(2)}) copy-start(bf16[64,512]{1,0:T(8,128)(2,1)} %param.28) | copy-start | bytes 196612
  7.3 7.7 %copy-start.8 = (bf16[64,512]{1,0:T(8,128)(2,1)S(1)}, bf16[64,512]{1,0:T(8,128)(2,1)}, u32[]{:S(2)}) copy-start(bf16[64,512]{1,0:T(8,128)(2,1)} %param.27) | copy-start | bytes 196612
  7.3 133.1 %all-gather.5.cloned.1.call-start = ((), (), s32[]{:S(2)}) async-start(), calls=%async_computation.3 | async-start | bytes 6684672 | tf_op jit(solution)/shard_map/all_gather | solution.py:1723
  10.3 150.8 %all-gather.3.cloned.1.call-start = ((), (), s32[]{:S(2)}) async-start(), calls=%async_computation.2 | async-start | bytes 7077888 | tf_op jit(solution)/shard_map/all_gather | solution.py:1718
  10.4 49.9 %collective-permute-start = (bf16[64,3072]{1,0:T(8,128)(2,1)S(1)}, bf16[64,3072]{1,0:T(8,128)(2,1)S(1)}, u32[]{:S(2)}, u32[]{:S(2)}) collective-permute-start(bf16[64,3072]{1,0:T(8,128)(2,1)S(1)} %pad_maximum_fusion.2), channel_id=1, source_target_pairs={{0,4},{4,0},{1,5},{5,1},{2,6},{6,2},{3,7},{7,3},{8,12},{12,8},{9,1... | collective-permute-start | bytes 1179656 | tf_op jit(solution)/shard_map/ppermute | solution.py:36
  15.0 0.8 copy-start.9
  61.5 252.3 %reduce-scatter.3.cloned.1.call-start = ((), (), s32[]{:S(2)}) async-start(), calls=%async_computation.4 | async-start | bytes 7077888 | tf_op jit(solution)/shard_map/reduce_scatter | solution.py:1759
  139.7 15.8 %collective-permute-start.1 = (bf16[256,1024]{1,0:T(8,128)(2,1)}, bf16[256,1024]{1,0:T(8,128)(2,1)S(1)}, u32[]{:S(2)}, u32[]{:S(2)}) collective-permute-start(bf16[256,1024]{1,0:T(8,128)(2,1)} %bitcast.49), channel_id=1, source_target_pairs={{0,1},{1,0},{2,3},{3,2},{4,5},{5,4},{6,7},{7,6},{8,9},{9,8},{10,11... | collective-permute-start | bytes 1572872 | tf_op jit(solution)/shard_map/ppermute | solution.py:36
  155.6 0.8 copy-start.3
  159.2 16.3 %collective-permute-start.2 = (bf16[256,1024]{1,0:T(8,128)(2,1)}, bf16[256,1024]{1,0:T(8,128)(2,1)S(1)}, u32[]{:S(2)}, u32[]{:S(2)}) collective-permute-start(bf16[256,1024]{1,0:T(8,128)(2,1)} %get-tuple-element.148.refs_5_), channel_id=1, source_target_pairs={{0,1},{1,0},{2,3},{3,2},{4,5},{5,4},{6,7},{7,6},{8,9},{9,8},{10,11... | collective-permute-start | bytes 1572872 | tf_op jit(solution)/shard_map/ppermute | solution.py:36
  175.5 0.8 copy-start.18
  206.9 161.5 %reduce-scatter.5.cloned.1.call-start = ((), (), s32[]{:S(2)}) async-start(), calls=%async_computation.5 | async-start | bytes 7077888 | tf_op jit(solution)/shard_map/reduce_scatter | solution.py:1759
  369.6 9.0 %collective-permute-start.3 = (bf16[64,3072]{1,0:T(8,128)(2,1)S(1)}, bf16[64,3072]{1,0:T(8,128)(2,1)S(1)}, u32[]{:S(2)}, u32[]{:S(2)}) collective-permute-start(bf16[64,3072]{1,0:T(8,128)(2,1)S(1)} %slice_select_fusion.2), channel_id=1, source_target_pairs={{0,4},{4,0},{1,5},{5,1},{2,6},{6,2},{3,7},{7,3},{8,12},{12,8},{9,1... | collective-permute-start | bytes 1179656 | tf_op jit(solution)/shard_map/ppermute | solution.py:36
  373.2 3.8 copy-start.2
  373.2 3.8 copy-start.4
  373.2 3.9 %copy-start.11 = (f32[8,128]{1,0:T(8,128)S(1)}, f32[8,128]{1,0:T(8,128)}, u32[]{:S(2)}) copy-start(f32[8,128]{1,0:T(8,128)} %get-tuple-element.199) | copy-start | bytes 12292
  376.9 1.7 copy-start
  378.7 2.6 copy-start.1
Sparse Core Ops, SparseCore 0:
  11.0 76.2 all-gather.4
  88.9 65.1 all-gather.2
  207.1 67.2 reduce-scatter.2
  276.5 76.8 reduce-scatter.4
